TPU v7x, 32 devices: a whole 2x2x4 slice. The times are simulated.
32 devices in a mesh: blk: 8 (over z, core), col: 4 (over y, x).
Axes of the slice: x: 2, y: 2, z: 4, core: 2. Of those that a mesh axis runs over, the one named last changes fastest.
Arguments:
- stiffness: bfloat16 [64, 3, 128, 128], P('blk'), may hold values from -0.3125 to 0.3125
- block_cols: int32 [64, 3], P('blk'), may hold values from 0 to 63, as said below
- basis: bfloat16 [8192, 3, 512], P('blk', None, 'col'), may hold values from -1.1953125 to 1.1953125
- patch_reach: int32 [8, 512, 2], P(None, 'col'), may hold values from 0 to 8
Outputs:
- coarse: float32 [4096, 5, 512], P(('blk', 'col'))
Inputs may be any that keep to these rules, and one draw needn't show every extreme that they name: `block_cols`: block row b lists block row b first and then two other distinct block rows among b - 2 .. b + 2 (periodic); the first block row of each slab lists b - 2 and b + 2.
All inputs are finite; a program needn't handle non-finite values.
Results may differ from a plain program's by a relative error of at most 0.0029.
Values may be sent and summed in bfloat16 or wider, within the bound.
No kernel may reach another device: no remote copies, remote signals or barrier semaphores. Data moves between devices by JAX's collectives and lax.ppermute only.
A program may use at most 64 MiB of HBM per device.

v0:
```python
import jax
import jax.numpy as jnp
from jax import lax
from jax.sharding import PartitionSpec as P


def extended_2(array, sides, width):
    for axis, dim in sides:
        peers, length = (lax.axis_size(axis), array.shape[dim])
        up = [(i, (i + 1) % peers) for i in range(peers)]
        down = [(j, i) for i, j in up]
        last = lax.slice_in_dim(array, length - width, length, axis=dim)
        leading = lax.slice_in_dim(array, 0, width, axis=dim)
        before = lax.ppermute(last, axis, up)
        after = lax.ppermute(leading, axis, down)
        array = jnp.concatenate([before, array, after], axis=dim)
    return array


def shifted(value, axis, steps):
    count = lax.axis_size(axis)
    pairs = [(source, (source + steps) % count) for source in range(count)]
    return lax.ppermute(value, axis, pairs)


def place_tile(tile, offset_pos):
    return jnp.pad(tile, ((0, 0), (offset_pos, 2 - offset_pos), (0, 0)))


def shards(stiffness, block_cols, basis, patch_reach):
    blocks = stiffness.shape[0]
    block_size = stiffness.shape[2]
    row_count = basis.shape[0]
    groups = basis.shape[1]
    local_cols = basis.shape[2]
    slab_count = lax.axis_size("blk")
    slab_index = lax.axis_index("blk")
    total_blocks = blocks * slab_count
    reach_low = lax.dynamic_index_in_dim(patch_reach, (slab_index - 1) % slab_count, 0, False)
    reach_high = lax.dynamic_index_in_dim(patch_reach, (slab_index + 1) % slab_count, 0, False)
    block_row = jnp.arange(row_count, dtype=jnp.int32) // block_size
    lower_mask = block_row[:, None] < reach_low[None, :, 1]
    upper_mask = block_row[:, None] >= blocks - reach_high[None, :, 0]
    support = jnp.stack([lower_mask, jnp.ones_like(lower_mask), upper_mask], 1)
    masked = jnp.where(support, basis, jnp.zeros_like(basis))
    rim_width = 2 * block_size
    padded = extended_2(masked, (("blk", 0),), rim_width)
    zero_rim = jnp.zeros((rim_width, 1, local_cols), masked.dtype)
    lower_rim = jnp.concatenate([padded[:rim_width, 1:], zero_rim], 1)
    upper_rim = jnp.concatenate([zero_rim, padded[rim_width + row_count :, :2]], 1)
    extended = jnp.concatenate([lower_rim, masked, upper_rim], 0)
    extended = extended.reshape(blocks + 4, block_size, groups * local_cols)
    position = (block_cols - slab_index * blocks + 2) % total_blocks
    picked = jnp.take(extended, position, axis=0)
    stiff_image = jnp.einsum(
        "rsij,rsjc->ric", stiffness, picked, preferred_element_type=jnp.float32
    )
    stiff_image = stiff_image.astype(jnp.bfloat16).reshape(row_count, groups, local_cols)
    tile_sums = jnp.einsum(
        "rgl,rhc->glhc",
        masked,
        lax.all_gather(stiff_image, "col", axis=2, tiled=True),
        preferred_element_type=jnp.float32,
    )
    from_prev = shifted(tile_sums[2], "blk", 1)
    from_next = shifted(tile_sums[0], "blk", -1)
    return place_tile(from_prev, 0) + place_tile(tile_sums[1], 1) + place_tile(from_next, 2)


def solution(mesh):
    in_specs = (
        P("blk", None, None, None),
        P("blk", None),
        P("blk", None, "col"),
        P(None, "col", None),
    )
    out_specs = P(("blk", "col"), None, None)
    return jax.shard_map(shards, mesh=mesh, in_specs=in_specs, out_specs=out_specs, check_vma=False)
```

profile of v0, /device:TPU:0, one launch (start us, length us, event | category | flops | bytes accessed | tf_op | source)
XLA Modules:
  0.0 117.1 jit_solution(4530870687081001309)
XLA Ops:
  6.6 0.7 dynamic-slice_bitcast_fusion.1
  7.3 0.2 broadcast_compare_fusion.1
  7.6 1.5 %add_select_fusion = bf16[1024,3,128]{2,0,1:T(8,128)(2,1)S(1)} fusion(bf16[1024,3,128]{2,0,1:T(8,128)(2,1)} %param.6, pred[1024,1,128]{2,0,1:T(8,128)(4,1)S(1)} %get-tuple-element.15, pred[1024,1,128]{2,0,1:T(8,128)(4,1)S(1)} %get-tuple-element.14, pred[3]{0:T(512)(128)(4,1)S(1)} %pad.21.clone), kind=kLoop, calls=%fused_computation.11 | loop fusion | flops 1179648 | bytes 1835011 | tf_op jit(solution)/shard_map/jit(_where)/select_n | solution.py:45
  9.1 0.5 collective-permute-start
  9.6 4.1 %collective-permute-start.1 = (bf16[256,3,128]{2,0,1:T(8,128)(2,1)S(1)}, bf16[256,3,128]{2,0,1:T(8,128)(2,1)S(1)}, u32[]{:S(2)}, u32[]{:S(2)}) collective-permute-start(bf16[256,3,128]{2,0,1:T(8,128)(2,1)S(1)} %get-tuple-element.11), channel_id=1, source_target_pairs={{4,0},{8,4},{12,8},{16,12},{20,16},{24,20},{28,24},{0,28},{5,1},{9... | collective-permute-start | bytes 589832 | tf_op jit(solution)/shard_map/ppermute | solution.py:15
  13.7 0.1 copy.8
  13.8 0.1 copy.10
  13.9 0.1 reshape.126
  14.0 3.1 %collective-permute-done = bf16[256,3,128]{2,0,1:T(8,128)(2,1)S(1)} collective-permute-done((bf16[256,3,128]{2,0,1:T(8,128)(2,1)S(1)}, bf16[256,3,128]{2,0,1:T(8,128)(2,1)S(1)}, u32[]{:S(2)}, u32[]{:S(2)}) %collective-permute-start) | collective-permute-done | bytes 196640 | tf_op jit(solution)/shard_map/ppermute | solution.py:14
  17.1 0.1 fusion.12
  17.2 8.3 %copy.20 = bf16[1536,3,128]{2,1,0:T(4,128)(2,1)} copy(bf16[1536,3,128]{2,0,1:T(8,128)(2,1)S(1)} %fusion.12) | data formatting | bytes 2359296 | tf_op jit(solution)/shard_map/reshape | solution.py:52
  25.4 3.4 %reshape.137 = bf16[12,128,384]{2,1,0:T(8,128)(2,1)S(1)} reshape(bf16[1536,3,128]{2,1,0:T(4,128)(2,1)} %copy.20) | data formatting | bytes 2359296 | tf_op jit(solution)/shard_map/reshape | solution.py:52
  28.8 2.4 %gather_fusion = bf16[24,128,384]{2,1,0:T(8,128)(2,1)} fusion(bf16[12,128,384]{2,1,0:T(8,128)(2,1)S(1)} %reshape.137, s32[1024]{0:T(1024)S(1)} %pad_clamp_fusion), kind=kCustom, calls=%fused_computation | custom fusion | bytes 4718688 | tf_op jit(solution)/shard_map/jit(_take)/gather | solution.py:54
  31.3 4.3 %copy.12 = bf16[8,3,128,384]{2,3,1,0:T(8,128)(2,1)} copy(bf16[8,3,128,384]{3,2,1,0:T(8,128)(2,1)} %bitcast.34) | data formatting | bytes 4718592 | tf_op jit(solution)/shard_map/jit(_take)/gather | solution.py:54
  35.6 2.5 %fusion.9 = bf16[8,128,384]{1,2,0:T(8,128)(2,1)S(1)} fusion(bf16[8,3,128,128]{3,2,1,0:T(8,128)(2,1)S(1)} %copy-done, bf16[8,3,128,384]{2,3,1,0:T(8,128)(2,1)} %copy.12, pred[8,3]{1,0:T(8,128)(4,1)S(1)} %copy.8), kind=kOutput, calls=%fused_computation.13 | convolution fusion | flops 303562752 | bytes 3932184 | tf_op jit(solution)/shard_map/rsij,rsjc->ric/dot_general | solution.py:55
  38.0 0.5 copy.13
  38.6 0.3 reshape.123
  38.9 1.2 copy.14
  40.1 45.6 %all-gather.2.cloned.1.call-done = bf16[1024,3,512]{2,0,1:T(8,128)(2,1)} async-done(((bf16[1024,3,128]{2,0,1:T(8,128)(2,1)}), bf16[1024,3,512]{2,0,1:T(8,128)(2,1)}) %all-gather.2.cloned.1.call-update) | async-done | bytes 3145744 | tf_op jit(solution)/shard_map/all_gather | solution.py:62
  85.7 3.3 %fusion = f32[3,128,3,512]{3,1,2,0:T(8,128)S(1)} fusion(bf16[1024,3,512]{2,0,1:T(8,128)(2,1)} %all-gather.2.cloned.1.call-done, bf16[1024,3,128]{2,0,1:T(8,128)(2,1)S(1)} %add_select_fusion), kind=kOutput, calls=%fused_computation.1 | convolution fusion | flops 1207959552 | bytes 6291456 | tf_op jit(solution)/shard_map/rgl,rhc->glhc/dot_general | solution.py:59
  89.0 0.2 slice_bitcast_fusion.2
  89.2 3.5 %collective-permute-start.3 = (f32[128,3,512]{2,0,1:T(8,128)S(1)}, f32[128,3,512]{2,0,1:T(8,128)S(1)}, u32[]{:S(2)}, u32[]{:S(2)}) collective-permute-start(f32[128,3,512]{2,0,1:T(8,128)S(1)} %get-tuple-element.8), channel_id=1, source_target_pairs={{0,28},{4,0},{8,4},{12,8},{16,12},{20,16},{24,20},{28,24},{1,29},{... | collective-permute-start | bytes 2359304 | tf_op jit(solution)/shard_map/ppermute | solution.py:23
  92.8 16.2 %collective-permute-done.2 = f32[128,3,512]{2,0,1:T(8,128)S(1)} collective-permute-done((f32[128,3,512]{2,0,1:T(8,128)S(1)}, f32[128,3,512]{2,0,1:T(8,128)S(1)}, u32[]{:S(2)}, u32[]{:S(2)}) %collective-permute-start.2) | collective-permute-done | bytes 786464 | tf_op jit(solution)/shard_map/ppermute | solution.py:23
  109.0 1.3 %pad_add_fusion = f32[128,5,512]{2,0,1:T(8,128)} fusion(f32[128,3,512]{2,0,1:T(8,128)S(1)} %collective-permute-done.3, f32[128,3,512]{2,0,1:T(8,128)S(1)} %get-tuple-element.9, f32[128,3,512]{2,0,1:T(8,128)S(1)} %collective-permute-done.2), kind=kLoop, calls=%fused_computation.12 | loop fusion | flops 655360 | bytes 3670016 | tf_op jit(solution)/shard_map/add | solution.py:67
  (17 shorter events, 0.2 us)
Async XLA Ops:
  6.5 29.0 %copy-start = (bf16[8,3,128,128]{3,2,1,0:T(8,128)(2,1)S(1)}, bf16[8,3,128,128]{3,2,1,0:T(8,128)(2,1)}, u32[]{:S(2)}) copy-start(bf16[8,3,128,128]{3,2,1,0:T(8,128)(2,1)} %param.4) | copy-start | bytes 2359300
  6.5 7.1 %copy-start.1 = (s32[8,3]{0,1:T(4,128)S(1)}, s32[8,3]{0,1:T(4,128)}, u32[]{:S(2)}) copy-start(s32[8,3]{0,1:T(4,128)} %param.5) | copy-start | bytes 292
  6.5 79.1 %all-gather.2.cloned.1.call-start = ((), (), s32[]{:S(2)}) async-start(), calls=%async_computation | async-start | bytes 3932160 | tf_op jit(solution)/shard_map/all_gather | solution.py:62
  9.1 8.0 %collective-permute-start = (bf16[256,3,128]{2,0,1:T(8,128)(2,1)S(1)}, bf16[256,3,128]{2,0,1:T(8,128)(2,1)S(1)}, u32[]{:S(2)}, u32[]{:S(2)}) collective-permute-start(bf16[256,3,128]{2,0,1:T(8,128)(2,1)S(1)} %get-tuple-element.10), channel_id=1, source_target_pairs={{0,4},{4,8},{8,12},{12,16},{16,20},{20,24},{24,28},{28,0},{1,5},{5... | collective-permute-start | bytes 589832 | tf_op jit(solution)/shard_map/ppermute | solution.py:14
  9.6 7.5 %collective-permute-start.1 = (bf16[256,3,128]{2,0,1:T(8,128)(2,1)S(1)}, bf16[256,3,128]{2,0,1:T(8,128)(2,1)S(1)}, u32[]{:S(2)}, u32[]{:S(2)}) collective-permute-start(bf16[256,3,128]{2,0,1:T(8,128)(2,1)S(1)} %get-tuple-element.11), channel_id=1, source_target_pairs={{4,0},{8,4},{12,8},{16,12},{20,16},{24,20},{28,24},{0,28},{5,1},{9... | collective-permute-start | bytes 589832 | tf_op jit(solution)/shard_map/ppermute | solution.py:15
  89.2 19.8 %collective-permute-start.2 = (f32[128,3,512]{2,0,1:T(8,128)S(1)}, f32[128,3,512]{2,0,1:T(8,128)S(1)}, u32[]{:S(2)}, u32[]{:S(2)}) collective-permute-start(f32[128,3,512]{2,0,1:T(8,128)S(1)} %get-tuple-element.7), channel_id=1, source_target_pairs={{0,4},{4,8},{8,12},{12,16},{16,20},{20,24},{24,28},{28,0},{1,5},{5... | collective-permute-start | bytes 2359304 | tf_op jit(solution)/shard_map/ppermute | solution.py:23
  89.2 19.7 %collective-permute-start.3 = (f32[128,3,512]{2,0,1:T(8,128)S(1)}, f32[128,3,512]{2,0,1:T(8,128)S(1)}, u32[]{:S(2)}, u32[]{:S(2)}) collective-permute-start(f32[128,3,512]{2,0,1:T(8,128)S(1)} %get-tuple-element.8), channel_id=1, source_target_pairs={{0,28},{4,0},{8,4},{12,8},{16,12},{20,16},{24,20},{28,24},{1,29},{... | collective-permute-start | bytes 2359304 | tf_op jit(solution)/shard_map/ppermute | solution.py:23
Sparse Core Ops, SparseCore 0:
  40.2 45.4 all-gather.1
where the time goes:
time: 119 us; the launch traced here: 117 us
  waiting for transfers between devices  64.9 us (55%)
  local copies, waits for them, and re-layouts  21.6 us (18%)
  between operations  13.5 us (11%)
  starting transfers between devices  8.2 us (7%)
  matrix products  5.78 us (5%)
  other arithmetic  3.1 us (3%)
    all_gather x1, waiting for transfers between devices, shards(): lax.all_gather(stiff_image, 'col', axis=2, tiled=True)  45.6 us
    ppermute x2, waiting for transfers between devices, shifted(): return lax.ppermute(value, axis, pairs)  16.2 us
    reshape x2, local copies, waits for them, and re-layouts, shards(): extended = extended.reshape(blocks + 4, block_size, groups * local_cols)  11.6 us
    gather x2, local copies, waits for them, and re-layouts, shards(): picked = jnp.take(extended, position, axis=0)  6.73 us
    ppermute x1, starting transfers between devices, extended_2(): after = lax.ppermute(leading, axis, down)  4.1 us
    ppermute x2, starting transfers between devices, shifted(): return lax.ppermute(value, axis, pairs)  3.59 us
    dot_general x1, matrix products, shards(): jnp.einsum('rgl,rhc->glhc', masked, lax.all_gather(stiff_image, 'col', ax...  3.29 us
    ppermute x1, waiting for transfers between devices, extended_2(): before = lax.ppermute(last, axis, up)  3.11 us
  transfers between devices with their start and end apart: 5, of which 3 were waited for; matrix products, arithmetic and copies ran while one was open for 0% of the time, Pallas kernels for 0%

commit v1 on v0

v1 whole, which is shorter than its diff:
```python
import functools

import jax
import jax.numpy as jnp
from jax import lax
from jax.experimental import pallas as pl
from jax.experimental.pallas import tpu as pltpu
from jax.sharding import PartitionSpec as P

BF16 = jnp.bfloat16
F32 = jnp.float32
VMEM = pl.BlockSpec(memory_space=pltpu.VMEM)
SMEM = pl.BlockSpec(memory_space=pltpu.SMEM)
HBM = pl.BlockSpec(memory_space=pl.ANY)
RIM = 2


def shape(dims, dtype):
    return jax.ShapeDtypeStruct(dims, dtype)


def dot(left, right):
    return jnp.dot(left, right, preferred_element_type=F32)


def call(kernel, out_shape, in_specs, out_specs, args, scratch=(), flops=0, aliases=None, name=None):
    outs = jax.tree.leaves(out_shape)
    moved = sum(x.size * x.dtype.itemsize for x in (*args, *outs))
    return pl.pallas_call(
        kernel,
        out_shape=out_shape,
        in_specs=in_specs,
        out_specs=out_specs,
        scratch_shapes=list(scratch),
        input_output_aliases=aliases or {},
        cost_estimate=pl.CostEstimate(flops=flops, bytes_accessed=moved, transcendentals=0),
        compiler_params=pltpu.CompilerParams(vmem_limit_bytes=24 << 20),
        name=name,
    )(*args)


def block_image(stiffness, source, b, block_size, starts):
    blocks = [source[pl.ds(pl.multiple_of(start * block_size, block_size), block_size), :] for start in starts]
    left = jnp.concatenate([stiffness[b, k] for k in range(len(starts))], axis=1)
    return dot(left, jnp.concatenate(blocks, axis=0)).astype(BF16)


def positions(cols, b, blocks, slots, total_blocks):
    first = lax.axis_index("blk") * blocks
    return [
        jnp.clip(lax.rem(cols[k, b] - first + RIM + total_blocks, total_blocks), 0, blocks + 2 * RIM - 1)
        for k in range(slots)
    ]


def mask_and_inner(total_blocks, cols, basis, reach, stiffness, masked, to_next, to_prev, inner):
    blocks, slots, size, _ = stiffness.shape
    groups, _, width = basis.shape
    slabs = reach.shape[0]
    slab = lax.axis_index("blk")
    low = reach[pl.ds(lax.rem(slab + slabs - 1, slabs), 1), 1, :]
    high = reach[pl.ds(lax.rem(slab + 1, slabs), 1), 0, :]
    for b in range(blocks):
        rows = slice(b * size, (b + 1) * size)
        keep = {0: (b < low).astype(F32).astype(BF16), 2: (b >= blocks - high).astype(F32).astype(BF16)}
        for g in range(groups):
            value = basis[g, rows, :]
            masked[rows, g * width : (g + 1) * width] = value * keep[g] if g in keep else value
    to_next[...] = masked[(blocks - RIM) * size :, width:]
    to_prev[...] = masked[: RIM * size, : 2 * width]
    for b in range(RIM, blocks - RIM):
        starts = [jnp.clip(p - RIM, 0, blocks - 1) for p in positions(cols, b, blocks, slots, total_blocks)]
        inner[(b - RIM) * size : (b - RIM + 1) * size, :] = block_image(stiffness, masked, b, size, starts)


def outer_image(total_blocks, cols, stiffness, masked, from_prev, from_next, outer, extended):
    blocks, slots, size, _ = stiffness.shape
    rows, wide = masked.shape
    rim = RIM * size
    width = wide // 3
    extended[:rim, : 2 * width] = from_prev[...]
    extended[:rim, 2 * width :] = jnp.zeros((rim, width), BF16)
    extended[rim : rim + rows, :] = masked[...]
    extended[rim + rows :, :width] = jnp.zeros((rim, width), BF16)
    extended[rim + rows :, width:] = from_next[...]
    for n, b in enumerate([*range(RIM), *range(blocks - RIM, blocks)]):
        starts = positions(cols, b, blocks, slots, total_blocks)
        outer[n * size : (n + 1) * size, :] = block_image(stiffness, extended, b, size, starts)


def store_tile(tile, own, up, down, n):
    width = own.shape[1]
    down[n] = tile[:width].astype(BF16)
    own[n] = tile[width : 2 * width]
    up[n] = tile[2 * width :].astype(BF16)


def own_tile(size, masked, inner, outer, own, up, down, left_inner, left_outer):
    rows = masked.shape[0]
    rim = RIM * size
    left_inner[...] = masked[rim : rows - rim, :].T
    left_outer[:, :rim] = masked[:rim, :].T
    left_outer[:, rim:] = masked[rows - rim :, :].T
    tile = dot(left_inner[...], inner[...]) + dot(left_outer[...], outer[...])
    store_tile(tile, own, up, down, 0)


def other_tiles(count, left_inner, left_outer, *refs):
    images, (own, up, down) = refs[: 2 * count], refs[2 * count :]
    for n in range(count):
        tile = dot(left_inner[...], images[2 * n][...]) + dot(left_outer[...], images[2 * n + 1][...])
        store_tile(tile, own, up, down, n)


def add_tiles(sources, *refs):
    count = len(sources)
    terms, refs = refs[: 3 * count], refs[3 * count :]
    coarse, total, sem = refs[-3:]
    width = total.shape[2]
    me = lax.axis_index("col")
    copies = []
    n = 0
    for group, source in enumerate(sources):
        own, prev, nxt = terms[3 * group : 3 * group + 3]
        for m, step in enumerate(source):
            for d in range(5):
                value = None
                for offset, ref in ((0, prev), (1, own), (2, nxt)):
                    if 0 <= d - offset <= 2:
                        lanes = slice((d - offset) * width, (d - offset + 1) * width)
                        term = ref[m, :, lanes].astype(F32)
                        value = term if value is None else value + term
                total[n, d] = value
            start = pl.multiple_of(lax.bitwise_xor(me, step) * width, width)
            copy = pltpu.make_async_copy(total.at[n], coarse.at[:, :, pl.ds(start, width)], sem.at[n])
            copy.start()
            copies.append(copy)
            n += 1
    for copy in copies:
        copy.wait()


def tile_shapes(count, width, wide):
    return (
        shape((count, width, wide), F32),
        shape((count, width, wide), BF16),
        shape((count, width, wide), BF16),
    )


def shards(stiffness, block_cols, basis, patch_reach):
    blocks, slots, size, _ = stiffness.shape
    rows, groups, width = basis.shape
    wide = groups * width
    slabs = lax.axis_size("blk")
    total_blocks = blocks * slabs
    ring = [(i, (i + 1) % slabs) for i in range(slabs)]
    back = [(j, i) for i, j in ring]

    def to_next(value):
        return lax.ppermute(value, "blk", ring)

    def to_prev(value):
        return lax.ppermute(value, "blk", back)

    def swap(value, step):
        return lax.ppermute(value, "col", [(i, i ^ step) for i in range(4)])

    cols = block_cols.T
    flat = basis.transpose(1, 0, 2)
    reach = patch_reach.transpose(0, 2, 1)
    inner_rows = (blocks - 2 * RIM) * size
    rim = RIM * size
    row_flops = 2 * slots * size * size * wide
    masked, last, leading, inner = call(
        functools.partial(mask_and_inner, total_blocks),
        (shape((rows, wide), BF16), shape((rim, 2 * width), BF16), shape((rim, 2 * width), BF16), shape((inner_rows, wide), BF16)),
        [SMEM, VMEM, VMEM, VMEM],
        [VMEM] * 4,
        (cols, flat, reach, stiffness),
        flops=row_flops * (blocks - 2 * RIM),
        name="mask_and_inner",
    )
    inner_x = swap(inner, 1)
    inner_y = swap(inner, 2)
    before = to_next(last)
    after = to_prev(leading)
    outer = call(
        functools.partial(outer_image, total_blocks),
        shape((2 * rim, wide), BF16),
        [SMEM] + [VMEM] * 4,
        VMEM,
        (cols, stiffness, masked, before, after),
        scratch=[pltpu.VMEM((rows + 2 * rim, wide), BF16)],
        flops=row_flops * 2 * RIM,
        name="outer_image",
    )
    outer_x = swap(outer, 1)
    outer_y = swap(outer, 2)
    tile_flops = 2 * rows * wide * wide
    own_a, up_a, down_a, left_inner, left_outer = call(
        functools.partial(own_tile, size),
        (*tile_shapes(1, width, wide), shape((wide, inner_rows), BF16), shape((wide, 2 * rim), BF16)),
        [VMEM] * 3,
        [VMEM] * 5,
        (masked, inner, outer),
        flops=tile_flops,
        name="own_tile",
    )
    prev_a = to_next(up_a)
    next_a = to_prev(down_a)
    inner_d = swap(inner_x, 2)
    outer_d = swap(outer_y, 1)

    def tiles(images, name):
        count = len(images) // 2
        return call(
            functools.partial(other_tiles, count),
            tile_shapes(count, width, wide),
            [VMEM] * (2 + 2 * count),
            [VMEM] * 3,
            (left_inner, left_outer, *images),
            flops=tile_flops * count,
            name=name,
        )

    own_b, up_b, down_b = tiles((inner_x, outer_x, inner_y, outer_y), "side_tiles")
    prev_b = to_next(up_b)
    next_b = to_prev(down_b)
    own_c, up_c, down_c = tiles((inner_d, outer_d), "diagonal_tile")
    prev_c = to_next(up_c)
    next_c = to_prev(down_c)

    def add(sources, terms, name, base=None):
        count = sum(map(len, sources))
        extra = () if base is None else (base,)
        return call(
            functools.partial(add_tiles, sources),
            shape((5, width, 4 * width), F32),
            [VMEM] * len(terms) + [HBM] * len(extra),
            HBM,
            (*terms, *extra),
            scratch=[pltpu.VMEM((count, 5, width, width), F32), pltpu.SemaphoreType.DMA((count,))],
            flops=5 * count * width * width,
            aliases={len(terms): 0} if extra else None,
            name=name,
        )

    coarse = add(((0,), (1, 2)), (own_a, prev_a, next_a, own_b, prev_b, next_b), "add_near")
    coarse = add(((3,),), (own_c, prev_c, next_c), "add_diagonal", coarse)
    return coarse.transpose(1, 0, 2)


def gathered(stiffness, block_cols, basis, patch_reach):
    blocks, slots, size, _ = stiffness.shape
    rows, groups, width = basis.shape
    slabs = lax.axis_size("blk")
    slab = lax.axis_index("blk")
    total_blocks = blocks * slabs
    ring = [(i, (i + 1) % slabs) for i in range(slabs)]
    back = [(j, i) for i, j in ring]
    low = lax.dynamic_index_in_dim(patch_reach, (slab - 1) % slabs, 0, False)[:, 1]
    high = lax.dynamic_index_in_dim(patch_reach, (slab + 1) % slabs, 0, False)[:, 0]
    block_row = jnp.arange(rows, dtype=jnp.int32) // size
    lower = block_row[:, None] < low[None, :]
    upper = block_row[:, None] >= blocks - high[None, :]
    support = jnp.stack([lower, jnp.ones_like(lower), upper], 1)
    masked = jnp.where(support, basis, jnp.zeros_like(basis))
    rim = RIM * size
    before = lax.ppermute(masked[rows - rim :, 1:], "blk", ring)
    after = lax.ppermute(masked[:rim, :2], "blk", back)
    none = jnp.zeros((rim, 1, width), masked.dtype)
    extended = jnp.concatenate(
        [jnp.concatenate([before, none], 1), masked, jnp.concatenate([none, after], 1)], 0
    ).reshape(blocks + 2 * RIM, size, groups * width)
    position = (block_cols - slab * blocks + RIM) % total_blocks
    picked = jnp.take(extended, position, axis=0)
    image = jnp.einsum("rsij,rsjc->ric", stiffness, picked, preferred_element_type=F32)
    image = image.astype(BF16).reshape(rows, groups, width)
    image = lax.all_gather(image, "col", axis=2, tiled=True)
    tiles = jnp.einsum("rgl,rhc->glhc", masked, image, preferred_element_type=F32)
    from_prev = lax.ppermute(tiles[2], "blk", ring)
    from_next = lax.ppermute(tiles[0], "blk", back)

    def place(tile, offset):
        return jnp.pad(tile, ((0, 0), (offset, 2 - offset), (0, 0)))

    return place(from_prev, 0) + place(tiles[1], 1) + place(from_next, 2)


def solution(mesh):
    in_specs = (
        P("blk", None, None, None),
        P("blk", None),
        P("blk", None, "col"),
        P(None, "col", None),
    )
    out_specs = P(("blk", "col"), None, None)
    body = shards if mesh.shape["col"] == 4 else gathered
    return jax.shard_map(body, mesh=mesh, in_specs=in_specs, out_specs=out_specs, check_vma=False)
```

time: 119 us -> 51.2 us (0.43); the launches traced: 117 us -> 51 us
  waiting for transfers between devices: 64.9 us -> 17.1 us
  local copies, waits for them, and re-layouts: 21.6 us -> 3.65 us
  starting transfers between devices: 8.2 us -> 24 us
  between operations: 13.5 us -> 0.08 us
  Pallas kernels: 0 us -> 6.14 us
  matrix products: 5.78 us -> 0 us
  other arithmetic: 3.1 us -> 0 us
    all_gather x1 -> x0, waiting for transfers between devices: 45.6 us -> none  [shards(): lax.all_gather(stiff_image, 'col', axis=2, tiled=True)]
    ppermute x4 -> x14, starting transfers between devices: 8.2 us -> 24 us  [the longest x4 12 us: to_prev(): return lax.ppermute(value, 'blk', back)]
    reshape x4 -> x0, local copies, waits for them, and re-layouts: 13.1 us -> none  [the longest x2 11.6 us: shards(): extended = extended.reshape(blocks + 4, block_size, groups * local_cols)]
    gather x2 -> x0, local copies, waits for them, and re-layouts: 6.73 us -> none  [shards(): picked = jnp.take(extended, position, axis=0)]
    pallas_call x0 -> x7, Pallas kernels: none -> 6.14 us  [call(): pl.pallas_call(kernel, out_shape=out_shape, in_specs=in_specs, out_specs=...]
    dot_general x2 -> x0, matrix products: 5.78 us -> none  [the longest x1 3.29 us: shards(): jnp.einsum('rgl,rhc->glhc', masked, lax.all_gather(stiff_image, 'col', ax...]
    unnamed x4 -> x10, local copies, waits for them, and re-layouts: 0.01 us -> 3.65 us
    ppermute x4 -> x14, waiting for transfers between devices: 19.3 us -> 17.1 us  [the longest x6 15.1 us: swap(): return lax.ppermute(value, 'col', [(i, i ^ step) for i in range(4)])]
  transfers between devices with their start and end apart: 5 -> 14, of which waited for: 3 -> 6; matrix products, arithmetic and copies ran while one was open for 0% -> 0% of each run, Pallas kernels for 0% -> 8%
where the time goes in v1:
time: 51.2 us; the launch traced here: 51 us
  starting transfers between devices  24 us (47%)
  waiting for transfers between devices  17.1 us (33%)
  Pallas kernels  6.14 us (12%)
  local copies, waits for them, and re-layouts  3.65 us (7%)
    ppermute x6, waiting for transfers between devices, swap(): return lax.ppermute(value, 'col', [(i, i ^ step) for i in range(4)])  15.1 us
    ppermute x4, starting transfers between devices, to_prev(): return lax.ppermute(value, 'blk', back)  12 us
    ppermute x6, starting transfers between devices, swap(): return lax.ppermute(value, 'col', [(i, i ^ step) for i in range(4)])  9.85 us
    pallas_call x7, Pallas kernels, call(): pl.pallas_call(kernel, out_shape=out_shape, in_specs=in_specs, out_specs=...  6.14 us
    unnamed x10, local copies, waits for them, and re-layouts  3.65 us
    ppermute x4, starting transfers between devices, to_next(): return lax.ppermute(value, 'blk', ring)  2.09 us
    ppermute x4, waiting for transfers between devices, to_next(): return lax.ppermute(value, 'blk', ring)  2.04 us
  transfers between devices with their start and end apart: 14, of which 6 were waited for; matrix products, arithmetic and copies ran while one was open for 0% of the time, Pallas kernels for 8%

profile of v1, /device:TPU:0, one launch (start us, length us, event | category | flops | bytes accessed | tf_op | source)
XLA Modules:
  0.0 51.0 jit_solution(111623374819248685)
XLA Ops:
  0.0 1.1 %copy-done = bf16[8,3,128,128]{3,2,1,0:T(8,128)(2,1)S(1)} copy-done((bf16[8,3,128,128]{3,2,1,0:T(8,128)(2,1)S(1)}, bf16[8,3,128,128]{3,2,1,0:T(8,128)(2,1)}, u32[]{:S(2)}) %copy-start) | copy-done | bytes 786456
  1.1 1.1 %copy-done.2 = bf16[1024,3,128]{2,0,1:T(8,128)(2,1)S(1)} copy-done((bf16[1024,3,128]{2,0,1:T(8,128)(2,1)S(1)}, bf16[1024,3,128]{2,0,1:T(8,128)(2,1)}, u32[]{:S(2)}) %copy-start.2) | copy-done | bytes 786456
  2.3 0.7 %copy-done.3 = s32[8,128,2]{1,2,0:T(2,128)S(1)} copy-done((s32[8,128,2]{1,2,0:T(2,128)S(1)}, s32[8,128,2]{1,2,0:T(2,128)}, u32[]{:S(2)}) %copy-start.3) | copy-done | bytes 8216
  3.6 1.1 %mask_and_inner.1 = (bf16[1024,384]{1,0:T(8,128)(2,1)S(1)}, bf16[256,256]{1,0:T(8,128)(2,1)S(1)}, bf16[256,256]{1,0:T(8,128)(2,1)S(1)}, bf16[512,384]{1,0:T(8,128)(2,1)S(1)}) custom-call(s32[3,8]{1,0:T(4,128)S(1)} %bitcast.6, bf16[3,1024,128]{2,1,0:T(8,128)(2,1)S(1)} %bitcast.4, s32[8,2,128]{2,1,0:T(2,128)S(1)} %bitcast.5, bf16[8,3,128,128]{3,2,1,0:T(8,128)(2,1)S(1)} %copy-done), custom_call_target="tpu_custom_call" | custom-call | flops 150994944 | bytes 3022944 | tf_op jit(solution)/shard_map/mask_and_inner/pallas_call | solution.py:29
  5.3 4.1 %collective-permute-start.1 = (bf16[256,256]{1,0:T(8,128)(2,1)S(1)}, bf16[256,256]{1,0:T(8,128)(2,1)S(1)}, u32[]{:S(2)}, u32[]{:S(2)}) collective-permute-start(bf16[256,256]{1,0:T(8,128)(2,1)S(1)} %get-tuple-element.23), channel_id=1, source_target_pairs={{4,0},{8,4},{12,8},{16,12},{20,16},{24,20},{28,24},{0,28},{5,1},{9... | collective-permute-start | bytes 393224 | tf_op jit(solution)/shard_map/ppermute | solution.py:164
  9.4 1.9 %collective-permute-start.2 = (bf16[512,384]{1,0:T(8,128)(2,1)S(1)}, bf16[512,384]{1,0:T(8,128)(2,1)S(1)}, u32[]{:S(2)}, u32[]{:S(2)}) collective-permute-start(bf16[512,384]{1,0:T(8,128)(2,1)S(1)} %get-tuple-element.21.inner), channel_id=1, source_target_pairs={{0,1},{1,0},{2,3},{3,2},{4,5},{5,4},{6,7},{7,6},{8,9},{9,8},{10,11... | collective-permute-start | bytes 1179656 | tf_op jit(solution)/shard_map/ppermute | solution.py:167
  11.3 0.7 %collective-permute-done.from_prev = bf16[256,256]{1,0:T(8,128)(2,1)S(1)} collective-permute-done((bf16[256,256]{1,0:T(8,128)(2,1)S(1)}, bf16[256,256]{1,0:T(8,128)(2,1)S(1)}, u32[]{:S(2)}, u32[]{:S(2)}) %collective-permute-start) | collective-permute-done | bytes 131104 | tf_op jit(solution)/shard_map/ppermute | solution.py:161
  12.1 1.1 %outer_image.1.outer = bf16[512,384]{1,0:T(8,128)(2,1)S(1)} custom-call(s32[3,8]{1,0:T(4,128)S(1)} %bitcast.7, bf16[8,3,128,128]{3,2,1,0:T(8,128)(2,1)S(1)} %copy-done.1, bf16[1024,384]{1,0:T(8,128)(2,1)S(1)} %get-tuple-element.20.masked, bf16[256,256]{1,0:T(8,128)(2,1)S(1)} %collective-permute-done.from_prev, ...), custom_call_target="tpu_custom_call" | custom-call | flops 150994944 | bytes 2228320 | tf_op jit(solution)/shard_map/outer_image/pallas_call | solution.py:29
  13.2 2.1 %collective-permute-start.4 = (bf16[512,384]{1,0:T(8,128)(2,1)S(1)}, bf16[512,384]{1,0:T(8,128)(2,1)S(1)}, u32[]{:S(2)}, u32[]{:S(2)}) collective-permute-start(bf16[512,384]{1,0:T(8,128)(2,1)S(1)} %outer_image.1.outer), channel_id=1, source_target_pairs={{0,2},{1,3},{2,0},{3,1},{4,6},{5,7},{6,4},{7,5},{8,10},{9,11},{10,... | collective-permute-start | bytes 1179656 | tf_op jit(solution)/shard_map/ppermute | solution.py:167
  15.4 1.9 %collective-permute-start.10 = (bf16[512,384]{1,0:T(8,128)(2,1)S(1)}, bf16[512,384]{1,0:T(8,128)(2,1)S(1)}, u32[]{:S(2)}, u32[]{:S(2)}) collective-permute-start(bf16[512,384]{1,0:T(8,128)(2,1)S(1)} %outer_image.1.outer), channel_id=1, source_target_pairs={{0,1},{1,0},{2,3},{3,2},{4,5},{5,4},{6,7},{7,6},{8,9},{9,8},{10,11... | collective-permute-start | bytes 1179656 | tf_op jit(solution)/shard_map/ppermute | solution.py:167
  17.3 1.7 %collective-permute-done.2.refs_0_ = bf16[512,384]{1,0:T(8,128)(2,1)S(1)} collective-permute-done((bf16[512,384]{1,0:T(8,128)(2,1)S(1)}, bf16[512,384]{1,0:T(8,128)(2,1)S(1)}, u32[]{:S(2)}, u32[]{:S(2)}) %collective-permute-start.2) | collective-permute-done | bytes 393248 | tf_op jit(solution)/shard_map/ppermute | solution.py:167
  19.0 1.5 %collective-permute-start.3 = (bf16[512,384]{1,0:T(8,128)(2,1)S(1)}, bf16[512,384]{1,0:T(8,128)(2,1)S(1)}, u32[]{:S(2)}, u32[]{:S(2)}) collective-permute-start(bf16[512,384]{1,0:T(8,128)(2,1)S(1)} %collective-permute-done.2.refs_0_), channel_id=1, source_target_pairs={{0,2},{1,3},{2,0},{3,1},{4,6},{5,7},{6,4},{7,5},{8,10},{9,11},{10,... | collective-permute-start | bytes 1179656 | tf_op jit(solution)/shard_map/ppermute | solution.py:167
  20.5 4.0 %collective-permute-done.4.refs_3_ = bf16[512,384]{1,0:T(8,128)(2,1)S(1)} collective-permute-done((bf16[512,384]{1,0:T(8,128)(2,1)S(1)}, bf16[512,384]{1,0:T(8,128)(2,1)S(1)}, u32[]{:S(2)}, u32[]{:S(2)}) %collective-permute-start.4) | collective-permute-done | bytes 393248 | tf_op jit(solution)/shard_map/ppermute | solution.py:167
  24.6 2.3 %collective-permute-start.5 = (bf16[512,384]{1,0:T(8,128)(2,1)S(1)}, bf16[512,384]{1,0:T(8,128)(2,1)S(1)}, u32[]{:S(2)}, u32[]{:S(2)}) collective-permute-start(bf16[512,384]{1,0:T(8,128)(2,1)S(1)} %collective-permute-done.4.refs_3_), channel_id=1, source_target_pairs={{0,1},{1,0},{2,3},{3,2},{4,5},{5,4},{6,7},{7,6},{8,9},{9,8},{10,11... | collective-permute-start | bytes 1179656 | tf_op jit(solution)/shard_map/ppermute | solution.py:167
  27.5 5.5 %collective-permute-done.11.refs_2_ = bf16[512,384]{1,0:T(8,128)(2,1)S(1)} collective-permute-done((bf16[512,384]{1,0:T(8,128)(2,1)S(1)}, bf16[512,384]{1,0:T(8,128)(2,1)S(1)}, u32[]{:S(2)}, u32[]{:S(2)}) %collective-permute-start.11) | collective-permute-done | bytes 393248 | tf_op jit(solution)/shard_map/ppermute | solution.py:167
  33.0 1.0 %side_tiles.1 = (f32[2,128,384]{2,1,0:T(8,128)S(1)}, bf16[2,128,384]{2,1,0:T(8,128)(2,1)S(1)}, bf16[2,128,384]{2,1,0:T(8,128)(2,1)S(1)}) custom-call(bf16[384,512]{1,0:T(8,128)(2,1)S(1)} %get-tuple-element.24.left_inner, bf16[384,512]{1,0:T(8,128)(2,1)S(1)} %get-tuple-element.25.left_outer, bf16[512,384]{1,0:T(8,128)(2,1)S(1)} %collective-permute-done.2.refs_0_, ...), custom_call_target="tpu_custom_call" | custom-call | flops 603979776 | bytes 3145728 | tf_op jit(solution)/shard_map/side_tiles/pallas_call | solution.py:29
  34.0 1.5 %collective-permute-start.12 = (bf16[2,128,384]{2,1,0:T(8,128)(2,1)S(1)}, bf16[2,128,384]{2,1,0:T(8,128)(2,1)S(1)}, u32[]{:S(2)}, u32[]{:S(2)}) collective-permute-start(bf16[2,128,384]{2,1,0:T(8,128)(2,1)S(1)} %get-tuple-element.33), channel_id=1, source_target_pairs={{0,4},{4,8},{8,12},{12,16},{16,20},{20,24},{24,28},{28,0},{1,5},{5... | collective-permute-start | bytes 589832 | tf_op jit(solution)/shard_map/ppermute | solution.py:161
  35.5 2.1 %collective-permute-start.13 = (bf16[2,128,384]{2,1,0:T(8,128)(2,1)S(1)}, bf16[2,128,384]{2,1,0:T(8,128)(2,1)S(1)}, u32[]{:S(2)}, u32[]{:S(2)}) collective-permute-start(bf16[2,128,384]{2,1,0:T(8,128)(2,1)S(1)} %get-tuple-element.34), channel_id=1, source_target_pairs={{4,0},{8,4},{12,8},{16,12},{20,16},{24,20},{28,24},{0,28},{5,1},{9... | collective-permute-start | bytes 589832 | tf_op jit(solution)/shard_map/ppermute | solution.py:164
  37.6 3.8 %collective-permute-done.3.refs_0_ = bf16[512,384]{1,0:T(8,128)(2,1)S(1)} collective-permute-done((bf16[512,384]{1,0:T(8,128)(2,1)S(1)}, bf16[512,384]{1,0:T(8,128)(2,1)S(1)}, u32[]{:S(2)}, u32[]{:S(2)}) %collective-permute-start.3) | collective-permute-done | bytes 393248 | tf_op jit(solution)/shard_map/ppermute | solution.py:167
  41.4 2.3 %collective-permute-start.9 = (bf16[1,128,384]{2,1,0:T(8,128)(2,1)S(1)}, bf16[1,128,384]{2,1,0:T(8,128)(2,1)S(1)}, u32[]{:S(2)}, u32[]{:S(2)}) collective-permute-start(bf16[1,128,384]{2,1,0:T(8,128)(2,1)S(1)} %get-tuple-element.31), channel_id=1, source_target_pairs={{4,0},{8,4},{12,8},{16,12},{20,16},{24,20},{28,24},{0,28},{5,1},{9... | collective-permute-start | bytes 294920 | tf_op jit(solution)/shard_map/ppermute | solution.py:164
  44.4 3.5 %collective-permute-start.7 = (bf16[1,128,384]{2,1,0:T(8,128)(2,1)S(1)}, bf16[1,128,384]{2,1,0:T(8,128)(2,1)S(1)}, u32[]{:S(2)}, u32[]{:S(2)}) collective-permute-start(bf16[1,128,384]{2,1,0:T(8,128)(2,1)S(1)} %get-tuple-element.28), channel_id=1, source_target_pairs={{4,0},{8,4},{12,8},{16,12},{20,16},{24,20},{28,24},{0,28},{5,1},{9... | collective-permute-start | bytes 294920 | tf_op jit(solution)/shard_map/ppermute | solution.py:164
  47.9 1.0 %add_near.1.refs_3_ = f32[5,128,512]{2,1,0:T(8,128)} custom-call(f32[1,128,384]{2,1,0:T(8,128)S(1)} %get-tuple-element.29.refs_0_, bf16[1,128,384]{2,1,0:T(8,128)(2,1)S(1)} %collective-permute-done.8.refs_1_, bf16[1,128,384]{2,1,0:T(8,128)(2,1)S(1)} %collective-permute-done.9.refs_2_, f32[2,128,384]{2,1,0:T(8,128)S(1)} %get-tuple-element.32.refs_3_, ...), custom_call_target="tpu_custom_call" | custom-call | flops 245760 | bytes 2490368 | tf_op jit(solution)/shard_map/add_near/pallas_call | solution.py:29
  48.9 1.3 %collective-permute-done.6.refs_1_ = bf16[1,128,384]{2,1,0:T(8,128)(2,1)S(1)} collective-permute-done((bf16[1,128,384]{2,1,0:T(8,128)(2,1)S(1)}, bf16[1,128,384]{2,1,0:T(8,128)(2,1)S(1)}, u32[]{:S(2)}, u32[]{:S(2)}) %collective-permute-start.6) | collective-permute-done | bytes 98336 | tf_op jit(solution)/shard_map/ppermute | solution.py:161
  50.2 0.8 %add_diagonal.1 = f32[5,128,512]{2,1,0:T(8,128)} custom-call(f32[1,128,384]{2,1,0:T(8,128)S(1)} %get-tuple-element.26.refs_0_, bf16[1,128,384]{2,1,0:T(8,128)(2,1)S(1)} %collective-permute-done.6.refs_1_, bf16[1,128,384]{2,1,0:T(8,128)(2,1)S(1)} %collective-permute-done.7.refs_2_, f32[5,128,512]{2,1,0:T(8,128)} %add_near.1.refs_3_), custom_call_target="tpu_custom_call", output_to_operand_aliasing={{}: (3, {})} | custom-call | flops 81920 | bytes 3014656 | tf_op jit(solution)/shard_map/add_diagonal/pallas_call | solution.py:29
  (21 shorter events, 2.5 us)
Async XLA Ops:
  0.0 1.1 %copy-start = (bf16[8,3,128,128]{3,2,1,0:T(8,128)(2,1)S(1)}, bf16[8,3,128,128]{3,2,1,0:T(8,128)(2,1)}, u32[]{:S(2)}) copy-start(bf16[8,3,128,128]{3,2,1,0:T(8,128)(2,1)} %stiffness.3) | copy-start | bytes 2359300
  1.1 1.1 %copy-start.2 = (bf16[1024,3,128]{2,0,1:T(8,128)(2,1)S(1)}, bf16[1024,3,128]{2,0,1:T(8,128)(2,1)}, u32[]{:S(2)}) copy-start(bf16[1024,3,128]{2,0,1:T(8,128)(2,1)} %param.6) | copy-start | bytes 2359300
  2.3 0.7 %copy-start.3 = (s32[8,128,2]{1,2,0:T(2,128)S(1)}, s32[8,128,2]{1,2,0:T(2,128)}, u32[]{:S(2)}) copy-start(s32[8,128,2]{1,2,0:T(2,128)} %param.7) | copy-start | bytes 24580
  3.0 0.7 %copy-start.4 = (s32[8,3]{0,1:T(4,128)S(1)}, s32[8,3]{0,1:T(4,128)}, u32[]{:S(2)}) copy-start(s32[8,3]{0,1:T(4,128)} %param.5) | copy-start | bytes 292
  3.6 8.4 %copy-start.1 = (bf16[8,3,128,128]{3,2,1,0:T(8,128)(2,1)S(1)}, bf16[8,3,128,128]{3,2,1,0:T(8,128)(2,1)}, u32[]{:S(2)}) copy-start(bf16[8,3,128,128]{3,2,1,0:T(8,128)(2,1)} %stiffness.3) | copy-start | bytes 2359300
  4.8 7.3 %collective-permute-start = (bf16[256,256]{1,0:T(8,128)(2,1)S(1)}, bf16[256,256]{1,0:T(8,128)(2,1)S(1)}, u32[]{:S(2)}, u32[]{:S(2)}) collective-permute-start(bf16[256,256]{1,0:T(8,128)(2,1)S(1)} %get-tuple-element.22), channel_id=1, source_target_pairs={{0,4},{4,8},{8,12},{12,16},{16,20},{20,24},{24,28},{28,0},{1,5},{5... | collective-permute-start | bytes 393224 | tf_op jit(solution)/shard_map/ppermute | solution.py:161
  5.3 6.8 %collective-permute-start.1 = (bf16[256,256]{1,0:T(8,128)(2,1)S(1)}, bf16[256,256]{1,0:T(8,128)(2,1)S(1)}, u32[]{:S(2)}, u32[]{:S(2)}) collective-permute-start(bf16[256,256]{1,0:T(8,128)(2,1)S(1)} %get-tuple-element.23), channel_id=1, source_target_pairs={{4,0},{8,4},{12,8},{16,12},{20,16},{24,20},{28,24},{0,28},{5,1},{9... | collective-permute-start | bytes 393224 | tf_op jit(solution)/shard_map/ppermute | solution.py:164
  9.4 9.6 %collective-permute-start.2 = (bf16[512,384]{1,0:T(8,128)(2,1)S(1)}, bf16[512,384]{1,0:T(8,128)(2,1)S(1)}, u32[]{:S(2)}, u32[]{:S(2)}) collective-permute-start(bf16[512,384]{1,0:T(8,128)(2,1)S(1)} %get-tuple-element.21.inner), channel_id=1, source_target_pairs={{0,1},{1,0},{2,3},{3,2},{4,5},{5,4},{6,7},{7,6},{8,9},{9,8},{10,11... | collective-permute-start | bytes 1179656 | tf_op jit(solution)/shard_map/ppermute | solution.py:167
  13.2 11.4 %collective-permute-start.4 = (bf16[512,384]{1,0:T(8,128)(2,1)S(1)}, bf16[512,384]{1,0:T(8,128)(2,1)S(1)}, u32[]{:S(2)}, u32[]{:S(2)}) collective-permute-start(bf16[512,384]{1,0:T(8,128)(2,1)S(1)} %outer_image.1.outer), channel_id=1, source_target_pairs={{0,2},{1,3},{2,0},{3,1},{4,6},{5,7},{6,4},{7,5},{8,10},{9,11},{10,... | collective-permute-start | bytes 1179656 | tf_op jit(solution)/shard_map/ppermute | solution.py:167
  15.3 17.7 %collective-permute-start.11 = (bf16[512,384]{1,0:T(8,128)(2,1)S(1)}, bf16[512,384]{1,0:T(8,128)(2,1)S(1)}, u32[]{:S(2)}, u32[]{:S(2)}) collective-permute-start(bf16[512,384]{1,0:T(8,128)(2,1)S(1)} %get-tuple-element.21.inner), channel_id=1, source_target_pairs={{0,2},{1,3},{2,0},{3,1},{4,6},{5,7},{6,4},{7,5},{8,10},{9,11},{10,... | collective-permute-start | bytes 1179656 | tf_op jit(solution)/shard_map/ppermute | solution.py:167
  15.4 17.6 %collective-permute-start.10 = (bf16[512,384]{1,0:T(8,128)(2,1)S(1)}, bf16[512,384]{1,0:T(8,128)(2,1)S(1)}, u32[]{:S(2)}, u32[]{:S(2)}) collective-permute-start(bf16[512,384]{1,0:T(8,128)(2,1)S(1)} %outer_image.1.outer), channel_id=1, source_target_pairs={{0,1},{1,0},{2,3},{3,2},{4,5},{5,4},{6,7},{7,6},{8,9},{9,8},{10,11... | collective-permute-start | bytes 1179656 | tf_op jit(solution)/shard_map/ppermute | solution.py:167
  19.0 22.4 %collective-permute-start.3 = (bf16[512,384]{1,0:T(8,128)(2,1)S(1)}, bf16[512,384]{1,0:T(8,128)(2,1)S(1)}, u32[]{:S(2)}, u32[]{:S(2)}) collective-permute-start(bf16[512,384]{1,0:T(8,128)(2,1)S(1)} %collective-permute-done.2.refs_0_), channel_id=1, source_target_pairs={{0,2},{1,3},{2,0},{3,1},{4,6},{5,7},{6,4},{7,5},{8,10},{9,11},{10,... | collective-permute-start | bytes 1179656 | tf_op jit(solution)/shard_map/ppermute | solution.py:167
  24.6 19.2 %collective-permute-start.5 = (bf16[512,384]{1,0:T(8,128)(2,1)S(1)}, bf16[512,384]{1,0:T(8,128)(2,1)S(1)}, u32[]{:S(2)}, u32[]{:S(2)}) collective-permute-start(bf16[512,384]{1,0:T(8,128)(2,1)S(1)} %collective-permute-done.4.refs_3_), channel_id=1, source_target_pairs={{0,1},{1,0},{2,3},{3,2},{4,5},{5,4},{6,7},{7,6},{8,9},{9,8},{10,11... | collective-permute-start | bytes 1179656 | tf_op jit(solution)/shard_map/ppermute | solution.py:167
  34.0 13.9 %collective-permute-start.12 = (bf16[2,128,384]{2,1,0:T(8,128)(2,1)S(1)}, bf16[2,128,384]{2,1,0:T(8,128)(2,1)S(1)}, u32[]{:S(2)}, u32[]{:S(2)}) collective-permute-start(bf16[2,128,384]{2,1,0:T(8,128)(2,1)S(1)} %get-tuple-element.33), channel_id=1, source_target_pairs={{0,4},{4,8},{8,12},{12,16},{16,20},{20,24},{24,28},{28,0},{1,5},{5... | collective-permute-start | bytes 589832 | tf_op jit(solution)/shard_map/ppermute | solution.py:161
  35.5 12.4 %collective-permute-start.13 = (bf16[2,128,384]{2,1,0:T(8,128)(2,1)S(1)}, bf16[2,128,384]{2,1,0:T(8,128)(2,1)S(1)}, u32[]{:S(2)}, u32[]{:S(2)}) collective-permute-start(bf16[2,128,384]{2,1,0:T(8,128)(2,1)S(1)} %get-tuple-element.34), channel_id=1, source_target_pairs={{4,0},{8,4},{12,8},{16,12},{20,16},{24,20},{28,24},{0,28},{5,1},{9... | collective-permute-start | bytes 589832 | tf_op jit(solution)/shard_map/ppermute | solution.py:164
  37.6 6.7 %collective-permute-start.8 = (bf16[1,128,384]{2,1,0:T(8,128)(2,1)S(1)}, bf16[1,128,384]{2,1,0:T(8,128)(2,1)S(1)}, u32[]{:S(2)}, u32[]{:S(2)}) collective-permute-start(bf16[1,128,384]{2,1,0:T(8,128)(2,1)S(1)} %get-tuple-element.30), channel_id=1, source_target_pairs={{0,4},{4,8},{8,12},{12,16},{16,20},{20,24},{24,28},{28,0},{1,5},{5... | collective-permute-start | bytes 294920 | tf_op jit(solution)/shard_map/ppermute | solution.py:161
  41.4 6.5 %collective-permute-start.9 = (bf16[1,128,384]{2,1,0:T(8,128)(2,1)S(1)}, bf16[1,128,384]{2,1,0:T(8,128)(2,1)S(1)}, u32[]{:S(2)}, u32[]{:S(2)}) collective-permute-start(bf16[1,128,384]{2,1,0:T(8,128)(2,1)S(1)} %get-tuple-element.31), channel_id=1, source_target_pairs={{4,0},{8,4},{12,8},{16,12},{20,16},{24,20},{28,24},{0,28},{5,1},{9... | collective-permute-start | bytes 294920 | tf_op jit(solution)/shard_map/ppermute | solution.py:164
  44.3 5.9 %collective-permute-start.6 = (bf16[1,128,384]{2,1,0:T(8,128)(2,1)S(1)}, bf16[1,128,384]{2,1,0:T(8,128)(2,1)S(1)}, u32[]{:S(2)}, u32[]{:S(2)}) collective-permute-start(bf16[1,128,384]{2,1,0:T(8,128)(2,1)S(1)} %get-tuple-element.27), channel_id=1, source_target_pairs={{0,4},{4,8},{8,12},{12,16},{16,20},{20,24},{24,28},{28,0},{1,5},{5... | collective-permute-start | bytes 294920 | tf_op jit(solution)/shard_map/ppermute | solution.py:161
  44.4 5.8 %collective-permute-start.7 = (bf16[1,128,384]{2,1,0:T(8,128)(2,1)S(1)}, bf16[1,128,384]{2,1,0:T(8,128)(2,1)S(1)}, u32[]{:S(2)}, u32[]{:S(2)}) collective-permute-start(bf16[1,128,384]{2,1,0:T(8,128)(2,1)S(1)} %get-tuple-element.28), channel_id=1, source_target_pairs={{4,0},{8,4},{12,8},{16,12},{20,16},{24,20},{28,24},{0,28},{5,1},{9... | collective-permute-start | bytes 294920 | tf_op jit(solution)/shard_map/ppermute | solution.py:164

commit v2 on v1

--- a/solution.py
+++ b/solution.py
@@ -11,7 +11,7 @@
 F32 = jnp.float32
 VMEM = pl.BlockSpec(memory_space=pltpu.VMEM)
 SMEM = pl.BlockSpec(memory_space=pltpu.SMEM)
-HBM = pl.BlockSpec(memory_space=pl.ANY)
+HBM = pl.BlockSpec(memory_space=pltpu.HBM)
 RIM = 2
 
 
@@ -23,7 +23,7 @@
     return jnp.dot(left, right, preferred_element_type=F32)
 
 
-def call(kernel, out_shape, in_specs, out_specs, args, scratch=(), flops=0, aliases=None, name=None):
+def call(kernel, out_shape, in_specs, out_specs, args, scratch=(), flops=0, aliases=None, name=None, vmem=24):
     outs = jax.tree.leaves(out_shape)
     moved = sum(x.size * x.dtype.itemsize for x in (*args, *outs))
     return pl.pallas_call(
@@ -34,7 +34,7 @@
         scratch_shapes=list(scratch),
         input_output_aliases=aliases or {},
         cost_estimate=pl.CostEstimate(flops=flops, bytes_accessed=moved, transcendentals=0),
-        compiler_params=pltpu.CompilerParams(vmem_limit_bytes=24 << 20),
+        compiler_params=pltpu.CompilerParams(vmem_limit_bytes=vmem << 20),
         name=name,
     )(*args)
 
@@ -53,11 +53,23 @@
     ]
 
 
-def mask_and_inner(total_blocks, cols, basis, reach, stiffness, masked, to_next, to_prev, inner):
+def mask_and_inner(
+    total_blocks, cols_hbm, basis_hbm, reach_hbm, stiffness_hbm, masked, to_next, to_prev, inner, cols, basis, reach, stiffness, sem
+):
     blocks, slots, size, _ = stiffness.shape
     groups, _, width = basis.shape
     slabs = reach.shape[0]
     slab = lax.axis_index("blk")
+    copies = [
+        pltpu.make_async_copy(source, target, sem.at[n])
+        for n, (source, target) in enumerate(
+            ((basis_hbm, basis), (stiffness_hbm, stiffness), (reach_hbm, reach), (cols_hbm, cols))
+        )
+    ]
+    for copy in copies:
+        copy.start()
+    copies[2].wait()
+    copies[0].wait()
     low = reach[pl.ds(lax.rem(slab + slabs - 1, slabs), 1), 1, :]
     high = reach[pl.ds(lax.rem(slab + 1, slabs), 1), 0, :]
     for b in range(blocks):
@@ -68,6 +80,8 @@
             masked[rows, g * width : (g + 1) * width] = value * keep[g] if g in keep else value
     to_next[...] = masked[(blocks - RIM) * size :, width:]
     to_prev[...] = masked[: RIM * size, : 2 * width]
+    copies[3].wait()
+    copies[1].wait()
     for b in range(RIM, blocks - RIM):
         starts = [jnp.clip(p - RIM, 0, blocks - 1) for p in positions(cols, b, blocks, slots, total_blocks)]
         inner[(b - RIM) * size : (b - RIM + 1) * size, :] = block_image(stiffness, masked, b, size, starts)
@@ -106,9 +120,16 @@
 
 
 def other_tiles(count, left_inner, left_outer, *refs):
-    images, (own, up, down) = refs[: 2 * count], refs[2 * count :]
+    images, (own, up, down) = refs[:-3], refs[-3:]
+    each = len(images) // count
     for n in range(count):
-        tile = dot(left_inner[...], images[2 * n][...]) + dot(left_outer[...], images[2 * n + 1][...])
+        tile, start = None, [0, 0]
+        for m, image in enumerate(images[n * each : (n + 1) * each]):
+            which = m * 2 // each
+            left = (left_inner, left_outer)[which][:, start[which] : start[which] + image.shape[0]]
+            start[which] += image.shape[0]
+            part = dot(left, image[...])
+            tile = part if tile is None else tile + part
         store_tile(tile, own, up, down, n)
 
 
@@ -175,10 +196,18 @@
     masked, last, leading, inner = call(
         functools.partial(mask_and_inner, total_blocks),
         (shape((rows, wide), BF16), shape((rim, 2 * width), BF16), shape((rim, 2 * width), BF16), shape((inner_rows, wide), BF16)),
-        [SMEM, VMEM, VMEM, VMEM],
+        [HBM] * 4,
         [VMEM] * 4,
         (cols, flat, reach, stiffness),
+        scratch=[
+            pltpu.SMEM(cols.shape, cols.dtype),
+            pltpu.VMEM(flat.shape, BF16),
+            pltpu.VMEM(reach.shape, reach.dtype),
+            pltpu.VMEM(stiffness.shape, BF16),
+            pltpu.SemaphoreType.DMA((4,)),
+        ],
         flops=row_flops * (blocks - 2 * RIM),
+        vmem=52,
         name="mask_and_inner",
     )
     inner_x = swap(inner, 1)
@@ -209,25 +238,24 @@
     )
     prev_a = to_next(up_a)
     next_a = to_prev(down_a)
-    inner_d = swap(inner_x, 2)
-    outer_d = swap(outer_y, 1)
-
-    def tiles(images, name):
-        count = len(images) // 2
+    half = inner_rows // 2
+    diagonal = (swap(inner_y[:half], 1), swap(inner_x[half:], 2), swap(outer_y[:rim], 1), swap(outer_x[rim:], 2))
+
+    def tiles(count, images, name):
         return call(
             functools.partial(other_tiles, count),
             tile_shapes(count, width, wide),
-            [VMEM] * (2 + 2 * count),
+            [VMEM] * (2 + len(images)),
             [VMEM] * 3,
             (left_inner, left_outer, *images),
             flops=tile_flops * count,
             name=name,
         )
 
-    own_b, up_b, down_b = tiles((inner_x, outer_x, inner_y, outer_y), "side_tiles")
+    own_b, up_b, down_b = tiles(2, (inner_x, outer_x, inner_y, outer_y), "side_tiles")
     prev_b = to_next(up_b)
     next_b = to_prev(down_b)
-    own_c, up_c, down_c = tiles((inner_d, outer_d), "diagonal_tile")
+    own_c, up_c, down_c = tiles(1, diagonal, "diagonal_tile")
     prev_c = to_next(up_c)
     next_c = to_prev(down_c)
 

time: 51.2 us -> 46.5 us (0.908)
  waiting for transfers between devices: 17.1 us -> 13.8 us
  local copies, waits for them, and re-layouts: 3.65 us -> 1.54 us
  Pallas kernels: 6.14 us -> 6.85 us
    ppermute x6 -> x8, waiting for transfers between devices: 15.1 us -> 9.78 us  [swap(): return lax.ppermute(value, 'col', [(i, i ^ step) for i in range(4)])]
    ppermute x6 -> x8, starting transfers between devices: 9.85 us -> 12.1 us  [swap(): return lax.ppermute(value, 'col', [(i, i ^ step) for i in range(4)])]
    unnamed x10 -> x6, local copies, waits for them, and re-layouts: 3.65 us -> 1.45 us
    ppermute x4, waiting for transfers between devices: 2.04 us -> 4.04 us  [to_next(): return lax.ppermute(value, 'blk', ring)]
    ppermute x4, starting transfers between devices: 2.09 us -> 0.62 us  [to_next(): return lax.ppermute(value, 'blk', ring)]
    ppermute x4, starting transfers between devices: 12 us -> 11.3 us  [to_prev(): return lax.ppermute(value, 'blk', back)]
    pallas_call x7, Pallas kernels: 6.14 us -> 6.85 us  [call(): pl.pallas_call(kernel, out_shape=out_shape, in_specs=in_specs, out_specs=...]
  transfers between devices with their start and end apart: 14 -> 16, of which waited for: 6 -> 6; matrix products, arithmetic and copies ran while one was open for 0% -> 0% of each run, Pallas kernels for 8% -> 9%
where the time goes in v2:
time: 46.5 us; the launch traced here: 46.3 us
  starting transfers between devices  24 us (52%)
  waiting for transfers between devices  13.8 us (30%)
  Pallas kernels  6.85 us (15%)
  local copies, waits for them, and re-layouts  1.54 us (3%)
    ppermute x8, starting transfers between devices, swap(): return lax.ppermute(value, 'col', [(i, i ^ step) for i in range(4)])  12.1 us
    ppermute x4, starting transfers between devices, to_prev(): return lax.ppermute(value, 'blk', back)  11.3 us
    ppermute x8, waiting for transfers between devices, swap(): return lax.ppermute(value, 'col', [(i, i ^ step) for i in range(4)])  9.78 us
    pallas_call x7, Pallas kernels, call(): pl.pallas_call(kernel, out_shape=out_shape, in_specs=in_specs, out_specs=...  6.85 us
    ppermute x4, waiting for transfers between devices, to_next(): return lax.ppermute(value, 'blk', ring)  4.04 us
    unnamed x6, local copies, waits for them, and re-layouts  1.45 us
  transfers between devices with their start and end apart: 16, of which 6 were waited for; matrix products, arithmetic and copies ran while one was open for 0% of the time, Pallas kernels for 9%

profile of v2, /device:TPU:0, one launch (start us, length us, event | category | flops | bytes accessed | tf_op | source)
XLA Modules:
  0.0 46.3 jit_solution(18087193786876187986)
XLA Ops:
  0.0 0.8 %copy-done.1 = s32[8,128,2]{1,2,0:T(2,128)S(1)} copy-done((s32[8,128,2]{1,2,0:T(2,128)S(1)}, s32[8,128,2]{1,2,0:T(2,128)}, u32[]{:S(2)}) %copy-start.1) | copy-done | bytes 8216
  0.8 0.7 %copy-done.2 = s32[8,3]{0,1:T(4,128)S(1)} copy-done((s32[8,3]{0,1:T(4,128)S(1)}, s32[8,3]{0,1:T(4,128)}, u32[]{:S(2)}) %copy-start.2) | copy-done | bytes 120
  1.5 1.8 %mask_and_inner.1 = (bf16[1024,384]{1,0:T(8,128)(2,1)S(1)}, bf16[256,256]{1,0:T(8,128)(2,1)S(1)}, bf16[256,256]{1,0:T(8,128)(2,1)S(1)}, bf16[512,384]{1,0:T(8,128)(2,1)S(1)}) custom-call(s32[3,8]{1,0:T(4,128)S(1)} %bitcast.5, bf16[3,1024,128]{2,1,0:T(8,128)(2,1)} %bitcast.7, s32[8,2,128]{2,1,0:T(2,128)S(1)} %bitcast.4, bf16[8,3,128,128]{3,2,1,0:T(8,128)(2,1)} %stiffness.1), custom_call_target="tpu_custom_call" | custom-call | flops 150994944 | bytes 3022944 | tf_op jit(solution)/shard_map/mask_and_inner/pallas_call | solution.py:29
  3.8 4.1 %collective-permute-start.1 = (bf16[256,256]{1,0:T(8,128)(2,1)S(1)}, bf16[256,256]{1,0:T(8,128)(2,1)S(1)}, u32[]{:S(2)}, u32[]{:S(2)}) collective-permute-start(bf16[256,256]{1,0:T(8,128)(2,1)S(1)} %get-tuple-element.23), channel_id=1, source_target_pairs={{4,0},{8,4},{12,8},{16,12},{20,16},{24,20},{28,24},{0,28},{5,1},{9... | collective-permute-start | bytes 393224 | tf_op jit(solution)/shard_map/ppermute | solution.py:185
  7.9 2.0 %collective-permute-start.2 = (bf16[512,384]{1,0:T(8,128)(2,1)S(1)}, bf16[512,384]{1,0:T(8,128)(2,1)S(1)}, u32[]{:S(2)}, u32[]{:S(2)}) collective-permute-start(bf16[512,384]{1,0:T(8,128)(2,1)S(1)} %get-tuple-element.21.inner), channel_id=1, source_target_pairs={{0,2},{1,3},{2,0},{3,1},{4,6},{5,7},{6,4},{7,5},{8,10},{9,11},{10,... | collective-permute-start | bytes 1179656 | tf_op jit(solution)/shard_map/ppermute | solution.py:188
  9.9 1.5 %collective-permute-start.4 = (bf16[512,384]{1,0:T(8,128)(2,1)S(1)}, bf16[512,384]{1,0:T(8,128)(2,1)S(1)}, u32[]{:S(2)}, u32[]{:S(2)}) collective-permute-start(bf16[512,384]{1,0:T(8,128)(2,1)S(1)} %get-tuple-element.21.inner), channel_id=1, source_target_pairs={{0,1},{1,0},{2,3},{3,2},{4,5},{5,4},{6,7},{7,6},{8,9},{9,8},{10,11... | collective-permute-start | bytes 1179656 | tf_op jit(solution)/shard_map/ppermute | solution.py:188
  11.4 1.1 %outer_image.1.outer = bf16[512,384]{1,0:T(8,128)(2,1)S(1)} custom-call(s32[3,8]{1,0:T(4,128)S(1)} %bitcast.6, bf16[8,3,128,128]{3,2,1,0:T(8,128)(2,1)S(1)} %copy-done, bf16[1024,384]{1,0:T(8,128)(2,1)S(1)} %get-tuple-element.20.masked, bf16[256,256]{1,0:T(8,128)(2,1)S(1)} %collective-permute-done.from_prev, ...), custom_call_target="tpu_custom_call" | custom-call | flops 150994944 | bytes 2228320 | tf_op jit(solution)/shard_map/outer_image/pallas_call | solution.py:29
  12.5 1.3 %collective-permute-start.6 = (bf16[512,384]{1,0:T(8,128)(2,1)S(1)}, bf16[512,384]{1,0:T(8,128)(2,1)S(1)}, u32[]{:S(2)}, u32[]{:S(2)}) collective-permute-start(bf16[512,384]{1,0:T(8,128)(2,1)S(1)} %outer_image.1.outer), channel_id=1, source_target_pairs={{0,2},{1,3},{2,0},{3,1},{4,6},{5,7},{6,4},{7,5},{8,10},{9,11},{10,... | collective-permute-start | bytes 1179656 | tf_op jit(solution)/shard_map/ppermute | solution.py:188
  13.8 1.5 %collective-permute-start.8 = (bf16[512,384]{1,0:T(8,128)(2,1)S(1)}, bf16[512,384]{1,0:T(8,128)(2,1)S(1)}, u32[]{:S(2)}, u32[]{:S(2)}) collective-permute-start(bf16[512,384]{1,0:T(8,128)(2,1)S(1)} %outer_image.1.outer), channel_id=1, source_target_pairs={{0,1},{1,0},{2,3},{3,2},{4,5},{5,4},{6,7},{7,6},{8,9},{9,8},{10,11... | collective-permute-start | bytes 1179656 | tf_op jit(solution)/shard_map/ppermute | solution.py:188
  15.3 3.6 %collective-permute-done.2.refs_2_ = bf16[512,384]{1,0:T(8,128)(2,1)S(1)} collective-permute-done((bf16[512,384]{1,0:T(8,128)(2,1)S(1)}, bf16[512,384]{1,0:T(8,128)(2,1)S(1)}, u32[]{:S(2)}, u32[]{:S(2)}) %collective-permute-start.2) | collective-permute-done | bytes 393248 | tf_op jit(solution)/shard_map/ppermute | solution.py:188
  18.9 1.3 %collective-permute-start.3 = (bf16[256,384]{1,0:T(8,128)(2,1)S(1)}, bf16[256,384]{1,0:T(8,128)(2,1)S(1)}, u32[]{:S(2)}, u32[]{:S(2)}) collective-permute-start(bf16[256,384]{1,0:T(8,128)(2,1)S(1)} %slice.16), channel_id=1, source_target_pairs={{0,1},{1,0},{2,3},{3,2},{4,5},{5,4},{6,7},{7,6},{8,9},{9,8},{10,11... | collective-permute-start | bytes 589832 | tf_op jit(solution)/shard_map/ppermute | solution.py:188
  20.3 1.6 %collective-permute-start.5 = (bf16[256,384]{1,0:T(8,128)(2,1)S(1)}, bf16[256,384]{1,0:T(8,128)(2,1)S(1)}, u32[]{:S(2)}, u32[]{:S(2)}) collective-permute-start(bf16[256,384]{1,0:T(8,128)(2,1)S(1)} %slice.17), channel_id=1, source_target_pairs={{0,2},{1,3},{2,0},{3,1},{4,6},{5,7},{6,4},{7,5},{8,10},{9,11},{10,... | collective-permute-start | bytes 589832 | tf_op jit(solution)/shard_map/ppermute | solution.py:188
  21.9 5.5 %collective-permute-done.6.refs_3_ = bf16[512,384]{1,0:T(8,128)(2,1)S(1)} collective-permute-done((bf16[512,384]{1,0:T(8,128)(2,1)S(1)}, bf16[512,384]{1,0:T(8,128)(2,1)S(1)}, u32[]{:S(2)}, u32[]{:S(2)}) %collective-permute-start.6) | collective-permute-done | bytes 393248 | tf_op jit(solution)/shard_map/ppermute | solution.py:188
  27.4 1.3 %collective-permute-start.7 = (bf16[256,384]{1,0:T(8,128)(2,1)S(1)}, bf16[256,384]{1,0:T(8,128)(2,1)S(1)}, u32[]{:S(2)}, u32[]{:S(2)}) collective-permute-start(bf16[256,384]{1,0:T(8,128)(2,1)S(1)} %slice.18), channel_id=1, source_target_pairs={{0,1},{1,0},{2,3},{3,2},{4,5},{5,4},{6,7},{7,6},{8,9},{9,8},{10,11... | collective-permute-start | bytes 589832 | tf_op jit(solution)/shard_map/ppermute | solution.py:188
  28.7 1.6 %collective-permute-start.9 = (bf16[256,384]{1,0:T(8,128)(2,1)S(1)}, bf16[256,384]{1,0:T(8,128)(2,1)S(1)}, u32[]{:S(2)}, u32[]{:S(2)}) collective-permute-start(bf16[256,384]{1,0:T(8,128)(2,1)S(1)} %slice.19), channel_id=1, source_target_pairs={{0,2},{1,3},{2,0},{3,1},{4,6},{5,7},{6,4},{7,5},{8,10},{9,11},{10,... | collective-permute-start | bytes 589832 | tf_op jit(solution)/shard_map/ppermute | solution.py:188
  30.3 0.6 %own_tile.1 = (f32[1,128,384]{2,1,0:T(8,128)S(1)}, bf16[1,128,384]{2,1,0:T(8,128)(2,1)S(1)}, bf16[1,128,384]{2,1,0:T(8,128)(2,1)S(1)}, bf16[384,512]{1,0:T(8,128)(2,1)S(1)}, bf16[384,512]{1,0:T(8,128)(2,1)S(1)}) custom-call(bf16[1024,384]{1,0:T(8,128)(2,1)S(1)} %get-tuple-element.20.masked, bf16[512,384]{1,0:T(8,128)(2,1)S(1)} %get-tuple-element.21.inner, ...), custom_call_target="tpu_custom_call" | custom-call | flops 301989888 | bytes 2752512 | tf_op jit(solution)/shard_map/own_tile/pallas_call | solution.py:29
  30.9 1.0 %side_tiles.1 = (f32[2,128,384]{2,1,0:T(8,128)S(1)}, bf16[2,128,384]{2,1,0:T(8,128)(2,1)S(1)}, bf16[2,128,384]{2,1,0:T(8,128)(2,1)S(1)}) custom-call(bf16[384,512]{1,0:T(8,128)(2,1)S(1)} %get-tuple-element.24.left_inner, bf16[384,512]{1,0:T(8,128)(2,1)S(1)} %get-tuple-element.25.left_outer, bf16[512,384]{1,0:T(8,128)(2,1)S(1)} %collective-permute-done.4.refs_0_, ...), custom_call_target="tpu_custom_call" | custom-call | flops 603979776 | bytes 3145728 | tf_op jit(solution)/shard_map/side_tiles/pallas_call | solution.py:29
  32.6 2.9 %collective-permute-start.15 = (bf16[2,128,384]{2,1,0:T(8,128)(2,1)S(1)}, bf16[2,128,384]{2,1,0:T(8,128)(2,1)S(1)}, u32[]{:S(2)}, u32[]{:S(2)}) collective-permute-start(bf16[2,128,384]{2,1,0:T(8,128)(2,1)S(1)} %get-tuple-element.34), channel_id=1, source_target_pairs={{4,0},{8,4},{12,8},{16,12},{20,16},{24,20},{28,24},{0,28},{5,1},{9... | collective-permute-start | bytes 589832 | tf_op jit(solution)/shard_map/ppermute | solution.py:185
  35.6 3.5 %collective-permute-start.13 = (bf16[1,128,384]{2,1,0:T(8,128)(2,1)S(1)}, bf16[1,128,384]{2,1,0:T(8,128)(2,1)S(1)}, u32[]{:S(2)}, u32[]{:S(2)}) collective-permute-start(bf16[1,128,384]{2,1,0:T(8,128)(2,1)S(1)} %get-tuple-element.31), channel_id=1, source_target_pairs={{4,0},{8,4},{12,8},{16,12},{20,16},{24,20},{28,24},{0,28},{5,1},{9... | collective-permute-start | bytes 294920 | tf_op jit(solution)/shard_map/ppermute | solution.py:185
  39.7 2.8 %collective-permute-done.12.refs_1_ = bf16[1,128,384]{2,1,0:T(8,128)(2,1)S(1)} collective-permute-done((bf16[1,128,384]{2,1,0:T(8,128)(2,1)S(1)}, bf16[1,128,384]{2,1,0:T(8,128)(2,1)S(1)}, u32[]{:S(2)}, u32[]{:S(2)}) %collective-permute-start.12) | collective-permute-done | bytes 98336 | tf_op jit(solution)/shard_map/ppermute | solution.py:182
  42.5 0.8 %collective-permute-start.11 = (bf16[1,128,384]{2,1,0:T(8,128)(2,1)S(1)}, bf16[1,128,384]{2,1,0:T(8,128)(2,1)S(1)}, u32[]{:S(2)}, u32[]{:S(2)}) collective-permute-start(bf16[1,128,384]{2,1,0:T(8,128)(2,1)S(1)} %get-tuple-element.28), channel_id=1, source_target_pairs={{4,0},{8,4},{12,8},{16,12},{20,16},{24,20},{28,24},{0,28},{5,1},{9... | collective-permute-start | bytes 294920 | tf_op jit(solution)/shard_map/ppermute | solution.py:185
  43.3 1.0 %add_near.1.refs_3_ = f32[5,128,512]{2,1,0:T(8,128)} custom-call(f32[1,128,384]{2,1,0:T(8,128)S(1)} %get-tuple-element.29.refs_0_, bf16[1,128,384]{2,1,0:T(8,128)(2,1)S(1)} %collective-permute-done.12.refs_1_, bf16[1,128,384]{2,1,0:T(8,128)(2,1)S(1)} %collective-permute-done.13.refs_2_, f32[2,128,384]{2,1,0:T(8,128)S(1)} %get-tuple-element.32.refs_3_, ...), custom_call_target="tpu_custom_call" | custom-call | flops 245760 | bytes 2490368 | tf_op jit(solution)/shard_map/add_near/pallas_call | solution.py:29
  44.3 1.3 %collective-permute-done.10.refs_1_ = bf16[1,128,384]{2,1,0:T(8,128)(2,1)S(1)} collective-permute-done((bf16[1,128,384]{2,1,0:T(8,128)(2,1)S(1)}, bf16[1,128,384]{2,1,0:T(8,128)(2,1)S(1)}, u32[]{:S(2)}, u32[]{:S(2)}) %collective-permute-start.10) | collective-permute-done | bytes 98336 | tf_op jit(solution)/shard_map/ppermute | solution.py:182
  45.6 0.8 %add_diagonal.1 = f32[5,128,512]{2,1,0:T(8,128)} custom-call(f32[1,128,384]{2,1,0:T(8,128)S(1)} %get-tuple-element.26.refs_0_, bf16[1,128,384]{2,1,0:T(8,128)(2,1)S(1)} %collective-permute-done.10.refs_1_, bf16[1,128,384]{2,1,0:T(8,128)(2,1)S(1)} %collective-permute-done.11.refs_2_, f32[5,128,512]{2,1,0:T(8,128)} %add_near.1.refs_3_), custom_call_target="tpu_custom_call", output_to_operand_aliasing={{}: (3, {})} | custom-call | flops 81920 | bytes 3014656 | tf_op jit(solution)/shard_map/add_diagonal/pallas_call | solution.py:29
  (25 shorter events, 2.0 us)
Async XLA Ops:
  0.0 11.4 %copy-start = (bf16[8,3,128,128]{3,2,1,0:T(8,128)(2,1)S(1)}, bf16[8,3,128,128]{3,2,1,0:T(8,128)(2,1)}, u32[]{:S(2)}) copy-start(bf16[8,3,128,128]{3,2,1,0:T(8,128)(2,1)} %stiffness.1) | copy-start | bytes 2359300
  0.0 0.8 %copy-start.1 = (s32[8,128,2]{1,2,0:T(2,128)S(1)}, s32[8,128,2]{1,2,0:T(2,128)}, u32[]{:S(2)}) copy-start(s32[8,128,2]{1,2,0:T(2,128)} %param.7) | copy-start | bytes 24580
  0.8 0.7 %copy-start.2 = (s32[8,3]{0,1:T(4,128)S(1)}, s32[8,3]{0,1:T(4,128)}, u32[]{:S(2)}) copy-start(s32[8,3]{0,1:T(4,128)} %param.5) | copy-start | bytes 292
  3.3 8.1 %collective-permute-start = (bf16[256,256]{1,0:T(8,128)(2,1)S(1)}, bf16[256,256]{1,0:T(8,128)(2,1)S(1)}, u32[]{:S(2)}, u32[]{:S(2)}) collective-permute-start(bf16[256,256]{1,0:T(8,128)(2,1)S(1)} %get-tuple-element.22), channel_id=1, source_target_pairs={{0,4},{4,8},{8,12},{12,16},{16,20},{20,24},{24,28},{28,0},{1,5},{5... | collective-permute-start | bytes 393224 | tf_op jit(solution)/shard_map/ppermute | solution.py:182
  3.8 7.6 %collective-permute-start.1 = (bf16[256,256]{1,0:T(8,128)(2,1)S(1)}, bf16[256,256]{1,0:T(8,128)(2,1)S(1)}, u32[]{:S(2)}, u32[]{:S(2)}) collective-permute-start(bf16[256,256]{1,0:T(8,128)(2,1)S(1)} %get-tuple-element.23), channel_id=1, source_target_pairs={{4,0},{8,4},{12,8},{16,12},{20,16},{24,20},{28,24},{0,28},{5,1},{9... | collective-permute-start | bytes 393224 | tf_op jit(solution)/shard_map/ppermute | solution.py:185
  7.9 11.0 %collective-permute-start.2 = (bf16[512,384]{1,0:T(8,128)(2,1)S(1)}, bf16[512,384]{1,0:T(8,128)(2,1)S(1)}, u32[]{:S(2)}, u32[]{:S(2)}) collective-permute-start(bf16[512,384]{1,0:T(8,128)(2,1)S(1)} %get-tuple-element.21.inner), channel_id=1, source_target_pairs={{0,2},{1,3},{2,0},{3,1},{4,6},{5,7},{6,4},{7,5},{8,10},{9,11},{10,... | collective-permute-start | bytes 1179656 | tf_op jit(solution)/shard_map/ppermute | solution.py:188
  9.9 10.4 %collective-permute-start.4 = (bf16[512,384]{1,0:T(8,128)(2,1)S(1)}, bf16[512,384]{1,0:T(8,128)(2,1)S(1)}, u32[]{:S(2)}, u32[]{:S(2)}) collective-permute-start(bf16[512,384]{1,0:T(8,128)(2,1)S(1)} %get-tuple-element.21.inner), channel_id=1, source_target_pairs={{0,1},{1,0},{2,3},{3,2},{4,5},{5,4},{6,7},{7,6},{8,9},{9,8},{10,11... | collective-permute-start | bytes 1179656 | tf_op jit(solution)/shard_map/ppermute | solution.py:188
  12.5 14.9 %collective-permute-start.6 = (bf16[512,384]{1,0:T(8,128)(2,1)S(1)}, bf16[512,384]{1,0:T(8,128)(2,1)S(1)}, u32[]{:S(2)}, u32[]{:S(2)}) collective-permute-start(bf16[512,384]{1,0:T(8,128)(2,1)S(1)} %outer_image.1.outer), channel_id=1, source_target_pairs={{0,2},{1,3},{2,0},{3,1},{4,6},{5,7},{6,4},{7,5},{8,10},{9,11},{10,... | collective-permute-start | bytes 1179656 | tf_op jit(solution)/shard_map/ppermute | solution.py:188
  13.8 14.9 %collective-permute-start.8 = (bf16[512,384]{1,0:T(8,128)(2,1)S(1)}, bf16[512,384]{1,0:T(8,128)(2,1)S(1)}, u32[]{:S(2)}, u32[]{:S(2)}) collective-permute-start(bf16[512,384]{1,0:T(8,128)(2,1)S(1)} %outer_image.1.outer), channel_id=1, source_target_pairs={{0,1},{1,0},{2,3},{3,2},{4,5},{5,4},{6,7},{7,6},{8,9},{9,8},{10,11... | collective-permute-start | bytes 1179656 | tf_op jit(solution)/shard_map/ppermute | solution.py:188
  18.9 13.6 %collective-permute-start.3 = (bf16[256,384]{1,0:T(8,128)(2,1)S(1)}, bf16[256,384]{1,0:T(8,128)(2,1)S(1)}, u32[]{:S(2)}, u32[]{:S(2)}) collective-permute-start(bf16[256,384]{1,0:T(8,128)(2,1)S(1)} %slice.16), channel_id=1, source_target_pairs={{0,1},{1,0},{2,3},{3,2},{4,5},{5,4},{6,7},{7,6},{8,9},{9,8},{10,11... | collective-permute-start | bytes 589832 | tf_op jit(solution)/shard_map/ppermute | solution.py:188
  20.3 15.2 %collective-permute-start.5 = (bf16[256,384]{1,0:T(8,128)(2,1)S(1)}, bf16[256,384]{1,0:T(8,128)(2,1)S(1)}, u32[]{:S(2)}, u32[]{:S(2)}) collective-permute-start(bf16[256,384]{1,0:T(8,128)(2,1)S(1)} %slice.17), channel_id=1, source_target_pairs={{0,2},{1,3},{2,0},{3,1},{4,6},{5,7},{6,4},{7,5},{8,10},{9,11},{10,... | collective-permute-start | bytes 589832 | tf_op jit(solution)/shard_map/ppermute | solution.py:188
  27.4 8.2 %collective-permute-start.7 = (bf16[256,384]{1,0:T(8,128)(2,1)S(1)}, bf16[256,384]{1,0:T(8,128)(2,1)S(1)}, u32[]{:S(2)}, u32[]{:S(2)}) collective-permute-start(bf16[256,384]{1,0:T(8,128)(2,1)S(1)} %slice.18), channel_id=1, source_target_pairs={{0,1},{1,0},{2,3},{3,2},{4,5},{5,4},{6,7},{7,6},{8,9},{9,8},{10,11... | collective-permute-start | bytes 589832 | tf_op jit(solution)/shard_map/ppermute | solution.py:188
  28.7 10.3 %collective-permute-start.9 = (bf16[256,384]{1,0:T(8,128)(2,1)S(1)}, bf16[256,384]{1,0:T(8,128)(2,1)S(1)}, u32[]{:S(2)}, u32[]{:S(2)}) collective-permute-start(bf16[256,384]{1,0:T(8,128)(2,1)S(1)} %slice.19), channel_id=1, source_target_pairs={{0,2},{1,3},{2,0},{3,1},{4,6},{5,7},{6,4},{7,5},{8,10},{9,11},{10,... | collective-permute-start | bytes 589832 | tf_op jit(solution)/shard_map/ppermute | solution.py:188
  31.9 11.3 %collective-permute-start.14 = (bf16[2,128,384]{2,1,0:T(8,128)(2,1)S(1)}, bf16[2,128,384]{2,1,0:T(8,128)(2,1)S(1)}, u32[]{:S(2)}, u32[]{:S(2)}) collective-permute-start(bf16[2,128,384]{2,1,0:T(8,128)(2,1)S(1)} %get-tuple-element.33), channel_id=1, source_target_pairs={{0,4},{4,8},{8,12},{12,16},{16,20},{20,24},{24,28},{28,0},{1,5},{5... | collective-permute-start | bytes 589832 | tf_op jit(solution)/shard_map/ppermute | solution.py:182
  32.6 10.7 %collective-permute-start.15 = (bf16[2,128,384]{2,1,0:T(8,128)(2,1)S(1)}, bf16[2,128,384]{2,1,0:T(8,128)(2,1)S(1)}, u32[]{:S(2)}, u32[]{:S(2)}) collective-permute-start(bf16[2,128,384]{2,1,0:T(8,128)(2,1)S(1)} %get-tuple-element.34), channel_id=1, source_target_pairs={{4,0},{8,4},{12,8},{16,12},{20,16},{24,20},{28,24},{0,28},{5,1},{9... | collective-permute-start | bytes 589832 | tf_op jit(solution)/shard_map/ppermute | solution.py:185
  35.5 7.0 %collective-permute-start.12 = (bf16[1,128,384]{2,1,0:T(8,128)(2,1)S(1)}, bf16[1,128,384]{2,1,0:T(8,128)(2,1)S(1)}, u32[]{:S(2)}, u32[]{:S(2)}) collective-permute-start(bf16[1,128,384]{2,1,0:T(8,128)(2,1)S(1)} %get-tuple-element.30), channel_id=1, source_target_pairs={{0,4},{4,8},{8,12},{12,16},{16,20},{20,24},{24,28},{28,0},{1,5},{5... | collective-permute-start | bytes 294920 | tf_op jit(solution)/shard_map/ppermute | solution.py:182
  35.6 7.6 %collective-permute-start.13 = (bf16[1,128,384]{2,1,0:T(8,128)(2,1)S(1)}, bf16[1,128,384]{2,1,0:T(8,128)(2,1)S(1)}, u32[]{:S(2)}, u32[]{:S(2)}) collective-permute-start(bf16[1,128,384]{2,1,0:T(8,128)(2,1)S(1)} %get-tuple-element.31), channel_id=1, source_target_pairs={{4,0},{8,4},{12,8},{16,12},{20,16},{24,20},{28,24},{0,28},{5,1},{9... | collective-permute-start | bytes 294920 | tf_op jit(solution)/shard_map/ppermute | solution.py:185
  39.6 5.9 %collective-permute-start.10 = (bf16[1,128,384]{2,1,0:T(8,128)(2,1)S(1)}, bf16[1,128,384]{2,1,0:T(8,128)(2,1)S(1)}, u32[]{:S(2)}, u32[]{:S(2)}) collective-permute-start(bf16[1,128,384]{2,1,0:T(8,128)(2,1)S(1)} %get-tuple-element.27), channel_id=1, source_target_pairs={{0,4},{4,8},{8,12},{12,16},{16,20},{20,24},{24,28},{28,0},{1,5},{5... | collective-permute-start | bytes 294920 | tf_op jit(solution)/shard_map/ppermute | solution.py:182
  42.5 3.1 %collective-permute-start.11 = (bf16[1,128,384]{2,1,0:T(8,128)(2,1)S(1)}, bf16[1,128,384]{2,1,0:T(8,128)(2,1)S(1)}, u32[]{:S(2)}, u32[]{:S(2)}) collective-permute-start(bf16[1,128,384]{2,1,0:T(8,128)(2,1)S(1)} %get-tuple-element.28), channel_id=1, source_target_pairs={{4,0},{8,4},{12,8},{16,12},{20,16},{24,20},{28,24},{0,28},{5,1},{9... | collective-permute-start | bytes 294920 | tf_op jit(solution)/shard_map/ppermute | solution.py:185

commit v3 on v2

--- a/solution.py
+++ b/solution.py
@@ -23,7 +23,7 @@
     return jnp.dot(left, right, preferred_element_type=F32)
 
 
-def call(kernel, out_shape, in_specs, out_specs, args, scratch=(), flops=0, aliases=None, name=None, vmem=24):
+def call(kernel, out_shape, in_specs, out_specs, args, scratch=(), flops=0, aliases=None, name=None, vmem=24 << 10):
     outs = jax.tree.leaves(out_shape)
     moved = sum(x.size * x.dtype.itemsize for x in (*args, *outs))
     return pl.pallas_call(
@@ -34,7 +34,7 @@
         scratch_shapes=list(scratch),
         input_output_aliases=aliases or {},
         cost_estimate=pl.CostEstimate(flops=flops, bytes_accessed=moved, transcendentals=0),
-        compiler_params=pltpu.CompilerParams(vmem_limit_bytes=vmem << 20),
+        compiler_params=pltpu.CompilerParams(vmem_limit_bytes=vmem << 10),
         name=name,
     )(*args)
 
@@ -54,7 +54,7 @@
 
 
 def mask_and_inner(
-    total_blocks, cols_hbm, basis_hbm, reach_hbm, stiffness_hbm, masked, to_next, to_prev, inner, cols, basis, reach, stiffness, sem
+    total_blocks, cols_hbm, basis_hbm, reach_hbm, stiffness_hbm, masked, to_link, to_chip, inner, cols, basis, reach, stiffness, sem
 ):
     blocks, slots, size, _ = stiffness.shape
     groups, _, width = basis.shape
@@ -78,8 +78,18 @@
         for g in range(groups):
             value = basis[g, rows, :]
             masked[rows, g * width : (g + 1) * width] = value * keep[g] if g in keep else value
-    to_next[...] = masked[(blocks - RIM) * size :, width:]
-    to_prev[...] = masked[: RIM * size, : 2 * width]
+    odd = parity()
+
+    @pl.when(odd == 0)
+    def _():
+        to_link[...] = masked[: RIM * size, : 2 * width]
+        to_chip[...] = masked[(blocks - RIM) * size :, width:]
+
+    @pl.when(odd == 1)
+    def _():
+        to_link[...] = masked[(blocks - RIM) * size :, width:]
+        to_chip[...] = masked[: RIM * size, : 2 * width]
+
     copies[3].wait()
     copies[1].wait()
     for b in range(RIM, blocks - RIM):
@@ -87,50 +97,73 @@
         inner[(b - RIM) * size : (b - RIM + 1) * size, :] = block_image(stiffness, masked, b, size, starts)
 
 
-def outer_image(total_blocks, cols, stiffness, masked, from_prev, from_next, outer, extended):
+def outer_image(total_blocks, cols, stiffness, masked, from_link, from_chip, outer, extended):
     blocks, slots, size, _ = stiffness.shape
     rows, wide = masked.shape
     rim = RIM * size
     width = wide // 3
-    extended[:rim, : 2 * width] = from_prev[...]
+    odd = parity()
+
+    @pl.when(odd == 0)
+    def _():
+        extended[:rim, : 2 * width] = from_link[...]
+        extended[rim + rows :, width:] = from_chip[...]
+
+    @pl.when(odd == 1)
+    def _():
+        extended[:rim, : 2 * width] = from_chip[...]
+        extended[rim + rows :, width:] = from_link[...]
+
     extended[:rim, 2 * width :] = jnp.zeros((rim, width), BF16)
     extended[rim : rim + rows, :] = masked[...]
     extended[rim + rows :, :width] = jnp.zeros((rim, width), BF16)
-    extended[rim + rows :, width:] = from_next[...]
     for n, b in enumerate([*range(RIM), *range(blocks - RIM, blocks)]):
         starts = positions(cols, b, blocks, slots, total_blocks)
         outer[n * size : (n + 1) * size, :] = block_image(stiffness, extended, b, size, starts)
 
 
-def store_tile(tile, own, up, down, n):
+def parity():
+    return lax.rem(lax.axis_index("blk"), 2)
+
+
+def store_tile(tile, own, link, chip, n):
     width = own.shape[1]
-    down[n] = tile[:width].astype(BF16)
+    odd = parity()
     own[n] = tile[width : 2 * width]
-    up[n] = tile[2 * width :].astype(BF16)
-
-
-def own_tile(size, masked, inner, outer, own, up, down, left_inner, left_outer):
+    down, up = tile[:width].astype(BF16), tile[2 * width :].astype(BF16)
+
+    @pl.when(odd == 0)
+    def _():
+        link[n] = down
+        chip[n] = up
+
+    @pl.when(odd == 1)
+    def _():
+        link[n] = up
+        chip[n] = down
+
+
+def near_tiles(size, masked, *refs):
+    images, (own, link, chip, left_inner, left_outer) = refs[:-5], refs[-5:]
     rows = masked.shape[0]
     rim = RIM * size
     left_inner[...] = masked[rim : rows - rim, :].T
     left_outer[:, :rim] = masked[:rim, :].T
     left_outer[:, rim:] = masked[rows - rim :, :].T
-    tile = dot(left_inner[...], inner[...]) + dot(left_outer[...], outer[...])
-    store_tile(tile, own, up, down, 0)
-
-
-def other_tiles(count, left_inner, left_outer, *refs):
-    images, (own, up, down) = refs[:-3], refs[-3:]
-    each = len(images) // count
-    for n in range(count):
-        tile, start = None, [0, 0]
-        for m, image in enumerate(images[n * each : (n + 1) * each]):
-            which = m * 2 // each
-            left = (left_inner, left_outer)[which][:, start[which] : start[which] + image.shape[0]]
-            start[which] += image.shape[0]
-            part = dot(left, image[...])
-            tile = part if tile is None else tile + part
-        store_tile(tile, own, up, down, n)
+    for n in range(len(images) // 2):
+        tile = dot(left_inner[...], images[2 * n][...]) + dot(left_outer[...], images[2 * n + 1][...])
+        store_tile(tile, own, link, chip, n)
+
+
+def diagonal_tile(left_inner, left_outer, *refs):
+    images, (own, link, chip) = refs[:-3], refs[-3:]
+    tile = None
+    for which, left in ((0, left_inner), (1, left_outer)):
+        first, second = images[2 * which], images[2 * which + 1]
+        half = first.shape[0]
+        part = dot(left[:, :half], first[...]) + dot(left[:, half:], second[...])
+        tile = part if tile is None else tile + part
+    store_tile(tile, own, link, chip, 0)
 
 
 def add_tiles(sources, *refs):
@@ -139,18 +172,20 @@
     coarse, total, sem = refs[-3:]
     width = total.shape[2]
     me = lax.axis_index("col")
+    even = parity() == 0
     copies = []
     n = 0
     for group, source in enumerate(sources):
-        own, prev, nxt = terms[3 * group : 3 * group + 3]
+        own, link, chip = terms[3 * group : 3 * group + 3]
         for m, step in enumerate(source):
+            prev = jnp.where(even, link[m].astype(F32), chip[m].astype(F32))
+            nxt = jnp.where(even, chip[m].astype(F32), link[m].astype(F32))
             for d in range(5):
                 value = None
-                for offset, ref in ((0, prev), (1, own), (2, nxt)):
+                for offset, term in ((0, prev), (1, own[m]), (2, nxt)):
                     if 0 <= d - offset <= 2:
-                        lanes = slice((d - offset) * width, (d - offset + 1) * width)
-                        term = ref[m, :, lanes].astype(F32)
-                        value = term if value is None else value + term
+                        part = term[:, (d - offset) * width : (d - offset + 1) * width]
+                        value = part if value is None else value + part
                 total[n, d] = value
             start = pl.multiple_of(lax.bitwise_xor(me, step) * width, width)
             copy = pltpu.make_async_copy(total.at[n], coarse.at[:, :, pl.ds(start, width)], sem.at[n])
@@ -175,14 +210,14 @@
     wide = groups * width
     slabs = lax.axis_size("blk")
     total_blocks = blocks * slabs
-    ring = [(i, (i + 1) % slabs) for i in range(slabs)]
-    back = [(j, i) for i, j in ring]
-
-    def to_next(value):
-        return lax.ppermute(value, "blk", ring)
-
-    def to_prev(value):
-        return lax.ppermute(value, "blk", back)
+    pairs = [(i, i ^ 1) for i in range(slabs)]
+    cross = [(i, (i - 1 if i % 2 == 0 else i + 1) % slabs) for i in range(slabs)]
+
+    def over_chip(value):
+        return lax.ppermute(value, "blk", pairs)
+
+    def over_link(value):
+        return lax.ppermute(value, "blk", cross)
 
     def swap(value, step):
         return lax.ppermute(value, "col", [(i, i ^ step) for i in range(4)])
@@ -193,7 +228,7 @@
     inner_rows = (blocks - 2 * RIM) * size
     rim = RIM * size
     row_flops = 2 * slots * size * size * wide
-    masked, last, leading, inner = call(
+    masked, rim_link, rim_chip, inner = call(
         functools.partial(mask_and_inner, total_blocks),
         (shape((rows, wide), BF16), shape((rim, 2 * width), BF16), shape((rim, 2 * width), BF16), shape((inner_rows, wide), BF16)),
         [HBM] * 4,
@@ -207,19 +242,19 @@
             pltpu.SemaphoreType.DMA((4,)),
         ],
         flops=row_flops * (blocks - 2 * RIM),
-        vmem=52,
+        vmem=53248,
         name="mask_and_inner",
     )
     inner_x = swap(inner, 1)
     inner_y = swap(inner, 2)
-    before = to_next(last)
-    after = to_prev(leading)
+    rim_link = over_link(rim_link)
+    rim_chip = over_chip(rim_chip)
     outer = call(
         functools.partial(outer_image, total_blocks),
         shape((2 * rim, wide), BF16),
         [SMEM] + [VMEM] * 4,
         VMEM,
-        (cols, stiffness, masked, before, after),
+        (cols, stiffness, masked, rim_link, rim_chip),
         scratch=[pltpu.VMEM((rows + 2 * rim, wide), BF16)],
         flops=row_flops * 2 * RIM,
         name="outer_image",
@@ -227,37 +262,30 @@
     outer_x = swap(outer, 1)
     outer_y = swap(outer, 2)
     tile_flops = 2 * rows * wide * wide
-    own_a, up_a, down_a, left_inner, left_outer = call(
-        functools.partial(own_tile, size),
-        (*tile_shapes(1, width, wide), shape((wide, inner_rows), BF16), shape((wide, 2 * rim), BF16)),
-        [VMEM] * 3,
-        [VMEM] * 5,
-        (masked, inner, outer),
-        flops=tile_flops,
-        name="own_tile",
-    )
-    prev_a = to_next(up_a)
-    next_a = to_prev(down_a)
     half = inner_rows // 2
     diagonal = (swap(inner_y[:half], 1), swap(inner_x[half:], 2), swap(outer_y[:rim], 1), swap(outer_x[rim:], 2))
-
-    def tiles(count, images, name):
-        return call(
-            functools.partial(other_tiles, count),
-            tile_shapes(count, width, wide),
-            [VMEM] * (2 + len(images)),
-            [VMEM] * 3,
-            (left_inner, left_outer, *images),
-            flops=tile_flops * count,
-            name=name,
-        )
-
-    own_b, up_b, down_b = tiles(2, (inner_x, outer_x, inner_y, outer_y), "side_tiles")
-    prev_b = to_next(up_b)
-    next_b = to_prev(down_b)
-    own_c, up_c, down_c = tiles(1, diagonal, "diagonal_tile")
-    prev_c = to_next(up_c)
-    next_c = to_prev(down_c)
+    near_own, near_link, near_chip, left_inner, left_outer = call(
+        functools.partial(near_tiles, size),
+        (*tile_shapes(3, width, wide), shape((wide, inner_rows), BF16), shape((wide, 2 * rim), BF16)),
+        [VMEM] * 7,
+        [VMEM] * 5,
+        (masked, inner, outer, inner_x, outer_x, inner_y, outer_y),
+        flops=3 * tile_flops,
+        name="near_tiles",
+    )
+    near_link = over_link(near_link)
+    near_chip = over_chip(near_chip)
+    far_own, far_link, far_chip = call(
+        diagonal_tile,
+        tile_shapes(1, width, wide),
+        [VMEM] * 6,
+        [VMEM] * 3,
+        (left_inner, left_outer, *diagonal),
+        flops=tile_flops,
+        name="diagonal_tile",
+    )
+    far_link = over_link(far_link)
+    far_chip = over_chip(far_chip)
 
     def add(sources, terms, name, base=None):
         count = sum(map(len, sources))
@@ -274,8 +302,8 @@
             name=name,
         )
 
-    coarse = add(((0,), (1, 2)), (own_a, prev_a, next_a, own_b, prev_b, next_b), "add_near")
-    coarse = add(((3,),), (own_c, prev_c, next_c), "add_diagonal", coarse)
+    coarse = add(((0, 1, 2),), (near_own, near_link, near_chip), "add_near")
+    coarse = add(((3,),), (far_own, far_link, far_chip), "add_diagonal", coarse)
     return coarse.transpose(1, 0, 2)
 
 

time: 46.5 us -> 45.3 us (0.974)
  starting transfers between devices: 24 us -> 18.2 us
  waiting for transfers between devices: 13.8 us -> 18.1 us
    ppermute x8 -> x6, starting transfers between devices: 11.9 us -> 4.77 us  [the longest x3 4.7 us: over_link(): return lax.ppermute(value, 'blk', cross)]
    ppermute x8, waiting for transfers between devices: 9.78 us -> 12.9 us  [swap(): return lax.ppermute(value, 'col', [(i, i ^ step) for i in range(4)])]
    ppermute x8, starting transfers between devices: 12.1 us -> 13.4 us  [swap(): return lax.ppermute(value, 'col', [(i, i ^ step) for i in range(4)])]
    ppermute x8 -> x6, waiting for transfers between devices: 4.05 us -> 5.2 us  [the longest x3 5.19 us: over_link(): return lax.ppermute(value, 'blk', cross)]
    pallas_call x7 -> x6, Pallas kernels: 6.85 us -> 7.14 us  [call(): pl.pallas_call(kernel, out_shape=out_shape, in_specs=in_specs, out_specs=...]
  transfers between devices with their start and end apart: 16 -> 14, of which waited for: 6 -> 6; matrix products, arithmetic and copies ran while one was open for 0% -> 0% of each run, Pallas kernels for 9% -> 10%
where the time goes in v3:
time: 45.3 us; the launch traced here: 45.1 us
  starting transfers between devices  18.2 us (40%)
  waiting for transfers between devices  18.1 us (40%)
  Pallas kernels  7.14 us (16%)
  local copies, waits for them, and re-layouts  1.54 us (3%)
    ppermute x8, starting transfers between devices, swap(): return lax.ppermute(value, 'col', [(i, i ^ step) for i in range(4)])  13.4 us
    ppermute x8, waiting for transfers between devices, swap(): return lax.ppermute(value, 'col', [(i, i ^ step) for i in range(4)])  12.9 us
    pallas_call x6, Pallas kernels, call(): pl.pallas_call(kernel, out_shape=out_shape, in_specs=in_specs, out_specs=...  7.14 us
    ppermute x3, waiting for transfers between devices, over_link(): return lax.ppermute(value, 'blk', cross)  5.19 us
    ppermute x3, starting transfers between devices, over_link(): return lax.ppermute(value, 'blk', cross)  4.7 us
    unnamed x6, local copies, waits for them, and re-layouts  1.45 us
  transfers between devices with their start and end apart: 14, of which 6 were waited for; matrix products, arithmetic and copies ran while one was open for 0% of the time, Pallas kernels for 10%

profile of v3, /device:TPU:0, one launch (start us, length us, event | category | flops | bytes accessed | tf_op | source)
XLA Modules:
  0.0 45.1 jit_solution(8877231674189239079)
XLA Ops:
  0.0 0.8 %copy-done.1 = s32[8,128,2]{1,2,0:T(2,128)S(1)} copy-done((s32[8,128,2]{1,2,0:T(2,128)S(1)}, s32[8,128,2]{1,2,0:T(2,128)}, u32[]{:S(2)}) %copy-start.1) | copy-done | bytes 8216
  0.8 0.7 %copy-done.2 = s32[8,3]{0,1:T(4,128)S(1)} copy-done((s32[8,3]{0,1:T(4,128)S(1)}, s32[8,3]{0,1:T(4,128)}, u32[]{:S(2)}) %copy-start.2) | copy-done | bytes 120
  1.5 1.8 %mask_and_inner.1 = (bf16[1024,384]{1,0:T(8,128)(2,1)S(1)}, bf16[256,256]{1,0:T(8,128)(2,1)S(1)}, bf16[256,256]{1,0:T(8,128)(2,1)S(1)}, bf16[512,384]{1,0:T(8,128)(2,1)S(1)}) custom-call(s32[3,8]{1,0:T(4,128)S(1)} %bitcast.5, bf16[3,1024,128]{2,1,0:T(8,128)(2,1)} %bitcast.7, s32[8,2,128]{2,1,0:T(2,128)S(1)} %bitcast.4, bf16[8,3,128,128]{3,2,1,0:T(8,128)(2,1)} %stiffness.1), custom_call_target="tpu_custom_call" | custom-call | flops 150994944 | bytes 3022944 | tf_op jit(solution)/shard_map/mask_and_inner/pallas_call | solution.py:29
  3.3 4.6 %collective-permute-start = (bf16[256,256]{1,0:T(8,128)(2,1)S(1)}, bf16[256,256]{1,0:T(8,128)(2,1)S(1)}, u32[]{:S(2)}, u32[]{:S(2)}) collective-permute-start(bf16[256,256]{1,0:T(8,128)(2,1)S(1)} %get-tuple-element.19), channel_id=1, source_target_pairs={{0,28},{4,8},{8,4},{12,16},{16,12},{20,24},{24,20},{28,0},{1,29},{... | collective-permute-start | bytes 393224 | tf_op jit(solution)/shard_map/ppermute | solution.py:220
  7.9 1.5 %collective-permute-start.4 = (bf16[512,384]{1,0:T(8,128)(2,1)S(1)}, bf16[512,384]{1,0:T(8,128)(2,1)S(1)}, u32[]{:S(2)}, u32[]{:S(2)}) collective-permute-start(bf16[512,384]{1,0:T(8,128)(2,1)S(1)} %get-tuple-element.18.refs_0_), channel_id=1, source_target_pairs={{0,2},{1,3},{2,0},{3,1},{4,6},{5,7},{6,4},{7,5},{8,10},{9,11},{10,... | collective-permute-start | bytes 1179656 | tf_op jit(solution)/shard_map/ppermute | solution.py:223
  9.4 1.5 %collective-permute-start.2 = (bf16[512,384]{1,0:T(8,128)(2,1)S(1)}, bf16[512,384]{1,0:T(8,128)(2,1)S(1)}, u32[]{:S(2)}, u32[]{:S(2)}) collective-permute-start(bf16[512,384]{1,0:T(8,128)(2,1)S(1)} %get-tuple-element.18.refs_0_), channel_id=1, source_target_pairs={{0,1},{1,0},{2,3},{3,2},{4,5},{5,4},{6,7},{7,6},{8,9},{9,8},{10,11... | collective-permute-start | bytes 1179656 | tf_op jit(solution)/shard_map/ppermute | solution.py:223
  10.9 0.2 collective-permute-done.from_link
  11.1 1.1 %outer_image.1.refs_1_ = bf16[512,384]{1,0:T(8,128)(2,1)S(1)} custom-call(s32[3,8]{1,0:T(4,128)S(1)} %bitcast.6, bf16[8,3,128,128]{3,2,1,0:T(8,128)(2,1)S(1)} %copy-done, bf16[1024,384]{1,0:T(8,128)(2,1)S(1)} %get-tuple-element.17.masked, bf16[256,256]{1,0:T(8,128)(2,1)S(1)} %collective-permute-done.from_link, ...), custom_call_target="tpu_custom_call" | custom-call | flops 150994944 | bytes 2228320 | tf_op jit(solution)/shard_map/outer_image/pallas_call | solution.py:29
  12.2 2.6 %collective-permute-start.5 = (bf16[512,384]{1,0:T(8,128)(2,1)S(1)}, bf16[512,384]{1,0:T(8,128)(2,1)S(1)}, u32[]{:S(2)}, u32[]{:S(2)}) collective-permute-start(bf16[512,384]{1,0:T(8,128)(2,1)S(1)} %outer_image.1.refs_1_), channel_id=1, source_target_pairs={{0,2},{1,3},{2,0},{3,1},{4,6},{5,7},{6,4},{7,5},{8,10},{9,11},{10,... | collective-permute-start | bytes 1179656 | tf_op jit(solution)/shard_map/ppermute | solution.py:223
  14.8 1.5 %collective-permute-start.3 = (bf16[512,384]{1,0:T(8,128)(2,1)S(1)}, bf16[512,384]{1,0:T(8,128)(2,1)S(1)}, u32[]{:S(2)}, u32[]{:S(2)}) collective-permute-start(bf16[512,384]{1,0:T(8,128)(2,1)S(1)} %outer_image.1.refs_1_), channel_id=1, source_target_pairs={{0,1},{1,0},{2,3},{3,2},{4,5},{5,4},{6,7},{7,6},{8,9},{9,8},{10,11... | collective-permute-start | bytes 1179656 | tf_op jit(solution)/shard_map/ppermute | solution.py:223
  16.3 3.4 %collective-permute-done.4.refs_4_ = bf16[512,384]{1,0:T(8,128)(2,1)S(1)} collective-permute-done((bf16[512,384]{1,0:T(8,128)(2,1)S(1)}, bf16[512,384]{1,0:T(8,128)(2,1)S(1)}, u32[]{:S(2)}, u32[]{:S(2)}) %collective-permute-start.4) | collective-permute-done | bytes 393248 | tf_op jit(solution)/shard_map/ppermute | solution.py:223
  19.8 1.6 %collective-permute-start.6 = (bf16[256,384]{1,0:T(8,128)(2,1)S(1)}, bf16[256,384]{1,0:T(8,128)(2,1)S(1)}, u32[]{:S(2)}, u32[]{:S(2)}) collective-permute-start(bf16[256,384]{1,0:T(8,128)(2,1)S(1)} %slice.16), channel_id=1, source_target_pairs={{0,1},{1,0},{2,3},{3,2},{4,5},{5,4},{6,7},{7,6},{8,9},{9,8},{10,11... | collective-permute-start | bytes 589832 | tf_op jit(solution)/shard_map/ppermute | solution.py:223
  21.4 1.6 %collective-permute-start.7 = (bf16[256,384]{1,0:T(8,128)(2,1)S(1)}, bf16[256,384]{1,0:T(8,128)(2,1)S(1)}, u32[]{:S(2)}, u32[]{:S(2)}) collective-permute-start(bf16[256,384]{1,0:T(8,128)(2,1)S(1)} %slice.17), channel_id=1, source_target_pairs={{0,2},{1,3},{2,0},{3,1},{4,6},{5,7},{6,4},{7,5},{8,10},{9,11},{10,... | collective-permute-start | bytes 589832 | tf_op jit(solution)/shard_map/ppermute | solution.py:223
  23.0 5.2 %collective-permute-done.5.refs_5_ = bf16[512,384]{1,0:T(8,128)(2,1)S(1)} collective-permute-done((bf16[512,384]{1,0:T(8,128)(2,1)S(1)}, bf16[512,384]{1,0:T(8,128)(2,1)S(1)}, u32[]{:S(2)}, u32[]{:S(2)}) %collective-permute-start.5) | collective-permute-done | bytes 393248 | tf_op jit(solution)/shard_map/ppermute | solution.py:223
  28.2 1.6 %collective-permute-start.8 = (bf16[256,384]{1,0:T(8,128)(2,1)S(1)}, bf16[256,384]{1,0:T(8,128)(2,1)S(1)}, u32[]{:S(2)}, u32[]{:S(2)}) collective-permute-start(bf16[256,384]{1,0:T(8,128)(2,1)S(1)} %slice.18), channel_id=1, source_target_pairs={{0,1},{1,0},{2,3},{3,2},{4,5},{5,4},{6,7},{7,6},{8,9},{9,8},{10,11... | collective-permute-start | bytes 589832 | tf_op jit(solution)/shard_map/ppermute | solution.py:223
  29.8 1.6 %collective-permute-start.9 = (bf16[256,384]{1,0:T(8,128)(2,1)S(1)}, bf16[256,384]{1,0:T(8,128)(2,1)S(1)}, u32[]{:S(2)}, u32[]{:S(2)}) collective-permute-start(bf16[256,384]{1,0:T(8,128)(2,1)S(1)} %slice.19), channel_id=1, source_target_pairs={{0,2},{1,3},{2,0},{3,1},{4,6},{5,7},{6,4},{7,5},{8,10},{9,11},{10,... | collective-permute-start | bytes 589832 | tf_op jit(solution)/shard_map/ppermute | solution.py:223
  31.4 1.8 %near_tiles.1 = (f32[3,128,384]{2,1,0:T(8,128)S(1)}, bf16[3,128,384]{2,1,0:T(8,128)(2,1)S(1)}, bf16[3,128,384]{2,1,0:T(8,128)(2,1)S(1)}, bf16[384,512]{1,0:T(8,128)(2,1)S(1)}, bf16[384,512]{1,0:T(8,128)(2,1)S(1)}) custom-call(bf16[1024,384]{1,0:T(8,128)(2,1)S(1)} %get-tuple-element.17.masked, bf16[512,384]{1,0:T(8,128)(2,1)S(1)} %get-tuple-element.18.refs_0_, ...), custom_call_target="tpu_custom_call" | custom-call | flops 905969664 | bytes 5111808 | tf_op jit(solution)/shard_map/near_tiles/pallas_call | solution.py:29
  33.2 0.1 collective-permute-start.12
  33.3 0.7 %collective-permute-done.6.refs_0_ = bf16[256,384]{1,0:T(8,128)(2,1)S(1)} collective-permute-done((bf16[256,384]{1,0:T(8,128)(2,1)S(1)}, bf16[256,384]{1,0:T(8,128)(2,1)S(1)}, u32[]{:S(2)}, u32[]{:S(2)}) %collective-permute-start.6) | collective-permute-done | bytes 196640 | tf_op jit(solution)/shard_map/ppermute | solution.py:223
  34.0 3.5 %collective-permute-done.8.refs_2_ = bf16[256,384]{1,0:T(8,128)(2,1)S(1)} collective-permute-done((bf16[256,384]{1,0:T(8,128)(2,1)S(1)}, bf16[256,384]{1,0:T(8,128)(2,1)S(1)}, u32[]{:S(2)}, u32[]{:S(2)}) %collective-permute-start.8) | collective-permute-done | bytes 196640 | tf_op jit(solution)/shard_map/ppermute | solution.py:223
  37.5 0.6 %diagonal_tile.1 = (f32[1,128,384]{2,1,0:T(8,128)S(1)}, bf16[1,128,384]{2,1,0:T(8,128)(2,1)S(1)}, bf16[1,128,384]{2,1,0:T(8,128)(2,1)S(1)}) custom-call(bf16[384,512]{1,0:T(8,128)(2,1)S(1)} %get-tuple-element.21.left_inner, bf16[384,512]{1,0:T(8,128)(2,1)S(1)} %get-tuple-element.22.left_outer, bf16[256,384]{1,0:T(8,128)(2,1)S(1)} %collective-permute-done.6.refs_0_, ...), custom_call_target="tpu_custom_call" | custom-call | flops 301989888 | bytes 1966080 | tf_op jit(solution)/shard_map/diagonal_tile/pallas_call | solution.py:29
  38.2 5.0 %collective-permute-done.12.refs_1_ = bf16[3,128,384]{2,1,0:T(8,128)(2,1)S(1)} collective-permute-done((bf16[3,128,384]{2,1,0:T(8,128)(2,1)S(1)}, bf16[3,128,384]{2,1,0:T(8,128)(2,1)S(1)}, u32[]{:S(2)}, u32[]{:S(2)}) %collective-permute-start.12) | collective-permute-done | bytes 294944 | tf_op jit(solution)/shard_map/ppermute | solution.py:220
  43.2 1.0 %add_near.1.refs_3_ = f32[5,128,512]{2,1,0:T(8,128)} custom-call(f32[3,128,384]{2,1,0:T(8,128)S(1)} %get-tuple-element.26.refs_0_, bf16[3,128,384]{2,1,0:T(8,128)(2,1)S(1)} %collective-permute-done.12.refs_1_, bf16[3,128,384]{2,1,0:T(8,128)(2,1)S(1)} %collective-permute-done.13.refs_2_), custom_call_target="tpu_custom_call" | custom-call | flops 245760 | bytes 2490368 | tf_op jit(solution)/shard_map/add_near/pallas_call | solution.py:29
  44.3 0.8 %add_diagonal.1 = f32[5,128,512]{2,1,0:T(8,128)} custom-call(f32[1,128,384]{2,1,0:T(8,128)S(1)} %get-tuple-element.23.refs_0_, bf16[1,128,384]{2,1,0:T(8,128)(2,1)S(1)} %collective-permute-done.10.refs_1_, bf16[1,128,384]{2,1,0:T(8,128)(2,1)S(1)} %collective-permute-done.11.refs_2_, f32[5,128,512]{2,1,0:T(8,128)} %add_near.1.refs_3_), custom_call_target="tpu_custom_call", output_to_operand_aliasing={{}: (3, {})} | custom-call | flops 81920 | bytes 3014656 | tf_op jit(solution)/shard_map/add_diagonal/pallas_call | solution.py:29
  (20 shorter events, 0.3 us)
Async XLA Ops:
  0.0 11.1 %copy-start = (bf16[8,3,128,128]{3,2,1,0:T(8,128)(2,1)S(1)}, bf16[8,3,128,128]{3,2,1,0:T(8,128)(2,1)}, u32[]{:S(2)}) copy-start(bf16[8,3,128,128]{3,2,1,0:T(8,128)(2,1)} %stiffness.1) | copy-start | bytes 2359300
  0.0 0.8 %copy-start.1 = (s32[8,128,2]{1,2,0:T(2,128)S(1)}, s32[8,128,2]{1,2,0:T(2,128)}, u32[]{:S(2)}) copy-start(s32[8,128,2]{1,2,0:T(2,128)} %param.7) | copy-start | bytes 24580
  0.8 0.7 %copy-start.2 = (s32[8,3]{0,1:T(4,128)S(1)}, s32[8,3]{0,1:T(4,128)}, u32[]{:S(2)}) copy-start(s32[8,3]{0,1:T(4,128)} %param.5) | copy-start | bytes 292
  3.3 7.8 %collective-permute-start = (bf16[256,256]{1,0:T(8,128)(2,1)S(1)}, bf16[256,256]{1,0:T(8,128)(2,1)S(1)}, u32[]{:S(2)}, u32[]{:S(2)}) collective-permute-start(bf16[256,256]{1,0:T(8,128)(2,1)S(1)} %get-tuple-element.19), channel_id=1, source_target_pairs={{0,28},{4,8},{8,4},{12,16},{16,12},{20,24},{24,20},{28,0},{1,29},{... | collective-permute-start | bytes 393224 | tf_op jit(solution)/shard_map/ppermute | solution.py:220
  7.8 3.2 %collective-permute-start.1 = (bf16[256,256]{1,0:T(8,128)(2,1)S(1)}, bf16[256,256]{1,0:T(8,128)(2,1)S(1)}, u32[]{:S(2)}, u32[]{:S(2)}) collective-permute-start(bf16[256,256]{1,0:T(8,128)(2,1)S(1)} %get-tuple-element.20), channel_id=1, source_target_pairs={{0,4},{4,0},{8,12},{12,8},{16,20},{20,16},{24,28},{28,24},{1,5},{5... | collective-permute-start | bytes 393224 | tf_op jit(solution)/shard_map/ppermute | solution.py:217
  7.9 11.9 %collective-permute-start.4 = (bf16[512,384]{1,0:T(8,128)(2,1)S(1)}, bf16[512,384]{1,0:T(8,128)(2,1)S(1)}, u32[]{:S(2)}, u32[]{:S(2)}) collective-permute-start(bf16[512,384]{1,0:T(8,128)(2,1)S(1)} %get-tuple-element.18.refs_0_), channel_id=1, source_target_pairs={{0,2},{1,3},{2,0},{3,1},{4,6},{5,7},{6,4},{7,5},{8,10},{9,11},{10,... | collective-permute-start | bytes 1179656 | tf_op jit(solution)/shard_map/ppermute | solution.py:223
  9.4 12.0 %collective-permute-start.2 = (bf16[512,384]{1,0:T(8,128)(2,1)S(1)}, bf16[512,384]{1,0:T(8,128)(2,1)S(1)}, u32[]{:S(2)}, u32[]{:S(2)}) collective-permute-start(bf16[512,384]{1,0:T(8,128)(2,1)S(1)} %get-tuple-element.18.refs_0_), channel_id=1, source_target_pairs={{0,1},{1,0},{2,3},{3,2},{4,5},{5,4},{6,7},{7,6},{8,9},{9,8},{10,11... | collective-permute-start | bytes 1179656 | tf_op jit(solution)/shard_map/ppermute | solution.py:223
  12.2 16.0 %collective-permute-start.5 = (bf16[512,384]{1,0:T(8,128)(2,1)S(1)}, bf16[512,384]{1,0:T(8,128)(2,1)S(1)}, u32[]{:S(2)}, u32[]{:S(2)}) collective-permute-start(bf16[512,384]{1,0:T(8,128)(2,1)S(1)} %outer_image.1.refs_1_), channel_id=1, source_target_pairs={{0,2},{1,3},{2,0},{3,1},{4,6},{5,7},{6,4},{7,5},{8,10},{9,11},{10,... | collective-permute-start | bytes 1179656 | tf_op jit(solution)/shard_map/ppermute | solution.py:223
  14.8 14.9 %collective-permute-start.3 = (bf16[512,384]{1,0:T(8,128)(2,1)S(1)}, bf16[512,384]{1,0:T(8,128)(2,1)S(1)}, u32[]{:S(2)}, u32[]{:S(2)}) collective-permute-start(bf16[512,384]{1,0:T(8,128)(2,1)S(1)} %outer_image.1.refs_1_), channel_id=1, source_target_pairs={{0,1},{1,0},{2,3},{3,2},{4,5},{5,4},{6,7},{7,6},{8,9},{9,8},{10,11... | collective-permute-start | bytes 1179656 | tf_op jit(solution)/shard_map/ppermute | solution.py:223
  19.8 14.2 %collective-permute-start.6 = (bf16[256,384]{1,0:T(8,128)(2,1)S(1)}, bf16[256,384]{1,0:T(8,128)(2,1)S(1)}, u32[]{:S(2)}, u32[]{:S(2)}) collective-permute-start(bf16[256,384]{1,0:T(8,128)(2,1)S(1)} %slice.16), channel_id=1, source_target_pairs={{0,1},{1,0},{2,3},{3,2},{4,5},{5,4},{6,7},{7,6},{8,9},{9,8},{10,11... | collective-permute-start | bytes 589832 | tf_op jit(solution)/shard_map/ppermute | solution.py:223
  21.4 12.6 %collective-permute-start.7 = (bf16[256,384]{1,0:T(8,128)(2,1)S(1)}, bf16[256,384]{1,0:T(8,128)(2,1)S(1)}, u32[]{:S(2)}, u32[]{:S(2)}) collective-permute-start(bf16[256,384]{1,0:T(8,128)(2,1)S(1)} %slice.17), channel_id=1, source_target_pairs={{0,2},{1,3},{2,0},{3,1},{4,6},{5,7},{6,4},{7,5},{8,10},{9,11},{10,... | collective-permute-start | bytes 589832 | tf_op jit(solution)/shard_map/ppermute | solution.py:223
  28.2 9.3 %collective-permute-start.8 = (bf16[256,384]{1,0:T(8,128)(2,1)S(1)}, bf16[256,384]{1,0:T(8,128)(2,1)S(1)}, u32[]{:S(2)}, u32[]{:S(2)}) collective-permute-start(bf16[256,384]{1,0:T(8,128)(2,1)S(1)} %slice.18), channel_id=1, source_target_pairs={{0,1},{1,0},{2,3},{3,2},{4,5},{5,4},{6,7},{7,6},{8,9},{9,8},{10,11... | collective-permute-start | bytes 589832 | tf_op jit(solution)/shard_map/ppermute | solution.py:223
  29.8 7.7 %collective-permute-start.9 = (bf16[256,384]{1,0:T(8,128)(2,1)S(1)}, bf16[256,384]{1,0:T(8,128)(2,1)S(1)}, u32[]{:S(2)}, u32[]{:S(2)}) collective-permute-start(bf16[256,384]{1,0:T(8,128)(2,1)S(1)} %slice.19), channel_id=1, source_target_pairs={{0,2},{1,3},{2,0},{3,1},{4,6},{5,7},{6,4},{7,5},{8,10},{9,11},{10,... | collective-permute-start | bytes 589832 | tf_op jit(solution)/shard_map/ppermute | solution.py:223
  33.2 10.0 %collective-permute-start.12 = (bf16[3,128,384]{2,1,0:T(8,128)(2,1)S(1)}, bf16[3,128,384]{2,1,0:T(8,128)(2,1)S(1)}, u32[]{:S(2)}, u32[]{:S(2)}) collective-permute-start(bf16[3,128,384]{2,1,0:T(8,128)(2,1)S(1)} %get-tuple-element.27), channel_id=1, source_target_pairs={{0,28},{4,8},{8,4},{12,16},{16,12},{20,24},{24,20},{28,0},{1,29},{... | collective-permute-start | bytes 884744 | tf_op jit(solution)/shard_map/ppermute | solution.py:220
  34.0 9.2 %collective-permute-start.13 = (bf16[3,128,384]{2,1,0:T(8,128)(2,1)S(1)}, bf16[3,128,384]{2,1,0:T(8,128)(2,1)S(1)}, u32[]{:S(2)}, u32[]{:S(2)}) collective-permute-start(bf16[3,128,384]{2,1,0:T(8,128)(2,1)S(1)} %get-tuple-element.28), channel_id=1, source_target_pairs={{0,4},{4,0},{8,12},{12,8},{16,20},{20,16},{24,28},{28,24},{1,5},{5... | collective-permute-start | bytes 884744 | tf_op jit(solution)/shard_map/ppermute | solution.py:217
  38.1 6.2 %collective-permute-start.10 = (bf16[1,128,384]{2,1,0:T(8,128)(2,1)S(1)}, bf16[1,128,384]{2,1,0:T(8,128)(2,1)S(1)}, u32[]{:S(2)}, u32[]{:S(2)}) collective-permute-start(bf16[1,128,384]{2,1,0:T(8,128)(2,1)S(1)} %get-tuple-element.24), channel_id=1, source_target_pairs={{0,28},{4,8},{8,4},{12,16},{16,12},{20,24},{24,20},{28,0},{1,29},{... | collective-permute-start | bytes 294920 | tf_op jit(solution)/shard_map/ppermute | solution.py:220
  38.2 6.1 %collective-permute-start.11 = (bf16[1,128,384]{2,1,0:T(8,128)(2,1)S(1)}, bf16[1,128,384]{2,1,0:T(8,128)(2,1)S(1)}, u32[]{:S(2)}, u32[]{:S(2)}) collective-permute-start(bf16[1,128,384]{2,1,0:T(8,128)(2,1)S(1)} %get-tuple-element.25), channel_id=1, source_target_pairs={{0,4},{4,0},{8,12},{12,8},{16,20},{20,16},{24,28},{28,24},{1,5},{5... | collective-permute-start | bytes 294920 | tf_op jit(solution)/shard_map/ppermute | solution.py:217

commit v4 on v3

--- a/solution.py
+++ b/solution.py
@@ -33,7 +33,7 @@
         out_specs=out_specs,
         scratch_shapes=list(scratch),
         input_output_aliases=aliases or {},
-        cost_estimate=pl.CostEstimate(flops=flops, bytes_accessed=moved, transcendentals=0),
+        cost_estimate=pl.CostEstimate(flops=flops, bytes_accessed=moved if flops else 0, transcendentals=0),
         compiler_params=pltpu.CompilerParams(vmem_limit_bytes=vmem << 10),
         name=name,
     )(*args)
@@ -259,6 +259,7 @@
         flops=row_flops * 2 * RIM,
         name="outer_image",
     )
+    outer, inner_x, inner_y = lax.optimization_barrier((outer, inner_x, inner_y))
     outer_x = swap(outer, 1)
     outer_y = swap(outer, 2)
     tile_flops = 2 * rows * wide * wide

time: 45.3 us -> 47 us (1.038)
  waiting for transfers between devices: 18.1 us -> 23.3 us
  starting transfers between devices: 18.2 us -> 14.8 us
    ppermute x3, waiting for transfers between devices: 5.19 us -> 11.2 us  [over_link(): return lax.ppermute(value, 'blk', cross)]
    ppermute x8, starting transfers between devices: 13.4 us -> 9.82 us  [swap(): return lax.ppermute(value, 'col', [(i, i ^ step) for i in range(4)])]
    ppermute x8, waiting for transfers between devices: 12.9 us -> 12 us  [swap(): return lax.ppermute(value, 'col', [(i, i ^ step) for i in range(4)])]
    ppermute x3, starting transfers between devices: 0.08 us -> 0.69 us  [over_chip(): return lax.ppermute(value, 'blk', pairs)]
  transfers between devices with their start and end apart: 14 -> 14, of which waited for: 6 -> 8; matrix products, arithmetic and copies ran while one was open for 0% -> 0% of each run, Pallas kernels for 10% -> 10%
where the time goes in v4:
time: 47 us; the launch traced here: 46.8 us
  waiting for transfers between devices  23.3 us (50%)
  starting transfers between devices  14.8 us (31%)
  Pallas kernels  7.14 us (15%)
  local copies, waits for them, and re-layouts  1.54 us (3%)
    ppermute x8, waiting for transfers between devices, swap(): return lax.ppermute(value, 'col', [(i, i ^ step) for i in range(4)])  12 us
    ppermute x3, waiting for transfers between devices, over_link(): return lax.ppermute(value, 'blk', cross)  11.2 us
    ppermute x8, starting transfers between devices, swap(): return lax.ppermute(value, 'col', [(i, i ^ step) for i in range(4)])  9.82 us
    pallas_call x6, Pallas kernels, call(): pl.pallas_call(kernel, out_shape=out_shape, in_specs=in_specs, out_specs=...  7.14 us
    ppermute x3, starting transfers between devices, over_link(): return lax.ppermute(value, 'blk', cross)  4.24 us
    unnamed x6, local copies, waits for them, and re-layouts  1.45 us
  transfers between devices with their start and end apart: 14, of which 8 were waited for; matrix products, arithmetic and copies ran while one was open for 0% of the time, Pallas kernels for 10%

profile of v4, /device:TPU:0, one launch (start us, length us, event | category | flops | bytes accessed | tf_op | source)
XLA Modules:
  0.0 46.8 jit_solution(10102291677852644593)
XLA Ops:
  0.0 0.8 %copy-done.1 = s32[8,128,2]{1,2,0:T(2,128)S(1)} copy-done((s32[8,128,2]{1,2,0:T(2,128)S(1)}, s32[8,128,2]{1,2,0:T(2,128)}, u32[]{:S(2)}) %copy-start.1) | copy-done | bytes 8216
  0.8 0.7 %copy-done.2 = s32[8,3]{0,1:T(4,128)S(1)} copy-done((s32[8,3]{0,1:T(4,128)S(1)}, s32[8,3]{0,1:T(4,128)}, u32[]{:S(2)}) %copy-start.2) | copy-done | bytes 120
  1.5 1.8 %mask_and_inner.1 = (bf16[1024,384]{1,0:T(8,128)(2,1)S(1)}, bf16[256,256]{1,0:T(8,128)(2,1)S(1)}, bf16[256,256]{1,0:T(8,128)(2,1)S(1)}, bf16[512,384]{1,0:T(8,128)(2,1)S(1)}) custom-call(s32[3,8]{1,0:T(4,128)S(1)} %bitcast.5, bf16[3,1024,128]{2,1,0:T(8,128)(2,1)} %bitcast.7, s32[8,2,128]{2,1,0:T(2,128)S(1)} %bitcast.4, bf16[8,3,128,128]{3,2,1,0:T(8,128)(2,1)} %stiffness.1), custom_call_target="tpu_custom_call" | custom-call | flops 150994944 | bytes 3022944 | tf_op jit(solution)/shard_map/mask_and_inner/pallas_call | solution.py:29
  3.3 3.0 %collective-permute-start.2 = (bf16[512,384]{1,0:T(8,128)(2,1)S(1)}, bf16[512,384]{1,0:T(8,128)(2,1)S(1)}, u32[]{:S(2)}, u32[]{:S(2)}) collective-permute-start(bf16[512,384]{1,0:T(8,128)(2,1)S(1)} %get-tuple-element.21.refs_0_), channel_id=1, source_target_pairs={{0,1},{1,0},{2,3},{3,2},{4,5},{5,4},{6,7},{7,6},{8,9},{9,8},{10,11... | collective-permute-start | bytes 1179656 | tf_op jit(solution)/shard_map/ppermute | solution.py:223
  6.3 1.5 %collective-permute-start.3 = (bf16[512,384]{1,0:T(8,128)(2,1)S(1)}, bf16[512,384]{1,0:T(8,128)(2,1)S(1)}, u32[]{:S(2)}, u32[]{:S(2)}) collective-permute-start(bf16[512,384]{1,0:T(8,128)(2,1)S(1)} %get-tuple-element.21.refs_0_), channel_id=1, source_target_pairs={{0,2},{1,3},{2,0},{3,1},{4,6},{5,7},{6,4},{7,5},{8,10},{9,11},{10,... | collective-permute-start | bytes 1179656 | tf_op jit(solution)/shard_map/ppermute | solution.py:223
  7.8 2.5 %collective-permute-start = (bf16[256,256]{1,0:T(8,128)(2,1)S(1)}, bf16[256,256]{1,0:T(8,128)(2,1)S(1)}, u32[]{:S(2)}, u32[]{:S(2)}) collective-permute-start(bf16[256,256]{1,0:T(8,128)(2,1)S(1)} %get-tuple-element.22), channel_id=1, source_target_pairs={{0,28},{4,8},{8,4},{12,16},{16,12},{20,24},{24,20},{28,0},{1,29},{... | collective-permute-start | bytes 393224 | tf_op jit(solution)/shard_map/ppermute | solution.py:220
  10.3 4.8 %collective-permute-done.from_link = bf16[256,256]{1,0:T(8,128)(2,1)S(1)} collective-permute-done((bf16[256,256]{1,0:T(8,128)(2,1)S(1)}, bf16[256,256]{1,0:T(8,128)(2,1)S(1)}, u32[]{:S(2)}, u32[]{:S(2)}) %collective-permute-start) | collective-permute-done | bytes 131104 | tf_op jit(solution)/shard_map/ppermute | solution.py:220
  15.2 1.1 %outer_image.1.refs_1_ = bf16[512,384]{1,0:T(8,128)(2,1)S(1)} custom-call(s32[3,8]{1,0:T(4,128)S(1)} %bitcast.6, bf16[8,3,128,128]{3,2,1,0:T(8,128)(2,1)S(1)} %copy-done, bf16[1024,384]{1,0:T(8,128)(2,1)S(1)} %get-tuple-element.20.masked, bf16[256,256]{1,0:T(8,128)(2,1)S(1)} %collective-permute-done.from_link, ...), custom_call_target="tpu_custom_call" | custom-call | flops 150994944 | bytes 2228320 | tf_op jit(solution)/shard_map/outer_image/pallas_call | solution.py:29
  16.3 0.6 %collective-permute-done.3.refs_4_ = bf16[512,384]{1,0:T(8,128)(2,1)S(1)} collective-permute-done((bf16[512,384]{1,0:T(8,128)(2,1)S(1)}, bf16[512,384]{1,0:T(8,128)(2,1)S(1)}, u32[]{:S(2)}, u32[]{:S(2)}) %collective-permute-start.3) | collective-permute-done | bytes 393248 | tf_op jit(solution)/shard_map/ppermute | solution.py:223
  16.9 1.5 %collective-permute-start.5 = (bf16[512,384]{1,0:T(8,128)(2,1)S(1)}, bf16[512,384]{1,0:T(8,128)(2,1)S(1)}, u32[]{:S(2)}, u32[]{:S(2)}) collective-permute-start(bf16[512,384]{1,0:T(8,128)(2,1)S(1)} %outer_image.1.refs_1_), channel_id=1, source_target_pairs={{0,2},{1,3},{2,0},{3,1},{4,6},{5,7},{6,4},{7,5},{8,10},{9,11},{10,... | collective-permute-start | bytes 1179656 | tf_op jit(solution)/shard_map/ppermute | solution.py:223
  19.0 1.6 %collective-permute-start.6 = (bf16[256,384]{1,0:T(8,128)(2,1)S(1)}, bf16[256,384]{1,0:T(8,128)(2,1)S(1)}, u32[]{:S(2)}, u32[]{:S(2)}) collective-permute-start(bf16[256,384]{1,0:T(8,128)(2,1)S(1)} %slice.12), channel_id=1, source_target_pairs={{0,1},{1,0},{2,3},{3,2},{4,5},{5,4},{6,7},{7,6},{8,9},{9,8},{10,11... | collective-permute-start | bytes 589832 | tf_op jit(solution)/shard_map/ppermute | solution.py:223
  21.1 7.8 %collective-permute-done.5.refs_5_ = bf16[512,384]{1,0:T(8,128)(2,1)S(1)} collective-permute-done((bf16[512,384]{1,0:T(8,128)(2,1)S(1)}, bf16[512,384]{1,0:T(8,128)(2,1)S(1)}, u32[]{:S(2)}, u32[]{:S(2)}) %collective-permute-start.5) | collective-permute-done | bytes 393248 | tf_op jit(solution)/shard_map/ppermute | solution.py:223
  29.4 1.1 %collective-permute-done.4.refs_3_ = bf16[512,384]{1,0:T(8,128)(2,1)S(1)} collective-permute-done((bf16[512,384]{1,0:T(8,128)(2,1)S(1)}, bf16[512,384]{1,0:T(8,128)(2,1)S(1)}, u32[]{:S(2)}, u32[]{:S(2)}) %collective-permute-start.4) | collective-permute-done | bytes 393248 | tf_op jit(solution)/shard_map/ppermute | solution.py:223
  30.5 0.7 %collective-permute-start.9 = (bf16[256,384]{1,0:T(8,128)(2,1)S(1)}, bf16[256,384]{1,0:T(8,128)(2,1)S(1)}, u32[]{:S(2)}, u32[]{:S(2)}) collective-permute-start(bf16[256,384]{1,0:T(8,128)(2,1)S(1)} %slice.17), channel_id=1, source_target_pairs={{0,2},{1,3},{2,0},{3,1},{4,6},{5,7},{6,4},{7,5},{8,10},{9,11},{10,... | collective-permute-start | bytes 589832 | tf_op jit(solution)/shard_map/ppermute | solution.py:223
  31.2 1.8 %near_tiles.1 = (f32[3,128,384]{2,1,0:T(8,128)S(1)}, bf16[3,128,384]{2,1,0:T(8,128)(2,1)S(1)}, bf16[3,128,384]{2,1,0:T(8,128)(2,1)S(1)}, bf16[384,512]{1,0:T(8,128)(2,1)S(1)}, bf16[384,512]{1,0:T(8,128)(2,1)S(1)}) custom-call(bf16[1024,384]{1,0:T(8,128)(2,1)S(1)} %get-tuple-element.20.masked, bf16[512,384]{1,0:T(8,128)(2,1)S(1)} %get-tuple-element.21.refs_0_, ...), custom_call_target="tpu_custom_call" | custom-call | flops 905969664 | bytes 5111808 | tf_op jit(solution)/shard_map/near_tiles/pallas_call | solution.py:29
  33.0 1.1 %collective-permute-done.6.refs_0_ = bf16[256,384]{1,0:T(8,128)(2,1)S(1)} collective-permute-done((bf16[256,384]{1,0:T(8,128)(2,1)S(1)}, bf16[256,384]{1,0:T(8,128)(2,1)S(1)}, u32[]{:S(2)}, u32[]{:S(2)}) %collective-permute-start.6) | collective-permute-done | bytes 196640 | tf_op jit(solution)/shard_map/ppermute | solution.py:223
  34.1 0.6 %collective-permute-start.13 = (bf16[3,128,384]{2,1,0:T(8,128)(2,1)S(1)}, bf16[3,128,384]{2,1,0:T(8,128)(2,1)S(1)}, u32[]{:S(2)}, u32[]{:S(2)}) collective-permute-start(bf16[3,128,384]{2,1,0:T(8,128)(2,1)S(1)} %get-tuple-element.34), channel_id=1, source_target_pairs={{0,4},{4,0},{8,12},{12,8},{16,20},{20,16},{24,28},{28,24},{1,5},{5... | collective-permute-start | bytes 884744 | tf_op jit(solution)/shard_map/ppermute | solution.py:217
  34.7 1.5 %collective-permute-done.8.refs_2_ = bf16[256,384]{1,0:T(8,128)(2,1)S(1)} collective-permute-done((bf16[256,384]{1,0:T(8,128)(2,1)S(1)}, bf16[256,384]{1,0:T(8,128)(2,1)S(1)}, u32[]{:S(2)}, u32[]{:S(2)}) %collective-permute-start.8) | collective-permute-done | bytes 196640 | tf_op jit(solution)/shard_map/ppermute | solution.py:223
  36.2 0.6 %diagonal_tile.1 = (f32[1,128,384]{2,1,0:T(8,128)S(1)}, bf16[1,128,384]{2,1,0:T(8,128)(2,1)S(1)}, bf16[1,128,384]{2,1,0:T(8,128)(2,1)S(1)}) custom-call(bf16[384,512]{1,0:T(8,128)(2,1)S(1)} %get-tuple-element.27.left_inner, bf16[384,512]{1,0:T(8,128)(2,1)S(1)} %get-tuple-element.28.left_outer, bf16[256,384]{1,0:T(8,128)(2,1)S(1)} %collective-permute-done.6.refs_0_, ...), custom_call_target="tpu_custom_call" | custom-call | flops 301989888 | bytes 1966080 | tf_op jit(solution)/shard_map/diagonal_tile/pallas_call | solution.py:29
  36.8 1.7 %collective-permute-start.10 = (bf16[1,128,384]{2,1,0:T(8,128)(2,1)S(1)}, bf16[1,128,384]{2,1,0:T(8,128)(2,1)S(1)}, u32[]{:S(2)}, u32[]{:S(2)}) collective-permute-start(bf16[1,128,384]{2,1,0:T(8,128)(2,1)S(1)} %get-tuple-element.30), channel_id=1, source_target_pairs={{0,28},{4,8},{8,4},{12,16},{16,12},{20,24},{24,20},{28,0},{1,29},{... | collective-permute-start | bytes 294920 | tf_op jit(solution)/shard_map/ppermute | solution.py:220
  38.6 5.3 %collective-permute-done.12.refs_1_ = bf16[3,128,384]{2,1,0:T(8,128)(2,1)S(1)} collective-permute-done((bf16[3,128,384]{2,1,0:T(8,128)(2,1)S(1)}, bf16[3,128,384]{2,1,0:T(8,128)(2,1)S(1)}, u32[]{:S(2)}, u32[]{:S(2)}) %collective-permute-start.12) | collective-permute-done | bytes 294944 | tf_op jit(solution)/shard_map/ppermute | solution.py:220
  43.9 1.0 %add_near.1.refs_3_ = f32[5,128,512]{2,1,0:T(8,128)} custom-call(f32[3,128,384]{2,1,0:T(8,128)S(1)} %get-tuple-element.32.refs_0_, bf16[3,128,384]{2,1,0:T(8,128)(2,1)S(1)} %collective-permute-done.12.refs_1_, bf16[3,128,384]{2,1,0:T(8,128)(2,1)S(1)} %collective-permute-done.13.refs_2_), custom_call_target="tpu_custom_call" | custom-call | flops 245760 | bytes 2490368 | tf_op jit(solution)/shard_map/add_near/pallas_call | solution.py:29
  44.9 1.1 %collective-permute-done.10.refs_1_ = bf16[1,128,384]{2,1,0:T(8,128)(2,1)S(1)} collective-permute-done((bf16[1,128,384]{2,1,0:T(8,128)(2,1)S(1)}, bf16[1,128,384]{2,1,0:T(8,128)(2,1)S(1)}, u32[]{:S(2)}, u32[]{:S(2)}) %collective-permute-start.10) | collective-permute-done | bytes 98336 | tf_op jit(solution)/shard_map/ppermute | solution.py:220
  46.0 0.8 %add_diagonal.1 = f32[5,128,512]{2,1,0:T(8,128)} custom-call(f32[1,128,384]{2,1,0:T(8,128)S(1)} %get-tuple-element.29.refs_0_, bf16[1,128,384]{2,1,0:T(8,128)(2,1)S(1)} %collective-permute-done.10.refs_1_, bf16[1,128,384]{2,1,0:T(8,128)(2,1)S(1)} %collective-permute-done.11.refs_2_, f32[5,128,512]{2,1,0:T(8,128)} %add_near.1.refs_3_), custom_call_target="tpu_custom_call", output_to_operand_aliasing={{}: (3, {})} | custom-call | flops 81920 | bytes 3014656 | tf_op jit(solution)/shard_map/add_diagonal/pallas_call | solution.py:29
  (20 shorter events, 1.8 us)
Async XLA Ops:
  0.0 15.2 %copy-start = (bf16[8,3,128,128]{3,2,1,0:T(8,128)(2,1)S(1)}, bf16[8,3,128,128]{3,2,1,0:T(8,128)(2,1)}, u32[]{:S(2)}) copy-start(bf16[8,3,128,128]{3,2,1,0:T(8,128)(2,1)} %stiffness.1) | copy-start | bytes 2359300
  0.0 0.8 %copy-start.1 = (s32[8,128,2]{1,2,0:T(2,128)S(1)}, s32[8,128,2]{1,2,0:T(2,128)}, u32[]{:S(2)}) copy-start(s32[8,128,2]{1,2,0:T(2,128)} %param.7) | copy-start | bytes 24580
  0.8 0.7 %copy-start.2 = (s32[8,3]{0,1:T(4,128)S(1)}, s32[8,3]{0,1:T(4,128)}, u32[]{:S(2)}) copy-start(s32[8,3]{0,1:T(4,128)} %param.5) | copy-start | bytes 292
  3.3 13.0 %collective-permute-start.2 = (bf16[512,384]{1,0:T(8,128)(2,1)S(1)}, bf16[512,384]{1,0:T(8,128)(2,1)S(1)}, u32[]{:S(2)}, u32[]{:S(2)}) collective-permute-start(bf16[512,384]{1,0:T(8,128)(2,1)S(1)} %get-tuple-element.21.refs_0_), channel_id=1, source_target_pairs={{0,1},{1,0},{2,3},{3,2},{4,5},{5,4},{6,7},{7,6},{8,9},{9,8},{10,11... | collective-permute-start | bytes 1179656 | tf_op jit(solution)/shard_map/ppermute | solution.py:223
  6.3 10.6 %collective-permute-start.3 = (bf16[512,384]{1,0:T(8,128)(2,1)S(1)}, bf16[512,384]{1,0:T(8,128)(2,1)S(1)}, u32[]{:S(2)}, u32[]{:S(2)}) collective-permute-start(bf16[512,384]{1,0:T(8,128)(2,1)S(1)} %get-tuple-element.21.refs_0_), channel_id=1, source_target_pairs={{0,2},{1,3},{2,0},{3,1},{4,6},{5,7},{6,4},{7,5},{8,10},{9,11},{10,... | collective-permute-start | bytes 1179656 | tf_op jit(solution)/shard_map/ppermute | solution.py:223
  7.8 7.3 %collective-permute-start = (bf16[256,256]{1,0:T(8,128)(2,1)S(1)}, bf16[256,256]{1,0:T(8,128)(2,1)S(1)}, u32[]{:S(2)}, u32[]{:S(2)}) collective-permute-start(bf16[256,256]{1,0:T(8,128)(2,1)S(1)} %get-tuple-element.22), channel_id=1, source_target_pairs={{0,28},{4,8},{8,4},{12,16},{16,12},{20,24},{24,20},{28,0},{1,29},{... | collective-permute-start | bytes 393224 | tf_op jit(solution)/shard_map/ppermute | solution.py:220
  10.3 4.9 %collective-permute-start.1 = (bf16[256,256]{1,0:T(8,128)(2,1)S(1)}, bf16[256,256]{1,0:T(8,128)(2,1)S(1)}, u32[]{:S(2)}, u32[]{:S(2)}) collective-permute-start(bf16[256,256]{1,0:T(8,128)(2,1)S(1)} %get-tuple-element.23), channel_id=1, source_target_pairs={{0,4},{4,0},{8,12},{12,8},{16,20},{20,16},{24,28},{28,24},{1,5},{5... | collective-permute-start | bytes 393224 | tf_op jit(solution)/shard_map/ppermute | solution.py:217
  16.9 12.1 %collective-permute-start.5 = (bf16[512,384]{1,0:T(8,128)(2,1)S(1)}, bf16[512,384]{1,0:T(8,128)(2,1)S(1)}, u32[]{:S(2)}, u32[]{:S(2)}) collective-permute-start(bf16[512,384]{1,0:T(8,128)(2,1)S(1)} %outer_image.1.refs_1_), channel_id=1, source_target_pairs={{0,2},{1,3},{2,0},{3,1},{4,6},{5,7},{6,4},{7,5},{8,10},{9,11},{10,... | collective-permute-start | bytes 1179656 | tf_op jit(solution)/shard_map/ppermute | solution.py:223
  18.4 12.1 %collective-permute-start.4 = (bf16[512,384]{1,0:T(8,128)(2,1)S(1)}, bf16[512,384]{1,0:T(8,128)(2,1)S(1)}, u32[]{:S(2)}, u32[]{:S(2)}) collective-permute-start(bf16[512,384]{1,0:T(8,128)(2,1)S(1)} %outer_image.1.refs_1_), channel_id=1, source_target_pairs={{0,1},{1,0},{2,3},{3,2},{4,5},{5,4},{6,7},{7,6},{8,9},{9,8},{10,11... | collective-permute-start | bytes 1179656 | tf_op jit(solution)/shard_map/ppermute | solution.py:223
  19.0 15.1 %collective-permute-start.6 = (bf16[256,384]{1,0:T(8,128)(2,1)S(1)}, bf16[256,384]{1,0:T(8,128)(2,1)S(1)}, u32[]{:S(2)}, u32[]{:S(2)}) collective-permute-start(bf16[256,384]{1,0:T(8,128)(2,1)S(1)} %slice.12), channel_id=1, source_target_pairs={{0,1},{1,0},{2,3},{3,2},{4,5},{5,4},{6,7},{7,6},{8,9},{9,8},{10,11... | collective-permute-start | bytes 589832 | tf_op jit(solution)/shard_map/ppermute | solution.py:223
  20.5 14.2 %collective-permute-start.7 = (bf16[256,384]{1,0:T(8,128)(2,1)S(1)}, bf16[256,384]{1,0:T(8,128)(2,1)S(1)}, u32[]{:S(2)}, u32[]{:S(2)}) collective-permute-start(bf16[256,384]{1,0:T(8,128)(2,1)S(1)} %slice.13), channel_id=1, source_target_pairs={{0,2},{1,3},{2,0},{3,1},{4,6},{5,7},{6,4},{7,5},{8,10},{9,11},{10,... | collective-permute-start | bytes 589832 | tf_op jit(solution)/shard_map/ppermute | solution.py:223
  29.0 7.3 %collective-permute-start.8 = (bf16[256,384]{1,0:T(8,128)(2,1)S(1)}, bf16[256,384]{1,0:T(8,128)(2,1)S(1)}, u32[]{:S(2)}, u32[]{:S(2)}) collective-permute-start(bf16[256,384]{1,0:T(8,128)(2,1)S(1)} %slice.16), channel_id=1, source_target_pairs={{0,1},{1,0},{2,3},{3,2},{4,5},{5,4},{6,7},{7,6},{8,9},{9,8},{10,11... | collective-permute-start | bytes 589832 | tf_op jit(solution)/shard_map/ppermute | solution.py:223
  30.5 5.7 %collective-permute-start.9 = (bf16[256,384]{1,0:T(8,128)(2,1)S(1)}, bf16[256,384]{1,0:T(8,128)(2,1)S(1)}, u32[]{:S(2)}, u32[]{:S(2)}) collective-permute-start(bf16[256,384]{1,0:T(8,128)(2,1)S(1)} %slice.17), channel_id=1, source_target_pairs={{0,2},{1,3},{2,0},{3,1},{4,6},{5,7},{6,4},{7,5},{8,10},{9,11},{10,... | collective-permute-start | bytes 589832 | tf_op jit(solution)/shard_map/ppermute | solution.py:223
  33.0 10.9 %collective-permute-start.12 = (bf16[3,128,384]{2,1,0:T(8,128)(2,1)S(1)}, bf16[3,128,384]{2,1,0:T(8,128)(2,1)S(1)}, u32[]{:S(2)}, u32[]{:S(2)}) collective-permute-start(bf16[3,128,384]{2,1,0:T(8,128)(2,1)S(1)} %get-tuple-element.33), channel_id=1, source_target_pairs={{0,28},{4,8},{8,4},{12,16},{16,12},{20,24},{24,20},{28,0},{1,29},{... | collective-permute-start | bytes 884744 | tf_op jit(solution)/shard_map/ppermute | solution.py:220
  34.1 9.8 %collective-permute-start.13 = (bf16[3,128,384]{2,1,0:T(8,128)(2,1)S(1)}, bf16[3,128,384]{2,1,0:T(8,128)(2,1)S(1)}, u32[]{:S(2)}, u32[]{:S(2)}) collective-permute-start(bf16[3,128,384]{2,1,0:T(8,128)(2,1)S(1)} %get-tuple-element.34), channel_id=1, source_target_pairs={{0,4},{4,0},{8,12},{12,8},{16,20},{20,16},{24,28},{28,24},{1,5},{5... | collective-permute-start | bytes 884744 | tf_op jit(solution)/shard_map/ppermute | solution.py:217
  36.8 9.2 %collective-permute-start.10 = (bf16[1,128,384]{2,1,0:T(8,128)(2,1)S(1)}, bf16[1,128,384]{2,1,0:T(8,128)(2,1)S(1)}, u32[]{:S(2)}, u32[]{:S(2)}) collective-permute-start(bf16[1,128,384]{2,1,0:T(8,128)(2,1)S(1)} %get-tuple-element.30), channel_id=1, source_target_pairs={{0,28},{4,8},{8,4},{12,16},{16,12},{20,24},{24,20},{28,0},{1,29},{... | collective-permute-start | bytes 294920 | tf_op jit(solution)/shard_map/ppermute | solution.py:220
  38.5 7.5 %collective-permute-start.11 = (bf16[1,128,384]{2,1,0:T(8,128)(2,1)S(1)}, bf16[1,128,384]{2,1,0:T(8,128)(2,1)S(1)}, u32[]{:S(2)}, u32[]{:S(2)}) collective-permute-start(bf16[1,128,384]{2,1,0:T(8,128)(2,1)S(1)} %get-tuple-element.31), channel_id=1, source_target_pairs={{0,4},{4,0},{8,12},{12,8},{16,20},{20,16},{24,28},{28,24},{1,5},{5... | collective-permute-start | bytes 294920 | tf_op jit(solution)/shard_map/ppermute | solution.py:217

commit v5 on v3

--- a/solution.py
+++ b/solution.py
@@ -143,13 +143,17 @@
         chip[n] = down
 
 
-def near_tiles(size, masked, *refs):
-    images, (own, link, chip, left_inner, left_outer) = refs[:-5], refs[-5:]
+def own_tile(size, masked, inner, outer, own, link, chip, left_inner, left_outer):
     rows = masked.shape[0]
     rim = RIM * size
     left_inner[...] = masked[rim : rows - rim, :].T
     left_outer[:, :rim] = masked[:rim, :].T
     left_outer[:, rim:] = masked[rows - rim :, :].T
+    store_tile(dot(left_inner[...], inner[...]) + dot(left_outer[...], outer[...]), own, link, chip, 0)
+
+
+def near_tiles(left_inner, left_outer, *refs):
+    images, (own, link, chip) = refs[:-3], refs[-3:]
     for n in range(len(images) // 2):
         tile = dot(left_inner[...], images[2 * n][...]) + dot(left_outer[...], images[2 * n + 1][...])
         store_tile(tile, own, link, chip, n)
@@ -262,15 +266,28 @@
     outer_x = swap(outer, 1)
     outer_y = swap(outer, 2)
     tile_flops = 2 * rows * wide * wide
+    own_own, own_link, own_chip, left_inner, left_outer = call(
+        functools.partial(own_tile, size),
+        (*tile_shapes(1, width, wide), shape((wide, inner_rows), BF16), shape((wide, 2 * rim), BF16)),
+        [VMEM] * 3,
+        [VMEM] * 5,
+        (masked, inner, outer),
+        flops=tile_flops,
+        name="own_tile",
+    )
+    own_link = over_link(own_link)
+    own_chip = over_chip(own_chip)
     half = inner_rows // 2
-    diagonal = (swap(inner_y[:half], 1), swap(inner_x[half:], 2), swap(outer_y[:rim], 1), swap(outer_x[rim:], 2))
-    near_own, near_link, near_chip, left_inner, left_outer = call(
-        functools.partial(near_tiles, size),
-        (*tile_shapes(3, width, wide), shape((wide, inner_rows), BF16), shape((wide, 2 * rim), BF16)),
-        [VMEM] * 7,
-        [VMEM] * 5,
-        (masked, inner, outer, inner_x, outer_x, inner_y, outer_y),
-        flops=3 * tile_flops,
+    inner_d = (swap(inner_y[:half], 1), swap(inner_x[half:], 2))
+    outer_x, outer_y, own_link, own_chip = lax.optimization_barrier((outer_x, outer_y, own_link, own_chip))
+    diagonal = (*inner_d, swap(outer_y[:rim], 1), swap(outer_x[rim:], 2))
+    near_own, near_link, near_chip = call(
+        near_tiles,
+        tile_shapes(2, width, wide),
+        [VMEM] * 6,
+        [VMEM] * 3,
+        (left_inner, left_outer, inner_x, outer_x, inner_y, outer_y),
+        flops=2 * tile_flops,
         name="near_tiles",
     )
     near_link = over_link(near_link)
@@ -302,7 +319,7 @@
             name=name,
         )
 
-    coarse = add(((0, 1, 2),), (near_own, near_link, near_chip), "add_near")
+    coarse = add(((0,), (1, 2)), (own_own, own_link, own_chip, near_own, near_link, near_chip), "add_near")
     coarse = add(((3,),), (far_own, far_link, far_chip), "add_diagonal", coarse)
     return coarse.transpose(1, 0, 2)
 

time: 45.3 us -> 45 us (level)
  starting transfers between devices: 18.2 us -> 17.5 us
    ppermute x8, starting transfers between devices: 13.4 us -> 11.3 us  [swap(): return lax.ppermute(value, 'col', [(i, i ^ step) for i in range(4)])]
    ppermute x3 -> x4, starting transfers between devices: 4.7 us -> 6.1 us  [over_link(): return lax.ppermute(value, 'blk', cross)]
    ppermute x8, waiting for transfers between devices: 12.9 us -> 13.5 us  [swap(): return lax.ppermute(value, 'col', [(i, i ^ step) for i in range(4)])]
    ppermute x3 -> x4, waiting for transfers between devices: 5.19 us -> 4.95 us  [over_link(): return lax.ppermute(value, 'blk', cross)]
    pallas_call x6 -> x7, Pallas kernels: 7.14 us -> 7.15 us  [call(): pl.pallas_call(kernel, out_shape=out_shape, in_specs=in_specs, out_specs=...]
  transfers between devices with their start and end apart: 14 -> 16, of which waited for: 6 -> 8; matrix products, arithmetic and copies ran while one was open for 0% -> 0% of each run, Pallas kernels for 10% -> 10%
where the time goes in v5:
time: 45 us; the launch traced here: 44.8 us
  waiting for transfers between devices  18.5 us (41%)
  starting transfers between devices  17.5 us (39%)
  Pallas kernels  7.15 us (16%)
  local copies, waits for them, and re-layouts  1.54 us (3%)
    ppermute x8, waiting for transfers between devices, swap(): return lax.ppermute(value, 'col', [(i, i ^ step) for i in range(4)])  13.5 us
    ppermute x8, starting transfers between devices, swap(): return lax.ppermute(value, 'col', [(i, i ^ step) for i in range(4)])  11.3 us
    pallas_call x7, Pallas kernels, call(): pl.pallas_call(kernel, out_shape=out_shape, in_specs=in_specs, out_specs=...  7.15 us
    ppermute x4, starting transfers between devices, over_link(): return lax.ppermute(value, 'blk', cross)  6.1 us
    ppermute x4, waiting for transfers between devices, over_link(): return lax.ppermute(value, 'blk', cross)  4.95 us
    unnamed x6, local copies, waits for them, and re-layouts  1.45 us
  transfers between devices with their start and end apart: 16, of which 8 were waited for; matrix products, arithmetic and copies ran while one was open for 0% of the time, Pallas kernels for 10%

profile of v5, /device:TPU:0, one launch (start us, length us, event | category | flops | bytes accessed | tf_op | source)
XLA Modules:
  0.0 44.8 jit_solution(15658509190516851479)
XLA Ops:
  0.0 0.8 %copy-done.1 = s32[8,128,2]{1,2,0:T(2,128)S(1)} copy-done((s32[8,128,2]{1,2,0:T(2,128)S(1)}, s32[8,128,2]{1,2,0:T(2,128)}, u32[]{:S(2)}) %copy-start.1) | copy-done | bytes 8216
  0.8 0.7 %copy-done.2 = s32[8,3]{0,1:T(4,128)S(1)} copy-done((s32[8,3]{0,1:T(4,128)S(1)}, s32[8,3]{0,1:T(4,128)}, u32[]{:S(2)}) %copy-start.2) | copy-done | bytes 120
  1.5 1.8 %mask_and_inner.1 = (bf16[1024,384]{1,0:T(8,128)(2,1)S(1)}, bf16[256,256]{1,0:T(8,128)(2,1)S(1)}, bf16[256,256]{1,0:T(8,128)(2,1)S(1)}, bf16[512,384]{1,0:T(8,128)(2,1)S(1)}) custom-call(s32[3,8]{1,0:T(4,128)S(1)} %bitcast.5, bf16[3,1024,128]{2,1,0:T(8,128)(2,1)} %bitcast.7, s32[8,2,128]{2,1,0:T(2,128)S(1)} %bitcast.4, bf16[8,3,128,128]{3,2,1,0:T(8,128)(2,1)} %stiffness.1), custom_call_target="tpu_custom_call" | custom-call | flops 150994944 | bytes 3022944 | tf_op jit(solution)/shard_map/mask_and_inner/pallas_call | solution.py:29
  3.3 4.6 %collective-permute-start = (bf16[256,256]{1,0:T(8,128)(2,1)S(1)}, bf16[256,256]{1,0:T(8,128)(2,1)S(1)}, u32[]{:S(2)}, u32[]{:S(2)}) collective-permute-start(bf16[256,256]{1,0:T(8,128)(2,1)S(1)} %get-tuple-element.26), channel_id=1, source_target_pairs={{0,28},{4,8},{8,4},{12,16},{16,12},{20,24},{24,20},{28,0},{1,29},{... | collective-permute-start | bytes 393224 | tf_op jit(solution)/shard_map/ppermute | solution.py:224
  7.9 1.5 %collective-permute-start.2 = (bf16[512,384]{1,0:T(8,128)(2,1)S(1)}, bf16[512,384]{1,0:T(8,128)(2,1)S(1)}, u32[]{:S(2)}, u32[]{:S(2)}) collective-permute-start(bf16[512,384]{1,0:T(8,128)(2,1)S(1)} %get-tuple-element.25.inner), channel_id=1, source_target_pairs={{0,2},{1,3},{2,0},{3,1},{4,6},{5,7},{6,4},{7,5},{8,10},{9,11},{10,... | collective-permute-start | bytes 1179656 | tf_op jit(solution)/shard_map/ppermute | solution.py:227
  9.4 1.5 %collective-permute-start.4 = (bf16[512,384]{1,0:T(8,128)(2,1)S(1)}, bf16[512,384]{1,0:T(8,128)(2,1)S(1)}, u32[]{:S(2)}, u32[]{:S(2)}) collective-permute-start(bf16[512,384]{1,0:T(8,128)(2,1)S(1)} %get-tuple-element.25.inner), channel_id=1, source_target_pairs={{0,1},{1,0},{2,3},{3,2},{4,5},{5,4},{6,7},{7,6},{8,9},{9,8},{10,11... | collective-permute-start | bytes 1179656 | tf_op jit(solution)/shard_map/ppermute | solution.py:227
  11.1 1.1 %outer_image.1.outer = bf16[512,384]{1,0:T(8,128)(2,1)S(1)} custom-call(s32[3,8]{1,0:T(4,128)S(1)} %bitcast.6, bf16[8,3,128,128]{3,2,1,0:T(8,128)(2,1)S(1)} %copy-done, bf16[1024,384]{1,0:T(8,128)(2,1)S(1)} %get-tuple-element.24.masked, bf16[256,256]{1,0:T(8,128)(2,1)S(1)} %collective-permute-done.from_link, ...), custom_call_target="tpu_custom_call" | custom-call | flops 150994944 | bytes 2228320 | tf_op jit(solution)/shard_map/outer_image/pallas_call | solution.py:29
  12.2 2.6 %collective-permute-start.6 = (bf16[512,384]{1,0:T(8,128)(2,1)S(1)}, bf16[512,384]{1,0:T(8,128)(2,1)S(1)}, u32[]{:S(2)}, u32[]{:S(2)}) collective-permute-start(bf16[512,384]{1,0:T(8,128)(2,1)S(1)} %outer_image.1.outer), channel_id=1, source_target_pairs={{0,1},{1,0},{2,3},{3,2},{4,5},{5,4},{6,7},{7,6},{8,9},{9,8},{10,11... | collective-permute-start | bytes 1179656 | tf_op jit(solution)/shard_map/ppermute | solution.py:227
  14.8 1.5 %collective-permute-start.7 = (bf16[512,384]{1,0:T(8,128)(2,1)S(1)}, bf16[512,384]{1,0:T(8,128)(2,1)S(1)}, u32[]{:S(2)}, u32[]{:S(2)}) collective-permute-start(bf16[512,384]{1,0:T(8,128)(2,1)S(1)} %outer_image.1.outer), channel_id=1, source_target_pairs={{0,2},{1,3},{2,0},{3,1},{4,6},{5,7},{6,4},{7,5},{8,10},{9,11},{10,... | collective-permute-start | bytes 1179656 | tf_op jit(solution)/shard_map/ppermute | solution.py:227
  16.3 0.6 %own_tile.1 = (f32[1,128,384]{2,1,0:T(8,128)S(1)}, bf16[1,128,384]{2,1,0:T(8,128)(2,1)S(1)}, bf16[1,128,384]{2,1,0:T(8,128)(2,1)S(1)}, bf16[384,512]{1,0:T(8,128)(2,1)S(1)}, bf16[384,512]{1,0:T(8,128)(2,1)S(1)}) custom-call(bf16[1024,384]{1,0:T(8,128)(2,1)S(1)} %get-tuple-element.24.masked, bf16[512,384]{1,0:T(8,128)(2,1)S(1)} %get-tuple-element.25.inner, ...), custom_call_target="tpu_custom_call" | custom-call | flops 301989888 | bytes 2752512 | tf_op jit(solution)/shard_map/own_tile/pallas_call | solution.py:29
  17.0 1.4 %collective-permute-start.8 = (bf16[1,128,384]{2,1,0:T(8,128)(2,1)S(1)}, bf16[1,128,384]{2,1,0:T(8,128)(2,1)S(1)}, u32[]{:S(2)}, u32[]{:S(2)}) collective-permute-start(bf16[1,128,384]{2,1,0:T(8,128)(2,1)S(1)} %get-tuple-element.30), channel_id=1, source_target_pairs={{0,28},{4,8},{8,4},{12,16},{16,12},{20,24},{24,20},{28,0},{1,29},{... | collective-permute-start | bytes 294920 | tf_op jit(solution)/shard_map/ppermute | solution.py:224
  18.4 1.4 %collective-permute-done.2.refs_2_ = bf16[512,384]{1,0:T(8,128)(2,1)S(1)} collective-permute-done((bf16[512,384]{1,0:T(8,128)(2,1)S(1)}, bf16[512,384]{1,0:T(8,128)(2,1)S(1)}, u32[]{:S(2)}, u32[]{:S(2)}) %collective-permute-start.2) | collective-permute-done | bytes 393248 | tf_op jit(solution)/shard_map/ppermute | solution.py:227
  19.8 1.5 %collective-permute-done.4.refs_0_ = bf16[512,384]{1,0:T(8,128)(2,1)S(1)} collective-permute-done((bf16[512,384]{1,0:T(8,128)(2,1)S(1)}, bf16[512,384]{1,0:T(8,128)(2,1)S(1)}, u32[]{:S(2)}, u32[]{:S(2)}) %collective-permute-start.4) | collective-permute-done | bytes 393248 | tf_op jit(solution)/shard_map/ppermute | solution.py:227
  21.3 1.5 %collective-permute-start.3 = (bf16[256,384]{1,0:T(8,128)(2,1)S(1)}, bf16[256,384]{1,0:T(8,128)(2,1)S(1)}, u32[]{:S(2)}, u32[]{:S(2)}) collective-permute-start(bf16[256,384]{1,0:T(8,128)(2,1)S(1)} %slice.16), channel_id=1, source_target_pairs={{0,1},{1,0},{2,3},{3,2},{4,5},{5,4},{6,7},{7,6},{8,9},{9,8},{10,11... | collective-permute-start | bytes 589832 | tf_op jit(solution)/shard_map/ppermute | solution.py:227
  23.4 6.3 %collective-permute-done.6.refs_1_ = bf16[512,384]{1,0:T(8,128)(2,1)S(1)} collective-permute-done((bf16[512,384]{1,0:T(8,128)(2,1)S(1)}, bf16[512,384]{1,0:T(8,128)(2,1)S(1)}, u32[]{:S(2)}, u32[]{:S(2)}) %collective-permute-start.6) | collective-permute-done | bytes 393248 | tf_op jit(solution)/shard_map/ppermute | solution.py:227
  29.8 1.6 %collective-permute-start.10 = (bf16[256,384]{1,0:T(8,128)(2,1)S(1)}, bf16[256,384]{1,0:T(8,128)(2,1)S(1)}, u32[]{:S(2)}, u32[]{:S(2)}) collective-permute-start(bf16[256,384]{1,0:T(8,128)(2,1)S(1)} %slice.14), channel_id=1, source_target_pairs={{0,1},{1,0},{2,3},{3,2},{4,5},{5,4},{6,7},{7,6},{8,9},{9,8},{10,11... | collective-permute-start | bytes 589832 | tf_op jit(solution)/shard_map/ppermute | solution.py:227
  31.9 1.2 %near_tiles.1 = (f32[2,128,384]{2,1,0:T(8,128)S(1)}, bf16[2,128,384]{2,1,0:T(8,128)(2,1)S(1)}, bf16[2,128,384]{2,1,0:T(8,128)(2,1)S(1)}) custom-call(bf16[384,512]{1,0:T(8,128)(2,1)S(1)} %get-tuple-element.28.left_inner, bf16[384,512]{1,0:T(8,128)(2,1)S(1)} %get-tuple-element.29.left_outer, bf16[512,384]{1,0:T(8,128)(2,1)S(1)} %collective-permute-done.4.refs_0_, ...), custom_call_target="tpu_custom_call" | custom-call | flops 603979776 | bytes 3145728 | tf_op jit(solution)/shard_map/near_tiles/pallas_call | solution.py:29
  33.2 0.8 %collective-permute-done.3.refs_0_ = bf16[256,384]{1,0:T(8,128)(2,1)S(1)} collective-permute-done((bf16[256,384]{1,0:T(8,128)(2,1)S(1)}, bf16[256,384]{1,0:T(8,128)(2,1)S(1)}, u32[]{:S(2)}, u32[]{:S(2)}) %collective-permute-start.3) | collective-permute-done | bytes 196640 | tf_op jit(solution)/shard_map/ppermute | solution.py:227
  34.0 3.5 %collective-permute-done.10.refs_2_ = bf16[256,384]{1,0:T(8,128)(2,1)S(1)} collective-permute-done((bf16[256,384]{1,0:T(8,128)(2,1)S(1)}, bf16[256,384]{1,0:T(8,128)(2,1)S(1)}, u32[]{:S(2)}, u32[]{:S(2)}) %collective-permute-start.10) | collective-permute-done | bytes 196640 | tf_op jit(solution)/shard_map/ppermute | solution.py:227
  37.5 0.6 %diagonal_tile.1 = (f32[1,128,384]{2,1,0:T(8,128)S(1)}, bf16[1,128,384]{2,1,0:T(8,128)(2,1)S(1)}, bf16[1,128,384]{2,1,0:T(8,128)(2,1)S(1)}) custom-call(bf16[384,512]{1,0:T(8,128)(2,1)S(1)} %get-tuple-element.28.left_inner, bf16[384,512]{1,0:T(8,128)(2,1)S(1)} %get-tuple-element.29.left_outer, bf16[256,384]{1,0:T(8,128)(2,1)S(1)} %collective-permute-done.3.refs_0_, ...), custom_call_target="tpu_custom_call" | custom-call | flops 301989888 | bytes 1966080 | tf_op jit(solution)/shard_map/diagonal_tile/pallas_call | solution.py:29
  38.2 1.9 %collective-permute-done.14.refs_4_ = bf16[2,128,384]{2,1,0:T(8,128)(2,1)S(1)} collective-permute-done((bf16[2,128,384]{2,1,0:T(8,128)(2,1)S(1)}, bf16[2,128,384]{2,1,0:T(8,128)(2,1)S(1)}, u32[]{:S(2)}, u32[]{:S(2)}) %collective-permute-start.14) | collective-permute-done | bytes 196640 | tf_op jit(solution)/shard_map/ppermute | solution.py:224
  40.2 1.0 %add_near.1.refs_3_ = f32[5,128,512]{2,1,0:T(8,128)} custom-call(f32[1,128,384]{2,1,0:T(8,128)S(1)} %get-tuple-element.37.refs_0_, bf16[1,128,384]{2,1,0:T(8,128)(2,1)S(1)} %collective-permute-done.8.refs_1_, bf16[1,128,384]{2,1,0:T(8,128)(2,1)S(1)} %collective-permute-done.9.refs_2_, f32[2,128,384]{2,1,0:T(8,128)S(1)} %get-tuple-element.40.refs_3_, ...), custom_call_target="tpu_custom_call" | custom-call | flops 245760 | bytes 2490368 | tf_op jit(solution)/shard_map/add_near/pallas_call | solution.py:29
  41.2 2.8 %collective-permute-done.12.refs_1_ = bf16[1,128,384]{2,1,0:T(8,128)(2,1)S(1)} collective-permute-done((bf16[1,128,384]{2,1,0:T(8,128)(2,1)S(1)}, bf16[1,128,384]{2,1,0:T(8,128)(2,1)S(1)}, u32[]{:S(2)}, u32[]{:S(2)}) %collective-permute-start.12) | collective-permute-done | bytes 98336 | tf_op jit(solution)/shard_map/ppermute | solution.py:224
  44.0 0.8 %add_diagonal.1 = f32[5,128,512]{2,1,0:T(8,128)} custom-call(f32[1,128,384]{2,1,0:T(8,128)S(1)} %get-tuple-element.34.refs_0_, bf16[1,128,384]{2,1,0:T(8,128)(2,1)S(1)} %collective-permute-done.12.refs_1_, bf16[1,128,384]{2,1,0:T(8,128)(2,1)S(1)} %collective-permute-done.13.refs_2_, f32[5,128,512]{2,1,0:T(8,128)} %add_near.1.refs_3_), custom_call_target="tpu_custom_call", output_to_operand_aliasing={{}: (3, {})} | custom-call | flops 81920 | bytes 3014656 | tf_op jit(solution)/shard_map/add_diagonal/pallas_call | solution.py:29
  (25 shorter events, 1.7 us)
Async XLA Ops:
  0.0 11.1 %copy-start = (bf16[8,3,128,128]{3,2,1,0:T(8,128)(2,1)S(1)}, bf16[8,3,128,128]{3,2,1,0:T(8,128)(2,1)}, u32[]{:S(2)}) copy-start(bf16[8,3,128,128]{3,2,1,0:T(8,128)(2,1)} %stiffness.1) | copy-start | bytes 2359300
  0.0 0.8 %copy-start.1 = (s32[8,128,2]{1,2,0:T(2,128)S(1)}, s32[8,128,2]{1,2,0:T(2,128)}, u32[]{:S(2)}) copy-start(s32[8,128,2]{1,2,0:T(2,128)} %param.7) | copy-start | bytes 24580
  0.8 0.7 %copy-start.2 = (s32[8,3]{0,1:T(4,128)S(1)}, s32[8,3]{0,1:T(4,128)}, u32[]{:S(2)}) copy-start(s32[8,3]{0,1:T(4,128)} %param.5) | copy-start | bytes 292
  3.3 7.8 %collective-permute-start = (bf16[256,256]{1,0:T(8,128)(2,1)S(1)}, bf16[256,256]{1,0:T(8,128)(2,1)S(1)}, u32[]{:S(2)}, u32[]{:S(2)}) collective-permute-start(bf16[256,256]{1,0:T(8,128)(2,1)S(1)} %get-tuple-element.26), channel_id=1, source_target_pairs={{0,28},{4,8},{8,4},{12,16},{16,12},{20,24},{24,20},{28,0},{1,29},{... | collective-permute-start | bytes 393224 | tf_op jit(solution)/shard_map/ppermute | solution.py:224
  7.8 3.2 %collective-permute-start.1 = (bf16[256,256]{1,0:T(8,128)(2,1)S(1)}, bf16[256,256]{1,0:T(8,128)(2,1)S(1)}, u32[]{:S(2)}, u32[]{:S(2)}) collective-permute-start(bf16[256,256]{1,0:T(8,128)(2,1)S(1)} %get-tuple-element.27), channel_id=1, source_target_pairs={{0,4},{4,0},{8,12},{12,8},{16,20},{20,16},{24,28},{28,24},{1,5},{5... | collective-permute-start | bytes 393224 | tf_op jit(solution)/shard_map/ppermute | solution.py:221
  7.9 11.9 %collective-permute-start.2 = (bf16[512,384]{1,0:T(8,128)(2,1)S(1)}, bf16[512,384]{1,0:T(8,128)(2,1)S(1)}, u32[]{:S(2)}, u32[]{:S(2)}) collective-permute-start(bf16[512,384]{1,0:T(8,128)(2,1)S(1)} %get-tuple-element.25.inner), channel_id=1, source_target_pairs={{0,2},{1,3},{2,0},{3,1},{4,6},{5,7},{6,4},{7,5},{8,10},{9,11},{10,... | collective-permute-start | bytes 1179656 | tf_op jit(solution)/shard_map/ppermute | solution.py:227
  9.4 11.9 %collective-permute-start.4 = (bf16[512,384]{1,0:T(8,128)(2,1)S(1)}, bf16[512,384]{1,0:T(8,128)(2,1)S(1)}, u32[]{:S(2)}, u32[]{:S(2)}) collective-permute-start(bf16[512,384]{1,0:T(8,128)(2,1)S(1)} %get-tuple-element.25.inner), channel_id=1, source_target_pairs={{0,1},{1,0},{2,3},{3,2},{4,5},{5,4},{6,7},{7,6},{8,9},{9,8},{10,11... | collective-permute-start | bytes 1179656 | tf_op jit(solution)/shard_map/ppermute | solution.py:227
  12.2 17.6 %collective-permute-start.6 = (bf16[512,384]{1,0:T(8,128)(2,1)S(1)}, bf16[512,384]{1,0:T(8,128)(2,1)S(1)}, u32[]{:S(2)}, u32[]{:S(2)}) collective-permute-start(bf16[512,384]{1,0:T(8,128)(2,1)S(1)} %outer_image.1.outer), channel_id=1, source_target_pairs={{0,1},{1,0},{2,3},{3,2},{4,5},{5,4},{6,7},{7,6},{8,9},{9,8},{10,11... | collective-permute-start | bytes 1179656 | tf_op jit(solution)/shard_map/ppermute | solution.py:227
  14.8 14.9 %collective-permute-start.7 = (bf16[512,384]{1,0:T(8,128)(2,1)S(1)}, bf16[512,384]{1,0:T(8,128)(2,1)S(1)}, u32[]{:S(2)}, u32[]{:S(2)}) collective-permute-start(bf16[512,384]{1,0:T(8,128)(2,1)S(1)} %outer_image.1.outer), channel_id=1, source_target_pairs={{0,2},{1,3},{2,0},{3,1},{4,6},{5,7},{6,4},{7,5},{8,10},{9,11},{10,... | collective-permute-start | bytes 1179656 | tf_op jit(solution)/shard_map/ppermute | solution.py:227
  17.0 5.9 %collective-permute-start.8 = (bf16[1,128,384]{2,1,0:T(8,128)(2,1)S(1)}, bf16[1,128,384]{2,1,0:T(8,128)(2,1)S(1)}, u32[]{:S(2)}, u32[]{:S(2)}) collective-permute-start(bf16[1,128,384]{2,1,0:T(8,128)(2,1)S(1)} %get-tuple-element.30), channel_id=1, source_target_pairs={{0,28},{4,8},{8,4},{12,16},{16,12},{20,24},{24,20},{28,0},{1,29},{... | collective-permute-start | bytes 294920 | tf_op jit(solution)/shard_map/ppermute | solution.py:224
  19.8 3.7 %collective-permute-start.9 = (bf16[1,128,384]{2,1,0:T(8,128)(2,1)S(1)}, bf16[1,128,384]{2,1,0:T(8,128)(2,1)S(1)}, u32[]{:S(2)}, u32[]{:S(2)}) collective-permute-start(bf16[1,128,384]{2,1,0:T(8,128)(2,1)S(1)} %get-tuple-element.31), channel_id=1, source_target_pairs={{0,4},{4,0},{8,12},{12,8},{16,20},{20,16},{24,28},{28,24},{1,5},{5... | collective-permute-start | bytes 294920 | tf_op jit(solution)/shard_map/ppermute | solution.py:221
  21.3 12.6 %collective-permute-start.3 = (bf16[256,384]{1,0:T(8,128)(2,1)S(1)}, bf16[256,384]{1,0:T(8,128)(2,1)S(1)}, u32[]{:S(2)}, u32[]{:S(2)}) collective-permute-start(bf16[256,384]{1,0:T(8,128)(2,1)S(1)} %slice.16), channel_id=1, source_target_pairs={{0,1},{1,0},{2,3},{3,2},{4,5},{5,4},{6,7},{7,6},{8,9},{9,8},{10,11... | collective-permute-start | bytes 589832 | tf_op jit(solution)/shard_map/ppermute | solution.py:227
  22.9 11.1 %collective-permute-start.5 = (bf16[256,384]{1,0:T(8,128)(2,1)S(1)}, bf16[256,384]{1,0:T(8,128)(2,1)S(1)}, u32[]{:S(2)}, u32[]{:S(2)}) collective-permute-start(bf16[256,384]{1,0:T(8,128)(2,1)S(1)} %slice.17), channel_id=1, source_target_pairs={{0,2},{1,3},{2,0},{3,1},{4,6},{5,7},{6,4},{7,5},{8,10},{9,11},{10,... | collective-permute-start | bytes 589832 | tf_op jit(solution)/shard_map/ppermute | solution.py:227
  29.8 7.7 %collective-permute-start.10 = (bf16[256,384]{1,0:T(8,128)(2,1)S(1)}, bf16[256,384]{1,0:T(8,128)(2,1)S(1)}, u32[]{:S(2)}, u32[]{:S(2)}) collective-permute-start(bf16[256,384]{1,0:T(8,128)(2,1)S(1)} %slice.14), channel_id=1, source_target_pairs={{0,1},{1,0},{2,3},{3,2},{4,5},{5,4},{6,7},{7,6},{8,9},{9,8},{10,11... | collective-permute-start | bytes 589832 | tf_op jit(solution)/shard_map/ppermute | solution.py:227
  31.4 6.1 %collective-permute-start.11 = (bf16[256,384]{1,0:T(8,128)(2,1)S(1)}, bf16[256,384]{1,0:T(8,128)(2,1)S(1)}, u32[]{:S(2)}, u32[]{:S(2)}) collective-permute-start(bf16[256,384]{1,0:T(8,128)(2,1)S(1)} %slice.15), channel_id=1, source_target_pairs={{0,2},{1,3},{2,0},{3,1},{4,6},{5,7},{6,4},{7,5},{8,10},{9,11},{10,... | collective-permute-start | bytes 589832 | tf_op jit(solution)/shard_map/ppermute | solution.py:227
  33.1 7.1 %collective-permute-start.14 = (bf16[2,128,384]{2,1,0:T(8,128)(2,1)S(1)}, bf16[2,128,384]{2,1,0:T(8,128)(2,1)S(1)}, u32[]{:S(2)}, u32[]{:S(2)}) collective-permute-start(bf16[2,128,384]{2,1,0:T(8,128)(2,1)S(1)} %get-tuple-element.41), channel_id=1, source_target_pairs={{0,28},{4,8},{8,4},{12,16},{16,12},{20,24},{24,20},{28,0},{1,29},{... | collective-permute-start | bytes 589832 | tf_op jit(solution)/shard_map/ppermute | solution.py:224
  34.0 6.2 %collective-permute-start.15 = (bf16[2,128,384]{2,1,0:T(8,128)(2,1)S(1)}, bf16[2,128,384]{2,1,0:T(8,128)(2,1)S(1)}, u32[]{:S(2)}, u32[]{:S(2)}) collective-permute-start(bf16[2,128,384]{2,1,0:T(8,128)(2,1)S(1)} %get-tuple-element.42), channel_id=1, source_target_pairs={{0,4},{4,0},{8,12},{12,8},{16,20},{20,16},{24,28},{28,24},{1,5},{5... | collective-permute-start | bytes 589832 | tf_op jit(solution)/shard_map/ppermute | solution.py:221
  38.1 5.9 %collective-permute-start.12 = (bf16[1,128,384]{2,1,0:T(8,128)(2,1)S(1)}, bf16[1,128,384]{2,1,0:T(8,128)(2,1)S(1)}, u32[]{:S(2)}, u32[]{:S(2)}) collective-permute-start(bf16[1,128,384]{2,1,0:T(8,128)(2,1)S(1)} %get-tuple-element.35), channel_id=1, source_target_pairs={{0,28},{4,8},{8,4},{12,16},{16,12},{20,24},{24,20},{28,0},{1,29},{... | collective-permute-start | bytes 294920 | tf_op jit(solution)/shard_map/ppermute | solution.py:224
  38.2 5.8 %collective-permute-start.13 = (bf16[1,128,384]{2,1,0:T(8,128)(2,1)S(1)}, bf16[1,128,384]{2,1,0:T(8,128)(2,1)S(1)}, u32[]{:S(2)}, u32[]{:S(2)}) collective-permute-start(bf16[1,128,384]{2,1,0:T(8,128)(2,1)S(1)} %get-tuple-element.36), channel_id=1, source_target_pairs={{0,4},{4,0},{8,12},{12,8},{16,20},{20,16},{24,28},{28,24},{1,5},{5... | collective-permute-start | bytes 294920 | tf_op jit(solution)/shard_map/ppermute | solution.py:221

commit v6 on v5

--- a/solution.py
+++ b/solution.py
@@ -23,7 +23,7 @@
     return jnp.dot(left, right, preferred_element_type=F32)
 
 
-def call(kernel, out_shape, in_specs, out_specs, args, scratch=(), flops=0, aliases=None, name=None, vmem=24 << 10):
+def call(kernel, out_shape, in_specs, out_specs, args, scratch=(), flops=0, aliases=None, name=None):
     outs = jax.tree.leaves(out_shape)
     moved = sum(x.size * x.dtype.itemsize for x in (*args, *outs))
     return pl.pallas_call(
@@ -34,7 +34,7 @@
         scratch_shapes=list(scratch),
         input_output_aliases=aliases or {},
         cost_estimate=pl.CostEstimate(flops=flops, bytes_accessed=moved, transcendentals=0),
-        compiler_params=pltpu.CompilerParams(vmem_limit_bytes=vmem << 10),
+        compiler_params=pltpu.CompilerParams(vmem_limit_bytes=24 << 20),
         name=name,
     )(*args)
 
@@ -60,19 +60,22 @@
     groups, _, width = basis.shape
     slabs = reach.shape[0]
     slab = lax.axis_index("blk")
-    copies = [
-        pltpu.make_async_copy(source, target, sem.at[n])
-        for n, (source, target) in enumerate(
-            ((basis_hbm, basis), (stiffness_hbm, stiffness), (reach_hbm, reach), (cols_hbm, cols))
-        )
+    inner_blocks = pl.ds(RIM, blocks - 2 * RIM)
+    moves = [(reach_hbm, reach), (cols_hbm, cols)]
+    moves += [
+        (basis_hbm.at[:, pl.ds(b * size, RIM * size)], basis.at[:, pl.ds(b * size, RIM * size)])
+        for b in range(0, blocks, RIM)
     ]
+    moves.append((stiffness_hbm.at[inner_blocks], stiffness.at[inner_blocks]))
+    copies = [pltpu.make_async_copy(source, target, sem.at[n]) for n, (source, target) in enumerate(moves)]
     for copy in copies:
         copy.start()
-    copies[2].wait()
     copies[0].wait()
     low = reach[pl.ds(lax.rem(slab + slabs - 1, slabs), 1), 1, :]
     high = reach[pl.ds(lax.rem(slab + 1, slabs), 1), 0, :]
     for b in range(blocks):
+        if b % RIM == 0:
+            copies[2 + b // RIM].wait()
         rows = slice(b * size, (b + 1) * size)
         keep = {0: (b < low).astype(F32).astype(BF16), 2: (b >= blocks - high).astype(F32).astype(BF16)}
         for g in range(groups):
@@ -90,8 +93,8 @@
         to_link[...] = masked[(blocks - RIM) * size :, width:]
         to_chip[...] = masked[: RIM * size, : 2 * width]
 
-    copies[3].wait()
     copies[1].wait()
+    copies[-1].wait()
     for b in range(RIM, blocks - RIM):
         starts = [jnp.clip(p - RIM, 0, blocks - 1) for p in positions(cols, b, blocks, slots, total_blocks)]
         inner[(b - RIM) * size : (b - RIM + 1) * size, :] = block_image(stiffness, masked, b, size, starts)
@@ -237,16 +240,15 @@
         (shape((rows, wide), BF16), shape((rim, 2 * width), BF16), shape((rim, 2 * width), BF16), shape((inner_rows, wide), BF16)),
         [HBM] * 4,
         [VMEM] * 4,
-        (cols, flat, reach, stiffness),
+        tuple(pltpu.with_memory_space_constraint(x, pltpu.HBM) for x in (cols, flat, reach, stiffness)),
         scratch=[
             pltpu.SMEM(cols.shape, cols.dtype),
             pltpu.VMEM(flat.shape, BF16),
             pltpu.VMEM(reach.shape, reach.dtype),
             pltpu.VMEM(stiffness.shape, BF16),
-            pltpu.SemaphoreType.DMA((4,)),
+            pltpu.SemaphoreType.DMA((3 + blocks // RIM,)),
         ],
         flops=row_flops * (blocks - 2 * RIM),
-        vmem=53248,
         name="mask_and_inner",
     )
     inner_x = swap(inner, 1)

time: 45 us -> 43.6 us (0.969)
  local copies, waits for them, and re-layouts: 1.54 us -> 0.09 us
    unnamed x6 -> x4, local copies, waits for them, and re-layouts: 1.45 us -> 0.01 us
where the time goes in v6:
time: 43.6 us; the launch traced here: 43.4 us
  waiting for transfers between devices  18.5 us (42%)
  starting transfers between devices  17.5 us (40%)
  Pallas kernels  7.24 us (17%)
    ppermute x8, waiting for transfers between devices, swap(): return lax.ppermute(value, 'col', [(i, i ^ step) for i in range(4)])  13.5 us
    ppermute x8, starting transfers between devices, swap(): return lax.ppermute(value, 'col', [(i, i ^ step) for i in range(4)])  11.3 us
    pallas_call x7, Pallas kernels, call(): pl.pallas_call(kernel, out_shape=out_shape, in_specs=in_specs, out_specs=...  7.24 us
    ppermute x4, starting transfers between devices, over_link(): return lax.ppermute(value, 'blk', cross)  6.1 us
    ppermute x4, waiting for transfers between devices, over_link(): return lax.ppermute(value, 'blk', cross)  4.97 us
  transfers between devices with their start and end apart: 16, of which 8 were waited for; matrix products, arithmetic and copies ran while one was open for 0% of the time, Pallas kernels for 10%

profile of v6, /device:TPU:0, one launch (start us, length us, event | category | flops | bytes accessed | tf_op | source)
XLA Modules:
  0.0 43.4 jit_solution(5763737232750735829)
XLA Ops:
  0.0 1.9 %mask_and_inner.1 = (bf16[1024,384]{1,0:T(8,128)(2,1)S(1)}, bf16[256,256]{1,0:T(8,128)(2,1)S(1)}, bf16[256,256]{1,0:T(8,128)(2,1)S(1)}, bf16[512,384]{1,0:T(8,128)(2,1)S(1)}) custom-call(s32[3,8]{1,0:T(4,128)} %bitcast.4, bf16[3,1024,128]{2,1,0:T(8,128)(2,1)} %bitcast.6, s32[8,2,128]{2,1,0:T(2,128)} %bitcast.7, bf16[8,3,128,128]{3,2,1,0:T(8,128)(2,1)} %stiffness.1), custom_call_target="tpu_custom_call" | custom-call | flops 150994944 | bytes 3022944 | tf_op jit(solution)/shard_map/mask_and_inner/pallas_call | solution.py:29
  1.9 4.6 %collective-permute-start = (bf16[256,256]{1,0:T(8,128)(2,1)S(1)}, bf16[256,256]{1,0:T(8,128)(2,1)S(1)}, u32[]{:S(2)}, u32[]{:S(2)}) collective-permute-start(bf16[256,256]{1,0:T(8,128)(2,1)S(1)} %get-tuple-element.26), channel_id=1, source_target_pairs={{0,28},{4,8},{8,4},{12,16},{16,12},{20,24},{24,20},{28,0},{1,29},{... | collective-permute-start | bytes 393224 | tf_op jit(solution)/shard_map/ppermute | solution.py:227
  6.5 1.5 %collective-permute-start.2 = (bf16[512,384]{1,0:T(8,128)(2,1)S(1)}, bf16[512,384]{1,0:T(8,128)(2,1)S(1)}, u32[]{:S(2)}, u32[]{:S(2)}) collective-permute-start(bf16[512,384]{1,0:T(8,128)(2,1)S(1)} %get-tuple-element.25.inner), channel_id=1, source_target_pairs={{0,2},{1,3},{2,0},{3,1},{4,6},{5,7},{6,4},{7,5},{8,10},{9,11},{10,... | collective-permute-start | bytes 1179656 | tf_op jit(solution)/shard_map/ppermute | solution.py:230
  8.0 1.5 %collective-permute-start.4 = (bf16[512,384]{1,0:T(8,128)(2,1)S(1)}, bf16[512,384]{1,0:T(8,128)(2,1)S(1)}, u32[]{:S(2)}, u32[]{:S(2)}) collective-permute-start(bf16[512,384]{1,0:T(8,128)(2,1)S(1)} %get-tuple-element.25.inner), channel_id=1, source_target_pairs={{0,1},{1,0},{2,3},{3,2},{4,5},{5,4},{6,7},{7,6},{8,9},{9,8},{10,11... | collective-permute-start | bytes 1179656 | tf_op jit(solution)/shard_map/ppermute | solution.py:230
  9.7 1.1 %outer_image.1.outer = bf16[512,384]{1,0:T(8,128)(2,1)S(1)} custom-call(s32[3,8]{1,0:T(4,128)S(1)} %bitcast.5, bf16[8,3,128,128]{3,2,1,0:T(8,128)(2,1)S(1)} %copy-done, bf16[1024,384]{1,0:T(8,128)(2,1)S(1)} %get-tuple-element.24.masked, bf16[256,256]{1,0:T(8,128)(2,1)S(1)} %collective-permute-done.from_link, ...), custom_call_target="tpu_custom_call" | custom-call | flops 150994944 | bytes 2228320 | tf_op jit(solution)/shard_map/outer_image/pallas_call | solution.py:29
  10.8 2.6 %collective-permute-start.6 = (bf16[512,384]{1,0:T(8,128)(2,1)S(1)}, bf16[512,384]{1,0:T(8,128)(2,1)S(1)}, u32[]{:S(2)}, u32[]{:S(2)}) collective-permute-start(bf16[512,384]{1,0:T(8,128)(2,1)S(1)} %outer_image.1.outer), channel_id=1, source_target_pairs={{0,1},{1,0},{2,3},{3,2},{4,5},{5,4},{6,7},{7,6},{8,9},{9,8},{10,11... | collective-permute-start | bytes 1179656 | tf_op jit(solution)/shard_map/ppermute | solution.py:230
  13.5 1.5 %collective-permute-start.7 = (bf16[512,384]{1,0:T(8,128)(2,1)S(1)}, bf16[512,384]{1,0:T(8,128)(2,1)S(1)}, u32[]{:S(2)}, u32[]{:S(2)}) collective-permute-start(bf16[512,384]{1,0:T(8,128)(2,1)S(1)} %outer_image.1.outer), channel_id=1, source_target_pairs={{0,2},{1,3},{2,0},{3,1},{4,6},{5,7},{6,4},{7,5},{8,10},{9,11},{10,... | collective-permute-start | bytes 1179656 | tf_op jit(solution)/shard_map/ppermute | solution.py:230
  15.0 0.6 %own_tile.1 = (f32[1,128,384]{2,1,0:T(8,128)S(1)}, bf16[1,128,384]{2,1,0:T(8,128)(2,1)S(1)}, bf16[1,128,384]{2,1,0:T(8,128)(2,1)S(1)}, bf16[384,512]{1,0:T(8,128)(2,1)S(1)}, bf16[384,512]{1,0:T(8,128)(2,1)S(1)}) custom-call(bf16[1024,384]{1,0:T(8,128)(2,1)S(1)} %get-tuple-element.24.masked, bf16[512,384]{1,0:T(8,128)(2,1)S(1)} %get-tuple-element.25.inner, ...), custom_call_target="tpu_custom_call" | custom-call | flops 301989888 | bytes 2752512 | tf_op jit(solution)/shard_map/own_tile/pallas_call | solution.py:29
  15.6 1.4 %collective-permute-start.8 = (bf16[1,128,384]{2,1,0:T(8,128)(2,1)S(1)}, bf16[1,128,384]{2,1,0:T(8,128)(2,1)S(1)}, u32[]{:S(2)}, u32[]{:S(2)}) collective-permute-start(bf16[1,128,384]{2,1,0:T(8,128)(2,1)S(1)} %get-tuple-element.30), channel_id=1, source_target_pairs={{0,28},{4,8},{8,4},{12,16},{16,12},{20,24},{24,20},{28,0},{1,29},{... | collective-permute-start | bytes 294920 | tf_op jit(solution)/shard_map/ppermute | solution.py:227
  17.0 1.4 %collective-permute-done.2.refs_2_ = bf16[512,384]{1,0:T(8,128)(2,1)S(1)} collective-permute-done((bf16[512,384]{1,0:T(8,128)(2,1)S(1)}, bf16[512,384]{1,0:T(8,128)(2,1)S(1)}, u32[]{:S(2)}, u32[]{:S(2)}) %collective-permute-start.2) | collective-permute-done | bytes 393248 | tf_op jit(solution)/shard_map/ppermute | solution.py:230
  18.4 1.5 %collective-permute-done.4.refs_0_ = bf16[512,384]{1,0:T(8,128)(2,1)S(1)} collective-permute-done((bf16[512,384]{1,0:T(8,128)(2,1)S(1)}, bf16[512,384]{1,0:T(8,128)(2,1)S(1)}, u32[]{:S(2)}, u32[]{:S(2)}) %collective-permute-start.4) | collective-permute-done | bytes 393248 | tf_op jit(solution)/shard_map/ppermute | solution.py:230
  20.0 1.5 %collective-permute-start.3 = (bf16[256,384]{1,0:T(8,128)(2,1)S(1)}, bf16[256,384]{1,0:T(8,128)(2,1)S(1)}, u32[]{:S(2)}, u32[]{:S(2)}) collective-permute-start(bf16[256,384]{1,0:T(8,128)(2,1)S(1)} %slice.16), channel_id=1, source_target_pairs={{0,1},{1,0},{2,3},{3,2},{4,5},{5,4},{6,7},{7,6},{8,9},{9,8},{10,11... | collective-permute-start | bytes 589832 | tf_op jit(solution)/shard_map/ppermute | solution.py:230
  21.5 0.5 %collective-permute-start.5 = (bf16[256,384]{1,0:T(8,128)(2,1)S(1)}, bf16[256,384]{1,0:T(8,128)(2,1)S(1)}, u32[]{:S(2)}, u32[]{:S(2)}) collective-permute-start(bf16[256,384]{1,0:T(8,128)(2,1)S(1)} %slice.17), channel_id=1, source_target_pairs={{0,2},{1,3},{2,0},{3,1},{4,6},{5,7},{6,4},{7,5},{8,10},{9,11},{10,... | collective-permute-start | bytes 589832 | tf_op jit(solution)/shard_map/ppermute | solution.py:230
  22.1 6.3 %collective-permute-done.6.refs_1_ = bf16[512,384]{1,0:T(8,128)(2,1)S(1)} collective-permute-done((bf16[512,384]{1,0:T(8,128)(2,1)S(1)}, bf16[512,384]{1,0:T(8,128)(2,1)S(1)}, u32[]{:S(2)}, u32[]{:S(2)}) %collective-permute-start.6) | collective-permute-done | bytes 393248 | tf_op jit(solution)/shard_map/ppermute | solution.py:230
  28.4 1.6 %collective-permute-start.10 = (bf16[256,384]{1,0:T(8,128)(2,1)S(1)}, bf16[256,384]{1,0:T(8,128)(2,1)S(1)}, u32[]{:S(2)}, u32[]{:S(2)}) collective-permute-start(bf16[256,384]{1,0:T(8,128)(2,1)S(1)} %slice.14), channel_id=1, source_target_pairs={{0,1},{1,0},{2,3},{3,2},{4,5},{5,4},{6,7},{7,6},{8,9},{9,8},{10,11... | collective-permute-start | bytes 589832 | tf_op jit(solution)/shard_map/ppermute | solution.py:230
  30.0 0.6 %collective-permute-start.11 = (bf16[256,384]{1,0:T(8,128)(2,1)S(1)}, bf16[256,384]{1,0:T(8,128)(2,1)S(1)}, u32[]{:S(2)}, u32[]{:S(2)}) collective-permute-start(bf16[256,384]{1,0:T(8,128)(2,1)S(1)} %slice.15), channel_id=1, source_target_pairs={{0,2},{1,3},{2,0},{3,1},{4,6},{5,7},{6,4},{7,5},{8,10},{9,11},{10,... | collective-permute-start | bytes 589832 | tf_op jit(solution)/shard_map/ppermute | solution.py:230
  30.6 1.2 %near_tiles.1 = (f32[2,128,384]{2,1,0:T(8,128)S(1)}, bf16[2,128,384]{2,1,0:T(8,128)(2,1)S(1)}, bf16[2,128,384]{2,1,0:T(8,128)(2,1)S(1)}) custom-call(bf16[384,512]{1,0:T(8,128)(2,1)S(1)} %get-tuple-element.28.left_inner, bf16[384,512]{1,0:T(8,128)(2,1)S(1)} %get-tuple-element.29.left_outer, bf16[512,384]{1,0:T(8,128)(2,1)S(1)} %collective-permute-done.4.refs_0_, ...), custom_call_target="tpu_custom_call" | custom-call | flops 603979776 | bytes 3145728 | tf_op jit(solution)/shard_map/near_tiles/pallas_call | solution.py:29
  31.8 0.8 %collective-permute-done.3.refs_0_ = bf16[256,384]{1,0:T(8,128)(2,1)S(1)} collective-permute-done((bf16[256,384]{1,0:T(8,128)(2,1)S(1)}, bf16[256,384]{1,0:T(8,128)(2,1)S(1)}, u32[]{:S(2)}, u32[]{:S(2)}) %collective-permute-start.3) | collective-permute-done | bytes 196640 | tf_op jit(solution)/shard_map/ppermute | solution.py:230
  32.6 3.5 %collective-permute-done.10.refs_2_ = bf16[256,384]{1,0:T(8,128)(2,1)S(1)} collective-permute-done((bf16[256,384]{1,0:T(8,128)(2,1)S(1)}, bf16[256,384]{1,0:T(8,128)(2,1)S(1)}, u32[]{:S(2)}, u32[]{:S(2)}) %collective-permute-start.10) | collective-permute-done | bytes 196640 | tf_op jit(solution)/shard_map/ppermute | solution.py:230
  36.1 0.6 %diagonal_tile.1 = (f32[1,128,384]{2,1,0:T(8,128)S(1)}, bf16[1,128,384]{2,1,0:T(8,128)(2,1)S(1)}, bf16[1,128,384]{2,1,0:T(8,128)(2,1)S(1)}) custom-call(bf16[384,512]{1,0:T(8,128)(2,1)S(1)} %get-tuple-element.28.left_inner, bf16[384,512]{1,0:T(8,128)(2,1)S(1)} %get-tuple-element.29.left_outer, bf16[256,384]{1,0:T(8,128)(2,1)S(1)} %collective-permute-done.3.refs_0_, ...), custom_call_target="tpu_custom_call" | custom-call | flops 301989888 | bytes 1966080 | tf_op jit(solution)/shard_map/diagonal_tile/pallas_call | solution.py:29
  36.9 1.9 %collective-permute-done.14.refs_4_ = bf16[2,128,384]{2,1,0:T(8,128)(2,1)S(1)} collective-permute-done((bf16[2,128,384]{2,1,0:T(8,128)(2,1)S(1)}, bf16[2,128,384]{2,1,0:T(8,128)(2,1)S(1)}, u32[]{:S(2)}, u32[]{:S(2)}) %collective-permute-start.14) | collective-permute-done | bytes 196640 | tf_op jit(solution)/shard_map/ppermute | solution.py:227
  38.8 1.0 %add_near.1.refs_3_ = f32[5,128,512]{2,1,0:T(8,128)} custom-call(f32[1,128,384]{2,1,0:T(8,128)S(1)} %get-tuple-element.37.refs_0_, bf16[1,128,384]{2,1,0:T(8,128)(2,1)S(1)} %collective-permute-done.8.refs_1_, bf16[1,128,384]{2,1,0:T(8,128)(2,1)S(1)} %collective-permute-done.9.refs_2_, f32[2,128,384]{2,1,0:T(8,128)S(1)} %get-tuple-element.40.refs_3_, ...), custom_call_target="tpu_custom_call" | custom-call | flops 245760 | bytes 2490368 | tf_op jit(solution)/shard_map/add_near/pallas_call | solution.py:29
  39.8 2.8 %collective-permute-done.12.refs_1_ = bf16[1,128,384]{2,1,0:T(8,128)(2,1)S(1)} collective-permute-done((bf16[1,128,384]{2,1,0:T(8,128)(2,1)S(1)}, bf16[1,128,384]{2,1,0:T(8,128)(2,1)S(1)}, u32[]{:S(2)}, u32[]{:S(2)}) %collective-permute-start.12) | collective-permute-done | bytes 98336 | tf_op jit(solution)/shard_map/ppermute | solution.py:227
  42.6 0.8 %add_diagonal.1 = f32[5,128,512]{2,1,0:T(8,128)} custom-call(f32[1,128,384]{2,1,0:T(8,128)S(1)} %get-tuple-element.34.refs_0_, bf16[1,128,384]{2,1,0:T(8,128)(2,1)S(1)} %collective-permute-done.12.refs_1_, bf16[1,128,384]{2,1,0:T(8,128)(2,1)S(1)} %collective-permute-done.13.refs_2_, f32[5,128,512]{2,1,0:T(8,128)} %add_near.1.refs_3_), custom_call_target="tpu_custom_call", output_to_operand_aliasing={{}: (3, {})} | custom-call | flops 81920 | bytes 3014656 | tf_op jit(solution)/shard_map/add_diagonal/pallas_call | solution.py:29
  (23 shorter events, 0.6 us)
Async XLA Ops:
  0.0 9.7 %copy-start.1 = (s32[8,3]{0,1:T(4,128)S(1)}, s32[8,3]{0,1:T(4,128)}, u32[]{:S(2)}) copy-start(s32[8,3]{0,1:T(4,128)} %param.5) | copy-start | bytes 292
  0.0 9.7 %copy-start = (bf16[8,3,128,128]{3,2,1,0:T(8,128)(2,1)S(1)}, bf16[8,3,128,128]{3,2,1,0:T(8,128)(2,1)}, u32[]{:S(2)}) copy-start(bf16[8,3,128,128]{3,2,1,0:T(8,128)(2,1)} %stiffness.1) | copy-start | bytes 2359300
  1.9 7.8 %collective-permute-start = (bf16[256,256]{1,0:T(8,128)(2,1)S(1)}, bf16[256,256]{1,0:T(8,128)(2,1)S(1)}, u32[]{:S(2)}, u32[]{:S(2)}) collective-permute-start(bf16[256,256]{1,0:T(8,128)(2,1)S(1)} %get-tuple-element.26), channel_id=1, source_target_pairs={{0,28},{4,8},{8,4},{12,16},{16,12},{20,24},{24,20},{28,0},{1,29},{... | collective-permute-start | bytes 393224 | tf_op jit(solution)/shard_map/ppermute | solution.py:227
  6.5 3.2 %collective-permute-start.1 = (bf16[256,256]{1,0:T(8,128)(2,1)S(1)}, bf16[256,256]{1,0:T(8,128)(2,1)S(1)}, u32[]{:S(2)}, u32[]{:S(2)}) collective-permute-start(bf16[256,256]{1,0:T(8,128)(2,1)S(1)} %get-tuple-element.27), channel_id=1, source_target_pairs={{0,4},{4,0},{8,12},{12,8},{16,20},{20,16},{24,28},{28,24},{1,5},{5... | collective-permute-start | bytes 393224 | tf_op jit(solution)/shard_map/ppermute | solution.py:224
  6.5 11.9 %collective-permute-start.2 = (bf16[512,384]{1,0:T(8,128)(2,1)S(1)}, bf16[512,384]{1,0:T(8,128)(2,1)S(1)}, u32[]{:S(2)}, u32[]{:S(2)}) collective-permute-start(bf16[512,384]{1,0:T(8,128)(2,1)S(1)} %get-tuple-element.25.inner), channel_id=1, source_target_pairs={{0,2},{1,3},{2,0},{3,1},{4,6},{5,7},{6,4},{7,5},{8,10},{9,11},{10,... | collective-permute-start | bytes 1179656 | tf_op jit(solution)/shard_map/ppermute | solution.py:230
  8.0 11.9 %collective-permute-start.4 = (bf16[512,384]{1,0:T(8,128)(2,1)S(1)}, bf16[512,384]{1,0:T(8,128)(2,1)S(1)}, u32[]{:S(2)}, u32[]{:S(2)}) collective-permute-start(bf16[512,384]{1,0:T(8,128)(2,1)S(1)} %get-tuple-element.25.inner), channel_id=1, source_target_pairs={{0,1},{1,0},{2,3},{3,2},{4,5},{5,4},{6,7},{7,6},{8,9},{9,8},{10,11... | collective-permute-start | bytes 1179656 | tf_op jit(solution)/shard_map/ppermute | solution.py:230
  10.8 17.6 %collective-permute-start.6 = (bf16[512,384]{1,0:T(8,128)(2,1)S(1)}, bf16[512,384]{1,0:T(8,128)(2,1)S(1)}, u32[]{:S(2)}, u32[]{:S(2)}) collective-permute-start(bf16[512,384]{1,0:T(8,128)(2,1)S(1)} %outer_image.1.outer), channel_id=1, source_target_pairs={{0,1},{1,0},{2,3},{3,2},{4,5},{5,4},{6,7},{7,6},{8,9},{9,8},{10,11... | collective-permute-start | bytes 1179656 | tf_op jit(solution)/shard_map/ppermute | solution.py:230
  13.5 14.9 %collective-permute-start.7 = (bf16[512,384]{1,0:T(8,128)(2,1)S(1)}, bf16[512,384]{1,0:T(8,128)(2,1)S(1)}, u32[]{:S(2)}, u32[]{:S(2)}) collective-permute-start(bf16[512,384]{1,0:T(8,128)(2,1)S(1)} %outer_image.1.outer), channel_id=1, source_target_pairs={{0,2},{1,3},{2,0},{3,1},{4,6},{5,7},{6,4},{7,5},{8,10},{9,11},{10,... | collective-permute-start | bytes 1179656 | tf_op jit(solution)/shard_map/ppermute | solution.py:230
  15.6 5.9 %collective-permute-start.8 = (bf16[1,128,384]{2,1,0:T(8,128)(2,1)S(1)}, bf16[1,128,384]{2,1,0:T(8,128)(2,1)S(1)}, u32[]{:S(2)}, u32[]{:S(2)}) collective-permute-start(bf16[1,128,384]{2,1,0:T(8,128)(2,1)S(1)} %get-tuple-element.30), channel_id=1, source_target_pairs={{0,28},{4,8},{8,4},{12,16},{16,12},{20,24},{24,20},{28,0},{1,29},{... | collective-permute-start | bytes 294920 | tf_op jit(solution)/shard_map/ppermute | solution.py:227
  18.4 3.7 %collective-permute-start.9 = (bf16[1,128,384]{2,1,0:T(8,128)(2,1)S(1)}, bf16[1,128,384]{2,1,0:T(8,128)(2,1)S(1)}, u32[]{:S(2)}, u32[]{:S(2)}) collective-permute-start(bf16[1,128,384]{2,1,0:T(8,128)(2,1)S(1)} %get-tuple-element.31), channel_id=1, source_target_pairs={{0,4},{4,0},{8,12},{12,8},{16,20},{20,16},{24,28},{28,24},{1,5},{5... | collective-permute-start | bytes 294920 | tf_op jit(solution)/shard_map/ppermute | solution.py:224
  20.0 12.6 %collective-permute-start.3 = (bf16[256,384]{1,0:T(8,128)(2,1)S(1)}, bf16[256,384]{1,0:T(8,128)(2,1)S(1)}, u32[]{:S(2)}, u32[]{:S(2)}) collective-permute-start(bf16[256,384]{1,0:T(8,128)(2,1)S(1)} %slice.16), channel_id=1, source_target_pairs={{0,1},{1,0},{2,3},{3,2},{4,5},{5,4},{6,7},{7,6},{8,9},{9,8},{10,11... | collective-permute-start | bytes 589832 | tf_op jit(solution)/shard_map/ppermute | solution.py:230
  21.5 11.1 %collective-permute-start.5 = (bf16[256,384]{1,0:T(8,128)(2,1)S(1)}, bf16[256,384]{1,0:T(8,128)(2,1)S(1)}, u32[]{:S(2)}, u32[]{:S(2)}) collective-permute-start(bf16[256,384]{1,0:T(8,128)(2,1)S(1)} %slice.17), channel_id=1, source_target_pairs={{0,2},{1,3},{2,0},{3,1},{4,6},{5,7},{6,4},{7,5},{8,10},{9,11},{10,... | collective-permute-start | bytes 589832 | tf_op jit(solution)/shard_map/ppermute | solution.py:230
  28.4 7.7 %collective-permute-start.10 = (bf16[256,384]{1,0:T(8,128)(2,1)S(1)}, bf16[256,384]{1,0:T(8,128)(2,1)S(1)}, u32[]{:S(2)}, u32[]{:S(2)}) collective-permute-start(bf16[256,384]{1,0:T(8,128)(2,1)S(1)} %slice.14), channel_id=1, source_target_pairs={{0,1},{1,0},{2,3},{3,2},{4,5},{5,4},{6,7},{7,6},{8,9},{9,8},{10,11... | collective-permute-start | bytes 589832 | tf_op jit(solution)/shard_map/ppermute | solution.py:230
  30.0 6.1 %collective-permute-start.11 = (bf16[256,384]{1,0:T(8,128)(2,1)S(1)}, bf16[256,384]{1,0:T(8,128)(2,1)S(1)}, u32[]{:S(2)}, u32[]{:S(2)}) collective-permute-start(bf16[256,384]{1,0:T(8,128)(2,1)S(1)} %slice.15), channel_id=1, source_target_pairs={{0,2},{1,3},{2,0},{3,1},{4,6},{5,7},{6,4},{7,5},{8,10},{9,11},{10,... | collective-permute-start | bytes 589832 | tf_op jit(solution)/shard_map/ppermute | solution.py:230
  31.8 7.1 %collective-permute-start.14 = (bf16[2,128,384]{2,1,0:T(8,128)(2,1)S(1)}, bf16[2,128,384]{2,1,0:T(8,128)(2,1)S(1)}, u32[]{:S(2)}, u32[]{:S(2)}) collective-permute-start(bf16[2,128,384]{2,1,0:T(8,128)(2,1)S(1)} %get-tuple-element.41), channel_id=1, source_target_pairs={{0,28},{4,8},{8,4},{12,16},{16,12},{20,24},{24,20},{28,0},{1,29},{... | collective-permute-start | bytes 589832 | tf_op jit(solution)/shard_map/ppermute | solution.py:227
  32.6 6.2 %collective-permute-start.15 = (bf16[2,128,384]{2,1,0:T(8,128)(2,1)S(1)}, bf16[2,128,384]{2,1,0:T(8,128)(2,1)S(1)}, u32[]{:S(2)}, u32[]{:S(2)}) collective-permute-start(bf16[2,128,384]{2,1,0:T(8,128)(2,1)S(1)} %get-tuple-element.42), channel_id=1, source_target_pairs={{0,4},{4,0},{8,12},{12,8},{16,20},{20,16},{24,28},{28,24},{1,5},{5... | collective-permute-start | bytes 589832 | tf_op jit(solution)/shard_map/ppermute | solution.py:224
  36.7 5.9 %collective-permute-start.12 = (bf16[1,128,384]{2,1,0:T(8,128)(2,1)S(1)}, bf16[1,128,384]{2,1,0:T(8,128)(2,1)S(1)}, u32[]{:S(2)}, u32[]{:S(2)}) collective-permute-start(bf16[1,128,384]{2,1,0:T(8,128)(2,1)S(1)} %get-tuple-element.35), channel_id=1, source_target_pairs={{0,28},{4,8},{8,4},{12,16},{16,12},{20,24},{24,20},{28,0},{1,29},{... | collective-permute-start | bytes 294920 | tf_op jit(solution)/shard_map/ppermute | solution.py:227
  36.8 5.8 %collective-permute-start.13 = (bf16[1,128,384]{2,1,0:T(8,128)(2,1)S(1)}, bf16[1,128,384]{2,1,0:T(8,128)(2,1)S(1)}, u32[]{:S(2)}, u32[]{:S(2)}) collective-permute-start(bf16[1,128,384]{2,1,0:T(8,128)(2,1)S(1)} %get-tuple-element.36), channel_id=1, source_target_pairs={{0,4},{4,0},{8,12},{12,8},{16,20},{20,16},{24,28},{28,24},{1,5},{5... | collective-permute-start | bytes 294920 | tf_op jit(solution)/shard_map/ppermute | solution.py:224

commit v7 on v6

--- a/solution.py
+++ b/solution.py
@@ -129,86 +129,66 @@
     return lax.rem(lax.axis_index("blk"), 2)
 
 
-def store_tile(tile, own, link, chip, n):
-    width = own.shape[1]
+def store_tile(tile, own, link, chip):
+    width = own.shape[0]
     odd = parity()
-    own[n] = tile[width : 2 * width]
+    own[...] = tile[width : 2 * width].astype(own.dtype)
     down, up = tile[:width].astype(BF16), tile[2 * width :].astype(BF16)
 
     @pl.when(odd == 0)
     def _():
-        link[n] = down
-        chip[n] = up
+        link[...] = down
+        chip[...] = up
 
     @pl.when(odd == 1)
     def _():
-        link[n] = up
-        chip[n] = down
-
-
-def own_tile(size, masked, inner, outer, own, link, chip, left_inner, left_outer):
+        link[...] = up
+        chip[...] = down
+
+
+def first_tile(size, masked, inner, outer, own, link, chip, left_inner, left_outer):
     rows = masked.shape[0]
     rim = RIM * size
     left_inner[...] = masked[rim : rows - rim, :].T
     left_outer[:, :rim] = masked[:rim, :].T
     left_outer[:, rim:] = masked[rows - rim :, :].T
-    store_tile(dot(left_inner[...], inner[...]) + dot(left_outer[...], outer[...]), own, link, chip, 0)
-
-
-def near_tiles(left_inner, left_outer, *refs):
-    images, (own, link, chip) = refs[:-3], refs[-3:]
-    for n in range(len(images) // 2):
-        tile = dot(left_inner[...], images[2 * n][...]) + dot(left_outer[...], images[2 * n + 1][...])
-        store_tile(tile, own, link, chip, n)
-
-
-def diagonal_tile(left_inner, left_outer, *refs):
-    images, (own, link, chip) = refs[:-3], refs[-3:]
-    tile = None
-    for which, left in ((0, left_inner), (1, left_outer)):
-        first, second = images[2 * which], images[2 * which + 1]
-        half = first.shape[0]
-        part = dot(left[:, :half], first[...]) + dot(left[:, half:], second[...])
-        tile = part if tile is None else tile + part
-    store_tile(tile, own, link, chip, 0)
-
-
-def add_tiles(sources, *refs):
-    count = len(sources)
-    terms, refs = refs[: 3 * count], refs[3 * count :]
+    second_tile(left_inner, left_outer, inner, outer, own, link, chip)
+
+
+def second_tile(left_inner, left_outer, inner, outer, own, link, chip):
+    store_tile(dot(left_inner[...], inner[...]) + dot(left_outer[...], outer[...]), own, link, chip)
+
+
+def add_tiles(steps, *refs):
+    count = len(steps)
+    terms = refs[: 3 * count]
     coarse, total, sem = refs[-3:]
     width = total.shape[2]
     me = lax.axis_index("col")
     even = parity() == 0
     copies = []
-    n = 0
-    for group, source in enumerate(sources):
-        own, link, chip = terms[3 * group : 3 * group + 3]
-        for m, step in enumerate(source):
-            prev = jnp.where(even, link[m].astype(F32), chip[m].astype(F32))
-            nxt = jnp.where(even, chip[m].astype(F32), link[m].astype(F32))
-            for d in range(5):
-                value = None
-                for offset, term in ((0, prev), (1, own[m]), (2, nxt)):
-                    if 0 <= d - offset <= 2:
-                        part = term[:, (d - offset) * width : (d - offset + 1) * width]
-                        value = part if value is None else value + part
-                total[n, d] = value
-            start = pl.multiple_of(lax.bitwise_xor(me, step) * width, width)
-            copy = pltpu.make_async_copy(total.at[n], coarse.at[:, :, pl.ds(start, width)], sem.at[n])
-            copy.start()
-            copies.append(copy)
-            n += 1
+    for n, (even_step, odd_step) in enumerate(steps):
+        own, link, chip = (ref[...].astype(F32) for ref in terms[3 * n : 3 * n + 3])
+        prev = jnp.where(even, link, chip)
+        nxt = jnp.where(even, chip, link)
+        for d in range(5):
+            value = None
+            for offset, term in ((0, prev), (1, own), (2, nxt)):
+                if 0 <= d - offset <= 2:
+                    part = term[:, (d - offset) * width : (d - offset + 1) * width]
+                    value = part if value is None else value + part
+            total[n, d] = value
+        column = lax.bitwise_xor(me, jnp.where(even, even_step, odd_step))
+        start = pl.multiple_of(column * width, width)
+        copy = pltpu.make_async_copy(total.at[n], coarse.at[:, :, pl.ds(start, width)], sem.at[n])
+        copy.start()
+        copies.append(copy)
     for copy in copies:
         copy.wait()
 
 
-def tile_shapes(count, width, wide):
-    return (
-        shape((count, width, wide), F32),
-        shape((count, width, wide), BF16),
-        shape((count, width, wide), BF16),
-    )
+def tile_shapes(width, wide, own):
+    return shape((width, wide), own), shape((width, wide), BF16), shape((width, wide), BF16)
 
 
 def shards(stiffness, block_cols, basis, patch_reach):
@@ -226,8 +206,27 @@
     def over_link(value):
         return lax.ppermute(value, "blk", cross)
 
-    def swap(value, step):
-        return lax.ppermute(value, "col", [(i, i ^ step) for i in range(4)])
+    def to(value, slab_of, column_of):
+        perm = [(4 * i + q, 4 * (slab_of(i) % slabs) + column_of(i, q)) for i in range(slabs) for q in range(4)]
+        return lax.ppermute(value, ("blk", "col"), perm)
+
+    def partner(i, q):
+        return q ^ (1 + i % 2)
+
+    def side(i, q):
+        return q ^ (2 - i % 2)
+
+    def to_partner(value):
+        return to(value, lambda i: i, partner)
+
+    def to_side(value):
+        return to(value, lambda i: i, side)
+
+    def spread(own, link, chip):
+        own = to_partner(own)
+        link = to(link, lambda i: i + 1 if i % 2 else i - 1, partner)
+        chip = to(chip, lambda i: i ^ 1, partner)
+        return own, link, chip
 
     cols = block_cols.T
     flat = basis.transpose(1, 0, 2)
@@ -251,8 +250,8 @@
         flops=row_flops * (blocks - 2 * RIM),
         name="mask_and_inner",
     )
-    inner_x = swap(inner, 1)
-    inner_y = swap(inner, 2)
+    masked_p = to_partner(masked)
+    inner_r = to_side(inner)
     rim_link = over_link(rim_link)
     rim_chip = over_chip(rim_chip)
     outer = call(
@@ -265,64 +264,62 @@
         flops=row_flops * 2 * RIM,
         name="outer_image",
     )
-    outer_x = swap(outer, 1)
-    outer_y = swap(outer, 2)
+    outer_r = to_side(outer)
     tile_flops = 2 * rows * wide * wide
-    own_own, own_link, own_chip, left_inner, left_outer = call(
-        functools.partial(own_tile, size),
-        (*tile_shapes(1, width, wide), shape((wide, inner_rows), BF16), shape((wide, 2 * rim), BF16)),
-        [VMEM] * 3,
-        [VMEM] * 5,
-        (masked, inner, outer),
-        flops=tile_flops,
-        name="own_tile",
-    )
-    own_link = over_link(own_link)
-    own_chip = over_chip(own_chip)
-    half = inner_rows // 2
-    inner_d = (swap(inner_y[:half], 1), swap(inner_x[half:], 2))
-    outer_x, outer_y, own_link, own_chip = lax.optimization_barrier((outer_x, outer_y, own_link, own_chip))
-    diagonal = (*inner_d, swap(outer_y[:rim], 1), swap(outer_x[rim:], 2))
-    near_own, near_link, near_chip = call(
-        near_tiles,
-        tile_shapes(2, width, wide),
-        [VMEM] * 6,
-        [VMEM] * 3,
-        (left_inner, left_outer, inner_x, outer_x, inner_y, outer_y),
-        flops=2 * tile_flops,
-        name="near_tiles",
-    )
-    near_link = over_link(near_link)
-    near_chip = over_chip(near_chip)
-    far_own, far_link, far_chip = call(
-        diagonal_tile,
-        tile_shapes(1, width, wide),
-        [VMEM] * 6,
-        [VMEM] * 3,
-        (left_inner, left_outer, *diagonal),
-        flops=tile_flops,
-        name="diagonal_tile",
-    )
-    far_link = over_link(far_link)
-    far_chip = over_chip(far_chip)
-
-    def add(sources, terms, name, base=None):
-        count = sum(map(len, sources))
+    lefts = (shape((wide, inner_rows), BF16), shape((wide, 2 * rim), BF16))
+
+    def first(masked, own, name):
+        return call(
+            functools.partial(first_tile, size),
+            (*tile_shapes(width, wide, own), *lefts),
+            [VMEM] * 3,
+            [VMEM] * 5,
+            (masked, inner, outer),
+            flops=tile_flops,
+            name=name,
+        )
+
+    def second(left_inner, left_outer, own, name):
+        return call(
+            second_tile,
+            tile_shapes(width, wide, own),
+            [VMEM] * 4,
+            [VMEM] * 3,
+            (left_inner, left_outer, inner_r, outer_r),
+            flops=tile_flops,
+            name=name,
+        )
+
+    own, own_link, own_chip, left_inner, left_outer = first(masked, F32, "own_tile")
+    own_link, own_chip = over_link(own_link), over_chip(own_chip)
+    *part, far_inner, far_outer = first(masked_p, BF16, "partner_tile")
+    outer_r, _ = lax.optimization_barrier((outer_r, part[1]))
+    part, part_link, part_chip = spread(*part)
+    far, far_link, far_chip = spread(*second(far_inner, far_outer, BF16, "far_tile"))
+    near, near_link, near_chip = second(left_inner, left_outer, F32, "near_tile")
+    near_link, near_chip = over_link(near_link), over_chip(near_chip)
+
+    def add(steps, terms, name, base=None):
         extra = () if base is None else (base,)
         return call(
-            functools.partial(add_tiles, sources),
+            functools.partial(add_tiles, steps),
             shape((5, width, 4 * width), F32),
             [VMEM] * len(terms) + [HBM] * len(extra),
             HBM,
             (*terms, *extra),
-            scratch=[pltpu.VMEM((count, 5, width, width), F32), pltpu.SemaphoreType.DMA((count,))],
-            flops=5 * count * width * width,
+            scratch=[pltpu.VMEM((len(steps), 5, width, width), F32), pltpu.SemaphoreType.DMA((len(steps),))],
+            flops=5 * len(steps) * width * width,
             aliases={len(terms): 0} if extra else None,
             name=name,
         )
 
-    coarse = add(((0,), (1, 2)), (own_own, own_link, own_chip, near_own, near_link, near_chip), "add_near")
-    coarse = add(((3,),), (far_own, far_link, far_chip), "add_diagonal", coarse)
+    coarse = add(((0, 0),), (own, own_link, own_chip), "add_own")
+    coarse = add(
+        ((2, 1), (1, 2), (3, 3)),
+        (near, part_link, part_chip, part, near_link, near_chip, far, far_link, far_chip),
+        "add_rest",
+        coarse,
+    )
     return coarse.transpose(1, 0, 2)
 
 
@@ -371,5 +368,5 @@
         P(None, "col", None),
     )
     out_specs = P(("blk", "col"), None, None)
-    body = shards if mesh.shape["col"] == 4 else gathered
+    body = shards if mesh.shape["col"] == 4 and mesh.shape["blk"] % 2 == 0 else gathered
     return jax.shard_map(body, mesh=mesh, in_specs=in_specs, out_specs=out_specs, check_vma=False)

time: 43.6 us -> 42.9 us (0.984)
  waiting for transfers between devices: 18.5 us -> 16 us
  starting transfers between devices: 17.5 us -> 19.4 us
    ppermute x8 -> x9, starting transfers between devices: 11.3 us -> 13.9 us  [to(): return lax.ppermute(value, ('blk', 'col'), perm)]
    ppermute x8 -> x9, waiting for transfers between devices: 13.5 us -> 11.5 us  [to(): return lax.ppermute(value, ('blk', 'col'), perm)]
    ppermute x4 -> x3, starting transfers between devices: 6.1 us -> 5.44 us  [over_link(): return lax.ppermute(value, 'blk', cross)]
    ppermute x4 -> x3, waiting for transfers between devices: 4.97 us -> 4.54 us  [over_link(): return lax.ppermute(value, 'blk', cross)]
    pallas_call x7 -> x8, Pallas kernels: 7.24 us -> 7.24 us  [call(): pl.pallas_call(kernel, out_shape=out_shape, in_specs=in_specs, out_specs=...]
  transfers between devices with their start and end apart: 16 -> 15, of which waited for: 8 -> 6; matrix products, arithmetic and copies ran while one was open for 0% -> 0% of each run, Pallas kernels for 10% -> 10%
where the time goes in v7:
time: 42.9 us; the launch traced here: 42.8 us
  starting transfers between devices  19.4 us (45%)
  waiting for transfers between devices  16 us (37%)
  Pallas kernels  7.24 us (17%)
    ppermute x9, starting transfers between devices, to(): return lax.ppermute(value, ('blk', 'col'), perm)  13.9 us
    ppermute x9, waiting for transfers between devices, to(): return lax.ppermute(value, ('blk', 'col'), perm)  11.5 us
    pallas_call x8, Pallas kernels, call(): pl.pallas_call(kernel, out_shape=out_shape, in_specs=in_specs, out_specs=...  7.24 us
    ppermute x3, starting transfers between devices, over_link(): return lax.ppermute(value, 'blk', cross)  5.44 us
    ppermute x3, waiting for transfers between devices, over_link(): return lax.ppermute(value, 'blk', cross)  4.54 us
  transfers between devices with their start and end apart: 15, of which 6 were waited for; matrix products, arithmetic and copies ran while one was open for 0% of the time, Pallas kernels for 10%

profile of v7, /device:TPU:0, one launch (start us, length us, event | category | flops | bytes accessed | tf_op | source)
XLA Modules:
  0.0 42.8 jit_solution(10704003137410840463)
XLA Ops:
  0.0 1.9 %mask_and_inner.1 = (bf16[1024,384]{1,0:T(8,128)(2,1)S(1)}, bf16[256,256]{1,0:T(8,128)(2,1)S(1)}, bf16[256,256]{1,0:T(8,128)(2,1)S(1)}, bf16[512,384]{1,0:T(8,128)(2,1)S(1)}) custom-call(s32[3,8]{1,0:T(4,128)} %bitcast.4, bf16[3,1024,128]{2,1,0:T(8,128)(2,1)} %bitcast.6, s32[8,2,128]{2,1,0:T(2,128)} %bitcast.7, bf16[8,3,128,128]{3,2,1,0:T(8,128)(2,1)} %stiffness.1), custom_call_target="tpu_custom_call" | custom-call | flops 150994944 | bytes 3022944 | tf_op jit(solution)/shard_map/mask_and_inner/pallas_call | solution.py:29
  1.9 3.0 %collective-permute-start.4 = (bf16[1024,384]{1,0:T(8,128)(2,1)S(1)}, bf16[1024,384]{1,0:T(8,128)(2,1)S(1)}, u32[]{:S(2)}, u32[]{:S(2)}) collective-permute-start(bf16[1024,384]{1,0:T(8,128)(2,1)S(1)} %get-tuple-element.26.masked), channel_id=1, source_target_pairs={{0,1},{1,0},{2,3},{3,2},{4,6},{5,7},{6,4},{7,5},{8,9},{9,8},{10,11... | collective-permute-start | bytes 2359304 | tf_op jit(solution)/shard_map/ppermute | solution.py:211
  4.9 2.8 %collective-permute-start = (bf16[256,256]{1,0:T(8,128)(2,1)S(1)}, bf16[256,256]{1,0:T(8,128)(2,1)S(1)}, u32[]{:S(2)}, u32[]{:S(2)}) collective-permute-start(bf16[256,256]{1,0:T(8,128)(2,1)S(1)} %get-tuple-element.28), channel_id=1, source_target_pairs={{0,28},{4,8},{8,4},{12,16},{16,12},{20,24},{24,20},{28,0},{1,29},{... | collective-permute-start | bytes 393224 | tf_op jit(solution)/shard_map/ppermute | solution.py:207
  7.7 4.5 %collective-permute-done.from_link = bf16[256,256]{1,0:T(8,128)(2,1)S(1)} collective-permute-done((bf16[256,256]{1,0:T(8,128)(2,1)S(1)}, bf16[256,256]{1,0:T(8,128)(2,1)S(1)}, u32[]{:S(2)}, u32[]{:S(2)}) %collective-permute-start) | collective-permute-done | bytes 131104 | tf_op jit(solution)/shard_map/ppermute | solution.py:207
  12.3 1.1 %outer_image.1.outer = bf16[512,384]{1,0:T(8,128)(2,1)S(1)} custom-call(s32[3,8]{1,0:T(4,128)S(1)} %bitcast.5, bf16[8,3,128,128]{3,2,1,0:T(8,128)(2,1)S(1)} %copy-done, bf16[1024,384]{1,0:T(8,128)(2,1)S(1)} %get-tuple-element.26.masked, bf16[256,256]{1,0:T(8,128)(2,1)S(1)} %collective-permute-done.from_link, ...), custom_call_target="tpu_custom_call" | custom-call | flops 150994944 | bytes 2228320 | tf_op jit(solution)/shard_map/outer_image/pallas_call | solution.py:29
  13.4 1.6 %collective-permute-start.3 = (bf16[512,384]{1,0:T(8,128)(2,1)S(1)}, bf16[512,384]{1,0:T(8,128)(2,1)S(1)}, u32[]{:S(2)}, u32[]{:S(2)}) collective-permute-start(bf16[512,384]{1,0:T(8,128)(2,1)S(1)} %outer_image.1.outer), channel_id=1, source_target_pairs={{0,2},{1,3},{2,0},{3,1},{4,5},{5,4},{6,7},{7,6},{8,10},{9,11},{10,... | collective-permute-start | bytes 1179656 | tf_op jit(solution)/shard_map/ppermute | solution.py:211
  15.0 0.5 %collective-permute-start.2 = (bf16[512,384]{1,0:T(8,128)(2,1)S(1)}, bf16[512,384]{1,0:T(8,128)(2,1)S(1)}, u32[]{:S(2)}, u32[]{:S(2)}) collective-permute-start(bf16[512,384]{1,0:T(8,128)(2,1)S(1)} %get-tuple-element.27.inner), channel_id=1, source_target_pairs={{0,2},{1,3},{2,0},{3,1},{4,5},{5,4},{6,7},{7,6},{8,10},{9,11},{10,... | collective-permute-start | bytes 1179656 | tf_op jit(solution)/shard_map/ppermute | solution.py:211
  15.5 0.6 %own_tile.1 = (f32[128,384]{1,0:T(8,128)S(1)}, bf16[128,384]{1,0:T(8,128)(2,1)S(1)}, bf16[128,384]{1,0:T(8,128)(2,1)S(1)}, bf16[384,512]{1,0:T(8,128)(2,1)S(1)}, bf16[384,512]{1,0:T(8,128)(2,1)S(1)}) custom-call(bf16[1024,384]{1,0:T(8,128)(2,1)S(1)} %get-tuple-element.26.masked, bf16[512,384]{1,0:T(8,128)(2,1)S(1)} %get-tuple-element.27.inner, ...), custom_call_target="tpu_custom_call" | custom-call | flops 301989888 | bytes 2752512 | tf_op jit(solution)/shard_map/own_tile/pallas_call | solution.py:29
  16.1 1.2 %collective-permute-start.13 = (bf16[128,384]{1,0:T(8,128)(2,1)S(1)}, bf16[128,384]{1,0:T(8,128)(2,1)S(1)}, u32[]{:S(2)}, u32[]{:S(2)}) collective-permute-start(bf16[128,384]{1,0:T(8,128)(2,1)S(1)} %get-tuple-element.45), channel_id=1, source_target_pairs={{0,28},{4,8},{8,4},{12,16},{16,12},{20,24},{24,20},{28,0},{1,29},{... | collective-permute-start | bytes 294920 | tf_op jit(solution)/shard_map/ppermute | solution.py:207
  17.3 0.6 %partner_tile.1 = (bf16[128,384]{1,0:T(8,128)(2,1)S(1)}, bf16[128,384]{1,0:T(8,128)(2,1)S(1)}, bf16[128,384]{1,0:T(8,128)(2,1)S(1)}, bf16[384,512]{1,0:T(8,128)(2,1)S(1)}, bf16[384,512]{1,0:T(8,128)(2,1)S(1)}) custom-call(bf16[1024,384]{1,0:T(8,128)(2,1)S(1)} %collective-permute-done.4.masked, bf16[512,384]{1,0:T(8,128)(2,1)S(1)} %get-tuple-element.27.inner, ...), custom_call_target="tpu_custom_call" | custom-call | flops 301989888 | bytes 2654208 | tf_op jit(solution)/shard_map/partner_tile/pallas_call | solution.py:29
  17.9 3.3 %collective-permute-done.3.outer = bf16[512,384]{1,0:T(8,128)(2,1)S(1)} collective-permute-done((bf16[512,384]{1,0:T(8,128)(2,1)S(1)}, bf16[512,384]{1,0:T(8,128)(2,1)S(1)}, u32[]{:S(2)}, u32[]{:S(2)}) %collective-permute-start.3) | collective-permute-done | bytes 393248 | tf_op jit(solution)/shard_map/ppermute | solution.py:211
  21.2 4.2 %collective-permute-done.2.inner = bf16[512,384]{1,0:T(8,128)(2,1)S(1)} collective-permute-done((bf16[512,384]{1,0:T(8,128)(2,1)S(1)}, bf16[512,384]{1,0:T(8,128)(2,1)S(1)}, u32[]{:S(2)}, u32[]{:S(2)}) %collective-permute-start.2) | collective-permute-done | bytes 393248 | tf_op jit(solution)/shard_map/ppermute | solution.py:211
  25.4 0.6 %far_tile.1 = (bf16[128,384]{1,0:T(8,128)(2,1)S(1)}, bf16[128,384]{1,0:T(8,128)(2,1)S(1)}, bf16[128,384]{1,0:T(8,128)(2,1)S(1)}) custom-call(bf16[384,512]{1,0:T(8,128)(2,1)S(1)} %get-tuple-element.39.left_inner, bf16[384,512]{1,0:T(8,128)(2,1)S(1)} %get-tuple-element.40.left_outer, bf16[512,384]{1,0:T(8,128)(2,1)S(1)} %collective-permute-done.2.inner, ...), custom_call_target="tpu_custom_call" | custom-call | flops 301989888 | bytes 1867776 | tf_op jit(solution)/shard_map/far_tile/pallas_call | solution.py:29
  26.4 3.3 %collective-permute-start.11 = (bf16[128,384]{1,0:T(8,128)(2,1)S(1)}, bf16[128,384]{1,0:T(8,128)(2,1)S(1)}, u32[]{:S(2)}, u32[]{:S(2)}) collective-permute-start(bf16[128,384]{1,0:T(8,128)(2,1)S(1)} %get-tuple-element.42), channel_id=1, source_target_pairs={{0,29},{1,28},{2,31},{3,30},{4,10},{5,11},{6,8},{7,9},{8,5},{9,4},... | collective-permute-start | bytes 294920 | tf_op jit(solution)/shard_map/ppermute | solution.py:211
  29.7 0.6 %near_tile.1 = (f32[128,384]{1,0:T(8,128)S(1)}, bf16[128,384]{1,0:T(8,128)(2,1)S(1)}, bf16[128,384]{1,0:T(8,128)(2,1)S(1)}) custom-call(bf16[384,512]{1,0:T(8,128)(2,1)S(1)} %get-tuple-element.30.left_inner, bf16[384,512]{1,0:T(8,128)(2,1)S(1)} %get-tuple-element.31.left_outer, bf16[512,384]{1,0:T(8,128)(2,1)S(1)} %collective-permute-done.2.inner, ...), custom_call_target="tpu_custom_call" | custom-call | flops 301989888 | bytes 1966080 | tf_op jit(solution)/shard_map/near_tile/pallas_call | solution.py:29
  30.3 1.5 %collective-permute-start.8 = (bf16[128,384]{1,0:T(8,128)(2,1)S(1)}, bf16[128,384]{1,0:T(8,128)(2,1)S(1)}, u32[]{:S(2)}, u32[]{:S(2)}) collective-permute-start(bf16[128,384]{1,0:T(8,128)(2,1)S(1)} %get-tuple-element.37), channel_id=1, source_target_pairs={{0,28},{4,8},{8,4},{12,16},{16,12},{20,24},{24,20},{28,0},{1,29},{... | collective-permute-start | bytes 294920 | tf_op jit(solution)/shard_map/ppermute | solution.py:207
  31.8 1.6 %collective-permute-start.6 = (bf16[128,384]{1,0:T(8,128)(2,1)S(1)}, bf16[128,384]{1,0:T(8,128)(2,1)S(1)}, u32[]{:S(2)}, u32[]{:S(2)}) collective-permute-start(bf16[128,384]{1,0:T(8,128)(2,1)S(1)} %get-tuple-element.35), channel_id=1, source_target_pairs={{0,5},{1,4},{2,7},{3,6},{4,2},{5,3},{6,0},{7,1},{8,13},{9,12},{10,... | collective-permute-start | bytes 294920 | tf_op jit(solution)/shard_map/ppermute | solution.py:211
  33.4 0.5 %collective-permute-done.11.refs_7_ = bf16[128,384]{1,0:T(8,128)(2,1)S(1)} collective-permute-done((bf16[128,384]{1,0:T(8,128)(2,1)S(1)}, bf16[128,384]{1,0:T(8,128)(2,1)S(1)}, u32[]{:S(2)}, u32[]{:S(2)}) %collective-permute-start.11) | collective-permute-done | bytes 98336 | tf_op jit(solution)/shard_map/ppermute | solution.py:211
  33.9 1.1 %collective-permute-start.7 = (bf16[128,384]{1,0:T(8,128)(2,1)S(1)}, bf16[128,384]{1,0:T(8,128)(2,1)S(1)}, u32[]{:S(2)}, u32[]{:S(2)}) collective-permute-start(bf16[128,384]{1,0:T(8,128)(2,1)S(1)} %get-tuple-element.36), channel_id=1, source_target_pairs={{0,1},{1,0},{2,3},{3,2},{4,6},{5,7},{6,4},{7,5},{8,9},{9,8},{10,11... | collective-permute-start | bytes 294920 | tf_op jit(solution)/shard_map/ppermute | solution.py:211
  35.0 2.4 %collective-permute-start.5 = (bf16[128,384]{1,0:T(8,128)(2,1)S(1)}, bf16[128,384]{1,0:T(8,128)(2,1)S(1)}, u32[]{:S(2)}, u32[]{:S(2)}) collective-permute-start(bf16[128,384]{1,0:T(8,128)(2,1)S(1)} %get-tuple-element.32), channel_id=1, source_target_pairs={{0,29},{1,28},{2,31},{3,30},{4,10},{5,11},{6,8},{7,9},{8,5},{9,4},... | collective-permute-start | bytes 294920 | tf_op jit(solution)/shard_map/ppermute | solution.py:211
  37.5 0.8 %add_own.1.refs_9_ = f32[5,128,512]{2,1,0:T(8,128)} custom-call(f32[128,384]{1,0:T(8,128)S(1)} %get-tuple-element.44.refs_0_, bf16[128,384]{1,0:T(8,128)(2,1)S(1)} %collective-permute-done.13.refs_1_, bf16[128,384]{1,0:T(8,128)(2,1)S(1)} %collective-permute-done.14.refs_2_), custom_call_target="tpu_custom_call" | custom-call | flops 81920 | bytes 1703936 | tf_op jit(solution)/shard_map/add_own/pallas_call | solution.py:29
  38.3 1.3 %collective-permute-done.7.refs_3_ = bf16[128,384]{1,0:T(8,128)(2,1)S(1)} collective-permute-done((bf16[128,384]{1,0:T(8,128)(2,1)S(1)}, bf16[128,384]{1,0:T(8,128)(2,1)S(1)}, u32[]{:S(2)}, u32[]{:S(2)}) %collective-permute-start.7) | collective-permute-done | bytes 98336 | tf_op jit(solution)/shard_map/ppermute | solution.py:211
  39.6 2.2 %collective-permute-done.5.refs_1_ = bf16[128,384]{1,0:T(8,128)(2,1)S(1)} collective-permute-done((bf16[128,384]{1,0:T(8,128)(2,1)S(1)}, bf16[128,384]{1,0:T(8,128)(2,1)S(1)}, u32[]{:S(2)}, u32[]{:S(2)}) %collective-permute-start.5) | collective-permute-done | bytes 98336 | tf_op jit(solution)/shard_map/ppermute | solution.py:211
  41.8 1.0 %add_rest.1 = f32[5,128,512]{2,1,0:T(8,128)} custom-call(f32[128,384]{1,0:T(8,128)S(1)} %get-tuple-element.34.refs_0_, bf16[128,384]{1,0:T(8,128)(2,1)S(1)} %collective-permute-done.5.refs_1_, bf16[128,384]{1,0:T(8,128)(2,1)S(1)} %collective-permute-done.6.refs_2_, ...), custom_call_target="tpu_custom_call", output_to_operand_aliasing={{}: (9, {})} | custom-call | flops 245760 | bytes 3604480 | tf_op jit(solution)/shard_map/add_rest/pallas_call | solution.py:29
  (18 shorter events, 0.4 us)
Async XLA Ops:
  0.0 12.3 %copy-start = (bf16[8,3,128,128]{3,2,1,0:T(8,128)(2,1)S(1)}, bf16[8,3,128,128]{3,2,1,0:T(8,128)(2,1)}, u32[]{:S(2)}) copy-start(bf16[8,3,128,128]{3,2,1,0:T(8,128)(2,1)} %stiffness.1) | copy-start | bytes 2359300
  0.0 12.3 %copy-start.1 = (s32[8,3]{0,1:T(4,128)S(1)}, s32[8,3]{0,1:T(4,128)}, u32[]{:S(2)}) copy-start(s32[8,3]{0,1:T(4,128)} %param.5) | copy-start | bytes 292
  1.9 15.3 %collective-permute-start.4 = (bf16[1024,384]{1,0:T(8,128)(2,1)S(1)}, bf16[1024,384]{1,0:T(8,128)(2,1)S(1)}, u32[]{:S(2)}, u32[]{:S(2)}) collective-permute-start(bf16[1024,384]{1,0:T(8,128)(2,1)S(1)} %get-tuple-element.26.masked), channel_id=1, source_target_pairs={{0,1},{1,0},{2,3},{3,2},{4,6},{5,7},{6,4},{7,5},{8,9},{9,8},{10,11... | collective-permute-start | bytes 2359304 | tf_op jit(solution)/shard_map/ppermute | solution.py:211
  4.9 7.3 %collective-permute-start = (bf16[256,256]{1,0:T(8,128)(2,1)S(1)}, bf16[256,256]{1,0:T(8,128)(2,1)S(1)}, u32[]{:S(2)}, u32[]{:S(2)}) collective-permute-start(bf16[256,256]{1,0:T(8,128)(2,1)S(1)} %get-tuple-element.28), channel_id=1, source_target_pairs={{0,28},{4,8},{8,4},{12,16},{16,12},{20,24},{24,20},{28,0},{1,29},{... | collective-permute-start | bytes 393224 | tf_op jit(solution)/shard_map/ppermute | solution.py:207
  7.7 4.5 %collective-permute-start.1 = (bf16[256,256]{1,0:T(8,128)(2,1)S(1)}, bf16[256,256]{1,0:T(8,128)(2,1)S(1)}, u32[]{:S(2)}, u32[]{:S(2)}) collective-permute-start(bf16[256,256]{1,0:T(8,128)(2,1)S(1)} %get-tuple-element.29), channel_id=1, source_target_pairs={{0,4},{4,0},{8,12},{12,8},{16,20},{20,16},{24,28},{28,24},{1,5},{5... | collective-permute-start | bytes 393224 | tf_op jit(solution)/shard_map/ppermute | solution.py:204
  13.4 7.8 %collective-permute-start.3 = (bf16[512,384]{1,0:T(8,128)(2,1)S(1)}, bf16[512,384]{1,0:T(8,128)(2,1)S(1)}, u32[]{:S(2)}, u32[]{:S(2)}) collective-permute-start(bf16[512,384]{1,0:T(8,128)(2,1)S(1)} %outer_image.1.outer), channel_id=1, source_target_pairs={{0,2},{1,3},{2,0},{3,1},{4,5},{5,4},{6,7},{7,6},{8,10},{9,11},{10,... | collective-permute-start | bytes 1179656 | tf_op jit(solution)/shard_map/ppermute | solution.py:211
  15.0 10.5 %collective-permute-start.2 = (bf16[512,384]{1,0:T(8,128)(2,1)S(1)}, bf16[512,384]{1,0:T(8,128)(2,1)S(1)}, u32[]{:S(2)}, u32[]{:S(2)}) collective-permute-start(bf16[512,384]{1,0:T(8,128)(2,1)S(1)} %get-tuple-element.27.inner), channel_id=1, source_target_pairs={{0,2},{1,3},{2,0},{3,1},{4,5},{5,4},{6,7},{7,6},{8,10},{9,11},{10,... | collective-permute-start | bytes 1179656 | tf_op jit(solution)/shard_map/ppermute | solution.py:211
  16.1 14.2 %collective-permute-start.13 = (bf16[128,384]{1,0:T(8,128)(2,1)S(1)}, bf16[128,384]{1,0:T(8,128)(2,1)S(1)}, u32[]{:S(2)}, u32[]{:S(2)}) collective-permute-start(bf16[128,384]{1,0:T(8,128)(2,1)S(1)} %get-tuple-element.45), channel_id=1, source_target_pairs={{0,28},{4,8},{8,4},{12,16},{16,12},{20,24},{24,20},{28,0},{1,29},{... | collective-permute-start | bytes 294920 | tf_op jit(solution)/shard_map/ppermute | solution.py:207
  17.3 14.6 %collective-permute-start.14 = (bf16[128,384]{1,0:T(8,128)(2,1)S(1)}, bf16[128,384]{1,0:T(8,128)(2,1)S(1)}, u32[]{:S(2)}, u32[]{:S(2)}) collective-permute-start(bf16[128,384]{1,0:T(8,128)(2,1)S(1)} %get-tuple-element.46), channel_id=1, source_target_pairs={{0,4},{4,0},{8,12},{12,8},{16,20},{20,16},{24,28},{28,24},{1,5},{5... | collective-permute-start | bytes 294920 | tf_op jit(solution)/shard_map/ppermute | solution.py:204
  26.0 5.8 %collective-permute-start.10 = (bf16[128,384]{1,0:T(8,128)(2,1)S(1)}, bf16[128,384]{1,0:T(8,128)(2,1)S(1)}, u32[]{:S(2)}, u32[]{:S(2)}) collective-permute-start(bf16[128,384]{1,0:T(8,128)(2,1)S(1)} %get-tuple-element.41), channel_id=1, source_target_pairs={{0,1},{1,0},{2,3},{3,2},{4,6},{5,7},{6,4},{7,5},{8,9},{9,8},{10,11... | collective-permute-start | bytes 294920 | tf_op jit(solution)/shard_map/ppermute | solution.py:211
  26.4 7.5 %collective-permute-start.11 = (bf16[128,384]{1,0:T(8,128)(2,1)S(1)}, bf16[128,384]{1,0:T(8,128)(2,1)S(1)}, u32[]{:S(2)}, u32[]{:S(2)}) collective-permute-start(bf16[128,384]{1,0:T(8,128)(2,1)S(1)} %get-tuple-element.42), channel_id=1, source_target_pairs={{0,29},{1,28},{2,31},{3,30},{4,10},{5,11},{6,8},{7,9},{8,5},{9,4},... | collective-permute-start | bytes 294920 | tf_op jit(solution)/shard_map/ppermute | solution.py:211
  29.7 5.3 %collective-permute-start.12 = (bf16[128,384]{1,0:T(8,128)(2,1)S(1)}, bf16[128,384]{1,0:T(8,128)(2,1)S(1)}, u32[]{:S(2)}, u32[]{:S(2)}) collective-permute-start(bf16[128,384]{1,0:T(8,128)(2,1)S(1)} %get-tuple-element.43), channel_id=1, source_target_pairs={{0,5},{1,4},{2,7},{3,6},{4,2},{5,3},{6,0},{7,1},{8,13},{9,12},{10,... | collective-permute-start | bytes 294920 | tf_op jit(solution)/shard_map/ppermute | solution.py:211
  30.3 7.9 %collective-permute-start.8 = (bf16[128,384]{1,0:T(8,128)(2,1)S(1)}, bf16[128,384]{1,0:T(8,128)(2,1)S(1)}, u32[]{:S(2)}, u32[]{:S(2)}) collective-permute-start(bf16[128,384]{1,0:T(8,128)(2,1)S(1)} %get-tuple-element.37), channel_id=1, source_target_pairs={{0,28},{4,8},{8,4},{12,16},{16,12},{20,24},{24,20},{28,0},{1,29},{... | collective-permute-start | bytes 294920 | tf_op jit(solution)/shard_map/ppermute | solution.py:207
  31.8 6.5 %collective-permute-start.9 = (bf16[128,384]{1,0:T(8,128)(2,1)S(1)}, bf16[128,384]{1,0:T(8,128)(2,1)S(1)}, u32[]{:S(2)}, u32[]{:S(2)}) collective-permute-start(bf16[128,384]{1,0:T(8,128)(2,1)S(1)} %get-tuple-element.38), channel_id=1, source_target_pairs={{0,4},{4,0},{8,12},{12,8},{16,20},{20,16},{24,28},{28,24},{1,5},{5... | collective-permute-start | bytes 294920 | tf_op jit(solution)/shard_map/ppermute | solution.py:204
  31.8 6.5 %collective-permute-start.6 = (bf16[128,384]{1,0:T(8,128)(2,1)S(1)}, bf16[128,384]{1,0:T(8,128)(2,1)S(1)}, u32[]{:S(2)}, u32[]{:S(2)}) collective-permute-start(bf16[128,384]{1,0:T(8,128)(2,1)S(1)} %get-tuple-element.35), channel_id=1, source_target_pairs={{0,5},{1,4},{2,7},{3,6},{4,2},{5,3},{6,0},{7,1},{8,13},{9,12},{10,... | collective-permute-start | bytes 294920 | tf_op jit(solution)/shard_map/ppermute | solution.py:211
  33.9 5.7 %collective-permute-start.7 = (bf16[128,384]{1,0:T(8,128)(2,1)S(1)}, bf16[128,384]{1,0:T(8,128)(2,1)S(1)}, u32[]{:S(2)}, u32[]{:S(2)}) collective-permute-start(bf16[128,384]{1,0:T(8,128)(2,1)S(1)} %get-tuple-element.36), channel_id=1, source_target_pairs={{0,1},{1,0},{2,3},{3,2},{4,6},{5,7},{6,4},{7,5},{8,9},{9,8},{10,11... | collective-permute-start | bytes 294920 | tf_op jit(solution)/shard_map/ppermute | solution.py:211
  35.0 6.7 %collective-permute-start.5 = (bf16[128,384]{1,0:T(8,128)(2,1)S(1)}, bf16[128,384]{1,0:T(8,128)(2,1)S(1)}, u32[]{:S(2)}, u32[]{:S(2)}) collective-permute-start(bf16[128,384]{1,0:T(8,128)(2,1)S(1)} %get-tuple-element.32), channel_id=1, source_target_pairs={{0,29},{1,28},{2,31},{3,30},{4,10},{5,11},{6,8},{7,9},{8,5},{9,4},... | collective-permute-start | bytes 294920 | tf_op jit(solution)/shard_map/ppermute | solution.py:211

commit v8 on v7

--- a/solution.py
+++ b/solution.py
@@ -146,17 +146,28 @@
         chip[...] = down
 
 
-def first_tile(size, masked, inner, outer, own, link, chip, left_inner, left_outer):
+def turn(size, masked, left_inner, left_outer):
     rows = masked.shape[0]
     rim = RIM * size
     left_inner[...] = masked[rim : rows - rim, :].T
     left_outer[:, :rim] = masked[:rim, :].T
     left_outer[:, rim:] = masked[rows - rim :, :].T
-    second_tile(left_inner, left_outer, inner, outer, own, link, chip)
-
-
-def second_tile(left_inner, left_outer, inner, outer, own, link, chip):
+
+
+def own_tile(size, masked, inner, outer, own, link, chip, left_inner, left_outer):
+    turn(size, masked, left_inner, left_outer)
     store_tile(dot(left_inner[...], inner[...]) + dot(left_outer[...], outer[...]), own, link, chip)
+
+
+def partner_tile(size, masked, inner, outer, near_left, inner_r, own, link, chip, far_outer, far, near, far_inner):
+    turn(size, masked, far_inner, far_outer)
+    store_tile(dot(far_inner[...], inner[...]) + dot(far_outer[...], outer[...]), own, link, chip)
+    far[...] = dot(far_inner[...], inner_r[...])
+    near[...] = dot(near_left[...], inner_r[...])
+
+
+def late_tile(base, left_outer, outer, own, link, chip):
+    store_tile(base[...] + dot(left_outer[...], outer[...]), own, link, chip)
 
 
 def add_tiles(steps, *refs):
@@ -266,37 +277,47 @@
     )
     outer_r = to_side(outer)
     tile_flops = 2 * rows * wide * wide
-    lefts = (shape((wide, inner_rows), BF16), shape((wide, 2 * rim), BF16))
-
-    def first(masked, own, name):
+    left_shapes = (shape((wide, inner_rows), BF16), shape((wide, 2 * rim), BF16))
+    base_shape = shape((wide, wide), F32)
+
+    own, own_link, own_chip, left_inner, left_outer = call(
+        functools.partial(own_tile, size),
+        (*tile_shapes(width, wide, F32), *left_shapes),
+        [VMEM] * 3,
+        [VMEM] * 5,
+        (masked, inner, outer),
+        flops=tile_flops,
+        name="own_tile",
+    )
+    own_link, own_chip = over_link(own_link), over_chip(own_chip)
+    part, part_link, part_chip, far_outer, far_base, near_base = call(
+        functools.partial(partner_tile, size),
+        (*tile_shapes(width, wide, BF16), left_shapes[1], base_shape, base_shape),
+        [VMEM] * 5,
+        [VMEM] * 6,
+        (masked_p, inner, outer, left_inner, inner_r),
+        scratch=[pltpu.VMEM((wide, inner_rows), BF16)],
+        flops=2 * tile_flops,
+        name="partner_tile",
+    )
+    part, part_link, part_chip = spread(part, part_link, part_chip)
+
+    outer_r, own_link, own_chip = lax.optimization_barrier((outer_r, own_link, own_chip))
+
+    def late(base, left, own, name):
         return call(
-            functools.partial(first_tile, size),
-            (*tile_shapes(width, wide, own), *lefts),
+            late_tile,
+            tile_shapes(width, wide, own),
             [VMEM] * 3,
-            [VMEM] * 5,
-            (masked, inner, outer),
-            flops=tile_flops,
+            [VMEM] * 3,
+            (base, left, outer_r),
+            flops=tile_flops // 2,
             name=name,
         )
 
-    def second(left_inner, left_outer, own, name):
-        return call(
-            second_tile,
-            tile_shapes(width, wide, own),
-            [VMEM] * 4,
-            [VMEM] * 3,
-            (left_inner, left_outer, inner_r, outer_r),
-            flops=tile_flops,
-            name=name,
-        )
-
-    own, own_link, own_chip, left_inner, left_outer = first(masked, F32, "own_tile")
-    own_link, own_chip = over_link(own_link), over_chip(own_chip)
-    *part, far_inner, far_outer = first(masked_p, BF16, "partner_tile")
-    outer_r, _ = lax.optimization_barrier((outer_r, part[1]))
-    part, part_link, part_chip = spread(*part)
-    far, far_link, far_chip = spread(*second(far_inner, far_outer, BF16, "far_tile"))
-    near, near_link, near_chip = second(left_inner, left_outer, F32, "near_tile")
+    far, far_link, far_chip = spread(*late(far_base, far_outer, BF16, "far_tile"))
+    near_base, part, part_link, part_chip = lax.optimization_barrier((near_base, part, part_link, part_chip))
+    near, near_link, near_chip = late(near_base, left_outer, F32, "near_tile")
     near_link, near_chip = over_link(near_link), over_chip(near_chip)
 
     def add(steps, terms, name, base=None):

time: 42.9 us -> 39.4 us (0.918)
  waiting for transfers between devices: 16 us -> 8.22 us
  starting transfers between devices: 19.4 us -> 23.2 us
    ppermute x9, waiting for transfers between devices: 11.5 us -> 4.02 us  [to(): return lax.ppermute(value, ('blk', 'col'), perm)]
    ppermute x9, starting transfers between devices: 13.9 us -> 16 us  [to(): return lax.ppermute(value, ('blk', 'col'), perm)]
    ppermute x3, starting transfers between devices: 5.44 us -> 7.19 us  [over_link(): return lax.ppermute(value, 'blk', cross)]
  transfers between devices with their start and end apart: 15 -> 15, of which waited for: 6 -> 5; matrix products, arithmetic and copies ran while one was open for 0% -> 0% of each run, Pallas kernels for 10% -> 12%
where the time goes in v8:
time: 39.4 us; the launch traced here: 38.9 us
  starting transfers between devices  23.2 us (59%)
  waiting for transfers between devices  8.22 us (21%)
  Pallas kernels  7.41 us (19%)
    ppermute x9, starting transfers between devices, to(): return lax.ppermute(value, ('blk', 'col'), perm)  16 us
    pallas_call x8, Pallas kernels, call(): pl.pallas_call(kernel, out_shape=out_shape, in_specs=in_specs, out_specs=...  7.41 us
    ppermute x3, starting transfers between devices, over_link(): return lax.ppermute(value, 'blk', cross)  7.19 us
    ppermute x3, waiting for transfers between devices, over_link(): return lax.ppermute(value, 'blk', cross)  4.19 us
    ppermute x9, waiting for transfers between devices, to(): return lax.ppermute(value, ('blk', 'col'), perm)  4.02 us
  transfers between devices with their start and end apart: 15, of which 5 were waited for; matrix products, arithmetic and copies ran while one was open for 0% of the time, Pallas kernels for 12%

profile of v8, /device:TPU:0, one launch (start us, length us, event | category | flops | bytes accessed | tf_op | source)
XLA Modules:
  0.0 38.9 jit_solution(3638414206243744514)
XLA Ops:
  0.0 1.9 %mask_and_inner.1 = (bf16[1024,384]{1,0:T(8,128)(2,1)S(1)}, bf16[256,256]{1,0:T(8,128)(2,1)S(1)}, bf16[256,256]{1,0:T(8,128)(2,1)S(1)}, bf16[512,384]{1,0:T(8,128)(2,1)S(1)}) custom-call(s32[3,8]{1,0:T(4,128)} %bitcast.4, bf16[3,1024,128]{2,1,0:T(8,128)(2,1)} %bitcast.6, s32[8,2,128]{2,1,0:T(2,128)} %bitcast.7, bf16[8,3,128,128]{3,2,1,0:T(8,128)(2,1)} %stiffness.1), custom_call_target="tpu_custom_call" | custom-call | flops 150994944 | bytes 3022944 | tf_op jit(solution)/shard_map/mask_and_inner/pallas_call | solution.py:29
  1.9 3.0 %collective-permute-start = (bf16[1024,384]{1,0:T(8,128)(2,1)S(1)}, bf16[1024,384]{1,0:T(8,128)(2,1)S(1)}, u32[]{:S(2)}, u32[]{:S(2)}) collective-permute-start(bf16[1024,384]{1,0:T(8,128)(2,1)S(1)} %get-tuple-element.33.masked), channel_id=1, source_target_pairs={{0,1},{1,0},{2,3},{3,2},{4,6},{5,7},{6,4},{7,5},{8,9},{9,8},{10,11... | collective-permute-start | bytes 2359304 | tf_op jit(solution)/shard_map/ppermute | solution.py:222
  4.9 2.8 %collective-permute-start.1 = (bf16[256,256]{1,0:T(8,128)(2,1)S(1)}, bf16[256,256]{1,0:T(8,128)(2,1)S(1)}, u32[]{:S(2)}, u32[]{:S(2)}) collective-permute-start(bf16[256,256]{1,0:T(8,128)(2,1)S(1)} %get-tuple-element.35), channel_id=1, source_target_pairs={{0,28},{4,8},{8,4},{12,16},{16,12},{20,24},{24,20},{28,0},{1,29},{... | collective-permute-start | bytes 393224 | tf_op jit(solution)/shard_map/ppermute | solution.py:218
  7.7 0.5 %collective-permute-start.3 = (bf16[512,384]{1,0:T(8,128)(2,1)S(1)}, bf16[512,384]{1,0:T(8,128)(2,1)S(1)}, u32[]{:S(2)}, u32[]{:S(2)}) collective-permute-start(bf16[512,384]{1,0:T(8,128)(2,1)S(1)} %get-tuple-element.34.inner), channel_id=1, source_target_pairs={{0,2},{1,3},{2,0},{3,1},{4,5},{5,4},{6,7},{7,6},{8,10},{9,11},{10,... | collective-permute-start | bytes 1179656 | tf_op jit(solution)/shard_map/ppermute | solution.py:222
  8.2 4.0 %collective-permute-done.1.from_link = bf16[256,256]{1,0:T(8,128)(2,1)S(1)} collective-permute-done((bf16[256,256]{1,0:T(8,128)(2,1)S(1)}, bf16[256,256]{1,0:T(8,128)(2,1)S(1)}, u32[]{:S(2)}, u32[]{:S(2)}) %collective-permute-start.1) | collective-permute-done | bytes 131104 | tf_op jit(solution)/shard_map/ppermute | solution.py:218
  12.3 1.1 %outer_image.1.outer = bf16[512,384]{1,0:T(8,128)(2,1)S(1)} custom-call(s32[3,8]{1,0:T(4,128)S(1)} %bitcast.5, bf16[8,3,128,128]{3,2,1,0:T(8,128)(2,1)S(1)} %copy-done, bf16[1024,384]{1,0:T(8,128)(2,1)S(1)} %get-tuple-element.33.masked, bf16[256,256]{1,0:T(8,128)(2,1)S(1)} %collective-permute-done.1.from_link, ...), custom_call_target="tpu_custom_call" | custom-call | flops 150994944 | bytes 2228320 | tf_op jit(solution)/shard_map/outer_image/pallas_call | solution.py:29
  13.4 1.6 %collective-permute-start.7 = (bf16[512,384]{1,0:T(8,128)(2,1)S(1)}, bf16[512,384]{1,0:T(8,128)(2,1)S(1)}, u32[]{:S(2)}, u32[]{:S(2)}) collective-permute-start(bf16[512,384]{1,0:T(8,128)(2,1)S(1)} %outer_image.1.outer), channel_id=1, source_target_pairs={{0,2},{1,3},{2,0},{3,1},{4,5},{5,4},{6,7},{7,6},{8,10},{9,11},{10,... | collective-permute-start | bytes 1179656 | tf_op jit(solution)/shard_map/ppermute | solution.py:222
  15.0 0.6 %own_tile.1 = (f32[128,384]{1,0:T(8,128)S(1)}, bf16[128,384]{1,0:T(8,128)(2,1)S(1)}, bf16[128,384]{1,0:T(8,128)(2,1)S(1)}, bf16[384,512]{1,0:T(8,128)(2,1)S(1)}, bf16[384,512]{1,0:T(8,128)(2,1)S(1)}) custom-call(bf16[1024,384]{1,0:T(8,128)(2,1)S(1)} %get-tuple-element.33.masked, bf16[512,384]{1,0:T(8,128)(2,1)S(1)} %get-tuple-element.34.inner, ...), custom_call_target="tpu_custom_call" | custom-call | flops 301989888 | bytes 2752512 | tf_op jit(solution)/shard_map/own_tile/pallas_call | solution.py:29
  15.6 1.4 %collective-permute-start.8 = (bf16[128,384]{1,0:T(8,128)(2,1)S(1)}, bf16[128,384]{1,0:T(8,128)(2,1)S(1)}, u32[]{:S(2)}, u32[]{:S(2)}) collective-permute-start(bf16[128,384]{1,0:T(8,128)(2,1)S(1)} %get-tuple-element.44), channel_id=1, source_target_pairs={{0,28},{4,8},{8,4},{12,16},{16,12},{20,24},{24,20},{28,0},{1,29},{... | collective-permute-start | bytes 294920 | tf_op jit(solution)/shard_map/ppermute | solution.py:218
  17.0 1.3 %collective-permute-done.3.inner_r = bf16[512,384]{1,0:T(8,128)(2,1)S(1)} collective-permute-done((bf16[512,384]{1,0:T(8,128)(2,1)S(1)}, bf16[512,384]{1,0:T(8,128)(2,1)S(1)}, u32[]{:S(2)}, u32[]{:S(2)}) %collective-permute-start.3) | collective-permute-done | bytes 393248 | tf_op jit(solution)/shard_map/ppermute | solution.py:222
  18.3 0.7 %collective-permute-done.masked = bf16[1024,384]{1,0:T(8,128)(2,1)S(1)} collective-permute-done((bf16[1024,384]{1,0:T(8,128)(2,1)S(1)}, bf16[1024,384]{1,0:T(8,128)(2,1)S(1)}, u32[]{:S(2)}, u32[]{:S(2)}) %collective-permute-start) | collective-permute-done | bytes 786464 | tf_op jit(solution)/shard_map/ppermute | solution.py:222
  19.0 1.2 %partner_tile.1 = (bf16[128,384]{1,0:T(8,128)(2,1)S(1)}, bf16[128,384]{1,0:T(8,128)(2,1)S(1)}, bf16[128,384]{1,0:T(8,128)(2,1)S(1)}, bf16[384,512]{1,0:T(8,128)(...) custom-call(bf16[1024,384]{1,0:T(8,128)(2,1)S(1)} %collective-permute-done.masked, ...), custom_call_target="tpu_custom_call" | custom-call | flops 603979776 | bytes 4227072 | tf_op jit(solution)/shard_map/partner_tile/pallas_call | solution.py:29
  20.2 2.5 %collective-permute-start.4 = (bf16[128,384]{1,0:T(8,128)(2,1)S(1)}, bf16[128,384]{1,0:T(8,128)(2,1)S(1)}, u32[]{:S(2)}, u32[]{:S(2)}) collective-permute-start(bf16[128,384]{1,0:T(8,128)(2,1)S(1)} %get-tuple-element.39), channel_id=1, source_target_pairs={{0,1},{1,0},{2,3},{3,2},{4,6},{5,7},{6,4},{7,5},{8,9},{9,8},{10,11... | collective-permute-start | bytes 294920 | tf_op jit(solution)/shard_map/ppermute | solution.py:222
  22.7 4.7 %collective-permute-start.5 = (bf16[128,384]{1,0:T(8,128)(2,1)S(1)}, bf16[128,384]{1,0:T(8,128)(2,1)S(1)}, u32[]{:S(2)}, u32[]{:S(2)}) collective-permute-start(bf16[128,384]{1,0:T(8,128)(2,1)S(1)} %get-tuple-element.40), channel_id=1, source_target_pairs={{0,29},{1,28},{2,31},{3,30},{4,10},{5,11},{6,8},{7,9},{8,5},{9,4},... | collective-permute-start | bytes 294920 | tf_op jit(solution)/shard_map/ppermute | solution.py:222
  27.4 0.2 collective-permute-start.6
  27.6 0.4 %far_tile.1 = (bf16[128,384]{1,0:T(8,128)(2,1)S(1)}, bf16[128,384]{1,0:T(8,128)(2,1)S(1)}, bf16[128,384]{1,0:T(8,128)(2,1)S(1)}) custom-call(f32[384,384]{1,0:T(8,128)S(1)} %get-tuple-element.53.base, bf16[384,512]{1,0:T(8,128)(2,1)S(1)} %get-tuple-element.54.left_outer, bf16[512,384]{1,0:T(8,128)(2,1)S(1)} %collective-permute-done.7.outer), custom_call_target="tpu_custom_call" | custom-call | flops 150994944 | bytes 1671168 | tf_op jit(solution)/shard_map/far_tile/pallas_call | solution.py:29
  28.0 2.0 %collective-permute-start.12 = (bf16[128,384]{1,0:T(8,128)(2,1)S(1)}, bf16[128,384]{1,0:T(8,128)(2,1)S(1)}, u32[]{:S(2)}, u32[]{:S(2)}) collective-permute-start(bf16[128,384]{1,0:T(8,128)(2,1)S(1)} %get-tuple-element.55), channel_id=1, source_target_pairs={{0,1},{1,0},{2,3},{3,2},{4,6},{5,7},{6,4},{7,5},{8,9},{9,8},{10,11... | collective-permute-start | bytes 294920 | tf_op jit(solution)/shard_map/ppermute | solution.py:222
  30.1 1.4 %collective-permute-start.13 = (bf16[128,384]{1,0:T(8,128)(2,1)S(1)}, bf16[128,384]{1,0:T(8,128)(2,1)S(1)}, u32[]{:S(2)}, u32[]{:S(2)}) collective-permute-start(bf16[128,384]{1,0:T(8,128)(2,1)S(1)} %get-tuple-element.56), channel_id=1, source_target_pairs={{0,29},{1,28},{2,31},{3,30},{4,10},{5,11},{6,8},{7,9},{8,5},{9,4},... | collective-permute-start | bytes 294920 | tf_op jit(solution)/shard_map/ppermute | solution.py:222
  31.5 0.4 %near_tile.1 = (f32[128,384]{1,0:T(8,128)S(1)}, bf16[128,384]{1,0:T(8,128)(2,1)S(1)}, bf16[128,384]{1,0:T(8,128)(2,1)S(1)}) custom-call(f32[384,384]{1,0:T(8,128)S(1)} %get-tuple-element.42.base, bf16[384,512]{1,0:T(8,128)(2,1)S(1)} %get-tuple-element.43.left_outer, bf16[512,384]{1,0:T(8,128)(2,1)S(1)} %collective-permute-done.7.outer), custom_call_target="tpu_custom_call" | custom-call | flops 150994944 | bytes 1769472 | tf_op jit(solution)/shard_map/near_tile/pallas_call | solution.py:29
  31.9 3.0 %collective-permute-start.10 = (bf16[128,384]{1,0:T(8,128)(2,1)S(1)}, bf16[128,384]{1,0:T(8,128)(2,1)S(1)}, u32[]{:S(2)}, u32[]{:S(2)}) collective-permute-start(bf16[128,384]{1,0:T(8,128)(2,1)S(1)} %get-tuple-element.51), channel_id=1, source_target_pairs={{0,28},{4,8},{8,4},{12,16},{16,12},{20,24},{24,20},{28,0},{1,29},{... | collective-permute-start | bytes 294920 | tf_op jit(solution)/shard_map/ppermute | solution.py:218
  34.9 0.8 %add_own.1.refs_9_ = f32[5,128,512]{2,1,0:T(8,128)} custom-call(f32[128,384]{1,0:T(8,128)S(1)} %get-tuple-element.58.refs_0_, bf16[128,384]{1,0:T(8,128)(2,1)S(1)} %collective-permute-done.8.refs_1_, bf16[128,384]{1,0:T(8,128)(2,1)S(1)} %collective-permute-done.9.refs_2_), custom_call_target="tpu_custom_call" | custom-call | flops 81920 | bytes 1703936 | tf_op jit(solution)/shard_map/add_own/pallas_call | solution.py:29
  35.7 2.0 %collective-permute-done.13.refs_7_ = bf16[128,384]{1,0:T(8,128)(2,1)S(1)} collective-permute-done((bf16[128,384]{1,0:T(8,128)(2,1)S(1)}, bf16[128,384]{1,0:T(8,128)(2,1)S(1)}, u32[]{:S(2)}, u32[]{:S(2)}) %collective-permute-start.13) | collective-permute-done | bytes 98336 | tf_op jit(solution)/shard_map/ppermute | solution.py:222
  37.7 0.2 collective-permute-done.10.refs_4_
  37.9 1.0 %add_rest.1 = f32[5,128,512]{2,1,0:T(8,128)} custom-call(f32[128,384]{1,0:T(8,128)S(1)} %get-tuple-element.47.refs_0_, bf16[128,384]{1,0:T(8,128)(2,1)S(1)} %collective-permute-done.5.refs_1_, bf16[128,384]{1,0:T(8,128)(2,1)S(1)} %collective-permute-done.6.refs_2_, ...), custom_call_target="tpu_custom_call", output_to_operand_aliasing={{}: (9, {})} | custom-call | flops 245760 | bytes 3604480 | tf_op jit(solution)/shard_map/add_rest/pallas_call | solution.py:29
  (18 shorter events, 0.0 us)
Async XLA Ops:
  0.0 12.3 %copy-start.1 = (s32[8,3]{0,1:T(4,128)S(1)}, s32[8,3]{0,1:T(4,128)}, u32[]{:S(2)}) copy-start(s32[8,3]{0,1:T(4,128)} %param.5) | copy-start | bytes 292
  0.0 12.3 %copy-start = (bf16[8,3,128,128]{3,2,1,0:T(8,128)(2,1)S(1)}, bf16[8,3,128,128]{3,2,1,0:T(8,128)(2,1)}, u32[]{:S(2)}) copy-start(bf16[8,3,128,128]{3,2,1,0:T(8,128)(2,1)} %stiffness.1) | copy-start | bytes 2359300
  1.9 17.1 %collective-permute-start = (bf16[1024,384]{1,0:T(8,128)(2,1)S(1)}, bf16[1024,384]{1,0:T(8,128)(2,1)S(1)}, u32[]{:S(2)}, u32[]{:S(2)}) collective-permute-start(bf16[1024,384]{1,0:T(8,128)(2,1)S(1)} %get-tuple-element.33.masked), channel_id=1, source_target_pairs={{0,1},{1,0},{2,3},{3,2},{4,6},{5,7},{6,4},{7,5},{8,9},{9,8},{10,11... | collective-permute-start | bytes 2359304 | tf_op jit(solution)/shard_map/ppermute | solution.py:222
  4.9 7.3 %collective-permute-start.1 = (bf16[256,256]{1,0:T(8,128)(2,1)S(1)}, bf16[256,256]{1,0:T(8,128)(2,1)S(1)}, u32[]{:S(2)}, u32[]{:S(2)}) collective-permute-start(bf16[256,256]{1,0:T(8,128)(2,1)S(1)} %get-tuple-element.35), channel_id=1, source_target_pairs={{0,28},{4,8},{8,4},{12,16},{16,12},{20,24},{24,20},{28,0},{1,29},{... | collective-permute-start | bytes 393224 | tf_op jit(solution)/shard_map/ppermute | solution.py:218
  7.7 4.5 %collective-permute-start.2 = (bf16[256,256]{1,0:T(8,128)(2,1)S(1)}, bf16[256,256]{1,0:T(8,128)(2,1)S(1)}, u32[]{:S(2)}, u32[]{:S(2)}) collective-permute-start(bf16[256,256]{1,0:T(8,128)(2,1)S(1)} %get-tuple-element.36), channel_id=1, source_target_pairs={{0,4},{4,0},{8,12},{12,8},{16,20},{20,16},{24,28},{28,24},{1,5},{5... | collective-permute-start | bytes 393224 | tf_op jit(solution)/shard_map/ppermute | solution.py:215
  7.7 10.6 %collective-permute-start.3 = (bf16[512,384]{1,0:T(8,128)(2,1)S(1)}, bf16[512,384]{1,0:T(8,128)(2,1)S(1)}, u32[]{:S(2)}, u32[]{:S(2)}) collective-permute-start(bf16[512,384]{1,0:T(8,128)(2,1)S(1)} %get-tuple-element.34.inner), channel_id=1, source_target_pairs={{0,2},{1,3},{2,0},{3,1},{4,5},{5,4},{6,7},{7,6},{8,10},{9,11},{10,... | collective-permute-start | bytes 1179656 | tf_op jit(solution)/shard_map/ppermute | solution.py:222
  13.4 14.2 %collective-permute-start.7 = (bf16[512,384]{1,0:T(8,128)(2,1)S(1)}, bf16[512,384]{1,0:T(8,128)(2,1)S(1)}, u32[]{:S(2)}, u32[]{:S(2)}) collective-permute-start(bf16[512,384]{1,0:T(8,128)(2,1)S(1)} %outer_image.1.outer), channel_id=1, source_target_pairs={{0,2},{1,3},{2,0},{3,1},{4,5},{5,4},{6,7},{7,6},{8,10},{9,11},{10,... | collective-permute-start | bytes 1179656 | tf_op jit(solution)/shard_map/ppermute | solution.py:222
  15.6 11.8 %collective-permute-start.8 = (bf16[128,384]{1,0:T(8,128)(2,1)S(1)}, bf16[128,384]{1,0:T(8,128)(2,1)S(1)}, u32[]{:S(2)}, u32[]{:S(2)}) collective-permute-start(bf16[128,384]{1,0:T(8,128)(2,1)S(1)} %get-tuple-element.44), channel_id=1, source_target_pairs={{0,28},{4,8},{8,4},{12,16},{16,12},{20,24},{24,20},{28,0},{1,29},{... | collective-permute-start | bytes 294920 | tf_op jit(solution)/shard_map/ppermute | solution.py:218
  17.0 10.6 %collective-permute-start.9 = (bf16[128,384]{1,0:T(8,128)(2,1)S(1)}, bf16[128,384]{1,0:T(8,128)(2,1)S(1)}, u32[]{:S(2)}, u32[]{:S(2)}) collective-permute-start(bf16[128,384]{1,0:T(8,128)(2,1)S(1)} %get-tuple-element.45), channel_id=1, source_target_pairs={{0,4},{4,0},{8,12},{12,8},{16,20},{20,16},{24,28},{28,24},{1,5},{5... | collective-permute-start | bytes 294920 | tf_op jit(solution)/shard_map/ppermute | solution.py:215
  20.2 11.3 %collective-permute-start.4 = (bf16[128,384]{1,0:T(8,128)(2,1)S(1)}, bf16[128,384]{1,0:T(8,128)(2,1)S(1)}, u32[]{:S(2)}, u32[]{:S(2)}) collective-permute-start(bf16[128,384]{1,0:T(8,128)(2,1)S(1)} %get-tuple-element.39), channel_id=1, source_target_pairs={{0,1},{1,0},{2,3},{3,2},{4,6},{5,7},{6,4},{7,5},{8,9},{9,8},{10,11... | collective-permute-start | bytes 294920 | tf_op jit(solution)/shard_map/ppermute | solution.py:222
  22.7 8.8 %collective-permute-start.5 = (bf16[128,384]{1,0:T(8,128)(2,1)S(1)}, bf16[128,384]{1,0:T(8,128)(2,1)S(1)}, u32[]{:S(2)}, u32[]{:S(2)}) collective-permute-start(bf16[128,384]{1,0:T(8,128)(2,1)S(1)} %get-tuple-element.40), channel_id=1, source_target_pairs={{0,29},{1,28},{2,31},{3,30},{4,10},{5,11},{6,8},{7,9},{8,5},{9,4},... | collective-permute-start | bytes 294920 | tf_op jit(solution)/shard_map/ppermute | solution.py:222
  27.4 4.1 %collective-permute-start.6 = (bf16[128,384]{1,0:T(8,128)(2,1)S(1)}, bf16[128,384]{1,0:T(8,128)(2,1)S(1)}, u32[]{:S(2)}, u32[]{:S(2)}) collective-permute-start(bf16[128,384]{1,0:T(8,128)(2,1)S(1)} %get-tuple-element.41), channel_id=1, source_target_pairs={{0,5},{1,4},{2,7},{3,6},{4,2},{5,3},{6,0},{7,1},{8,13},{9,12},{10,... | collective-permute-start | bytes 294920 | tf_op jit(solution)/shard_map/ppermute | solution.py:222
  28.0 7.7 %collective-permute-start.12 = (bf16[128,384]{1,0:T(8,128)(2,1)S(1)}, bf16[128,384]{1,0:T(8,128)(2,1)S(1)}, u32[]{:S(2)}, u32[]{:S(2)}) collective-permute-start(bf16[128,384]{1,0:T(8,128)(2,1)S(1)} %get-tuple-element.55), channel_id=1, source_target_pairs={{0,1},{1,0},{2,3},{3,2},{4,6},{5,7},{6,4},{7,5},{8,9},{9,8},{10,11... | collective-permute-start | bytes 294920 | tf_op jit(solution)/shard_map/ppermute | solution.py:222
  30.1 7.7 %collective-permute-start.13 = (bf16[128,384]{1,0:T(8,128)(2,1)S(1)}, bf16[128,384]{1,0:T(8,128)(2,1)S(1)}, u32[]{:S(2)}, u32[]{:S(2)}) collective-permute-start(bf16[128,384]{1,0:T(8,128)(2,1)S(1)} %get-tuple-element.56), channel_id=1, source_target_pairs={{0,29},{1,28},{2,31},{3,30},{4,10},{5,11},{6,8},{7,9},{8,5},{9,4},... | collective-permute-start | bytes 294920 | tf_op jit(solution)/shard_map/ppermute | solution.py:222
  31.5 6.3 %collective-permute-start.14 = (bf16[128,384]{1,0:T(8,128)(2,1)S(1)}, bf16[128,384]{1,0:T(8,128)(2,1)S(1)}, u32[]{:S(2)}, u32[]{:S(2)}) collective-permute-start(bf16[128,384]{1,0:T(8,128)(2,1)S(1)} %get-tuple-element.57), channel_id=1, source_target_pairs={{0,5},{1,4},{2,7},{3,6},{4,2},{5,3},{6,0},{7,1},{8,13},{9,12},{10,... | collective-permute-start | bytes 294920 | tf_op jit(solution)/shard_map/ppermute | solution.py:222
  31.9 6.0 %collective-permute-start.10 = (bf16[128,384]{1,0:T(8,128)(2,1)S(1)}, bf16[128,384]{1,0:T(8,128)(2,1)S(1)}, u32[]{:S(2)}, u32[]{:S(2)}) collective-permute-start(bf16[128,384]{1,0:T(8,128)(2,1)S(1)} %get-tuple-element.51), channel_id=1, source_target_pairs={{0,28},{4,8},{8,4},{12,16},{16,12},{20,24},{24,20},{28,0},{1,29},{... | collective-permute-start | bytes 294920 | tf_op jit(solution)/shard_map/ppermute | solution.py:218
  34.9 3.0 %collective-permute-start.11 = (bf16[128,384]{1,0:T(8,128)(2,1)S(1)}, bf16[128,384]{1,0:T(8,128)(2,1)S(1)}, u32[]{:S(2)}, u32[]{:S(2)}) collective-permute-start(bf16[128,384]{1,0:T(8,128)(2,1)S(1)} %get-tuple-element.52), channel_id=1, source_target_pairs={{0,4},{4,0},{8,12},{12,8},{16,20},{20,16},{24,28},{28,24},{1,5},{5... | collective-permute-start | bytes 294920 | tf_op jit(solution)/shard_map/ppermute | solution.py:215

commit v9 on v8

--- a/solution.py
+++ b/solution.py
@@ -130,7 +130,7 @@
 
 
 def store_tile(tile, own, link, chip):
-    width = own.shape[0]
+    width = tile.shape[0] // 3
     odd = parity()
     own[...] = tile[width : 2 * width].astype(own.dtype)
     down, up = tile[:width].astype(BF16), tile[2 * width :].astype(BF16)
@@ -159,14 +159,20 @@
     store_tile(dot(left_inner[...], inner[...]) + dot(left_outer[...], outer[...]), own, link, chip)
 
 
-def partner_tile(size, masked, inner, outer, near_left, inner_r, own, link, chip, far_outer, far, near, far_inner):
-    turn(size, masked, far_inner, far_outer)
-    store_tile(dot(far_inner[...], inner[...]) + dot(far_outer[...], outer[...]), own, link, chip)
-    far[...] = dot(far_inner[...], inner_r[...])
-    near[...] = dot(near_left[...], inner_r[...])
-
-
-def late_tile(base, left_outer, outer, own, link, chip):
+def partner_tiles(size, masked, inner, outer, inner_r, outer_r, own, link, chip, left_inner, left_outer):
+    turn(size, masked, left_inner, left_outer)
+    wide = masked.shape[1]
+    for n, (first, second) in enumerate(((inner, outer), (inner_r, outer_r))):
+        lanes = slice(n * wide, (n + 1) * wide)
+        tile = dot(left_inner[...], first[...]) + dot(left_outer[...], second[...])
+        store_tile(tile, own.at[:, lanes], link.at[:, lanes], chip.at[:, lanes])
+
+
+def half_tile(left_inner, inner, base):
+    base[...] = dot(left_inner[...], inner[...])
+
+
+def near_tile(base, left_outer, outer, own, link, chip):
     store_tile(base[...] + dot(left_outer[...], outer[...]), own, link, chip)
 
 
@@ -178,8 +184,10 @@
     me = lax.axis_index("col")
     even = parity() == 0
     copies = []
-    for n, (even_step, odd_step) in enumerate(steps):
-        own, link, chip = (ref[...].astype(F32) for ref in terms[3 * n : 3 * n + 3])
+    for n, ((even_step, odd_step), chunks) in enumerate(steps):
+        own, link, chip = (
+            ref[:, m * 3 * width : (m + 1) * 3 * width].astype(F32) for ref, m in zip(terms[3 * n : 3 * n + 3], chunks)
+        )
         prev = jnp.where(even, link, chip)
         nxt = jnp.where(even, chip, link)
         for d in range(5):
@@ -290,35 +298,39 @@
         name="own_tile",
     )
     own_link, own_chip = over_link(own_link), over_chip(own_chip)
-    part, part_link, part_chip, far_outer, far_base, near_base = call(
-        functools.partial(partner_tile, size),
-        (*tile_shapes(width, wide, BF16), left_shapes[1], base_shape, base_shape),
-        [VMEM] * 5,
-        [VMEM] * 6,
-        (masked_p, inner, outer, left_inner, inner_r),
-        scratch=[pltpu.VMEM((wide, inner_rows), BF16)],
-        flops=2 * tile_flops,
-        name="partner_tile",
-    )
-    part, part_link, part_chip = spread(part, part_link, part_chip)
-
+    base = call(
+        half_tile,
+        shape((wide, wide), F32),
+        [VMEM] * 2,
+        VMEM,
+        (left_inner, inner_r),
+        flops=tile_flops // 2,
+        name="half_tile",
+    )
     outer_r, own_link, own_chip = lax.optimization_barrier((outer_r, own_link, own_chip))
-
-    def late(base, left, own, name):
-        return call(
-            late_tile,
-            tile_shapes(width, wide, own),
+    masked_p, base = lax.optimization_barrier((masked_p, base))
+    near, near_link, near_chip = call(
+        near_tile,
+        tile_shapes(width, wide, F32),
+        [VMEM] * 3,
+        [VMEM] * 3,
+        (base, left_outer, outer_r),
+        flops=tile_flops // 2,
+        name="near_tile",
+    )
+    near_link, near_chip = over_link(near_link), over_chip(near_chip)
+    part, part_link, part_chip = spread(
+        *call(
+            functools.partial(partner_tiles, size),
+            tile_shapes(width, 2 * wide, BF16),
+            [VMEM] * 5,
             [VMEM] * 3,
-            [VMEM] * 3,
-            (base, left, outer_r),
-            flops=tile_flops // 2,
-            name=name,
+            (masked_p, inner, outer, inner_r, outer_r),
+            scratch=[pltpu.VMEM((wide, inner_rows), BF16), pltpu.VMEM((wide, 2 * rim), BF16)],
+            flops=2 * tile_flops,
+            name="partner_tiles",
         )
-
-    far, far_link, far_chip = spread(*late(far_base, far_outer, BF16, "far_tile"))
-    near_base, part, part_link, part_chip = lax.optimization_barrier((near_base, part, part_link, part_chip))
-    near, near_link, near_chip = late(near_base, left_outer, F32, "near_tile")
-    near_link, near_chip = over_link(near_link), over_chip(near_chip)
+    )
 
     def add(steps, terms, name, base=None):
         extra = () if base is None else (base,)
@@ -334,10 +346,10 @@
             name=name,
         )
 
-    coarse = add(((0, 0),), (own, own_link, own_chip), "add_own")
+    coarse = add((((0, 0), (0, 0, 0)),), (own, own_link, own_chip), "add_own")
     coarse = add(
-        ((2, 1), (1, 2), (3, 3)),
-        (near, part_link, part_chip, part, near_link, near_chip, far, far_link, far_chip),
+        (((2, 1), (0, 0, 0)), ((1, 2), (0, 0, 0)), ((3, 3), (1, 1, 1))),
+        (near, part_link, part_chip, part, near_link, near_chip, part, part_link, part_chip),
         "add_rest",
         coarse,
     )

time: 39.4 us -> 37.4 us (0.949)
  starting transfers between devices: 23.2 us -> 16.7 us
  waiting for transfers between devices: 8.22 us -> 13 us
    ppermute x3, waiting for transfers between devices: 4.19 us -> 10.7 us  [over_link(): return lax.ppermute(value, 'blk', cross)]
    ppermute x9 -> x6, starting transfers between devices: 16 us -> 11 us  [to(): return lax.ppermute(value, ('blk', 'col'), perm)]
    ppermute x9 -> x6, waiting for transfers between devices: 4.02 us -> 2.28 us  [to(): return lax.ppermute(value, ('blk', 'col'), perm)]
    ppermute x3, starting transfers between devices: 7.19 us -> 5.63 us  [over_link(): return lax.ppermute(value, 'blk', cross)]
  transfers between devices with their start and end apart: 15 -> 12, of which waited for: 5 -> 5; matrix products, arithmetic and copies ran while one was open for 0% -> 0% of each run, Pallas kernels for 12% -> 9%
where the time goes in v9:
time: 37.4 us; the launch traced here: 37.2 us
  starting transfers between devices  16.7 us (45%)
  waiting for transfers between devices  13 us (35%)
  Pallas kernels  7.41 us (20%)
    ppermute x6, starting transfers between devices, to(): return lax.ppermute(value, ('blk', 'col'), perm)  11 us
    ppermute x3, waiting for transfers between devices, over_link(): return lax.ppermute(value, 'blk', cross)  10.7 us
    pallas_call x8, Pallas kernels, call(): pl.pallas_call(kernel, out_shape=out_shape, in_specs=in_specs, out_specs=...  7.41 us
    ppermute x3, starting transfers between devices, over_link(): return lax.ppermute(value, 'blk', cross)  5.63 us
    ppermute x6, waiting for transfers between devices, to(): return lax.ppermute(value, ('blk', 'col'), perm)  2.28 us
  transfers between devices with their start and end apart: 12, of which 5 were waited for; matrix products, arithmetic and copies ran while one was open for 0% of the time, Pallas kernels for 9%

profile of v9, /device:TPU:0, one launch (start us, length us, event | category | flops | bytes accessed | tf_op | source)
XLA Modules:
  0.0 37.2 jit_solution(11992144708273025387)
XLA Ops:
  0.0 1.9 %mask_and_inner.1 = (bf16[1024,384]{1,0:T(8,128)(2,1)S(1)}, bf16[256,256]{1,0:T(8,128)(2,1)S(1)}, bf16[256,256]{1,0:T(8,128)(2,1)S(1)}, bf16[512,384]{1,0:T(8,128)(2,1)S(1)}) custom-call(s32[3,8]{1,0:T(4,128)} %bitcast.4, bf16[3,1024,128]{2,1,0:T(8,128)(2,1)} %bitcast.6, s32[8,2,128]{2,1,0:T(2,128)} %bitcast.7, bf16[8,3,128,128]{3,2,1,0:T(8,128)(2,1)} %stiffness.1), custom_call_target="tpu_custom_call" | custom-call | flops 150994944 | bytes 3022944 | tf_op jit(solution)/shard_map/mask_and_inner/pallas_call | solution.py:29
  1.9 3.0 %collective-permute-start = (bf16[1024,384]{1,0:T(8,128)(2,1)S(1)}, bf16[1024,384]{1,0:T(8,128)(2,1)S(1)}, u32[]{:S(2)}, u32[]{:S(2)}) collective-permute-start(bf16[1024,384]{1,0:T(8,128)(2,1)S(1)} %get-tuple-element.25.masked), channel_id=1, source_target_pairs={{0,1},{1,0},{2,3},{3,2},{4,6},{5,7},{6,4},{7,5},{8,9},{9,8},{10,11... | collective-permute-start | bytes 2359304 | tf_op jit(solution)/shard_map/ppermute | solution.py:230
  4.9 2.8 %collective-permute-start.1 = (bf16[256,256]{1,0:T(8,128)(2,1)S(1)}, bf16[256,256]{1,0:T(8,128)(2,1)S(1)}, u32[]{:S(2)}, u32[]{:S(2)}) collective-permute-start(bf16[256,256]{1,0:T(8,128)(2,1)S(1)} %get-tuple-element.27), channel_id=1, source_target_pairs={{0,28},{4,8},{8,4},{12,16},{16,12},{20,24},{24,20},{28,0},{1,29},{... | collective-permute-start | bytes 393224 | tf_op jit(solution)/shard_map/ppermute | solution.py:226
  7.7 0.0 collective-permute-start.2
  7.7 0.5 %collective-permute-start.3 = (bf16[512,384]{1,0:T(8,128)(2,1)S(1)}, bf16[512,384]{1,0:T(8,128)(2,1)S(1)}, u32[]{:S(2)}, u32[]{:S(2)}) collective-permute-start(bf16[512,384]{1,0:T(8,128)(2,1)S(1)} %get-tuple-element.26.inner), channel_id=1, source_target_pairs={{0,2},{1,3},{2,0},{3,1},{4,5},{5,4},{6,7},{7,6},{8,10},{9,11},{10,... | collective-permute-start | bytes 1179656 | tf_op jit(solution)/shard_map/ppermute | solution.py:230
  8.2 4.0 %collective-permute-done.1.from_link = bf16[256,256]{1,0:T(8,128)(2,1)S(1)} collective-permute-done((bf16[256,256]{1,0:T(8,128)(2,1)S(1)}, bf16[256,256]{1,0:T(8,128)(2,1)S(1)}, u32[]{:S(2)}, u32[]{:S(2)}) %collective-permute-start.1) | collective-permute-done | bytes 131104 | tf_op jit(solution)/shard_map/ppermute | solution.py:226
  12.3 1.1 %outer_image.1.outer = bf16[512,384]{1,0:T(8,128)(2,1)S(1)} custom-call(s32[3,8]{1,0:T(4,128)S(1)} %bitcast.5, bf16[8,3,128,128]{3,2,1,0:T(8,128)(2,1)S(1)} %copy-done, bf16[1024,384]{1,0:T(8,128)(2,1)S(1)} %get-tuple-element.25.masked, bf16[256,256]{1,0:T(8,128)(2,1)S(1)} %collective-permute-done.1.from_link, ...), custom_call_target="tpu_custom_call" | custom-call | flops 150994944 | bytes 2228320 | tf_op jit(solution)/shard_map/outer_image/pallas_call | solution.py:29
  13.4 1.6 %collective-permute-start.4 = (bf16[512,384]{1,0:T(8,128)(2,1)S(1)}, bf16[512,384]{1,0:T(8,128)(2,1)S(1)}, u32[]{:S(2)}, u32[]{:S(2)}) collective-permute-start(bf16[512,384]{1,0:T(8,128)(2,1)S(1)} %outer_image.1.outer), channel_id=1, source_target_pairs={{0,2},{1,3},{2,0},{3,1},{4,5},{5,4},{6,7},{7,6},{8,10},{9,11},{10,... | collective-permute-start | bytes 1179656 | tf_op jit(solution)/shard_map/ppermute | solution.py:230
  15.0 0.6 %own_tile.1 = (f32[128,384]{1,0:T(8,128)S(1)}, bf16[128,384]{1,0:T(8,128)(2,1)S(1)}, bf16[128,384]{1,0:T(8,128)(2,1)S(1)}, bf16[384,512]{1,0:T(8,128)(2,1)S(1)}, bf16[384,512]{1,0:T(8,128)(2,1)S(1)}) custom-call(bf16[1024,384]{1,0:T(8,128)(2,1)S(1)} %get-tuple-element.25.masked, bf16[512,384]{1,0:T(8,128)(2,1)S(1)} %get-tuple-element.26.inner, ...), custom_call_target="tpu_custom_call" | custom-call | flops 301989888 | bytes 2752512 | tf_op jit(solution)/shard_map/own_tile/pallas_call | solution.py:29
  15.6 1.4 %collective-permute-start.5 = (bf16[128,384]{1,0:T(8,128)(2,1)S(1)}, bf16[128,384]{1,0:T(8,128)(2,1)S(1)}, u32[]{:S(2)}, u32[]{:S(2)}) collective-permute-start(bf16[128,384]{1,0:T(8,128)(2,1)S(1)} %get-tuple-element.32), channel_id=1, source_target_pairs={{0,28},{4,8},{8,4},{12,16},{16,12},{20,24},{24,20},{28,0},{1,29},{... | collective-permute-start | bytes 294920 | tf_op jit(solution)/shard_map/ppermute | solution.py:226
  17.0 1.3 %collective-permute-done.3.inner.inner_r = bf16[512,384]{1,0:T(8,128)(2,1)S(1)} collective-permute-done((bf16[512,384]{1,0:T(8,128)(2,1)S(1)}, bf16[512,384]{1,0:T(8,128)(2,1)S(1)}, u32[]{:S(2)}, u32[]{:S(2)}) %collective-permute-start.3) | collective-permute-done | bytes 393248 | tf_op jit(solution)/shard_map/ppermute | solution.py:230
  18.3 0.4 half_tile.1.base
  18.7 2.8 %collective-permute-done.5.refs_1_ = bf16[128,384]{1,0:T(8,128)(2,1)S(1)} collective-permute-done((bf16[128,384]{1,0:T(8,128)(2,1)S(1)}, bf16[128,384]{1,0:T(8,128)(2,1)S(1)}, u32[]{:S(2)}, u32[]{:S(2)}) %collective-permute-start.5) | collective-permute-done | bytes 98336 | tf_op jit(solution)/shard_map/ppermute | solution.py:226
  21.5 1.0 %collective-permute-done.4.outer.outer_r = bf16[512,384]{1,0:T(8,128)(2,1)S(1)} collective-permute-done((bf16[512,384]{1,0:T(8,128)(2,1)S(1)}, bf16[512,384]{1,0:T(8,128)(2,1)S(1)}, u32[]{:S(2)}, u32[]{:S(2)}) %collective-permute-start.4) | collective-permute-done | bytes 393248 | tf_op jit(solution)/shard_map/ppermute | solution.py:230
  22.5 0.0 collective-permute-done.masked
  22.5 1.2 %partner_tiles.1 = (bf16[128,768]{1,0:T(8,128)(2,1)S(1)}, bf16[128,768]{1,0:T(8,128)(2,1)S(1)}, bf16[128,768]{1,0:T(8,128)(2,1)S(1)}) custom-call(bf16[1024,384]{1,0:T(8,128)(2,1)S(1)} %collective-permute-done.masked, bf16[512,384]{1,0:T(8,128)(2,1)S(1)} %get-tuple-element.26.inner, bf16[512,384]{1,0:T(8,128)(2,1)S(1)} %outer_image.1.outer, ...), custom_call_target="tpu_custom_call" | custom-call | flops 603979776 | bytes 2949120 | tf_op jit(solution)/shard_map/partner_tiles/pallas_call | solution.py:29
  23.7 5.4 %collective-permute-start.7 = (bf16[128,768]{1,0:T(8,128)(2,1)S(1)}, bf16[128,768]{1,0:T(8,128)(2,1)S(1)}, u32[]{:S(2)}, u32[]{:S(2)}) collective-permute-start(bf16[128,768]{1,0:T(8,128)(2,1)S(1)} %get-tuple-element.37), channel_id=1, source_target_pairs={{0,29},{1,28},{2,31},{3,30},{4,10},{5,11},{6,8},{7,9},{8,5},{9,4},... | collective-permute-start | bytes 589832 | tf_op jit(solution)/shard_map/ppermute | solution.py:230
  29.1 0.5 %collective-permute-start.9 = (bf16[128,768]{1,0:T(8,128)(2,1)S(1)}, bf16[128,768]{1,0:T(8,128)(2,1)S(1)}, u32[]{:S(2)}, u32[]{:S(2)}) collective-permute-start(bf16[128,768]{1,0:T(8,128)(2,1)S(1)} %get-tuple-element.39), channel_id=1, source_target_pairs={{0,1},{1,0},{2,3},{3,2},{4,6},{5,7},{6,4},{7,5},{8,9},{9,8},{10,11... | collective-permute-start | bytes 589832 | tf_op jit(solution)/shard_map/ppermute | solution.py:230
  29.6 0.4 %near_tile.1 = (f32[128,384]{1,0:T(8,128)S(1)}, bf16[128,384]{1,0:T(8,128)(2,1)S(1)}, bf16[128,384]{1,0:T(8,128)(2,1)S(1)}) custom-call(f32[384,384]{1,0:T(8,128)S(1)} %half_tile.1.base, bf16[384,512]{1,0:T(8,128)(2,1)S(1)} %get-tuple-element.31.left_outer, bf16[512,384]{1,0:T(8,128)(2,1)S(1)} %collective-permute-done.4.outer.outer_r), custom_call_target="tpu_custom_call" | custom-call | flops 150994944 | bytes 1769472 | tf_op jit(solution)/shard_map/near_tile/pallas_call | solution.py:29
  30.0 1.4 %collective-permute-start.10 = (bf16[128,384]{1,0:T(8,128)(2,1)S(1)}, bf16[128,384]{1,0:T(8,128)(2,1)S(1)}, u32[]{:S(2)}, u32[]{:S(2)}) collective-permute-start(bf16[128,384]{1,0:T(8,128)(2,1)S(1)} %get-tuple-element.40), channel_id=1, source_target_pairs={{0,28},{4,8},{8,4},{12,16},{16,12},{20,24},{24,20},{28,0},{1,29},{... | collective-permute-start | bytes 294920 | tf_op jit(solution)/shard_map/ppermute | solution.py:226
  31.5 0.0 collective-permute-start.11
  31.5 0.8 %add_own.1.refs_9_ = f32[5,128,512]{2,1,0:T(8,128)} custom-call(f32[128,384]{1,0:T(8,128)S(1)} %get-tuple-element.42.refs_0_, bf16[128,384]{1,0:T(8,128)(2,1)S(1)} %collective-permute-done.5.refs_1_, bf16[128,384]{1,0:T(8,128)(2,1)S(1)} %collective-permute-done.6.refs_2_), custom_call_target="tpu_custom_call" | custom-call | flops 81920 | bytes 1703936 | tf_op jit(solution)/shard_map/add_own/pallas_call | solution.py:29
  32.3 3.9 %collective-permute-done.10.refs_4_ = bf16[128,384]{1,0:T(8,128)(2,1)S(1)} collective-permute-done((bf16[128,384]{1,0:T(8,128)(2,1)S(1)}, bf16[128,384]{1,0:T(8,128)(2,1)S(1)}, u32[]{:S(2)}, u32[]{:S(2)}) %collective-permute-start.10) | collective-permute-done | bytes 98336 | tf_op jit(solution)/shard_map/ppermute | solution.py:226
  36.2 1.0 %add_rest.1 = f32[5,128,512]{2,1,0:T(8,128)} custom-call(f32[128,384]{1,0:T(8,128)S(1)} %get-tuple-element.35.refs_0_, bf16[128,768]{1,0:T(8,128)(2,1)S(1)} %collective-permute-done.7.refs_1_.refs_7_, bf16[128,768]{1,0:T(8,128)(2,1)S(1)} %collective-permute-done.8.refs_2_.refs_8_, ...), custom_call_target="tpu_custom_call", output_to_operand_aliasing={{}: (9, {})} | custom-call | flops 245760 | bytes 4194304 | tf_op jit(solution)/shard_map/add_rest/pallas_call | solution.py:29
  (12 shorter events, 0.0 us)
Async XLA Ops:
  0.0 12.3 %copy-start.1 = (s32[8,3]{0,1:T(4,128)S(1)}, s32[8,3]{0,1:T(4,128)}, u32[]{:S(2)}) copy-start(s32[8,3]{0,1:T(4,128)} %param.5) | copy-start | bytes 292
  0.0 12.3 %copy-start = (bf16[8,3,128,128]{3,2,1,0:T(8,128)(2,1)S(1)}, bf16[8,3,128,128]{3,2,1,0:T(8,128)(2,1)}, u32[]{:S(2)}) copy-start(bf16[8,3,128,128]{3,2,1,0:T(8,128)(2,1)} %stiffness.1) | copy-start | bytes 2359300
  1.9 20.6 %collective-permute-start = (bf16[1024,384]{1,0:T(8,128)(2,1)S(1)}, bf16[1024,384]{1,0:T(8,128)(2,1)S(1)}, u32[]{:S(2)}, u32[]{:S(2)}) collective-permute-start(bf16[1024,384]{1,0:T(8,128)(2,1)S(1)} %get-tuple-element.25.masked), channel_id=1, source_target_pairs={{0,1},{1,0},{2,3},{3,2},{4,6},{5,7},{6,4},{7,5},{8,9},{9,8},{10,11... | collective-permute-start | bytes 2359304 | tf_op jit(solution)/shard_map/ppermute | solution.py:230
  4.9 7.3 %collective-permute-start.1 = (bf16[256,256]{1,0:T(8,128)(2,1)S(1)}, bf16[256,256]{1,0:T(8,128)(2,1)S(1)}, u32[]{:S(2)}, u32[]{:S(2)}) collective-permute-start(bf16[256,256]{1,0:T(8,128)(2,1)S(1)} %get-tuple-element.27), channel_id=1, source_target_pairs={{0,28},{4,8},{8,4},{12,16},{16,12},{20,24},{24,20},{28,0},{1,29},{... | collective-permute-start | bytes 393224 | tf_op jit(solution)/shard_map/ppermute | solution.py:226
  7.7 4.5 %collective-permute-start.2 = (bf16[256,256]{1,0:T(8,128)(2,1)S(1)}, bf16[256,256]{1,0:T(8,128)(2,1)S(1)}, u32[]{:S(2)}, u32[]{:S(2)}) collective-permute-start(bf16[256,256]{1,0:T(8,128)(2,1)S(1)} %get-tuple-element.28), channel_id=1, source_target_pairs={{0,4},{4,0},{8,12},{12,8},{16,20},{20,16},{24,28},{28,24},{1,5},{5... | collective-permute-start | bytes 393224 | tf_op jit(solution)/shard_map/ppermute | solution.py:223
  7.7 10.6 %collective-permute-start.3 = (bf16[512,384]{1,0:T(8,128)(2,1)S(1)}, bf16[512,384]{1,0:T(8,128)(2,1)S(1)}, u32[]{:S(2)}, u32[]{:S(2)}) collective-permute-start(bf16[512,384]{1,0:T(8,128)(2,1)S(1)} %get-tuple-element.26.inner), channel_id=1, source_target_pairs={{0,2},{1,3},{2,0},{3,1},{4,5},{5,4},{6,7},{7,6},{8,10},{9,11},{10,... | collective-permute-start | bytes 1179656 | tf_op jit(solution)/shard_map/ppermute | solution.py:230
  13.4 9.1 %collective-permute-start.4 = (bf16[512,384]{1,0:T(8,128)(2,1)S(1)}, bf16[512,384]{1,0:T(8,128)(2,1)S(1)}, u32[]{:S(2)}, u32[]{:S(2)}) collective-permute-start(bf16[512,384]{1,0:T(8,128)(2,1)S(1)} %outer_image.1.outer), channel_id=1, source_target_pairs={{0,2},{1,3},{2,0},{3,1},{4,5},{5,4},{6,7},{7,6},{8,10},{9,11},{10,... | collective-permute-start | bytes 1179656 | tf_op jit(solution)/shard_map/ppermute | solution.py:230
  15.6 5.9 %collective-permute-start.5 = (bf16[128,384]{1,0:T(8,128)(2,1)S(1)}, bf16[128,384]{1,0:T(8,128)(2,1)S(1)}, u32[]{:S(2)}, u32[]{:S(2)}) collective-permute-start(bf16[128,384]{1,0:T(8,128)(2,1)S(1)} %get-tuple-element.32), channel_id=1, source_target_pairs={{0,28},{4,8},{8,4},{12,16},{16,12},{20,24},{24,20},{28,0},{1,29},{... | collective-permute-start | bytes 294920 | tf_op jit(solution)/shard_map/ppermute | solution.py:226
  17.0 4.5 %collective-permute-start.6 = (bf16[128,384]{1,0:T(8,128)(2,1)S(1)}, bf16[128,384]{1,0:T(8,128)(2,1)S(1)}, u32[]{:S(2)}, u32[]{:S(2)}) collective-permute-start(bf16[128,384]{1,0:T(8,128)(2,1)S(1)} %get-tuple-element.33), channel_id=1, source_target_pairs={{0,4},{4,0},{8,12},{12,8},{16,20},{20,16},{24,28},{28,24},{1,5},{5... | collective-permute-start | bytes 294920 | tf_op jit(solution)/shard_map/ppermute | solution.py:223
  23.7 12.5 %collective-permute-start.7 = (bf16[128,768]{1,0:T(8,128)(2,1)S(1)}, bf16[128,768]{1,0:T(8,128)(2,1)S(1)}, u32[]{:S(2)}, u32[]{:S(2)}) collective-permute-start(bf16[128,768]{1,0:T(8,128)(2,1)S(1)} %get-tuple-element.37), channel_id=1, source_target_pairs={{0,29},{1,28},{2,31},{3,30},{4,10},{5,11},{6,8},{7,9},{8,5},{9,4},... | collective-permute-start | bytes 589832 | tf_op jit(solution)/shard_map/ppermute | solution.py:230
  29.1 7.1 %collective-permute-start.8 = (bf16[128,768]{1,0:T(8,128)(2,1)S(1)}, bf16[128,768]{1,0:T(8,128)(2,1)S(1)}, u32[]{:S(2)}, u32[]{:S(2)}) collective-permute-start(bf16[128,768]{1,0:T(8,128)(2,1)S(1)} %get-tuple-element.38), channel_id=1, source_target_pairs={{0,5},{1,4},{2,7},{3,6},{4,2},{5,3},{6,0},{7,1},{8,13},{9,12},{10,... | collective-permute-start | bytes 589832 | tf_op jit(solution)/shard_map/ppermute | solution.py:230
  29.1 7.1 %collective-permute-start.9 = (bf16[128,768]{1,0:T(8,128)(2,1)S(1)}, bf16[128,768]{1,0:T(8,128)(2,1)S(1)}, u32[]{:S(2)}, u32[]{:S(2)}) collective-permute-start(bf16[128,768]{1,0:T(8,128)(2,1)S(1)} %get-tuple-element.39), channel_id=1, source_target_pairs={{0,1},{1,0},{2,3},{3,2},{4,6},{5,7},{6,4},{7,5},{8,9},{9,8},{10,11... | collective-permute-start | bytes 589832 | tf_op jit(solution)/shard_map/ppermute | solution.py:230
  30.0 6.1 %collective-permute-start.10 = (bf16[128,384]{1,0:T(8,128)(2,1)S(1)}, bf16[128,384]{1,0:T(8,128)(2,1)S(1)}, u32[]{:S(2)}, u32[]{:S(2)}) collective-permute-start(bf16[128,384]{1,0:T(8,128)(2,1)S(1)} %get-tuple-element.40), channel_id=1, source_target_pairs={{0,28},{4,8},{8,4},{12,16},{16,12},{20,24},{24,20},{28,0},{1,29},{... | collective-permute-start | bytes 294920 | tf_op jit(solution)/shard_map/ppermute | solution.py:226
  31.5 4.7 %collective-permute-start.11 = (bf16[128,384]{1,0:T(8,128)(2,1)S(1)}, bf16[128,384]{1,0:T(8,128)(2,1)S(1)}, u32[]{:S(2)}, u32[]{:S(2)}) collective-permute-start(bf16[128,384]{1,0:T(8,128)(2,1)S(1)} %get-tuple-element.41), channel_id=1, source_target_pairs={{0,4},{4,0},{8,12},{12,8},{16,20},{20,16},{24,28},{28,24},{1,5},{5... | collective-permute-start | bytes 294920 | tf_op jit(solution)/shard_map/ppermute | solution.py:223

commit v10 on v8

--- a/solution.py
+++ b/solution.py
@@ -53,13 +53,28 @@
     ]
 
 
+def reaches(reach):
+    slabs = reach.shape[0]
+    slab = lax.axis_index("blk")
+    low = reach[pl.ds(lax.rem(slab + slabs - 1, slabs), 1), 1, :]
+    high = reach[pl.ds(lax.rem(slab + 1, slabs), 1), 0, :]
+    return low, high
+
+
+def mask_block(basis, b, blocks, size, low, high, masked):
+    groups, _, width = basis.shape
+    rows = slice(b * size, (b + 1) * size)
+    keep = {0: (b < low).astype(F32).astype(BF16), 2: (b >= blocks - high).astype(F32).astype(BF16)}
+    for g in range(groups):
+        value = basis[g, rows, :]
+        masked[rows, g * width : (g + 1) * width] = value * keep[g] if g in keep else value
+
+
 def mask_and_inner(
     total_blocks, cols_hbm, basis_hbm, reach_hbm, stiffness_hbm, masked, to_link, to_chip, inner, cols, basis, reach, stiffness, sem
 ):
     blocks, slots, size, _ = stiffness.shape
-    groups, _, width = basis.shape
-    slabs = reach.shape[0]
-    slab = lax.axis_index("blk")
+    width = basis.shape[2]
     inner_blocks = pl.ds(RIM, blocks - 2 * RIM)
     moves = [(reach_hbm, reach), (cols_hbm, cols)]
     moves += [
@@ -71,16 +86,11 @@
     for copy in copies:
         copy.start()
     copies[0].wait()
-    low = reach[pl.ds(lax.rem(slab + slabs - 1, slabs), 1), 1, :]
-    high = reach[pl.ds(lax.rem(slab + 1, slabs), 1), 0, :]
+    low, high = reaches(reach)
     for b in range(blocks):
         if b % RIM == 0:
             copies[2 + b // RIM].wait()
-        rows = slice(b * size, (b + 1) * size)
-        keep = {0: (b < low).astype(F32).astype(BF16), 2: (b >= blocks - high).astype(F32).astype(BF16)}
-        for g in range(groups):
-            value = basis[g, rows, :]
-            masked[rows, g * width : (g + 1) * width] = value * keep[g] if g in keep else value
+        mask_block(basis, b, blocks, size, low, high, masked)
     odd = parity()
 
     @pl.when(odd == 0)
@@ -159,7 +169,13 @@
     store_tile(dot(left_inner[...], inner[...]) + dot(left_outer[...], outer[...]), own, link, chip)
 
 
-def partner_tile(size, masked, inner, outer, near_left, inner_r, own, link, chip, far_outer, far, near, far_inner):
+def partner_tile(
+    size, basis, reach, inner, outer, near_left, inner_r, own, link, chip, far_outer, far, near, masked, far_inner
+):
+    low, high = reaches(reach)
+    blocks = basis.shape[1] // size
+    for b in range(blocks):
+        mask_block(basis, b, blocks, size, low, high, masked)
     turn(size, masked, far_inner, far_outer)
     store_tile(dot(far_inner[...], inner[...]) + dot(far_outer[...], outer[...]), own, link, chip)
     far[...] = dot(far_inner[...], inner_r[...])
@@ -239,6 +255,8 @@
         chip = to(chip, lambda i: i ^ 1, partner)
         return own, link, chip
 
+    basis_p = to_partner(basis).transpose(1, 0, 2)
+    reach_p = to_partner(patch_reach).transpose(0, 2, 1)
     cols = block_cols.T
     flat = basis.transpose(1, 0, 2)
     reach = patch_reach.transpose(0, 2, 1)
@@ -261,7 +279,6 @@
         flops=row_flops * (blocks - 2 * RIM),
         name="mask_and_inner",
     )
-    masked_p = to_partner(masked)
     inner_r = to_side(inner)
     rim_link = over_link(rim_link)
     rim_chip = over_chip(rim_chip)
@@ -293,10 +310,10 @@
     part, part_link, part_chip, far_outer, far_base, near_base = call(
         functools.partial(partner_tile, size),
         (*tile_shapes(width, wide, BF16), left_shapes[1], base_shape, base_shape),
-        [VMEM] * 5,
         [VMEM] * 6,
-        (masked_p, inner, outer, left_inner, inner_r),
-        scratch=[pltpu.VMEM((wide, inner_rows), BF16)],
+        [VMEM] * 6,
+        (basis_p, reach_p, inner, outer, left_inner, inner_r),
+        scratch=[pltpu.VMEM((rows, wide), BF16), pltpu.VMEM((wide, inner_rows), BF16)],
         flops=2 * tile_flops,
         name="partner_tile",
     )

time: 39.4 us -> 39.1 us (level)
  starting transfers between devices: 23.2 us -> 17.4 us
  waiting for transfers between devices: 8.22 us -> 13.9 us
    ppermute x9 -> x10, starting transfers between devices: 16 us -> 12.2 us  [to(): return lax.ppermute(value, ('blk', 'col'), perm)]
    ppermute x9 -> x10, waiting for transfers between devices: 4.02 us -> 6.92 us  [to(): return lax.ppermute(value, ('blk', 'col'), perm)]
    ppermute x3, waiting for transfers between devices: 4.19 us -> 7.01 us  [over_link(): return lax.ppermute(value, 'blk', cross)]
    ppermute x3, starting transfers between devices: 7.19 us -> 5.23 us  [over_link(): return lax.ppermute(value, 'blk', cross)]
  transfers between devices with their start and end apart: 15 -> 16, of which waited for: 5 -> 6; matrix products, arithmetic and copies ran while one was open for 0% -> 0% of each run, Pallas kernels for 12% -> 16%
where the time goes in v10:
time: 39.1 us; the launch traced here: 39 us
  starting transfers between devices  17.4 us (45%)
  waiting for transfers between devices  13.9 us (36%)
  Pallas kernels  7.44 us (19%)
    ppermute x10, starting transfers between devices, to(): return lax.ppermute(value, ('blk', 'col'), perm)  12.2 us
    pallas_call x8, Pallas kernels, call(): pl.pallas_call(kernel, out_shape=out_shape, in_specs=in_specs, out_specs=...  7.44 us
    ppermute x3, waiting for transfers between devices, over_link(): return lax.ppermute(value, 'blk', cross)  7.01 us
    ppermute x10, waiting for transfers between devices, to(): return lax.ppermute(value, ('blk', 'col'), perm)  6.92 us
    ppermute x3, starting transfers between devices, over_link(): return lax.ppermute(value, 'blk', cross)  5.23 us
  transfers between devices with their start and end apart: 16, of which 6 were waited for; matrix products, arithmetic and copies ran while one was open for 0% of the time, Pallas kernels for 16%

profile of v10, /device:TPU:0, one launch (start us, length us, event | category | flops | bytes accessed | tf_op | source)
XLA Modules:
  0.0 39.0 jit_solution(7669116061507743002)
XLA Ops:
  0.0 2.9 %collective-permute-start = (bf16[1024,3,128]{2,0,1:T(8,128)(2,1)}, bf16[1024,3,128]{2,0,1:T(8,128)(2,1)S(1)}, u32[]{:S(2)}, u32[]{:S(2)}) collective-permute-start(bf16[1024,3,128]{2,0,1:T(8,128)(2,1)} %param.6), channel_id=1, source_target_pairs={{0,1},{1,0},{2,3},{3,2},{4,6},{5,7},{6,4},{7,5},{8,9},{9,8},{10,11... | collective-permute-start | bytes 2359304 | tf_op jit(solution)/shard_map/ppermute | solution.py:238
  2.9 1.8 %mask_and_inner.1 = (bf16[1024,384]{1,0:T(8,128)(2,1)S(1)}, bf16[256,256]{1,0:T(8,128)(2,1)S(1)}, bf16[256,256]{1,0:T(8,128)(2,1)S(1)}, bf16[512,384]{1,0:T(8,128)(2,1)S(1)}) custom-call(s32[3,8]{1,0:T(4,128)} %bitcast.8, bf16[3,1024,128]{2,1,0:T(8,128)(2,1)} %bitcast.10, s32[8,2,128]{2,1,0:T(2,128)} %bitcast.11, bf16[8,3,128,128]{3,2,1,0:T(8,128)(2,1)} %stiffness.1), custom_call_target="tpu_custom_call" | custom-call | flops 150994944 | bytes 3022944 | tf_op jit(solution)/shard_map/mask_and_inner/pallas_call | solution.py:29
  4.8 2.9 %collective-permute-start.2 = (bf16[256,256]{1,0:T(8,128)(2,1)S(1)}, bf16[256,256]{1,0:T(8,128)(2,1)S(1)}, u32[]{:S(2)}, u32[]{:S(2)}) collective-permute-start(bf16[256,256]{1,0:T(8,128)(2,1)S(1)} %get-tuple-element.35), channel_id=1, source_target_pairs={{0,28},{4,8},{8,4},{12,16},{16,12},{20,24},{24,20},{28,0},{1,29},{... | collective-permute-start | bytes 393224 | tf_op jit(solution)/shard_map/ppermute | solution.py:234
  7.6 0.5 %collective-permute-start.4 = (bf16[512,384]{1,0:T(8,128)(2,1)S(1)}, bf16[512,384]{1,0:T(8,128)(2,1)S(1)}, u32[]{:S(2)}, u32[]{:S(2)}) collective-permute-start(bf16[512,384]{1,0:T(8,128)(2,1)S(1)} %get-tuple-element.33.inner), channel_id=1, source_target_pairs={{0,2},{1,3},{2,0},{3,1},{4,5},{5,4},{6,7},{7,6},{8,10},{9,11},{10,... | collective-permute-start | bytes 1179656 | tf_op jit(solution)/shard_map/ppermute | solution.py:238
  8.2 4.0 %collective-permute-done.2.from_link = bf16[256,256]{1,0:T(8,128)(2,1)S(1)} collective-permute-done((bf16[256,256]{1,0:T(8,128)(2,1)S(1)}, bf16[256,256]{1,0:T(8,128)(2,1)S(1)}, u32[]{:S(2)}, u32[]{:S(2)}) %collective-permute-start.2) | collective-permute-done | bytes 131104 | tf_op jit(solution)/shard_map/ppermute | solution.py:234
  12.2 1.1 %outer_image.1.outer = bf16[512,384]{1,0:T(8,128)(2,1)S(1)} custom-call(s32[3,8]{1,0:T(4,128)S(1)} %bitcast.9, bf16[8,3,128,128]{3,2,1,0:T(8,128)(2,1)S(1)} %copy-done, bf16[1024,384]{1,0:T(8,128)(2,1)S(1)} %get-tuple-element.34.masked, bf16[256,256]{1,0:T(8,128)(2,1)S(1)} %collective-permute-done.2.from_link, ...), custom_call_target="tpu_custom_call" | custom-call | flops 150994944 | bytes 2228320 | tf_op jit(solution)/shard_map/outer_image/pallas_call | solution.py:29
  13.3 1.6 %collective-permute-start.8 = (bf16[512,384]{1,0:T(8,128)(2,1)S(1)}, bf16[512,384]{1,0:T(8,128)(2,1)S(1)}, u32[]{:S(2)}, u32[]{:S(2)}) collective-permute-start(bf16[512,384]{1,0:T(8,128)(2,1)S(1)} %outer_image.1.outer), channel_id=1, source_target_pairs={{0,2},{1,3},{2,0},{3,1},{4,5},{5,4},{6,7},{7,6},{8,10},{9,11},{10,... | collective-permute-start | bytes 1179656 | tf_op jit(solution)/shard_map/ppermute | solution.py:238
  14.9 0.6 %own_tile.1 = (f32[128,384]{1,0:T(8,128)S(1)}, bf16[128,384]{1,0:T(8,128)(2,1)S(1)}, bf16[128,384]{1,0:T(8,128)(2,1)S(1)}, bf16[384,512]{1,0:T(8,128)(2,1)S(1)}, bf16[384,512]{1,0:T(8,128)(2,1)S(1)}) custom-call(bf16[1024,384]{1,0:T(8,128)(2,1)S(1)} %get-tuple-element.34.masked, bf16[512,384]{1,0:T(8,128)(2,1)S(1)} %get-tuple-element.33.inner, ...), custom_call_target="tpu_custom_call" | custom-call | flops 301989888 | bytes 2752512 | tf_op jit(solution)/shard_map/own_tile/pallas_call | solution.py:29
  15.5 1.4 %collective-permute-start.9 = (bf16[128,384]{1,0:T(8,128)(2,1)S(1)}, bf16[128,384]{1,0:T(8,128)(2,1)S(1)}, u32[]{:S(2)}, u32[]{:S(2)}) collective-permute-start(bf16[128,384]{1,0:T(8,128)(2,1)S(1)} %get-tuple-element.44), channel_id=1, source_target_pairs={{0,28},{4,8},{8,4},{12,16},{16,12},{20,24},{24,20},{28,0},{1,29},{... | collective-permute-start | bytes 294920 | tf_op jit(solution)/shard_map/ppermute | solution.py:234
  16.9 0.5 %collective-permute-start.1 = (s32[8,128,2]{1,2,0:T(2,128)S(1)}, s32[8,128,2]{1,2,0:T(2,128)S(1)}, u32[]{:S(2)}, u32[]{:S(2)}) collective-permute-start(s32[8,128,2]{1,2,0:T(2,128)S(1)} %copy-done.2), channel_id=1, source_target_pairs={{0,1},{1,0},{2,3},{3,2},{4,6},{5,7},{6,4},{7,5},{8,9},{9,8},{10,11... | collective-permute-start | bytes 24584 | tf_op jit(solution)/shard_map/ppermute | solution.py:238
  17.5 3.3 %collective-permute-done.1 = s32[8,128,2]{1,2,0:T(2,128)S(1)} collective-permute-done((s32[8,128,2]{1,2,0:T(2,128)S(1)}, s32[8,128,2]{1,2,0:T(2,128)S(1)}, u32[]{:S(2)}, u32[]{:S(2)}) %collective-permute-start.1) | collective-permute-done | bytes 8224 | tf_op jit(solution)/shard_map/ppermute | solution.py:238
  20.8 1.3 %partner_tile.1 = (bf16[128,384]{1,0:T(8,128)(2,1)S(1)}, bf16[128,384]{1,0:T(8,128)(2,1)S(1)}, bf16[128,384]{1,0:T(8,128)(2,1)S(1)}, bf16[384,512]{1,0:T(8,128)(...) custom-call(bf16[3,1024,128]{2,1,0:T(8,128)(2,1)S(1)} %bitcast.6, s32[8,2,128]{2,1,0:T(2,128)S(1)} %bitcast.7, ...), custom_call_target="tpu_custom_call" | custom-call | flops 603979776 | bytes 4235264 | tf_op jit(solution)/shard_map/partner_tile/pallas_call | solution.py:29
  22.0 0.6 %collective-permute-start.5 = (bf16[128,384]{1,0:T(8,128)(2,1)S(1)}, bf16[128,384]{1,0:T(8,128)(2,1)S(1)}, u32[]{:S(2)}, u32[]{:S(2)}) collective-permute-start(bf16[128,384]{1,0:T(8,128)(2,1)S(1)} %get-tuple-element.39), channel_id=1, source_target_pairs={{0,1},{1,0},{2,3},{3,2},{4,6},{5,7},{6,4},{7,5},{8,9},{9,8},{10,11... | collective-permute-start | bytes 294920 | tf_op jit(solution)/shard_map/ppermute | solution.py:238
  22.6 4.9 %collective-permute-start.6 = (bf16[128,384]{1,0:T(8,128)(2,1)S(1)}, bf16[128,384]{1,0:T(8,128)(2,1)S(1)}, u32[]{:S(2)}, u32[]{:S(2)}) collective-permute-start(bf16[128,384]{1,0:T(8,128)(2,1)S(1)} %get-tuple-element.40), channel_id=1, source_target_pairs={{0,29},{1,28},{2,31},{3,30},{4,10},{5,11},{6,8},{7,9},{8,5},{9,4},... | collective-permute-start | bytes 294920 | tf_op jit(solution)/shard_map/ppermute | solution.py:238
  27.6 0.4 %far_tile.1 = (bf16[128,384]{1,0:T(8,128)(2,1)S(1)}, bf16[128,384]{1,0:T(8,128)(2,1)S(1)}, bf16[128,384]{1,0:T(8,128)(2,1)S(1)}) custom-call(f32[384,384]{1,0:T(8,128)S(1)} %get-tuple-element.53.base, bf16[384,512]{1,0:T(8,128)(2,1)S(1)} %get-tuple-element.54.left_outer, bf16[512,384]{1,0:T(8,128)(2,1)S(1)} %collective-permute-done.8.outer), custom_call_target="tpu_custom_call" | custom-call | flops 150994944 | bytes 1671168 | tf_op jit(solution)/shard_map/far_tile/pallas_call | solution.py:29
  28.1 0.7 %collective-permute-start.14 = (bf16[128,384]{1,0:T(8,128)(2,1)S(1)}, bf16[128,384]{1,0:T(8,128)(2,1)S(1)}, u32[]{:S(2)}, u32[]{:S(2)}) collective-permute-start(bf16[128,384]{1,0:T(8,128)(2,1)S(1)} %get-tuple-element.56), channel_id=1, source_target_pairs={{0,29},{1,28},{2,31},{3,30},{4,10},{5,11},{6,8},{7,9},{8,5},{9,4},... | collective-permute-start | bytes 294920 | tf_op jit(solution)/shard_map/ppermute | solution.py:238
  29.1 0.7 %collective-permute-done.6.refs_1_ = bf16[128,384]{1,0:T(8,128)(2,1)S(1)} collective-permute-done((bf16[128,384]{1,0:T(8,128)(2,1)S(1)}, bf16[128,384]{1,0:T(8,128)(2,1)S(1)}, u32[]{:S(2)}, u32[]{:S(2)}) %collective-permute-start.6) | collective-permute-done | bytes 98336 | tf_op jit(solution)/shard_map/ppermute | solution.py:238
  29.8 1.8 %collective-permute-done.7.refs_2_ = bf16[128,384]{1,0:T(8,128)(2,1)S(1)} collective-permute-done((bf16[128,384]{1,0:T(8,128)(2,1)S(1)}, bf16[128,384]{1,0:T(8,128)(2,1)S(1)}, u32[]{:S(2)}, u32[]{:S(2)}) %collective-permute-start.7) | collective-permute-done | bytes 98336 | tf_op jit(solution)/shard_map/ppermute | solution.py:238
  31.6 0.4 %near_tile.1 = (f32[128,384]{1,0:T(8,128)S(1)}, bf16[128,384]{1,0:T(8,128)(2,1)S(1)}, bf16[128,384]{1,0:T(8,128)(2,1)S(1)}) custom-call(f32[384,384]{1,0:T(8,128)S(1)} %get-tuple-element.42.base, bf16[384,512]{1,0:T(8,128)(2,1)S(1)} %get-tuple-element.43.left_outer, bf16[512,384]{1,0:T(8,128)(2,1)S(1)} %collective-permute-done.8.outer), custom_call_target="tpu_custom_call" | custom-call | flops 150994944 | bytes 1769472 | tf_op jit(solution)/shard_map/near_tile/pallas_call | solution.py:29
  32.0 1.0 %collective-permute-start.11 = (bf16[128,384]{1,0:T(8,128)(2,1)S(1)}, bf16[128,384]{1,0:T(8,128)(2,1)S(1)}, u32[]{:S(2)}, u32[]{:S(2)}) collective-permute-start(bf16[128,384]{1,0:T(8,128)(2,1)S(1)} %get-tuple-element.51), channel_id=1, source_target_pairs={{0,28},{4,8},{8,4},{12,16},{16,12},{20,24},{24,20},{28,0},{1,29},{... | collective-permute-start | bytes 294920 | tf_op jit(solution)/shard_map/ppermute | solution.py:234
  33.0 0.8 %add_own.1.refs_9_ = f32[5,128,512]{2,1,0:T(8,128)} custom-call(f32[128,384]{1,0:T(8,128)S(1)} %get-tuple-element.58.refs_0_, bf16[128,384]{1,0:T(8,128)(2,1)S(1)} %collective-permute-done.9.refs_1_, bf16[128,384]{1,0:T(8,128)(2,1)S(1)} %collective-permute-done.10.refs_2_), custom_call_target="tpu_custom_call" | custom-call | flops 81920 | bytes 1703936 | tf_op jit(solution)/shard_map/add_own/pallas_call | solution.py:29
  33.8 1.1 %collective-permute-done.14.refs_7_ = bf16[128,384]{1,0:T(8,128)(2,1)S(1)} collective-permute-done((bf16[128,384]{1,0:T(8,128)(2,1)S(1)}, bf16[128,384]{1,0:T(8,128)(2,1)S(1)}, u32[]{:S(2)}, u32[]{:S(2)}) %collective-permute-start.14) | collective-permute-done | bytes 98336 | tf_op jit(solution)/shard_map/ppermute | solution.py:238
  34.9 3.0 %collective-permute-done.11.refs_4_ = bf16[128,384]{1,0:T(8,128)(2,1)S(1)} collective-permute-done((bf16[128,384]{1,0:T(8,128)(2,1)S(1)}, bf16[128,384]{1,0:T(8,128)(2,1)S(1)}, u32[]{:S(2)}, u32[]{:S(2)}) %collective-permute-start.11) | collective-permute-done | bytes 98336 | tf_op jit(solution)/shard_map/ppermute | solution.py:234
  37.9 1.0 %add_rest.1 = f32[5,128,512]{2,1,0:T(8,128)} custom-call(f32[128,384]{1,0:T(8,128)S(1)} %get-tuple-element.47.refs_0_, bf16[128,384]{1,0:T(8,128)(2,1)S(1)} %collective-permute-done.6.refs_1_, bf16[128,384]{1,0:T(8,128)(2,1)S(1)} %collective-permute-done.7.refs_2_, ...), custom_call_target="tpu_custom_call", output_to_operand_aliasing={{}: (9, {})} | custom-call | flops 245760 | bytes 3604480 | tf_op jit(solution)/shard_map/add_rest/pallas_call | solution.py:29
  (22 shorter events, 0.4 us)
Async XLA Ops:
  0.0 12.2 %copy-start.1 = (s32[8,3]{0,1:T(4,128)S(1)}, s32[8,3]{0,1:T(4,128)}, u32[]{:S(2)}) copy-start(s32[8,3]{0,1:T(4,128)} %param.5) | copy-start | bytes 292
  0.0 12.2 %copy-start = (bf16[8,3,128,128]{3,2,1,0:T(8,128)(2,1)S(1)}, bf16[8,3,128,128]{3,2,1,0:T(8,128)(2,1)}, u32[]{:S(2)}) copy-start(bf16[8,3,128,128]{3,2,1,0:T(8,128)(2,1)} %stiffness.1) | copy-start | bytes 2359300
  0.0 20.8 %collective-permute-start = (bf16[1024,3,128]{2,0,1:T(8,128)(2,1)}, bf16[1024,3,128]{2,0,1:T(8,128)(2,1)S(1)}, u32[]{:S(2)}, u32[]{:S(2)}) collective-permute-start(bf16[1024,3,128]{2,0,1:T(8,128)(2,1)} %param.6), channel_id=1, source_target_pairs={{0,1},{1,0},{2,3},{3,2},{4,6},{5,7},{6,4},{7,5},{8,9},{9,8},{10,11... | collective-permute-start | bytes 2359304 | tf_op jit(solution)/shard_map/ppermute | solution.py:238
  4.8 7.4 %collective-permute-start.2 = (bf16[256,256]{1,0:T(8,128)(2,1)S(1)}, bf16[256,256]{1,0:T(8,128)(2,1)S(1)}, u32[]{:S(2)}, u32[]{:S(2)}) collective-permute-start(bf16[256,256]{1,0:T(8,128)(2,1)S(1)} %get-tuple-element.35), channel_id=1, source_target_pairs={{0,28},{4,8},{8,4},{12,16},{16,12},{20,24},{24,20},{28,0},{1,29},{... | collective-permute-start | bytes 393224 | tf_op jit(solution)/shard_map/ppermute | solution.py:234
  7.6 4.5 %collective-permute-start.3 = (bf16[256,256]{1,0:T(8,128)(2,1)S(1)}, bf16[256,256]{1,0:T(8,128)(2,1)S(1)}, u32[]{:S(2)}, u32[]{:S(2)}) collective-permute-start(bf16[256,256]{1,0:T(8,128)(2,1)S(1)} %get-tuple-element.36), channel_id=1, source_target_pairs={{0,4},{4,0},{8,12},{12,8},{16,20},{20,16},{24,28},{28,24},{1,5},{5... | collective-permute-start | bytes 393224 | tf_op jit(solution)/shard_map/ppermute | solution.py:231
  7.6 13.1 %collective-permute-start.4 = (bf16[512,384]{1,0:T(8,128)(2,1)S(1)}, bf16[512,384]{1,0:T(8,128)(2,1)S(1)}, u32[]{:S(2)}, u32[]{:S(2)}) collective-permute-start(bf16[512,384]{1,0:T(8,128)(2,1)S(1)} %get-tuple-element.33.inner), channel_id=1, source_target_pairs={{0,2},{1,3},{2,0},{3,1},{4,5},{5,4},{6,7},{7,6},{8,10},{9,11},{10,... | collective-permute-start | bytes 1179656 | tf_op jit(solution)/shard_map/ppermute | solution.py:238
  13.3 3.6 %copy-start.2 = (s32[8,128,2]{1,2,0:T(2,128)S(1)}, s32[8,128,2]{1,2,0:T(2,128)}, u32[]{:S(2)}) copy-start(s32[8,128,2]{1,2,0:T(2,128)} %param.7) | copy-start | bytes 24580
  13.3 14.3 %collective-permute-start.8 = (bf16[512,384]{1,0:T(8,128)(2,1)S(1)}, bf16[512,384]{1,0:T(8,128)(2,1)S(1)}, u32[]{:S(2)}, u32[]{:S(2)}) collective-permute-start(bf16[512,384]{1,0:T(8,128)(2,1)S(1)} %outer_image.1.outer), channel_id=1, source_target_pairs={{0,2},{1,3},{2,0},{3,1},{4,5},{5,4},{6,7},{7,6},{8,10},{9,11},{10,... | collective-permute-start | bytes 1179656 | tf_op jit(solution)/shard_map/ppermute | solution.py:238
  15.5 12.0 %collective-permute-start.9 = (bf16[128,384]{1,0:T(8,128)(2,1)S(1)}, bf16[128,384]{1,0:T(8,128)(2,1)S(1)}, u32[]{:S(2)}, u32[]{:S(2)}) collective-permute-start(bf16[128,384]{1,0:T(8,128)(2,1)S(1)} %get-tuple-element.44), channel_id=1, source_target_pairs={{0,28},{4,8},{8,4},{12,16},{16,12},{20,24},{24,20},{28,0},{1,29},{... | collective-permute-start | bytes 294920 | tf_op jit(solution)/shard_map/ppermute | solution.py:234
  16.9 3.8 %collective-permute-start.1 = (s32[8,128,2]{1,2,0:T(2,128)S(1)}, s32[8,128,2]{1,2,0:T(2,128)S(1)}, u32[]{:S(2)}, u32[]{:S(2)}) collective-permute-start(s32[8,128,2]{1,2,0:T(2,128)S(1)} %copy-done.2), channel_id=1, source_target_pairs={{0,1},{1,0},{2,3},{3,2},{4,6},{5,7},{6,4},{7,5},{8,9},{9,8},{10,11... | collective-permute-start | bytes 24584 | tf_op jit(solution)/shard_map/ppermute | solution.py:238
  20.8 6.8 %collective-permute-start.10 = (bf16[128,384]{1,0:T(8,128)(2,1)S(1)}, bf16[128,384]{1,0:T(8,128)(2,1)S(1)}, u32[]{:S(2)}, u32[]{:S(2)}) collective-permute-start(bf16[128,384]{1,0:T(8,128)(2,1)S(1)} %get-tuple-element.45), channel_id=1, source_target_pairs={{0,4},{4,0},{8,12},{12,8},{16,20},{20,16},{24,28},{28,24},{1,5},{5... | collective-permute-start | bytes 294920 | tf_op jit(solution)/shard_map/ppermute | solution.py:231
  22.0 6.7 %collective-permute-start.5 = (bf16[128,384]{1,0:T(8,128)(2,1)S(1)}, bf16[128,384]{1,0:T(8,128)(2,1)S(1)}, u32[]{:S(2)}, u32[]{:S(2)}) collective-permute-start(bf16[128,384]{1,0:T(8,128)(2,1)S(1)} %get-tuple-element.39), channel_id=1, source_target_pairs={{0,1},{1,0},{2,3},{3,2},{4,6},{5,7},{6,4},{7,5},{8,9},{9,8},{10,11... | collective-permute-start | bytes 294920 | tf_op jit(solution)/shard_map/ppermute | solution.py:238
  22.6 7.1 %collective-permute-start.6 = (bf16[128,384]{1,0:T(8,128)(2,1)S(1)}, bf16[128,384]{1,0:T(8,128)(2,1)S(1)}, u32[]{:S(2)}, u32[]{:S(2)}) collective-permute-start(bf16[128,384]{1,0:T(8,128)(2,1)S(1)} %get-tuple-element.40), channel_id=1, source_target_pairs={{0,29},{1,28},{2,31},{3,30},{4,10},{5,11},{6,8},{7,9},{8,5},{9,4},... | collective-permute-start | bytes 294920 | tf_op jit(solution)/shard_map/ppermute | solution.py:238
  27.6 4.0 %collective-permute-start.7 = (bf16[128,384]{1,0:T(8,128)(2,1)S(1)}, bf16[128,384]{1,0:T(8,128)(2,1)S(1)}, u32[]{:S(2)}, u32[]{:S(2)}) collective-permute-start(bf16[128,384]{1,0:T(8,128)(2,1)S(1)} %get-tuple-element.41), channel_id=1, source_target_pairs={{0,5},{1,4},{2,7},{3,6},{4,2},{5,3},{6,0},{7,1},{8,13},{9,12},{10,... | collective-permute-start | bytes 294920 | tf_op jit(solution)/shard_map/ppermute | solution.py:238
  28.0 5.8 %collective-permute-start.13 = (bf16[128,384]{1,0:T(8,128)(2,1)S(1)}, bf16[128,384]{1,0:T(8,128)(2,1)S(1)}, u32[]{:S(2)}, u32[]{:S(2)}) collective-permute-start(bf16[128,384]{1,0:T(8,128)(2,1)S(1)} %get-tuple-element.55), channel_id=1, source_target_pairs={{0,1},{1,0},{2,3},{3,2},{4,6},{5,7},{6,4},{7,5},{8,9},{9,8},{10,11... | collective-permute-start | bytes 294920 | tf_op jit(solution)/shard_map/ppermute | solution.py:238
  28.1 6.8 %collective-permute-start.14 = (bf16[128,384]{1,0:T(8,128)(2,1)S(1)}, bf16[128,384]{1,0:T(8,128)(2,1)S(1)}, u32[]{:S(2)}, u32[]{:S(2)}) collective-permute-start(bf16[128,384]{1,0:T(8,128)(2,1)S(1)} %get-tuple-element.56), channel_id=1, source_target_pairs={{0,29},{1,28},{2,31},{3,30},{4,10},{5,11},{6,8},{7,9},{8,5},{9,4},... | collective-permute-start | bytes 294920 | tf_op jit(solution)/shard_map/ppermute | solution.py:238
  28.8 6.1 %collective-permute-start.15 = (bf16[128,384]{1,0:T(8,128)(2,1)S(1)}, bf16[128,384]{1,0:T(8,128)(2,1)S(1)}, u32[]{:S(2)}, u32[]{:S(2)}) collective-permute-start(bf16[128,384]{1,0:T(8,128)(2,1)S(1)} %get-tuple-element.57), channel_id=1, source_target_pairs={{0,5},{1,4},{2,7},{3,6},{4,2},{5,3},{6,0},{7,1},{8,13},{9,12},{10,... | collective-permute-start | bytes 294920 | tf_op jit(solution)/shard_map/ppermute | solution.py:238
  32.0 5.9 %collective-permute-start.11 = (bf16[128,384]{1,0:T(8,128)(2,1)S(1)}, bf16[128,384]{1,0:T(8,128)(2,1)S(1)}, u32[]{:S(2)}, u32[]{:S(2)}) collective-permute-start(bf16[128,384]{1,0:T(8,128)(2,1)S(1)} %get-tuple-element.51), channel_id=1, source_target_pairs={{0,28},{4,8},{8,4},{12,16},{16,12},{20,24},{24,20},{28,0},{1,29},{... | collective-permute-start | bytes 294920 | tf_op jit(solution)/shard_map/ppermute | solution.py:234
  33.0 4.9 %collective-permute-start.12 = (bf16[128,384]{1,0:T(8,128)(2,1)S(1)}, bf16[128,384]{1,0:T(8,128)(2,1)S(1)}, u32[]{:S(2)}, u32[]{:S(2)}) collective-permute-start(bf16[128,384]{1,0:T(8,128)(2,1)S(1)} %get-tuple-element.52), channel_id=1, source_target_pairs={{0,4},{4,0},{8,12},{12,8},{16,20},{20,16},{24,28},{28,24},{1,5},{5... | collective-permute-start | bytes 294920 | tf_op jit(solution)/shard_map/ppermute | solution.py:231

commit v11 on v10

--- a/solution.py
+++ b/solution.py
@@ -282,6 +282,7 @@
     inner_r = to_side(inner)
     rim_link = over_link(rim_link)
     rim_chip = over_chip(rim_chip)
+    rim_link, rim_chip, reach_p = lax.optimization_barrier((rim_link, rim_chip, reach_p))
     outer = call(
         functools.partial(outer_image, total_blocks),
         shape((2 * rim, wide), BF16),

time: 39.1 us -> 41.2 us (1.054)
  starting transfers between devices: 17.4 us -> 24.1 us
  waiting for transfers between devices: 13.9 us -> 9.4 us
    ppermute x3, waiting for transfers between devices: 7.01 us -> 2.32 us  [over_link(): return lax.ppermute(value, 'blk', cross)]
    ppermute x10, starting transfers between devices: 12.2 us -> 16.2 us  [to(): return lax.ppermute(value, ('blk', 'col'), perm)]
    ppermute x3, starting transfers between devices: 5.23 us -> 7.94 us  [over_link(): return lax.ppermute(value, 'blk', cross)]
  transfers between devices with their start and end apart: 16 -> 16, of which waited for: 6 -> 3; matrix products, arithmetic and copies ran while one was open for 0% -> 0% of each run, Pallas kernels for 16% -> 16%
where the time goes in v11:
time: 41.2 us; the launch traced here: 41.1 us
  starting transfers between devices  24.1 us (58%)
  waiting for transfers between devices  9.4 us (23%)
  Pallas kernels  7.44 us (18%)
    ppermute x10, starting transfers between devices, to(): return lax.ppermute(value, ('blk', 'col'), perm)  16.2 us
    ppermute x3, starting transfers between devices, over_link(): return lax.ppermute(value, 'blk', cross)  7.94 us
    pallas_call x8, Pallas kernels, call(): pl.pallas_call(kernel, out_shape=out_shape, in_specs=in_specs, out_specs=...  7.44 us
    ppermute x10, waiting for transfers between devices, to(): return lax.ppermute(value, ('blk', 'col'), perm)  7.08 us
    ppermute x3, waiting for transfers between devices, over_link(): return lax.ppermute(value, 'blk', cross)  2.32 us
  transfers between devices with their start and end apart: 16, of which 3 were waited for; matrix products, arithmetic and copies ran while one was open for 0% of the time, Pallas kernels for 16%

profile of v11, /device:TPU:0, one launch (start us, length us, event | category | flops | bytes accessed | tf_op | source)
XLA Modules:
  0.0 41.1 jit_solution(8787248065498714203)
XLA Ops:
  0.0 3.0 %collective-permute-start = (bf16[1024,3,128]{2,0,1:T(8,128)(2,1)}, bf16[1024,3,128]{2,0,1:T(8,128)(2,1)S(1)}, u32[]{:S(2)}, u32[]{:S(2)}) collective-permute-start(bf16[1024,3,128]{2,0,1:T(8,128)(2,1)} %param.6), channel_id=1, source_target_pairs={{0,1},{1,0},{2,3},{3,2},{4,6},{5,7},{6,4},{7,5},{8,9},{9,8},{10,11... | collective-permute-start | bytes 2359304 | tf_op jit(solution)/shard_map/ppermute | solution.py:238
  3.0 1.8 %mask_and_inner.1 = (bf16[1024,384]{1,0:T(8,128)(2,1)S(1)}, bf16[256,256]{1,0:T(8,128)(2,1)S(1)}, bf16[256,256]{1,0:T(8,128)(2,1)S(1)}, bf16[512,384]{1,0:T(8,128)(2,1)S(1)}) custom-call(s32[3,8]{1,0:T(4,128)} %bitcast.8, bf16[3,1024,128]{2,1,0:T(8,128)(2,1)} %bitcast.10, s32[8,2,128]{2,1,0:T(2,128)} %bitcast.11, bf16[8,3,128,128]{3,2,1,0:T(8,128)(2,1)} %stiffness.1), custom_call_target="tpu_custom_call" | custom-call | flops 150994944 | bytes 3022944 | tf_op jit(solution)/shard_map/mask_and_inner/pallas_call | solution.py:29
  4.9 2.9 %collective-permute-start.1 = (bf16[256,256]{1,0:T(8,128)(2,1)S(1)}, bf16[256,256]{1,0:T(8,128)(2,1)S(1)}, u32[]{:S(2)}, u32[]{:S(2)}) collective-permute-start(bf16[256,256]{1,0:T(8,128)(2,1)S(1)} %get-tuple-element.36), channel_id=1, source_target_pairs={{0,28},{4,8},{8,4},{12,16},{16,12},{20,24},{24,20},{28,0},{1,29},{... | collective-permute-start | bytes 393224 | tf_op jit(solution)/shard_map/ppermute | solution.py:234
  7.7 0.5 %collective-permute-start.4 = (bf16[512,384]{1,0:T(8,128)(2,1)S(1)}, bf16[512,384]{1,0:T(8,128)(2,1)S(1)}, u32[]{:S(2)}, u32[]{:S(2)}) collective-permute-start(bf16[512,384]{1,0:T(8,128)(2,1)S(1)} %get-tuple-element.39.inner), channel_id=1, source_target_pairs={{0,2},{1,3},{2,0},{3,1},{4,5},{5,4},{6,7},{7,6},{8,10},{9,11},{10,... | collective-permute-start | bytes 1179656 | tf_op jit(solution)/shard_map/ppermute | solution.py:238
  8.2 1.5 %collective-permute-start.3 = (s32[8,128,2]{1,2,0:T(2,128)S(1)}, s32[8,128,2]{1,2,0:T(2,128)S(1)}, u32[]{:S(2)}, u32[]{:S(2)}) collective-permute-start(s32[8,128,2]{1,2,0:T(2,128)S(1)} %copy-done.2), channel_id=1, source_target_pairs={{0,1},{1,0},{2,3},{3,2},{4,6},{5,7},{6,4},{7,5},{8,9},{9,8},{10,11... | collective-permute-start | bytes 24584 | tf_op jit(solution)/shard_map/ppermute | solution.py:238
  9.7 6.0 %collective-permute-done.3 = s32[8,128,2]{1,2,0:T(2,128)S(1)} collective-permute-done((s32[8,128,2]{1,2,0:T(2,128)S(1)}, s32[8,128,2]{1,2,0:T(2,128)S(1)}, u32[]{:S(2)}, u32[]{:S(2)}) %collective-permute-start.3) | collective-permute-done | bytes 8224 | tf_op jit(solution)/shard_map/ppermute | solution.py:238
  15.8 1.1 %outer_image.1.outer = bf16[512,384]{1,0:T(8,128)(2,1)S(1)} custom-call(s32[3,8]{1,0:T(4,128)S(1)} %bitcast.9, bf16[8,3,128,128]{3,2,1,0:T(8,128)(2,1)S(1)} %copy-done, bf16[1024,384]{1,0:T(8,128)(2,1)S(1)} %get-tuple-element.40.masked, bf16[256,256]{1,0:T(8,128)(2,1)S(1)} %collective-permute-done.1.from_link, ...), custom_call_target="tpu_custom_call" | custom-call | flops 150994944 | bytes 2228320 | tf_op jit(solution)/shard_map/outer_image/pallas_call | solution.py:29
  16.9 3.6 %collective-permute-start.8 = (bf16[512,384]{1,0:T(8,128)(2,1)S(1)}, bf16[512,384]{1,0:T(8,128)(2,1)S(1)}, u32[]{:S(2)}, u32[]{:S(2)}) collective-permute-start(bf16[512,384]{1,0:T(8,128)(2,1)S(1)} %outer_image.1.outer), channel_id=1, source_target_pairs={{0,2},{1,3},{2,0},{3,1},{4,5},{5,4},{6,7},{7,6},{8,10},{9,11},{10,... | collective-permute-start | bytes 1179656 | tf_op jit(solution)/shard_map/ppermute | solution.py:238
  20.5 0.6 %own_tile.1 = (f32[128,384]{1,0:T(8,128)S(1)}, bf16[128,384]{1,0:T(8,128)(2,1)S(1)}, bf16[128,384]{1,0:T(8,128)(2,1)S(1)}, bf16[384,512]{1,0:T(8,128)(2,1)S(1)}, bf16[384,512]{1,0:T(8,128)(2,1)S(1)}) custom-call(bf16[1024,384]{1,0:T(8,128)(2,1)S(1)} %get-tuple-element.40.masked, bf16[512,384]{1,0:T(8,128)(2,1)S(1)} %get-tuple-element.39.inner, ...), custom_call_target="tpu_custom_call" | custom-call | flops 301989888 | bytes 2752512 | tf_op jit(solution)/shard_map/own_tile/pallas_call | solution.py:29
  21.1 2.2 %collective-permute-start.9 = (bf16[128,384]{1,0:T(8,128)(2,1)S(1)}, bf16[128,384]{1,0:T(8,128)(2,1)S(1)}, u32[]{:S(2)}, u32[]{:S(2)}) collective-permute-start(bf16[128,384]{1,0:T(8,128)(2,1)S(1)} %get-tuple-element.50), channel_id=1, source_target_pairs={{0,28},{4,8},{8,4},{12,16},{16,12},{20,24},{24,20},{28,0},{1,29},{... | collective-permute-start | bytes 294920 | tf_op jit(solution)/shard_map/ppermute | solution.py:234
  23.3 1.3 %partner_tile.1 = (bf16[128,384]{1,0:T(8,128)(2,1)S(1)}, bf16[128,384]{1,0:T(8,128)(2,1)S(1)}, bf16[128,384]{1,0:T(8,128)(2,1)S(1)}, bf16[384,512]{1,0:T(8,128)(...) custom-call(bf16[3,1024,128]{2,1,0:T(8,128)(2,1)S(1)} %bitcast.6, s32[8,2,128]{2,1,0:T(2,128)S(1)} %bitcast.7, ...), custom_call_target="tpu_custom_call" | custom-call | flops 603979776 | bytes 4235264 | tf_op jit(solution)/shard_map/partner_tile/pallas_call | solution.py:29
  24.6 1.4 %collective-permute-start.5 = (bf16[128,384]{1,0:T(8,128)(2,1)S(1)}, bf16[128,384]{1,0:T(8,128)(2,1)S(1)}, u32[]{:S(2)}, u32[]{:S(2)}) collective-permute-start(bf16[128,384]{1,0:T(8,128)(2,1)S(1)} %get-tuple-element.45), channel_id=1, source_target_pairs={{0,1},{1,0},{2,3},{3,2},{4,6},{5,7},{6,4},{7,5},{8,9},{9,8},{10,11... | collective-permute-start | bytes 294920 | tf_op jit(solution)/shard_map/ppermute | solution.py:238
  26.0 1.8 %collective-permute-start.6 = (bf16[128,384]{1,0:T(8,128)(2,1)S(1)}, bf16[128,384]{1,0:T(8,128)(2,1)S(1)}, u32[]{:S(2)}, u32[]{:S(2)}) collective-permute-start(bf16[128,384]{1,0:T(8,128)(2,1)S(1)} %get-tuple-element.46), channel_id=1, source_target_pairs={{0,29},{1,28},{2,31},{3,30},{4,10},{5,11},{6,8},{7,9},{8,5},{9,4},... | collective-permute-start | bytes 294920 | tf_op jit(solution)/shard_map/ppermute | solution.py:238
  27.8 0.0 collective-permute-start.7
  27.8 0.4 far_tile.1
  28.2 1.5 %collective-permute-start.13 = (bf16[128,384]{1,0:T(8,128)(2,1)S(1)}, bf16[128,384]{1,0:T(8,128)(2,1)S(1)}, u32[]{:S(2)}, u32[]{:S(2)}) collective-permute-start(bf16[128,384]{1,0:T(8,128)(2,1)S(1)} %get-tuple-element.61), channel_id=1, source_target_pairs={{0,1},{1,0},{2,3},{3,2},{4,6},{5,7},{6,4},{7,5},{8,9},{9,8},{10,11... | collective-permute-start | bytes 294920 | tf_op jit(solution)/shard_map/ppermute | solution.py:238
  29.7 2.9 %collective-permute-start.14 = (bf16[128,384]{1,0:T(8,128)(2,1)S(1)}, bf16[128,384]{1,0:T(8,128)(2,1)S(1)}, u32[]{:S(2)}, u32[]{:S(2)}) collective-permute-start(bf16[128,384]{1,0:T(8,128)(2,1)S(1)} %get-tuple-element.62), channel_id=1, source_target_pairs={{0,29},{1,28},{2,31},{3,30},{4,10},{5,11},{6,8},{7,9},{8,5},{9,4},... | collective-permute-start | bytes 294920 | tf_op jit(solution)/shard_map/ppermute | solution.py:238
  32.6 0.0 collective-permute-start.15
  32.6 1.0 %collective-permute-done.6.refs_1_ = bf16[128,384]{1,0:T(8,128)(2,1)S(1)} collective-permute-done((bf16[128,384]{1,0:T(8,128)(2,1)S(1)}, bf16[128,384]{1,0:T(8,128)(2,1)S(1)}, u32[]{:S(2)}, u32[]{:S(2)}) %collective-permute-start.6) | collective-permute-done | bytes 98336 | tf_op jit(solution)/shard_map/ppermute | solution.py:238
  33.6 0.4 near_tile.1
  34.0 2.9 %collective-permute-start.11 = (bf16[128,384]{1,0:T(8,128)(2,1)S(1)}, bf16[128,384]{1,0:T(8,128)(2,1)S(1)}, u32[]{:S(2)}, u32[]{:S(2)}) collective-permute-start(bf16[128,384]{1,0:T(8,128)(2,1)S(1)} %get-tuple-element.57), channel_id=1, source_target_pairs={{0,28},{4,8},{8,4},{12,16},{16,12},{20,24},{24,20},{28,0},{1,29},{... | collective-permute-start | bytes 294920 | tf_op jit(solution)/shard_map/ppermute | solution.py:234
  36.9 0.8 %add_own.1.refs_9_ = f32[5,128,512]{2,1,0:T(8,128)} custom-call(f32[128,384]{1,0:T(8,128)S(1)} %get-tuple-element.64.refs_0_, bf16[128,384]{1,0:T(8,128)(2,1)S(1)} %collective-permute-done.9.refs_1_, bf16[128,384]{1,0:T(8,128)(2,1)S(1)} %collective-permute-done.10.refs_2_), custom_call_target="tpu_custom_call" | custom-call | flops 81920 | bytes 1703936 | tf_op jit(solution)/shard_map/add_own/pallas_call | solution.py:29
  37.7 2.3 %collective-permute-done.11.refs_4_ = bf16[128,384]{1,0:T(8,128)(2,1)S(1)} collective-permute-done((bf16[128,384]{1,0:T(8,128)(2,1)S(1)}, bf16[128,384]{1,0:T(8,128)(2,1)S(1)}, u32[]{:S(2)}, u32[]{:S(2)}) %collective-permute-start.11) | collective-permute-done | bytes 98336 | tf_op jit(solution)/shard_map/ppermute | solution.py:234
  40.0 1.0 %add_rest.1 = f32[5,128,512]{2,1,0:T(8,128)} custom-call(f32[128,384]{1,0:T(8,128)S(1)} %get-tuple-element.53.refs_0_, bf16[128,384]{1,0:T(8,128)(2,1)S(1)} %collective-permute-done.6.refs_1_, bf16[128,384]{1,0:T(8,128)(2,1)S(1)} %collective-permute-done.7.refs_2_, ...), custom_call_target="tpu_custom_call", output_to_operand_aliasing={{}: (9, {})} | custom-call | flops 245760 | bytes 3604480 | tf_op jit(solution)/shard_map/add_rest/pallas_call | solution.py:29
  (22 shorter events, 0.1 us)
Async XLA Ops:
  0.0 15.8 %copy-start.1 = (s32[8,3]{0,1:T(4,128)S(1)}, s32[8,3]{0,1:T(4,128)}, u32[]{:S(2)}) copy-start(s32[8,3]{0,1:T(4,128)} %param.5) | copy-start | bytes 292
  0.0 8.2 %copy-start.2 = (s32[8,128,2]{1,2,0:T(2,128)S(1)}, s32[8,128,2]{1,2,0:T(2,128)}, u32[]{:S(2)}) copy-start(s32[8,128,2]{1,2,0:T(2,128)} %param.7) | copy-start | bytes 24580
  0.0 15.8 %copy-start = (bf16[8,3,128,128]{3,2,1,0:T(8,128)(2,1)S(1)}, bf16[8,3,128,128]{3,2,1,0:T(8,128)(2,1)}, u32[]{:S(2)}) copy-start(bf16[8,3,128,128]{3,2,1,0:T(8,128)(2,1)} %stiffness.1) | copy-start | bytes 2359300
  0.0 23.3 %collective-permute-start = (bf16[1024,3,128]{2,0,1:T(8,128)(2,1)}, bf16[1024,3,128]{2,0,1:T(8,128)(2,1)S(1)}, u32[]{:S(2)}, u32[]{:S(2)}) collective-permute-start(bf16[1024,3,128]{2,0,1:T(8,128)(2,1)} %param.6), channel_id=1, source_target_pairs={{0,1},{1,0},{2,3},{3,2},{4,6},{5,7},{6,4},{7,5},{8,9},{9,8},{10,11... | collective-permute-start | bytes 2359304 | tf_op jit(solution)/shard_map/ppermute | solution.py:238
  4.9 10.9 %collective-permute-start.1 = (bf16[256,256]{1,0:T(8,128)(2,1)S(1)}, bf16[256,256]{1,0:T(8,128)(2,1)S(1)}, u32[]{:S(2)}, u32[]{:S(2)}) collective-permute-start(bf16[256,256]{1,0:T(8,128)(2,1)S(1)} %get-tuple-element.36), channel_id=1, source_target_pairs={{0,28},{4,8},{8,4},{12,16},{16,12},{20,24},{24,20},{28,0},{1,29},{... | collective-permute-start | bytes 393224 | tf_op jit(solution)/shard_map/ppermute | solution.py:234
  7.7 8.0 %collective-permute-start.2 = (bf16[256,256]{1,0:T(8,128)(2,1)S(1)}, bf16[256,256]{1,0:T(8,128)(2,1)S(1)}, u32[]{:S(2)}, u32[]{:S(2)}) collective-permute-start(bf16[256,256]{1,0:T(8,128)(2,1)S(1)} %get-tuple-element.37), channel_id=1, source_target_pairs={{0,4},{4,0},{8,12},{12,8},{16,20},{20,16},{24,28},{28,24},{1,5},{5... | collective-permute-start | bytes 393224 | tf_op jit(solution)/shard_map/ppermute | solution.py:231
  7.7 15.6 %collective-permute-start.4 = (bf16[512,384]{1,0:T(8,128)(2,1)S(1)}, bf16[512,384]{1,0:T(8,128)(2,1)S(1)}, u32[]{:S(2)}, u32[]{:S(2)}) collective-permute-start(bf16[512,384]{1,0:T(8,128)(2,1)S(1)} %get-tuple-element.39.inner), channel_id=1, source_target_pairs={{0,2},{1,3},{2,0},{3,1},{4,5},{5,4},{6,7},{7,6},{8,10},{9,11},{10,... | collective-permute-start | bytes 1179656 | tf_op jit(solution)/shard_map/ppermute | solution.py:238
  8.2 7.5 %collective-permute-start.3 = (s32[8,128,2]{1,2,0:T(2,128)S(1)}, s32[8,128,2]{1,2,0:T(2,128)S(1)}, u32[]{:S(2)}, u32[]{:S(2)}) collective-permute-start(s32[8,128,2]{1,2,0:T(2,128)S(1)} %copy-done.2), channel_id=1, source_target_pairs={{0,1},{1,0},{2,3},{3,2},{4,6},{5,7},{6,4},{7,5},{8,9},{9,8},{10,11... | collective-permute-start | bytes 24584 | tf_op jit(solution)/shard_map/ppermute | solution.py:238
  16.9 10.9 %collective-permute-start.8 = (bf16[512,384]{1,0:T(8,128)(2,1)S(1)}, bf16[512,384]{1,0:T(8,128)(2,1)S(1)}, u32[]{:S(2)}, u32[]{:S(2)}) collective-permute-start(bf16[512,384]{1,0:T(8,128)(2,1)S(1)} %outer_image.1.outer), channel_id=1, source_target_pairs={{0,2},{1,3},{2,0},{3,1},{4,5},{5,4},{6,7},{7,6},{8,10},{9,11},{10,... | collective-permute-start | bytes 1179656 | tf_op jit(solution)/shard_map/ppermute | solution.py:238
  21.1 6.7 %collective-permute-start.9 = (bf16[128,384]{1,0:T(8,128)(2,1)S(1)}, bf16[128,384]{1,0:T(8,128)(2,1)S(1)}, u32[]{:S(2)}, u32[]{:S(2)}) collective-permute-start(bf16[128,384]{1,0:T(8,128)(2,1)S(1)} %get-tuple-element.50), channel_id=1, source_target_pairs={{0,28},{4,8},{8,4},{12,16},{16,12},{20,24},{24,20},{28,0},{1,29},{... | collective-permute-start | bytes 294920 | tf_op jit(solution)/shard_map/ppermute | solution.py:234
  23.3 4.5 %collective-permute-start.10 = (bf16[128,384]{1,0:T(8,128)(2,1)S(1)}, bf16[128,384]{1,0:T(8,128)(2,1)S(1)}, u32[]{:S(2)}, u32[]{:S(2)}) collective-permute-start(bf16[128,384]{1,0:T(8,128)(2,1)S(1)} %get-tuple-element.51), channel_id=1, source_target_pairs={{0,4},{4,0},{8,12},{12,8},{16,20},{20,16},{24,28},{28,24},{1,5},{5... | collective-permute-start | bytes 294920 | tf_op jit(solution)/shard_map/ppermute | solution.py:231
  24.6 8.0 %collective-permute-start.5 = (bf16[128,384]{1,0:T(8,128)(2,1)S(1)}, bf16[128,384]{1,0:T(8,128)(2,1)S(1)}, u32[]{:S(2)}, u32[]{:S(2)}) collective-permute-start(bf16[128,384]{1,0:T(8,128)(2,1)S(1)} %get-tuple-element.45), channel_id=1, source_target_pairs={{0,1},{1,0},{2,3},{3,2},{4,6},{5,7},{6,4},{7,5},{8,9},{9,8},{10,11... | collective-permute-start | bytes 294920 | tf_op jit(solution)/shard_map/ppermute | solution.py:238
  26.0 7.6 %collective-permute-start.6 = (bf16[128,384]{1,0:T(8,128)(2,1)S(1)}, bf16[128,384]{1,0:T(8,128)(2,1)S(1)}, u32[]{:S(2)}, u32[]{:S(2)}) collective-permute-start(bf16[128,384]{1,0:T(8,128)(2,1)S(1)} %get-tuple-element.46), channel_id=1, source_target_pairs={{0,29},{1,28},{2,31},{3,30},{4,10},{5,11},{6,8},{7,9},{8,5},{9,4},... | collective-permute-start | bytes 294920 | tf_op jit(solution)/shard_map/ppermute | solution.py:238
  27.8 5.9 %collective-permute-start.7 = (bf16[128,384]{1,0:T(8,128)(2,1)S(1)}, bf16[128,384]{1,0:T(8,128)(2,1)S(1)}, u32[]{:S(2)}, u32[]{:S(2)}) collective-permute-start(bf16[128,384]{1,0:T(8,128)(2,1)S(1)} %get-tuple-element.47), channel_id=1, source_target_pairs={{0,5},{1,4},{2,7},{3,6},{4,2},{5,3},{6,0},{7,1},{8,13},{9,12},{10,... | collective-permute-start | bytes 294920 | tf_op jit(solution)/shard_map/ppermute | solution.py:238
  28.2 9.5 %collective-permute-start.13 = (bf16[128,384]{1,0:T(8,128)(2,1)S(1)}, bf16[128,384]{1,0:T(8,128)(2,1)S(1)}, u32[]{:S(2)}, u32[]{:S(2)}) collective-permute-start(bf16[128,384]{1,0:T(8,128)(2,1)S(1)} %get-tuple-element.61), channel_id=1, source_target_pairs={{0,1},{1,0},{2,3},{3,2},{4,6},{5,7},{6,4},{7,5},{8,9},{9,8},{10,11... | collective-permute-start | bytes 294920 | tf_op jit(solution)/shard_map/ppermute | solution.py:238
  29.7 8.0 %collective-permute-start.14 = (bf16[128,384]{1,0:T(8,128)(2,1)S(1)}, bf16[128,384]{1,0:T(8,128)(2,1)S(1)}, u32[]{:S(2)}, u32[]{:S(2)}) collective-permute-start(bf16[128,384]{1,0:T(8,128)(2,1)S(1)} %get-tuple-element.62), channel_id=1, source_target_pairs={{0,29},{1,28},{2,31},{3,30},{4,10},{5,11},{6,8},{7,9},{8,5},{9,4},... | collective-permute-start | bytes 294920 | tf_op jit(solution)/shard_map/ppermute | solution.py:238
  32.6 5.1 %collective-permute-start.15 = (bf16[128,384]{1,0:T(8,128)(2,1)S(1)}, bf16[128,384]{1,0:T(8,128)(2,1)S(1)}, u32[]{:S(2)}, u32[]{:S(2)}) collective-permute-start(bf16[128,384]{1,0:T(8,128)(2,1)S(1)} %get-tuple-element.63), channel_id=1, source_target_pairs={{0,5},{1,4},{2,7},{3,6},{4,2},{5,3},{6,0},{7,1},{8,13},{9,12},{10,... | collective-permute-start | bytes 294920 | tf_op jit(solution)/shard_map/ppermute | solution.py:238
  34.0 6.0 %collective-permute-start.11 = (bf16[128,384]{1,0:T(8,128)(2,1)S(1)}, bf16[128,384]{1,0:T(8,128)(2,1)S(1)}, u32[]{:S(2)}, u32[]{:S(2)}) collective-permute-start(bf16[128,384]{1,0:T(8,128)(2,1)S(1)} %get-tuple-element.57), channel_id=1, source_target_pairs={{0,28},{4,8},{8,4},{12,16},{16,12},{20,24},{24,20},{28,0},{1,29},{... | collective-permute-start | bytes 294920 | tf_op jit(solution)/shard_map/ppermute | solution.py:234
  36.9 3.1 %collective-permute-start.12 = (bf16[128,384]{1,0:T(8,128)(2,1)S(1)}, bf16[128,384]{1,0:T(8,128)(2,1)S(1)}, u32[]{:S(2)}, u32[]{:S(2)}) collective-permute-start(bf16[128,384]{1,0:T(8,128)(2,1)S(1)} %get-tuple-element.58), channel_id=1, source_target_pairs={{0,4},{4,0},{8,12},{12,8},{16,20},{20,16},{24,28},{28,24},{1,5},{5... | collective-permute-start | bytes 294920 | tf_op jit(solution)/shard_map/ppermute | solution.py:231

commit v12 on v10

--- a/solution.py
+++ b/solution.py
@@ -140,7 +140,7 @@
 
 
 def store_tile(tile, own, link, chip):
-    width = own.shape[0]
+    width = tile.shape[0] // 3
     odd = parity()
     own[...] = tile[width : 2 * width].astype(own.dtype)
     down, up = tile[:width].astype(BF16), tile[2 * width :].astype(BF16)
@@ -182,8 +182,11 @@
     near[...] = dot(near_left[...], inner_r[...])
 
 
-def late_tile(base, left_outer, outer, own, link, chip):
-    store_tile(base[...] + dot(left_outer[...], outer[...]), own, link, chip)
+def late_tiles(
+    far_base, near_base, far_outer, near_outer, outer_r, near, near_link, near_chip, far, far_link, far_chip
+):
+    store_tile(far_base[...] + dot(far_outer[...], outer_r[...]), far, far_link, far_chip)
+    store_tile(near_base[...] + dot(near_outer[...], outer_r[...]), near, near_link, near_chip)
 
 
 def add_tiles(steps, *refs):
@@ -195,7 +198,7 @@
     even = parity() == 0
     copies = []
     for n, (even_step, odd_step) in enumerate(steps):
-        own, link, chip = (ref[...].astype(F32) for ref in terms[3 * n : 3 * n + 3])
+        link, chip, own = (terms[n + m * count][...].astype(F32) for m in range(3))
         prev = jnp.where(even, link, chip)
         nxt = jnp.where(even, chip, link)
         for d in range(5):
@@ -249,11 +252,11 @@
     def to_side(value):
         return to(value, lambda i: i, side)
 
-    def spread(own, link, chip):
-        own = to_partner(own)
-        link = to(link, lambda i: i + 1 if i % 2 else i - 1, partner)
-        chip = to(chip, lambda i: i ^ 1, partner)
-        return own, link, chip
+    def to_partner_chip(value):
+        return to(value, lambda i: i ^ 1, partner)
+
+    def to_partner_link(value):
+        return to(value, lambda i: i + 1 if i % 2 else i - 1, partner)
 
     basis_p = to_partner(basis).transpose(1, 0, 2)
     reach_p = to_partner(patch_reach).transpose(0, 2, 1)
@@ -317,25 +320,23 @@
         flops=2 * tile_flops,
         name="partner_tile",
     )
-    part, part_link, part_chip = spread(part, part_link, part_chip)
-
-    outer_r, own_link, own_chip = lax.optimization_barrier((outer_r, own_link, own_chip))
-
-    def late(base, left, own, name):
-        return call(
-            late_tile,
-            tile_shapes(width, wide, own),
-            [VMEM] * 3,
-            [VMEM] * 3,
-            (base, left, outer_r),
-            flops=tile_flops // 2,
-            name=name,
-        )
-
-    far, far_link, far_chip = spread(*late(far_base, far_outer, BF16, "far_tile"))
-    near_base, part, part_link, part_chip = lax.optimization_barrier((near_base, part, part_link, part_chip))
-    near, near_link, near_chip = late(near_base, left_outer, F32, "near_tile")
-    near_link, near_chip = over_link(near_link), over_chip(near_chip)
+    part, part_link, part_chip = to_partner(part), to_partner_link(part_link), to_partner_chip(part_chip)
+    outer_r, own_link, own_chip, far_base = lax.optimization_barrier((outer_r, own_link, own_chip, far_base))
+    near, near_link, near_chip, far, far_link, far_chip = call(
+        late_tiles,
+        (*tile_shapes(width, wide, F32), *tile_shapes(width, wide, BF16)),
+        [VMEM] * 5,
+        [VMEM] * 6,
+        (far_base, near_base, far_outer, left_outer, outer_r),
+        flops=tile_flops,
+        name="late_tiles",
+    )
+    far, part, part_link, part_chip = lax.optimization_barrier((far, part, part_link, part_chip))
+    far_link = to_partner_link(far_link)
+    near_link = over_link(near_link)
+    far_chip = to_partner_chip(far_chip)
+    far = to_partner(far)
+    near_chip = over_chip(near_chip)
 
     def add(steps, terms, name, base=None):
         extra = () if base is None else (base,)
@@ -351,13 +352,8 @@
             name=name,
         )
 
-    coarse = add(((0, 0),), (own, own_link, own_chip), "add_own")
-    coarse = add(
-        ((2, 1), (1, 2), (3, 3)),
-        (near, part_link, part_chip, part, near_link, near_chip, far, far_link, far_chip),
-        "add_rest",
-        coarse,
-    )
+    coarse = add(((0, 0), (2, 1)), (own_link, part_link, own_chip, part_chip, own, near), "add_first")
+    coarse = add(((3, 3), (1, 2)), (far_link, near_link, far_chip, near_chip, far, part), "add_second", coarse)
     return coarse.transpose(1, 0, 2)
 
 

time: 39.1 us -> 39.3 us (level)
  starting transfers between devices: 17.4 us -> 22.2 us
  waiting for transfers between devices: 13.9 us -> 9.42 us
    ppermute x10, waiting for transfers between devices: 6.92 us -> 4.32 us  [to(): return lax.ppermute(value, ('blk', 'col'), perm)]
    ppermute x10, starting transfers between devices: 12.2 us -> 14.4 us  [to(): return lax.ppermute(value, ('blk', 'col'), perm)]
    ppermute x3, starting transfers between devices: 5.23 us -> 7.26 us  [over_link(): return lax.ppermute(value, 'blk', cross)]
    ppermute x3, waiting for transfers between devices: 7.01 us -> 5.09 us  [over_link(): return lax.ppermute(value, 'blk', cross)]
    ppermute x3, starting transfers between devices: 0.01 us -> 0.52 us  [over_chip(): return lax.ppermute(value, 'blk', pairs)]
    pallas_call x8 -> x7, Pallas kernels: 7.44 us -> 7.45 us  [call(): pl.pallas_call(kernel, out_shape=out_shape, in_specs=in_specs, out_specs=...]
  transfers between devices with their start and end apart: 16 -> 16, of which waited for: 6 -> 5; matrix products, arithmetic and copies ran while one was open for 0% -> 0% of each run, Pallas kernels for 16% -> 17%
where the time goes in v12:
time: 39.3 us; the launch traced here: 39.2 us
  starting transfers between devices  22.2 us (56%)
  waiting for transfers between devices  9.42 us (24%)
  Pallas kernels  7.45 us (19%)
    ppermute x10, starting transfers between devices, to(): return lax.ppermute(value, ('blk', 'col'), perm)  14.4 us
    pallas_call x7, Pallas kernels, call(): pl.pallas_call(kernel, out_shape=out_shape, in_specs=in_specs, out_specs=...  7.45 us
    ppermute x3, starting transfers between devices, over_link(): return lax.ppermute(value, 'blk', cross)  7.26 us
    ppermute x3, waiting for transfers between devices, over_link(): return lax.ppermute(value, 'blk', cross)  5.09 us
    ppermute x10, waiting for transfers between devices, to(): return lax.ppermute(value, ('blk', 'col'), perm)  4.32 us
  transfers between devices with their start and end apart: 16, of which 5 were waited for; matrix products, arithmetic and copies ran while one was open for 0% of the time, Pallas kernels for 17%

profile of v12, /device:TPU:0, one launch (start us, length us, event | category | flops | bytes accessed | tf_op | source)
XLA Modules:
  0.0 39.2 jit_solution(5179357604839743717)
XLA Ops:
  0.0 2.9 %collective-permute-start.5 = (bf16[1024,3,128]{2,0,1:T(8,128)(2,1)}, bf16[1024,3,128]{2,0,1:T(8,128)(2,1)S(1)}, u32[]{:S(2)}, u32[]{:S(2)}) collective-permute-start(bf16[1024,3,128]{2,0,1:T(8,128)(2,1)} %param.6), channel_id=1, source_target_pairs={{0,1},{1,0},{2,3},{3,2},{4,6},{5,7},{6,4},{7,5},{8,9},{9,8},{10,11... | collective-permute-start | bytes 2359304 | tf_op jit(solution)/shard_map/ppermute | solution.py:241
  2.9 1.8 %mask_and_inner.1 = (bf16[1024,384]{1,0:T(8,128)(2,1)S(1)}, bf16[256,256]{1,0:T(8,128)(2,1)S(1)}, bf16[256,256]{1,0:T(8,128)(2,1)S(1)}, bf16[512,384]{1,0:T(8,128)(2,1)S(1)}) custom-call(s32[3,8]{1,0:T(4,128)} %bitcast.8, bf16[3,1024,128]{2,1,0:T(8,128)(2,1)} %bitcast.10, s32[8,2,128]{2,1,0:T(2,128)} %bitcast.11, bf16[8,3,128,128]{3,2,1,0:T(8,128)(2,1)} %stiffness.1), custom_call_target="tpu_custom_call" | custom-call | flops 150994944 | bytes 3022944 | tf_op jit(solution)/shard_map/mask_and_inner/pallas_call | solution.py:29
  4.8 2.9 %collective-permute-start = (bf16[256,256]{1,0:T(8,128)(2,1)S(1)}, bf16[256,256]{1,0:T(8,128)(2,1)S(1)}, u32[]{:S(2)}, u32[]{:S(2)}) collective-permute-start(bf16[256,256]{1,0:T(8,128)(2,1)S(1)} %get-tuple-element.35), channel_id=1, source_target_pairs={{0,28},{4,8},{8,4},{12,16},{16,12},{20,24},{24,20},{28,0},{1,29},{... | collective-permute-start | bytes 393224 | tf_op jit(solution)/shard_map/ppermute | solution.py:237
  7.6 0.5 %collective-permute-start.7 = (bf16[512,384]{1,0:T(8,128)(2,1)S(1)}, bf16[512,384]{1,0:T(8,128)(2,1)S(1)}, u32[]{:S(2)}, u32[]{:S(2)}) collective-permute-start(bf16[512,384]{1,0:T(8,128)(2,1)S(1)} %get-tuple-element.37.inner), channel_id=1, source_target_pairs={{0,2},{1,3},{2,0},{3,1},{4,5},{5,4},{6,7},{7,6},{8,10},{9,11},{10,... | collective-permute-start | bytes 1179656 | tf_op jit(solution)/shard_map/ppermute | solution.py:241
  8.2 4.0 %collective-permute-done.from_link = bf16[256,256]{1,0:T(8,128)(2,1)S(1)} collective-permute-done((bf16[256,256]{1,0:T(8,128)(2,1)S(1)}, bf16[256,256]{1,0:T(8,128)(2,1)S(1)}, u32[]{:S(2)}, u32[]{:S(2)}) %collective-permute-start) | collective-permute-done | bytes 131104 | tf_op jit(solution)/shard_map/ppermute | solution.py:237
  12.2 1.1 %outer_image.1.outer = bf16[512,384]{1,0:T(8,128)(2,1)S(1)} custom-call(s32[3,8]{1,0:T(4,128)S(1)} %bitcast.9, bf16[8,3,128,128]{3,2,1,0:T(8,128)(2,1)S(1)} %copy-done, bf16[1024,384]{1,0:T(8,128)(2,1)S(1)} %get-tuple-element.34.masked, bf16[256,256]{1,0:T(8,128)(2,1)S(1)} %collective-permute-done.from_link, ...), custom_call_target="tpu_custom_call" | custom-call | flops 150994944 | bytes 2228320 | tf_op jit(solution)/shard_map/outer_image/pallas_call | solution.py:29
  13.3 1.6 %collective-permute-start.2 = (bf16[512,384]{1,0:T(8,128)(2,1)S(1)}, bf16[512,384]{1,0:T(8,128)(2,1)S(1)}, u32[]{:S(2)}, u32[]{:S(2)}) collective-permute-start(bf16[512,384]{1,0:T(8,128)(2,1)S(1)} %outer_image.1.outer), channel_id=1, source_target_pairs={{0,2},{1,3},{2,0},{3,1},{4,5},{5,4},{6,7},{7,6},{8,10},{9,11},{10,... | collective-permute-start | bytes 1179656 | tf_op jit(solution)/shard_map/ppermute | solution.py:241
  14.9 0.6 %own_tile.1 = (f32[128,384]{1,0:T(8,128)S(1)}, bf16[128,384]{1,0:T(8,128)(2,1)S(1)}, bf16[128,384]{1,0:T(8,128)(2,1)S(1)}, bf16[384,512]{1,0:T(8,128)(2,1)S(1)}, bf16[384,512]{1,0:T(8,128)(2,1)S(1)}) custom-call(bf16[1024,384]{1,0:T(8,128)(2,1)S(1)} %get-tuple-element.34.masked, bf16[512,384]{1,0:T(8,128)(2,1)S(1)} %get-tuple-element.37.inner, ...), custom_call_target="tpu_custom_call" | custom-call | flops 301989888 | bytes 2752512 | tf_op jit(solution)/shard_map/own_tile/pallas_call | solution.py:29
  15.5 1.4 %collective-permute-start.3 = (bf16[128,384]{1,0:T(8,128)(2,1)S(1)}, bf16[128,384]{1,0:T(8,128)(2,1)S(1)}, u32[]{:S(2)}, u32[]{:S(2)}) collective-permute-start(bf16[128,384]{1,0:T(8,128)(2,1)S(1)} %get-tuple-element.38), channel_id=1, source_target_pairs={{0,28},{4,8},{8,4},{12,16},{16,12},{20,24},{24,20},{28,0},{1,29},{... | collective-permute-start | bytes 294920 | tf_op jit(solution)/shard_map/ppermute | solution.py:237
  16.9 0.5 %collective-permute-start.6 = (s32[8,128,2]{1,2,0:T(2,128)S(1)}, s32[8,128,2]{1,2,0:T(2,128)S(1)}, u32[]{:S(2)}, u32[]{:S(2)}) collective-permute-start(s32[8,128,2]{1,2,0:T(2,128)S(1)} %copy-done.2), channel_id=1, source_target_pairs={{0,1},{1,0},{2,3},{3,2},{4,6},{5,7},{6,4},{7,5},{8,9},{9,8},{10,11... | collective-permute-start | bytes 24584 | tf_op jit(solution)/shard_map/ppermute | solution.py:241
  17.5 3.3 %collective-permute-done.6 = s32[8,128,2]{1,2,0:T(2,128)S(1)} collective-permute-done((s32[8,128,2]{1,2,0:T(2,128)S(1)}, s32[8,128,2]{1,2,0:T(2,128)S(1)}, u32[]{:S(2)}, u32[]{:S(2)}) %collective-permute-start.6) | collective-permute-done | bytes 8224 | tf_op jit(solution)/shard_map/ppermute | solution.py:241
  20.8 1.3 %partner_tile.1 = (bf16[128,384]{1,0:T(8,128)(2,1)S(1)}, bf16[128,384]{1,0:T(8,128)(2,1)S(1)}, bf16[128,384]{1,0:T(8,128)(2,1)S(1)}, bf16[384,512]{1,0:T(8,128)(...) custom-call(bf16[3,1024,128]{2,1,0:T(8,128)(2,1)S(1)} %bitcast.6, s32[8,2,128]{2,1,0:T(2,128)S(1)} %bitcast.7, ...), custom_call_target="tpu_custom_call" | custom-call | flops 603979776 | bytes 4235264 | tf_op jit(solution)/shard_map/partner_tile/pallas_call | solution.py:29
  22.0 0.6 %collective-permute-start.12 = (bf16[128,384]{1,0:T(8,128)(2,1)S(1)}, bf16[128,384]{1,0:T(8,128)(2,1)S(1)}, u32[]{:S(2)}, u32[]{:S(2)}) collective-permute-start(bf16[128,384]{1,0:T(8,128)(2,1)S(1)} %get-tuple-element.52), channel_id=1, source_target_pairs={{0,1},{1,0},{2,3},{3,2},{4,6},{5,7},{6,4},{7,5},{8,9},{9,8},{10,11... | collective-permute-start | bytes 294920 | tf_op jit(solution)/shard_map/ppermute | solution.py:241
  22.6 4.9 %collective-permute-start.13 = (bf16[128,384]{1,0:T(8,128)(2,1)S(1)}, bf16[128,384]{1,0:T(8,128)(2,1)S(1)}, u32[]{:S(2)}, u32[]{:S(2)}) collective-permute-start(bf16[128,384]{1,0:T(8,128)(2,1)S(1)} %get-tuple-element.53), channel_id=1, source_target_pairs={{0,29},{1,28},{2,31},{3,30},{4,10},{5,11},{6,8},{7,9},{8,5},{9,4},... | collective-permute-start | bytes 294920 | tf_op jit(solution)/shard_map/ppermute | solution.py:241
  27.6 0.8 %late_tiles.1 = (f32[128,384]{1,0:T(8,128)S(1)}, bf16[128,384]{1,0:T(8,128)(2,1)S(1)}, bf16[128,384]{1,0:T(8,128)(2,1)S(1)}, bf16[128,384]{1,0:T(8,128)(2,1)S(1)...) custom-call(f32[384,384]{1,0:T(8,128)S(1)} %get-tuple-element.42.far_base, ...), custom_call_target="tpu_custom_call" | custom-call | flops 301989888 | bytes 3047424 | tf_op jit(solution)/shard_map/late_tiles/pallas_call | solution.py:29
  28.5 0.5 %collective-permute-start.11 = (bf16[128,384]{1,0:T(8,128)(2,1)S(1)}, bf16[128,384]{1,0:T(8,128)(2,1)S(1)}, u32[]{:S(2)}, u32[]{:S(2)}) collective-permute-start(bf16[128,384]{1,0:T(8,128)(2,1)S(1)} %get-tuple-element.50), channel_id=1, source_target_pairs={{0,4},{4,0},{8,12},{12,8},{16,20},{20,16},{24,28},{28,24},{1,5},{5... | collective-permute-start | bytes 294920 | tf_op jit(solution)/shard_map/ppermute | solution.py:234
  29.0 1.7 %collective-permute-start.8 = (bf16[128,384]{1,0:T(8,128)(2,1)S(1)}, bf16[128,384]{1,0:T(8,128)(2,1)S(1)}, u32[]{:S(2)}, u32[]{:S(2)}) collective-permute-start(bf16[128,384]{1,0:T(8,128)(2,1)S(1)} %get-tuple-element.47), channel_id=1, source_target_pairs={{0,29},{1,28},{2,31},{3,30},{4,10},{5,11},{6,8},{7,9},{8,5},{9,4},... | collective-permute-start | bytes 294920 | tf_op jit(solution)/shard_map/ppermute | solution.py:241
  30.6 3.0 %collective-permute-start.9 = (bf16[128,384]{1,0:T(8,128)(2,1)S(1)}, bf16[128,384]{1,0:T(8,128)(2,1)S(1)}, u32[]{:S(2)}, u32[]{:S(2)}) collective-permute-start(bf16[128,384]{1,0:T(8,128)(2,1)S(1)} %get-tuple-element.48), channel_id=1, source_target_pairs={{0,28},{4,8},{8,4},{12,16},{16,12},{20,24},{24,20},{28,0},{1,29},{... | collective-permute-start | bytes 294920 | tf_op jit(solution)/shard_map/ppermute | solution.py:237
  33.6 1.6 %collective-permute-start.15 = (bf16[128,384]{1,0:T(8,128)(2,1)S(1)}, bf16[128,384]{1,0:T(8,128)(2,1)S(1)}, u32[]{:S(2)}, u32[]{:S(2)}) collective-permute-start(bf16[128,384]{1,0:T(8,128)(2,1)S(1)} %get-tuple-element.55), channel_id=1, source_target_pairs={{0,1},{1,0},{2,3},{3,2},{4,6},{5,7},{6,4},{7,5},{8,9},{9,8},{10,11... | collective-permute-start | bytes 294920 | tf_op jit(solution)/shard_map/ppermute | solution.py:241
  35.2 0.9 %add_first.1.refs_6_ = f32[5,128,512]{2,1,0:T(8,128)} custom-call(bf16[128,384]{1,0:T(8,128)(2,1)S(1)} %collective-permute-done.3.refs_0_, bf16[128,384]{1,0:T(8,128)(2,1)S(1)} %collective-permute-done.13.refs_1_, bf16[128,384]{1,0:T(8,128)(2,1)S(1)} %collective-permute-done.4.refs_2_, bf16[128,384]{1,0:T(8,128)(2,1)S(1)} %collective-permute-done.14.refs_3_, ...), custom_call_target="tpu_custom_call" | custom-call | flops 163840 | bytes 2097152 | tf_op jit(solution)/shard_map/add_first/pallas_call | solution.py:29
  36.1 0.6 %collective-permute-done.8.refs_0_ = bf16[128,384]{1,0:T(8,128)(2,1)S(1)} collective-permute-done((bf16[128,384]{1,0:T(8,128)(2,1)S(1)}, bf16[128,384]{1,0:T(8,128)(2,1)S(1)}, u32[]{:S(2)}, u32[]{:S(2)}) %collective-permute-start.8) | collective-permute-done | bytes 98336 | tf_op jit(solution)/shard_map/ppermute | solution.py:241
  36.8 1.1 %collective-permute-done.9.refs_1_ = bf16[128,384]{1,0:T(8,128)(2,1)S(1)} collective-permute-done((bf16[128,384]{1,0:T(8,128)(2,1)S(1)}, bf16[128,384]{1,0:T(8,128)(2,1)S(1)}, u32[]{:S(2)}, u32[]{:S(2)}) %collective-permute-start.9) | collective-permute-done | bytes 98336 | tf_op jit(solution)/shard_map/ppermute | solution.py:237
  37.9 0.4 %collective-permute-done.15.refs_4_ = bf16[128,384]{1,0:T(8,128)(2,1)S(1)} collective-permute-done((bf16[128,384]{1,0:T(8,128)(2,1)S(1)}, bf16[128,384]{1,0:T(8,128)(2,1)S(1)}, u32[]{:S(2)}, u32[]{:S(2)}) %collective-permute-start.15) | collective-permute-done | bytes 98336 | tf_op jit(solution)/shard_map/ppermute | solution.py:241
  38.3 0.9 %add_second.1 = f32[5,128,512]{2,1,0:T(8,128)} custom-call(bf16[128,384]{1,0:T(8,128)(2,1)S(1)} %collective-permute-done.8.refs_0_, bf16[128,384]{1,0:T(8,128)(2,1)S(1)} %collective-permute-done.9.refs_1_, bf16[128,384]{1,0:T(8,128)(2,1)S(1)} %collective-permute-done.10.refs_2_, ...), custom_call_target="tpu_custom_call", output_to_operand_aliasing={{}: (6, {})} | custom-call | flops 163840 | bytes 3211264 | tf_op jit(solution)/shard_map/add_second/pallas_call | solution.py:29
  (21 shorter events, 0.1 us)
Async XLA Ops:
  0.0 12.2 %copy-start.1 = (s32[8,3]{0,1:T(4,128)S(1)}, s32[8,3]{0,1:T(4,128)}, u32[]{:S(2)}) copy-start(s32[8,3]{0,1:T(4,128)} %param.5) | copy-start | bytes 292
  0.0 12.2 %copy-start = (bf16[8,3,128,128]{3,2,1,0:T(8,128)(2,1)S(1)}, bf16[8,3,128,128]{3,2,1,0:T(8,128)(2,1)}, u32[]{:S(2)}) copy-start(bf16[8,3,128,128]{3,2,1,0:T(8,128)(2,1)} %stiffness.1) | copy-start | bytes 2359300
  0.0 20.8 %collective-permute-start.5 = (bf16[1024,3,128]{2,0,1:T(8,128)(2,1)}, bf16[1024,3,128]{2,0,1:T(8,128)(2,1)S(1)}, u32[]{:S(2)}, u32[]{:S(2)}) collective-permute-start(bf16[1024,3,128]{2,0,1:T(8,128)(2,1)} %param.6), channel_id=1, source_target_pairs={{0,1},{1,0},{2,3},{3,2},{4,6},{5,7},{6,4},{7,5},{8,9},{9,8},{10,11... | collective-permute-start | bytes 2359304 | tf_op jit(solution)/shard_map/ppermute | solution.py:241
  4.8 7.4 %collective-permute-start = (bf16[256,256]{1,0:T(8,128)(2,1)S(1)}, bf16[256,256]{1,0:T(8,128)(2,1)S(1)}, u32[]{:S(2)}, u32[]{:S(2)}) collective-permute-start(bf16[256,256]{1,0:T(8,128)(2,1)S(1)} %get-tuple-element.35), channel_id=1, source_target_pairs={{0,28},{4,8},{8,4},{12,16},{16,12},{20,24},{24,20},{28,0},{1,29},{... | collective-permute-start | bytes 393224 | tf_op jit(solution)/shard_map/ppermute | solution.py:237
  7.6 4.5 %collective-permute-start.1 = (bf16[256,256]{1,0:T(8,128)(2,1)S(1)}, bf16[256,256]{1,0:T(8,128)(2,1)S(1)}, u32[]{:S(2)}, u32[]{:S(2)}) collective-permute-start(bf16[256,256]{1,0:T(8,128)(2,1)S(1)} %get-tuple-element.36), channel_id=1, source_target_pairs={{0,4},{4,0},{8,12},{12,8},{16,20},{20,16},{24,28},{28,24},{1,5},{5... | collective-permute-start | bytes 393224 | tf_op jit(solution)/shard_map/ppermute | solution.py:234
  7.6 13.1 %collective-permute-start.7 = (bf16[512,384]{1,0:T(8,128)(2,1)S(1)}, bf16[512,384]{1,0:T(8,128)(2,1)S(1)}, u32[]{:S(2)}, u32[]{:S(2)}) collective-permute-start(bf16[512,384]{1,0:T(8,128)(2,1)S(1)} %get-tuple-element.37.inner), channel_id=1, source_target_pairs={{0,2},{1,3},{2,0},{3,1},{4,5},{5,4},{6,7},{7,6},{8,10},{9,11},{10,... | collective-permute-start | bytes 1179656 | tf_op jit(solution)/shard_map/ppermute | solution.py:241
  13.3 3.6 %copy-start.2 = (s32[8,128,2]{1,2,0:T(2,128)S(1)}, s32[8,128,2]{1,2,0:T(2,128)}, u32[]{:S(2)}) copy-start(s32[8,128,2]{1,2,0:T(2,128)} %param.7) | copy-start | bytes 24580
  13.3 14.3 %collective-permute-start.2 = (bf16[512,384]{1,0:T(8,128)(2,1)S(1)}, bf16[512,384]{1,0:T(8,128)(2,1)S(1)}, u32[]{:S(2)}, u32[]{:S(2)}) collective-permute-start(bf16[512,384]{1,0:T(8,128)(2,1)S(1)} %outer_image.1.outer), channel_id=1, source_target_pairs={{0,2},{1,3},{2,0},{3,1},{4,5},{5,4},{6,7},{7,6},{8,10},{9,11},{10,... | collective-permute-start | bytes 1179656 | tf_op jit(solution)/shard_map/ppermute | solution.py:241
  15.5 12.0 %collective-permute-start.3 = (bf16[128,384]{1,0:T(8,128)(2,1)S(1)}, bf16[128,384]{1,0:T(8,128)(2,1)S(1)}, u32[]{:S(2)}, u32[]{:S(2)}) collective-permute-start(bf16[128,384]{1,0:T(8,128)(2,1)S(1)} %get-tuple-element.38), channel_id=1, source_target_pairs={{0,28},{4,8},{8,4},{12,16},{16,12},{20,24},{24,20},{28,0},{1,29},{... | collective-permute-start | bytes 294920 | tf_op jit(solution)/shard_map/ppermute | solution.py:237
  16.9 3.8 %collective-permute-start.6 = (s32[8,128,2]{1,2,0:T(2,128)S(1)}, s32[8,128,2]{1,2,0:T(2,128)S(1)}, u32[]{:S(2)}, u32[]{:S(2)}) collective-permute-start(s32[8,128,2]{1,2,0:T(2,128)S(1)} %copy-done.2), channel_id=1, source_target_pairs={{0,1},{1,0},{2,3},{3,2},{4,6},{5,7},{6,4},{7,5},{8,9},{9,8},{10,11... | collective-permute-start | bytes 24584 | tf_op jit(solution)/shard_map/ppermute | solution.py:241
  20.8 6.8 %collective-permute-start.4 = (bf16[128,384]{1,0:T(8,128)(2,1)S(1)}, bf16[128,384]{1,0:T(8,128)(2,1)S(1)}, u32[]{:S(2)}, u32[]{:S(2)}) collective-permute-start(bf16[128,384]{1,0:T(8,128)(2,1)S(1)} %get-tuple-element.39), channel_id=1, source_target_pairs={{0,4},{4,0},{8,12},{12,8},{16,20},{20,16},{24,28},{28,24},{1,5},{5... | collective-permute-start | bytes 294920 | tf_op jit(solution)/shard_map/ppermute | solution.py:234
  22.0 6.9 %collective-permute-start.12 = (bf16[128,384]{1,0:T(8,128)(2,1)S(1)}, bf16[128,384]{1,0:T(8,128)(2,1)S(1)}, u32[]{:S(2)}, u32[]{:S(2)}) collective-permute-start(bf16[128,384]{1,0:T(8,128)(2,1)S(1)} %get-tuple-element.52), channel_id=1, source_target_pairs={{0,1},{1,0},{2,3},{3,2},{4,6},{5,7},{6,4},{7,5},{8,9},{9,8},{10,11... | collective-permute-start | bytes 294920 | tf_op jit(solution)/shard_map/ppermute | solution.py:241
  22.6 8.0 %collective-permute-start.13 = (bf16[128,384]{1,0:T(8,128)(2,1)S(1)}, bf16[128,384]{1,0:T(8,128)(2,1)S(1)}, u32[]{:S(2)}, u32[]{:S(2)}) collective-permute-start(bf16[128,384]{1,0:T(8,128)(2,1)S(1)} %get-tuple-element.53), channel_id=1, source_target_pairs={{0,29},{1,28},{2,31},{3,30},{4,10},{5,11},{6,8},{7,9},{8,5},{9,4},... | collective-permute-start | bytes 294920 | tf_op jit(solution)/shard_map/ppermute | solution.py:241
  27.6 6.1 %collective-permute-start.14 = (bf16[128,384]{1,0:T(8,128)(2,1)S(1)}, bf16[128,384]{1,0:T(8,128)(2,1)S(1)}, u32[]{:S(2)}, u32[]{:S(2)}) collective-permute-start(bf16[128,384]{1,0:T(8,128)(2,1)S(1)} %get-tuple-element.54), channel_id=1, source_target_pairs={{0,5},{1,4},{2,7},{3,6},{4,2},{5,3},{6,0},{7,1},{8,13},{9,12},{10,... | collective-permute-start | bytes 294920 | tf_op jit(solution)/shard_map/ppermute | solution.py:241
  28.4 7.7 %collective-permute-start.10 = (bf16[128,384]{1,0:T(8,128)(2,1)S(1)}, bf16[128,384]{1,0:T(8,128)(2,1)S(1)}, u32[]{:S(2)}, u32[]{:S(2)}) collective-permute-start(bf16[128,384]{1,0:T(8,128)(2,1)S(1)} %get-tuple-element.49), channel_id=1, source_target_pairs={{0,5},{1,4},{2,7},{3,6},{4,2},{5,3},{6,0},{7,1},{8,13},{9,12},{10,... | collective-permute-start | bytes 294920 | tf_op jit(solution)/shard_map/ppermute | solution.py:241
  28.5 7.7 %collective-permute-start.11 = (bf16[128,384]{1,0:T(8,128)(2,1)S(1)}, bf16[128,384]{1,0:T(8,128)(2,1)S(1)}, u32[]{:S(2)}, u32[]{:S(2)}) collective-permute-start(bf16[128,384]{1,0:T(8,128)(2,1)S(1)} %get-tuple-element.50), channel_id=1, source_target_pairs={{0,4},{4,0},{8,12},{12,8},{16,20},{20,16},{24,28},{28,24},{1,5},{5... | collective-permute-start | bytes 294920 | tf_op jit(solution)/shard_map/ppermute | solution.py:234
  29.0 7.8 %collective-permute-start.8 = (bf16[128,384]{1,0:T(8,128)(2,1)S(1)}, bf16[128,384]{1,0:T(8,128)(2,1)S(1)}, u32[]{:S(2)}, u32[]{:S(2)}) collective-permute-start(bf16[128,384]{1,0:T(8,128)(2,1)S(1)} %get-tuple-element.47), channel_id=1, source_target_pairs={{0,29},{1,28},{2,31},{3,30},{4,10},{5,11},{6,8},{7,9},{8,5},{9,4},... | collective-permute-start | bytes 294920 | tf_op jit(solution)/shard_map/ppermute | solution.py:241
  30.6 7.2 %collective-permute-start.9 = (bf16[128,384]{1,0:T(8,128)(2,1)S(1)}, bf16[128,384]{1,0:T(8,128)(2,1)S(1)}, u32[]{:S(2)}, u32[]{:S(2)}) collective-permute-start(bf16[128,384]{1,0:T(8,128)(2,1)S(1)} %get-tuple-element.48), channel_id=1, source_target_pairs={{0,28},{4,8},{8,4},{12,16},{16,12},{20,24},{24,20},{28,0},{1,29},{... | collective-permute-start | bytes 294920 | tf_op jit(solution)/shard_map/ppermute | solution.py:237
  33.6 4.6 %collective-permute-start.15 = (bf16[128,384]{1,0:T(8,128)(2,1)S(1)}, bf16[128,384]{1,0:T(8,128)(2,1)S(1)}, u32[]{:S(2)}, u32[]{:S(2)}) collective-permute-start(bf16[128,384]{1,0:T(8,128)(2,1)S(1)} %get-tuple-element.55), channel_id=1, source_target_pairs={{0,1},{1,0},{2,3},{3,2},{4,6},{5,7},{6,4},{7,5},{8,9},{9,8},{10,11... | collective-permute-start | bytes 294920 | tf_op jit(solution)/shard_map/ppermute | solution.py:241

commit v13 on v12

--- a/solution.py
+++ b/solution.py
@@ -183,9 +183,27 @@
 
 
 def late_tiles(
-    far_base, near_base, far_outer, near_outer, outer_r, near, near_link, near_chip, far, far_link, far_chip
+    part,
+    part_link,
+    part_chip,
+    far_base,
+    near_base,
+    far_outer,
+    near_outer,
+    outer_r,
+    near,
+    near_link,
+    near_chip,
+    far,
+    far_link,
+    far_chip,
 ):
-    store_tile(far_base[...] + dot(far_outer[...], outer_r[...]), far, far_link, far_chip)
+    wide = outer_r.shape[1]
+    far[:, :wide] = part[...]
+    far_link[:, :wide] = part_link[...]
+    far_chip[:, :wide] = part_chip[...]
+    tile = far_base[...] + dot(far_outer[...], outer_r[...])
+    store_tile(tile, far.at[:, wide:], far_link.at[:, wide:], far_chip.at[:, wide:])
     store_tile(near_base[...] + dot(near_outer[...], outer_r[...]), near, near_link, near_chip)
 
 
@@ -197,8 +215,10 @@
     me = lax.axis_index("col")
     even = parity() == 0
     copies = []
-    for n, (even_step, odd_step) in enumerate(steps):
-        link, chip, own = (terms[n + m * count][...].astype(F32) for m in range(3))
+    for n, ((even_step, odd_step), chunks) in enumerate(steps):
+        chip, link, own = (
+            terms[n + k * count][:, m * 3 * width : (m + 1) * 3 * width].astype(F32) for k, m in enumerate(chunks)
+        )
         prev = jnp.where(even, link, chip)
         nxt = jnp.where(even, chip, link)
         for d in range(5):
@@ -251,9 +271,6 @@
 
     def to_side(value):
         return to(value, lambda i: i, side)
-
-    def to_partner_chip(value):
-        return to(value, lambda i: i ^ 1, partner)
 
     def to_partner_link(value):
         return to(value, lambda i: i + 1 if i % 2 else i - 1, partner)
@@ -320,21 +337,19 @@
         flops=2 * tile_flops,
         name="partner_tile",
     )
-    part, part_link, part_chip = to_partner(part), to_partner_link(part_link), to_partner_chip(part_chip)
     outer_r, own_link, own_chip, far_base = lax.optimization_barrier((outer_r, own_link, own_chip, far_base))
     near, near_link, near_chip, far, far_link, far_chip = call(
         late_tiles,
-        (*tile_shapes(width, wide, F32), *tile_shapes(width, wide, BF16)),
-        [VMEM] * 5,
+        (*tile_shapes(width, wide, F32), *(shape((width, 2 * wide), BF16),) * 3),
+        [VMEM] * 8,
         [VMEM] * 6,
-        (far_base, near_base, far_outer, left_outer, outer_r),
+        (part, part_link, part_chip, far_base, near_base, far_outer, left_outer, outer_r),
         flops=tile_flops,
         name="late_tiles",
     )
-    far, part, part_link, part_chip = lax.optimization_barrier((far, part, part_link, part_chip))
     far_link = to_partner_link(far_link)
     near_link = over_link(near_link)
-    far_chip = to_partner_chip(far_chip)
+    far_chip = to(far_chip, lambda i: i ^ 1, partner)
     far = to_partner(far)
     near_chip = over_chip(near_chip)
 
@@ -352,8 +367,13 @@
             name=name,
         )
 
-    coarse = add(((0, 0), (2, 1)), (own_link, part_link, own_chip, part_chip, own, near), "add_first")
-    coarse = add(((3, 3), (1, 2)), (far_link, near_link, far_chip, near_chip, far, part), "add_second", coarse)
+    coarse = add((((0, 0), (0, 0, 0)),), (own_chip, own_link, own), "add_own")
+    coarse = add(
+        (((3, 3), (1, 1, 1)), ((1, 2), (0, 0, 0)), ((2, 1), (0, 0, 0))),
+        (far_chip, near_chip, far_chip, far_link, near_link, far_link, far, far, near),
+        "add_rest",
+        coarse,
+    )
     return coarse.transpose(1, 0, 2)
 
 

time: 39.3 us -> 35.4 us (0.901)
  starting transfers between devices: 22.2 us -> 16 us
  waiting for transfers between devices: 9.42 us -> 11.7 us
    ppermute x3, waiting for transfers between devices: 5.09 us -> 10.2 us  [over_link(): return lax.ppermute(value, 'blk', cross)]
    ppermute x10 -> x7, starting transfers between devices: 14.4 us -> 10.3 us  [to(): return lax.ppermute(value, ('blk', 'col'), perm)]
    ppermute x10 -> x7, waiting for transfers between devices: 4.32 us -> 1.51 us  [to(): return lax.ppermute(value, ('blk', 'col'), perm)]
    ppermute x3, starting transfers between devices: 7.26 us -> 5.67 us  [over_link(): return lax.ppermute(value, 'blk', cross)]
    ppermute x3, starting transfers between devices: 0.52 us -> 0.01 us  [over_chip(): return lax.ppermute(value, 'blk', pairs)]
  transfers between devices with their start and end apart: 16 -> 13, of which waited for: 5 -> 4; matrix products, arithmetic and copies ran while one was open for 0% -> 0% of each run, Pallas kernels for 17% -> 16%
where the time goes in v13:
time: 35.4 us; the launch traced here: 35.3 us
  starting transfers between devices  16 us (45%)
  waiting for transfers between devices  11.7 us (33%)
  Pallas kernels  7.47 us (21%)
    ppermute x7, starting transfers between devices, to(): return lax.ppermute(value, ('blk', 'col'), perm)  10.3 us
    ppermute x3, waiting for transfers between devices, over_link(): return lax.ppermute(value, 'blk', cross)  10.2 us
    pallas_call x7, Pallas kernels, call(): pl.pallas_call(kernel, out_shape=out_shape, in_specs=in_specs, out_specs=...  7.47 us
    ppermute x3, starting transfers between devices, over_link(): return lax.ppermute(value, 'blk', cross)  5.67 us
    ppermute x7, waiting for transfers between devices, to(): return lax.ppermute(value, ('blk', 'col'), perm)  1.51 us
  transfers between devices with their start and end apart: 13, of which 4 were waited for; matrix products, arithmetic and copies ran while one was open for 0% of the time, Pallas kernels for 16%

profile of v13, /device:TPU:0, one launch (start us, length us, event | category | flops | bytes accessed | tf_op | source)
XLA Modules:
  0.0 35.3 jit_solution(16656765998183156621)
XLA Ops:
  0.0 2.9 %collective-permute-start = (bf16[1024,3,128]{2,0,1:T(8,128)(2,1)}, bf16[1024,3,128]{2,0,1:T(8,128)(2,1)S(1)}, u32[]{:S(2)}, u32[]{:S(2)}) collective-permute-start(bf16[1024,3,128]{2,0,1:T(8,128)(2,1)} %param.6), channel_id=1, source_target_pairs={{0,1},{1,0},{2,3},{3,2},{4,6},{5,7},{6,4},{7,5},{8,9},{9,8},{10,11... | collective-permute-start | bytes 2359304 | tf_op jit(solution)/shard_map/ppermute | solution.py:261
  2.9 1.8 %mask_and_inner.1 = (bf16[1024,384]{1,0:T(8,128)(2,1)S(1)}, bf16[256,256]{1,0:T(8,128)(2,1)S(1)}, bf16[256,256]{1,0:T(8,128)(2,1)S(1)}, bf16[512,384]{1,0:T(8,128)(2,1)S(1)}) custom-call(s32[3,8]{1,0:T(4,128)} %bitcast.8, bf16[3,1024,128]{2,1,0:T(8,128)(2,1)} %bitcast.10, s32[8,2,128]{2,1,0:T(2,128)} %bitcast.11, bf16[8,3,128,128]{3,2,1,0:T(8,128)(2,1)} %stiffness.1), custom_call_target="tpu_custom_call" | custom-call | flops 150994944 | bytes 3022944 | tf_op jit(solution)/shard_map/mask_and_inner/pallas_call | solution.py:29
  4.8 0.0 copy-start.2
  4.8 2.9 %collective-permute-start.2 = (bf16[256,256]{1,0:T(8,128)(2,1)S(1)}, bf16[256,256]{1,0:T(8,128)(2,1)S(1)}, u32[]{:S(2)}, u32[]{:S(2)}) collective-permute-start(bf16[256,256]{1,0:T(8,128)(2,1)S(1)} %get-tuple-element.32), channel_id=1, source_target_pairs={{0,28},{4,8},{8,4},{12,16},{16,12},{20,24},{24,20},{28,0},{1,29},{... | collective-permute-start | bytes 393224 | tf_op jit(solution)/shard_map/ppermute | solution.py:257
  7.7 0.0 collective-permute-start.3
  7.7 0.5 %collective-permute-start.4 = (bf16[512,384]{1,0:T(8,128)(2,1)S(1)}, bf16[512,384]{1,0:T(8,128)(2,1)S(1)}, u32[]{:S(2)}, u32[]{:S(2)}) collective-permute-start(bf16[512,384]{1,0:T(8,128)(2,1)S(1)} %get-tuple-element.30.inner), channel_id=1, source_target_pairs={{0,2},{1,3},{2,0},{3,1},{4,5},{5,4},{6,7},{7,6},{8,10},{9,11},{10,... | collective-permute-start | bytes 1179656 | tf_op jit(solution)/shard_map/ppermute | solution.py:261
  8.2 4.0 %collective-permute-done.2.from_link = bf16[256,256]{1,0:T(8,128)(2,1)S(1)} collective-permute-done((bf16[256,256]{1,0:T(8,128)(2,1)S(1)}, bf16[256,256]{1,0:T(8,128)(2,1)S(1)}, u32[]{:S(2)}, u32[]{:S(2)}) %collective-permute-start.2) | collective-permute-done | bytes 131104 | tf_op jit(solution)/shard_map/ppermute | solution.py:257
  12.2 1.1 %outer_image.1.outer = bf16[512,384]{1,0:T(8,128)(2,1)S(1)} custom-call(s32[3,8]{1,0:T(4,128)S(1)} %bitcast.9, bf16[8,3,128,128]{3,2,1,0:T(8,128)(2,1)S(1)} %copy-done, bf16[1024,384]{1,0:T(8,128)(2,1)S(1)} %get-tuple-element.31.masked, bf16[256,256]{1,0:T(8,128)(2,1)S(1)} %collective-permute-done.2.from_link, ...), custom_call_target="tpu_custom_call" | custom-call | flops 150994944 | bytes 2228320 | tf_op jit(solution)/shard_map/outer_image/pallas_call | solution.py:29
  13.3 1.6 %collective-permute-start.5 = (bf16[512,384]{1,0:T(8,128)(2,1)S(1)}, bf16[512,384]{1,0:T(8,128)(2,1)S(1)}, u32[]{:S(2)}, u32[]{:S(2)}) collective-permute-start(bf16[512,384]{1,0:T(8,128)(2,1)S(1)} %outer_image.1.outer), channel_id=1, source_target_pairs={{0,2},{1,3},{2,0},{3,1},{4,5},{5,4},{6,7},{7,6},{8,10},{9,11},{10,... | collective-permute-start | bytes 1179656 | tf_op jit(solution)/shard_map/ppermute | solution.py:261
  14.9 0.5 %collective-permute-start.1 = (s32[8,128,2]{1,2,0:T(2,128)S(1)}, s32[8,128,2]{1,2,0:T(2,128)S(1)}, u32[]{:S(2)}, u32[]{:S(2)}) collective-permute-start(s32[8,128,2]{1,2,0:T(2,128)S(1)} %copy-done.2), channel_id=1, source_target_pairs={{0,1},{1,0},{2,3},{3,2},{4,6},{5,7},{6,4},{7,5},{8,9},{9,8},{10,11... | collective-permute-start | bytes 24584 | tf_op jit(solution)/shard_map/ppermute | solution.py:261
  15.4 0.6 %own_tile.1 = (f32[128,384]{1,0:T(8,128)S(1)}, bf16[128,384]{1,0:T(8,128)(2,1)S(1)}, bf16[128,384]{1,0:T(8,128)(2,1)S(1)}, bf16[384,512]{1,0:T(8,128)(2,1)S(1)}, bf16[384,512]{1,0:T(8,128)(2,1)S(1)}) custom-call(bf16[1024,384]{1,0:T(8,128)(2,1)S(1)} %get-tuple-element.31.masked, bf16[512,384]{1,0:T(8,128)(2,1)S(1)} %get-tuple-element.30.inner, ...), custom_call_target="tpu_custom_call" | custom-call | flops 301989888 | bytes 2752512 | tf_op jit(solution)/shard_map/own_tile/pallas_call | solution.py:29
  16.1 1.1 %collective-permute-start.6 = (bf16[128,384]{1,0:T(8,128)(2,1)S(1)}, bf16[128,384]{1,0:T(8,128)(2,1)S(1)}, u32[]{:S(2)}, u32[]{:S(2)}) collective-permute-start(bf16[128,384]{1,0:T(8,128)(2,1)S(1)} %get-tuple-element.38), channel_id=1, source_target_pairs={{0,28},{4,8},{8,4},{12,16},{16,12},{20,24},{24,20},{28,0},{1,29},{... | collective-permute-start | bytes 294920 | tf_op jit(solution)/shard_map/ppermute | solution.py:257
  17.2 1.5 %collective-permute-done.1 = s32[8,128,2]{1,2,0:T(2,128)S(1)} collective-permute-done((s32[8,128,2]{1,2,0:T(2,128)S(1)}, s32[8,128,2]{1,2,0:T(2,128)S(1)}, u32[]{:S(2)}, u32[]{:S(2)}) %collective-permute-start.1) | collective-permute-done | bytes 8224 | tf_op jit(solution)/shard_map/ppermute | solution.py:261
  18.7 0.0 collective-permute-start.7
  18.7 0.0 collective-permute-done.4.inner_r
  18.7 1.3 %partner_tile.1 = (bf16[128,384]{1,0:T(8,128)(2,1)S(1)}, bf16[128,384]{1,0:T(8,128)(2,1)S(1)}, bf16[128,384]{1,0:T(8,128)(2,1)S(1)}, bf16[384,512]{1,0:T(8,128)(...) custom-call(bf16[3,1024,128]{2,1,0:T(8,128)(2,1)S(1)} %bitcast.6, s32[8,2,128]{2,1,0:T(2,128)S(1)} %bitcast.7, ...), custom_call_target="tpu_custom_call" | custom-call | flops 603979776 | bytes 4235264 | tf_op jit(solution)/shard_map/partner_tile/pallas_call | solution.py:29
  20.0 2.0 %collective-permute-done.6.refs_1_ = bf16[128,384]{1,0:T(8,128)(2,1)S(1)} collective-permute-done((bf16[128,384]{1,0:T(8,128)(2,1)S(1)}, bf16[128,384]{1,0:T(8,128)(2,1)S(1)}, u32[]{:S(2)}, u32[]{:S(2)}) %collective-permute-start.6) | collective-permute-done | bytes 98336 | tf_op jit(solution)/shard_map/ppermute | solution.py:257
  22.0 0.8 %late_tiles.1 = (f32[128,384]{1,0:T(8,128)S(1)}, bf16[128,384]{1,0:T(8,128)(2,1)S(1)}, bf16[128,384]{1,0:T(8,128)(2,1)S(1)}, bf16[128,768]{1,0:T(8,128)(2,1)S(1)...) custom-call(bf16[128,384]{1,0:T(8,128)(2,1)S(1)} %get-tuple-element.35.part, ...), custom_call_target="tpu_custom_call" | custom-call | flops 301989888 | bytes 3637248 | tf_op jit(solution)/shard_map/late_tiles/pallas_call | solution.py:29
  22.8 4.2 %collective-permute-start.10 = (bf16[128,768]{1,0:T(8,128)(2,1)S(1)}, bf16[128,768]{1,0:T(8,128)(2,1)S(1)}, u32[]{:S(2)}, u32[]{:S(2)}) collective-permute-start(bf16[128,768]{1,0:T(8,128)(2,1)S(1)} %get-tuple-element.48), channel_id=1, source_target_pairs={{0,29},{1,28},{2,31},{3,30},{4,10},{5,11},{6,8},{7,9},{8,5},{9,4},... | collective-permute-start | bytes 589832 | tf_op jit(solution)/shard_map/ppermute | solution.py:261
  27.0 0.5 %collective-permute-start.12 = (bf16[128,768]{1,0:T(8,128)(2,1)S(1)}, bf16[128,768]{1,0:T(8,128)(2,1)S(1)}, u32[]{:S(2)}, u32[]{:S(2)}) collective-permute-start(bf16[128,768]{1,0:T(8,128)(2,1)S(1)} %get-tuple-element.50), channel_id=1, source_target_pairs={{0,1},{1,0},{2,3},{3,2},{4,6},{5,7},{6,4},{7,5},{8,9},{9,8},{10,11... | collective-permute-start | bytes 589832 | tf_op jit(solution)/shard_map/ppermute | solution.py:261
  27.5 1.7 %collective-permute-start.11 = (bf16[128,384]{1,0:T(8,128)(2,1)S(1)}, bf16[128,384]{1,0:T(8,128)(2,1)S(1)}, u32[]{:S(2)}, u32[]{:S(2)}) collective-permute-start(bf16[128,384]{1,0:T(8,128)(2,1)S(1)} %get-tuple-element.49), channel_id=1, source_target_pairs={{0,28},{4,8},{8,4},{12,16},{16,12},{20,24},{24,20},{28,0},{1,29},{... | collective-permute-start | bytes 294920 | tf_op jit(solution)/shard_map/ppermute | solution.py:257
  29.2 0.8 %add_own.1.refs_9_ = f32[5,128,512]{2,1,0:T(8,128)} custom-call(bf16[128,384]{1,0:T(8,128)(2,1)S(1)} %collective-permute-done.7.refs_0_, bf16[128,384]{1,0:T(8,128)(2,1)S(1)} %collective-permute-done.6.refs_1_, f32[128,384]{1,0:T(8,128)S(1)} %get-tuple-element.54.refs_2_), custom_call_target="tpu_custom_call" | custom-call | flops 81920 | bytes 1703936 | tf_op jit(solution)/shard_map/add_own/pallas_call | solution.py:29
  30.0 4.2 %collective-permute-done.11.refs_4_ = bf16[128,384]{1,0:T(8,128)(2,1)S(1)} collective-permute-done((bf16[128,384]{1,0:T(8,128)(2,1)S(1)}, bf16[128,384]{1,0:T(8,128)(2,1)S(1)}, u32[]{:S(2)}, u32[]{:S(2)}) %collective-permute-start.11) | collective-permute-done | bytes 98336 | tf_op jit(solution)/shard_map/ppermute | solution.py:257
  34.3 1.0 %add_rest.1 = f32[5,128,512]{2,1,0:T(8,128)} custom-call(bf16[128,768]{1,0:T(8,128)(2,1)S(1)} %collective-permute-done.8.refs_0_.refs_2_, bf16[128,384]{1,0:T(8,128)(2,1)S(1)} %collective-permute-done.9.refs_1_, bf16[128,768]{1,0:T(8,128)(2,1)S(1)} %collective-permute-done.8.refs_0_.refs_2_, ...), custom_call_target="tpu_custom_call", output_to_operand_aliasing={{}: (9, {})} | custom-call | flops 245760 | bytes 4194304 | tf_op jit(solution)/shard_map/add_rest/pallas_call | solution.py:29
  (15 shorter events, 0.0 us)
Async XLA Ops:
  0.0 12.2 %copy-start.1 = (s32[8,3]{0,1:T(4,128)S(1)}, s32[8,3]{0,1:T(4,128)}, u32[]{:S(2)}) copy-start(s32[8,3]{0,1:T(4,128)} %param.5) | copy-start | bytes 292
  0.0 12.2 %copy-start = (bf16[8,3,128,128]{3,2,1,0:T(8,128)(2,1)S(1)}, bf16[8,3,128,128]{3,2,1,0:T(8,128)(2,1)}, u32[]{:S(2)}) copy-start(bf16[8,3,128,128]{3,2,1,0:T(8,128)(2,1)} %stiffness.1) | copy-start | bytes 2359300
  0.0 18.7 %collective-permute-start = (bf16[1024,3,128]{2,0,1:T(8,128)(2,1)}, bf16[1024,3,128]{2,0,1:T(8,128)(2,1)S(1)}, u32[]{:S(2)}, u32[]{:S(2)}) collective-permute-start(bf16[1024,3,128]{2,0,1:T(8,128)(2,1)} %param.6), channel_id=1, source_target_pairs={{0,1},{1,0},{2,3},{3,2},{4,6},{5,7},{6,4},{7,5},{8,9},{9,8},{10,11... | collective-permute-start | bytes 2359304 | tf_op jit(solution)/shard_map/ppermute | solution.py:261
  4.8 10.1 %copy-start.2 = (s32[8,128,2]{1,2,0:T(2,128)S(1)}, s32[8,128,2]{1,2,0:T(2,128)}, u32[]{:S(2)}) copy-start(s32[8,128,2]{1,2,0:T(2,128)} %param.7) | copy-start | bytes 24580
  4.8 7.4 %collective-permute-start.2 = (bf16[256,256]{1,0:T(8,128)(2,1)S(1)}, bf16[256,256]{1,0:T(8,128)(2,1)S(1)}, u32[]{:S(2)}, u32[]{:S(2)}) collective-permute-start(bf16[256,256]{1,0:T(8,128)(2,1)S(1)} %get-tuple-element.32), channel_id=1, source_target_pairs={{0,28},{4,8},{8,4},{12,16},{16,12},{20,24},{24,20},{28,0},{1,29},{... | collective-permute-start | bytes 393224 | tf_op jit(solution)/shard_map/ppermute | solution.py:257
  7.7 4.5 %collective-permute-start.3 = (bf16[256,256]{1,0:T(8,128)(2,1)S(1)}, bf16[256,256]{1,0:T(8,128)(2,1)S(1)}, u32[]{:S(2)}, u32[]{:S(2)}) collective-permute-start(bf16[256,256]{1,0:T(8,128)(2,1)S(1)} %get-tuple-element.33), channel_id=1, source_target_pairs={{0,4},{4,0},{8,12},{12,8},{16,20},{20,16},{24,28},{28,24},{1,5},{5... | collective-permute-start | bytes 393224 | tf_op jit(solution)/shard_map/ppermute | solution.py:254
  7.7 11.1 %collective-permute-start.4 = (bf16[512,384]{1,0:T(8,128)(2,1)S(1)}, bf16[512,384]{1,0:T(8,128)(2,1)S(1)}, u32[]{:S(2)}, u32[]{:S(2)}) collective-permute-start(bf16[512,384]{1,0:T(8,128)(2,1)S(1)} %get-tuple-element.30.inner), channel_id=1, source_target_pairs={{0,2},{1,3},{2,0},{3,1},{4,5},{5,4},{6,7},{7,6},{8,10},{9,11},{10,... | collective-permute-start | bytes 1179656 | tf_op jit(solution)/shard_map/ppermute | solution.py:261
  13.3 8.7 %collective-permute-start.5 = (bf16[512,384]{1,0:T(8,128)(2,1)S(1)}, bf16[512,384]{1,0:T(8,128)(2,1)S(1)}, u32[]{:S(2)}, u32[]{:S(2)}) collective-permute-start(bf16[512,384]{1,0:T(8,128)(2,1)S(1)} %outer_image.1.outer), channel_id=1, source_target_pairs={{0,2},{1,3},{2,0},{3,1},{4,5},{5,4},{6,7},{7,6},{8,10},{9,11},{10,... | collective-permute-start | bytes 1179656 | tf_op jit(solution)/shard_map/ppermute | solution.py:261
  14.9 3.8 %collective-permute-start.1 = (s32[8,128,2]{1,2,0:T(2,128)S(1)}, s32[8,128,2]{1,2,0:T(2,128)S(1)}, u32[]{:S(2)}, u32[]{:S(2)}) collective-permute-start(s32[8,128,2]{1,2,0:T(2,128)S(1)} %copy-done.2), channel_id=1, source_target_pairs={{0,1},{1,0},{2,3},{3,2},{4,6},{5,7},{6,4},{7,5},{8,9},{9,8},{10,11... | collective-permute-start | bytes 24584 | tf_op jit(solution)/shard_map/ppermute | solution.py:261
  16.1 5.9 %collective-permute-start.6 = (bf16[128,384]{1,0:T(8,128)(2,1)S(1)}, bf16[128,384]{1,0:T(8,128)(2,1)S(1)}, u32[]{:S(2)}, u32[]{:S(2)}) collective-permute-start(bf16[128,384]{1,0:T(8,128)(2,1)S(1)} %get-tuple-element.38), channel_id=1, source_target_pairs={{0,28},{4,8},{8,4},{12,16},{16,12},{20,24},{24,20},{28,0},{1,29},{... | collective-permute-start | bytes 294920 | tf_op jit(solution)/shard_map/ppermute | solution.py:257
  18.7 3.3 %collective-permute-start.7 = (bf16[128,384]{1,0:T(8,128)(2,1)S(1)}, bf16[128,384]{1,0:T(8,128)(2,1)S(1)}, u32[]{:S(2)}, u32[]{:S(2)}) collective-permute-start(bf16[128,384]{1,0:T(8,128)(2,1)S(1)} %get-tuple-element.39), channel_id=1, source_target_pairs={{0,4},{4,0},{8,12},{12,8},{16,20},{20,16},{24,28},{28,24},{1,5},{5... | collective-permute-start | bytes 294920 | tf_op jit(solution)/shard_map/ppermute | solution.py:254
  22.8 11.4 %collective-permute-start.10 = (bf16[128,768]{1,0:T(8,128)(2,1)S(1)}, bf16[128,768]{1,0:T(8,128)(2,1)S(1)}, u32[]{:S(2)}, u32[]{:S(2)}) collective-permute-start(bf16[128,768]{1,0:T(8,128)(2,1)S(1)} %get-tuple-element.48), channel_id=1, source_target_pairs={{0,29},{1,28},{2,31},{3,30},{4,10},{5,11},{6,8},{7,9},{8,5},{9,4},... | collective-permute-start | bytes 589832 | tf_op jit(solution)/shard_map/ppermute | solution.py:261
  27.0 7.3 %collective-permute-start.12 = (bf16[128,768]{1,0:T(8,128)(2,1)S(1)}, bf16[128,768]{1,0:T(8,128)(2,1)S(1)}, u32[]{:S(2)}, u32[]{:S(2)}) collective-permute-start(bf16[128,768]{1,0:T(8,128)(2,1)S(1)} %get-tuple-element.50), channel_id=1, source_target_pairs={{0,1},{1,0},{2,3},{3,2},{4,6},{5,7},{6,4},{7,5},{8,9},{9,8},{10,11... | collective-permute-start | bytes 589832 | tf_op jit(solution)/shard_map/ppermute | solution.py:261
  27.5 6.7 %collective-permute-start.8 = (bf16[128,768]{1,0:T(8,128)(2,1)S(1)}, bf16[128,768]{1,0:T(8,128)(2,1)S(1)}, u32[]{:S(2)}, u32[]{:S(2)}) collective-permute-start(bf16[128,768]{1,0:T(8,128)(2,1)S(1)} %get-tuple-element.46), channel_id=1, source_target_pairs={{0,5},{1,4},{2,7},{3,6},{4,2},{5,3},{6,0},{7,1},{8,13},{9,12},{10,... | collective-permute-start | bytes 589832 | tf_op jit(solution)/shard_map/ppermute | solution.py:261
  27.5 6.7 %collective-permute-start.11 = (bf16[128,384]{1,0:T(8,128)(2,1)S(1)}, bf16[128,384]{1,0:T(8,128)(2,1)S(1)}, u32[]{:S(2)}, u32[]{:S(2)}) collective-permute-start(bf16[128,384]{1,0:T(8,128)(2,1)S(1)} %get-tuple-element.49), channel_id=1, source_target_pairs={{0,28},{4,8},{8,4},{12,16},{16,12},{20,24},{24,20},{28,0},{1,29},{... | collective-permute-start | bytes 294920 | tf_op jit(solution)/shard_map/ppermute | solution.py:257
  29.2 5.0 %collective-permute-start.9 = (bf16[128,384]{1,0:T(8,128)(2,1)S(1)}, bf16[128,384]{1,0:T(8,128)(2,1)S(1)}, u32[]{:S(2)}, u32[]{:S(2)}) collective-permute-start(bf16[128,384]{1,0:T(8,128)(2,1)S(1)} %get-tuple-element.47), channel_id=1, source_target_pairs={{0,4},{4,0},{8,12},{12,8},{16,20},{20,16},{24,28},{28,24},{1,5},{5... | collective-permute-start | bytes 294920 | tf_op jit(solution)/shard_map/ppermute | solution.py:254

commit v14 on v13

--- a/solution.py
+++ b/solution.py
@@ -184,7 +184,6 @@
 
 def late_tiles(
     part,
-    part_link,
     part_chip,
     far_base,
     near_base,
@@ -200,10 +199,9 @@
 ):
     wide = outer_r.shape[1]
     far[:, :wide] = part[...]
-    far_link[:, :wide] = part_link[...]
     far_chip[:, :wide] = part_chip[...]
     tile = far_base[...] + dot(far_outer[...], outer_r[...])
-    store_tile(tile, far.at[:, wide:], far_link.at[:, wide:], far_chip.at[:, wide:])
+    store_tile(tile, far.at[:, wide:], far_link, far_chip.at[:, wide:])
     store_tile(near_base[...] + dot(near_outer[...], outer_r[...]), near, near_link, near_chip)
 
 
@@ -337,16 +335,23 @@
         flops=2 * tile_flops,
         name="partner_tile",
     )
+    part_link = to_partner_link(part_link)
     outer_r, own_link, own_chip, far_base = lax.optimization_barrier((outer_r, own_link, own_chip, far_base))
     near, near_link, near_chip, far, far_link, far_chip = call(
         late_tiles,
-        (*tile_shapes(width, wide, F32), *(shape((width, 2 * wide), BF16),) * 3),
-        [VMEM] * 8,
+        (
+            *tile_shapes(width, wide, F32),
+            shape((width, 2 * wide), BF16),
+            shape((width, wide), BF16),
+            shape((width, 2 * wide), BF16),
+        ),
+        [VMEM] * 7,
         [VMEM] * 6,
-        (part, part_link, part_chip, far_base, near_base, far_outer, left_outer, outer_r),
+        (part, part_chip, far_base, near_base, far_outer, left_outer, outer_r),
         flops=tile_flops,
         name="late_tiles",
     )
+    far, part_link = lax.optimization_barrier((far, part_link))
     far_link = to_partner_link(far_link)
     near_link = over_link(near_link)
     far_chip = to(far_chip, lambda i: i ^ 1, partner)
@@ -369,8 +374,8 @@
 
     coarse = add((((0, 0), (0, 0, 0)),), (own_chip, own_link, own), "add_own")
     coarse = add(
-        (((3, 3), (1, 1, 1)), ((1, 2), (0, 0, 0)), ((2, 1), (0, 0, 0))),
-        (far_chip, near_chip, far_chip, far_link, near_link, far_link, far, far, near),
+        (((3, 3), (1, 0, 1)), ((1, 2), (0, 0, 0)), ((2, 1), (0, 0, 0))),
+        (far_chip, near_chip, far_chip, far_link, near_link, part_link, far, far, near),
         "add_rest",
         coarse,
     )

time: 35.4 us -> 41.4 us (1.17)
  starting transfers between devices: 16 us -> 21.8 us
    ppermute x7 -> x8, starting transfers between devices: 10.3 us -> 17.8 us  [to(): return lax.ppermute(value, ('blk', 'col'), perm)]
    ppermute x7 -> x8, waiting for transfers between devices: 1.51 us -> 6.17 us  [to(): return lax.ppermute(value, ('blk', 'col'), perm)]
    ppermute x3, waiting for transfers between devices: 10.2 us -> 5.72 us  [over_link(): return lax.ppermute(value, 'blk', cross)]
    ppermute x3, starting transfers between devices: 5.67 us -> 3.99 us  [over_link(): return lax.ppermute(value, 'blk', cross)]
  transfers between devices with their start and end apart: 13 -> 14, of which waited for: 4 -> 5; matrix products, arithmetic and copies ran while one was open for 0% -> 0% of each run, Pallas kernels for 16% -> 16%
where the time goes in v14:
time: 41.4 us; the launch traced here: 41.3 us
  starting transfers between devices  21.8 us (53%)
  waiting for transfers between devices  11.9 us (29%)
  Pallas kernels  7.46 us (18%)
    ppermute x8, starting transfers between devices, to(): return lax.ppermute(value, ('blk', 'col'), perm)  17.8 us
    pallas_call x7, Pallas kernels, call(): pl.pallas_call(kernel, out_shape=out_shape, in_specs=in_specs, out_specs=...  7.46 us
    ppermute x8, waiting for transfers between devices, to(): return lax.ppermute(value, ('blk', 'col'), perm)  6.17 us
    ppermute x3, waiting for transfers between devices, over_link(): return lax.ppermute(value, 'blk', cross)  5.72 us
    ppermute x3, starting transfers between devices, over_link(): return lax.ppermute(value, 'blk', cross)  3.99 us
  transfers between devices with their start and end apart: 14, of which 5 were waited for; matrix products, arithmetic and copies ran while one was open for 0% of the time, Pallas kernels for 16%

profile of v14, /device:TPU:0, one launch (start us, length us, event | category | flops | bytes accessed | tf_op | source)
XLA Modules:
  0.0 41.3 jit_solution(16071808385415130980)
XLA Ops:
  0.0 2.9 %collective-permute-start = (bf16[1024,3,128]{2,0,1:T(8,128)(2,1)}, bf16[1024,3,128]{2,0,1:T(8,128)(2,1)S(1)}, u32[]{:S(2)}, u32[]{:S(2)}) collective-permute-start(bf16[1024,3,128]{2,0,1:T(8,128)(2,1)} %param.6), channel_id=1, source_target_pairs={{0,1},{1,0},{2,3},{3,2},{4,6},{5,7},{6,4},{7,5},{8,9},{9,8},{10,11... | collective-permute-start | bytes 2359304 | tf_op jit(solution)/shard_map/ppermute | solution.py:259
  2.9 1.8 %mask_and_inner.1 = (bf16[1024,384]{1,0:T(8,128)(2,1)S(1)}, bf16[256,256]{1,0:T(8,128)(2,1)S(1)}, bf16[256,256]{1,0:T(8,128)(2,1)S(1)}, bf16[512,384]{1,0:T(8,128)(2,1)S(1)}) custom-call(s32[3,8]{1,0:T(4,128)} %bitcast.8, bf16[3,1024,128]{2,1,0:T(8,128)(2,1)} %bitcast.10, s32[8,2,128]{2,1,0:T(2,128)} %bitcast.11, bf16[8,3,128,128]{3,2,1,0:T(8,128)(2,1)} %stiffness.1), custom_call_target="tpu_custom_call" | custom-call | flops 150994944 | bytes 3022944 | tf_op jit(solution)/shard_map/mask_and_inner/pallas_call | solution.py:29
  4.8 0.0 copy-start.2
  4.8 2.9 %collective-permute-start.2 = (bf16[256,256]{1,0:T(8,128)(2,1)S(1)}, bf16[256,256]{1,0:T(8,128)(2,1)S(1)}, u32[]{:S(2)}, u32[]{:S(2)}) collective-permute-start(bf16[256,256]{1,0:T(8,128)(2,1)S(1)} %get-tuple-element.34), channel_id=1, source_target_pairs={{0,28},{4,8},{8,4},{12,16},{16,12},{20,24},{24,20},{28,0},{1,29},{... | collective-permute-start | bytes 393224 | tf_op jit(solution)/shard_map/ppermute | solution.py:255
  7.7 0.0 collective-permute-start.3
  7.7 0.5 %collective-permute-start.4 = (bf16[512,384]{1,0:T(8,128)(2,1)S(1)}, bf16[512,384]{1,0:T(8,128)(2,1)S(1)}, u32[]{:S(2)}, u32[]{:S(2)}) collective-permute-start(bf16[512,384]{1,0:T(8,128)(2,1)S(1)} %get-tuple-element.32.inner), channel_id=1, source_target_pairs={{0,2},{1,3},{2,0},{3,1},{4,5},{5,4},{6,7},{7,6},{8,10},{9,11},{10,... | collective-permute-start | bytes 1179656 | tf_op jit(solution)/shard_map/ppermute | solution.py:259
  8.2 4.0 %collective-permute-done.2.from_link = bf16[256,256]{1,0:T(8,128)(2,1)S(1)} collective-permute-done((bf16[256,256]{1,0:T(8,128)(2,1)S(1)}, bf16[256,256]{1,0:T(8,128)(2,1)S(1)}, u32[]{:S(2)}, u32[]{:S(2)}) %collective-permute-start.2) | collective-permute-done | bytes 131104 | tf_op jit(solution)/shard_map/ppermute | solution.py:255
  12.2 1.1 %outer_image.1.outer = bf16[512,384]{1,0:T(8,128)(2,1)S(1)} custom-call(s32[3,8]{1,0:T(4,128)S(1)} %bitcast.9, bf16[8,3,128,128]{3,2,1,0:T(8,128)(2,1)S(1)} %copy-done, bf16[1024,384]{1,0:T(8,128)(2,1)S(1)} %get-tuple-element.33.masked, bf16[256,256]{1,0:T(8,128)(2,1)S(1)} %collective-permute-done.2.from_link, ...), custom_call_target="tpu_custom_call" | custom-call | flops 150994944 | bytes 2228320 | tf_op jit(solution)/shard_map/outer_image/pallas_call | solution.py:29
  13.3 1.6 %collective-permute-start.5 = (bf16[512,384]{1,0:T(8,128)(2,1)S(1)}, bf16[512,384]{1,0:T(8,128)(2,1)S(1)}, u32[]{:S(2)}, u32[]{:S(2)}) collective-permute-start(bf16[512,384]{1,0:T(8,128)(2,1)S(1)} %outer_image.1.outer), channel_id=1, source_target_pairs={{0,2},{1,3},{2,0},{3,1},{4,5},{5,4},{6,7},{7,6},{8,10},{9,11},{10,... | collective-permute-start | bytes 1179656 | tf_op jit(solution)/shard_map/ppermute | solution.py:259
  14.9 0.5 %collective-permute-start.1 = (s32[8,128,2]{1,2,0:T(2,128)S(1)}, s32[8,128,2]{1,2,0:T(2,128)S(1)}, u32[]{:S(2)}, u32[]{:S(2)}) collective-permute-start(s32[8,128,2]{1,2,0:T(2,128)S(1)} %copy-done.2), channel_id=1, source_target_pairs={{0,1},{1,0},{2,3},{3,2},{4,6},{5,7},{6,4},{7,5},{8,9},{9,8},{10,11... | collective-permute-start | bytes 24584 | tf_op jit(solution)/shard_map/ppermute | solution.py:259
  15.4 0.6 %own_tile.1 = (f32[128,384]{1,0:T(8,128)S(1)}, bf16[128,384]{1,0:T(8,128)(2,1)S(1)}, bf16[128,384]{1,0:T(8,128)(2,1)S(1)}, bf16[384,512]{1,0:T(8,128)(2,1)S(1)}, bf16[384,512]{1,0:T(8,128)(2,1)S(1)}) custom-call(bf16[1024,384]{1,0:T(8,128)(2,1)S(1)} %get-tuple-element.33.masked, bf16[512,384]{1,0:T(8,128)(2,1)S(1)} %get-tuple-element.32.inner, ...), custom_call_target="tpu_custom_call" | custom-call | flops 301989888 | bytes 2752512 | tf_op jit(solution)/shard_map/own_tile/pallas_call | solution.py:29
  16.1 1.1 %collective-permute-start.6 = (bf16[128,384]{1,0:T(8,128)(2,1)S(1)}, bf16[128,384]{1,0:T(8,128)(2,1)S(1)}, u32[]{:S(2)}, u32[]{:S(2)}) collective-permute-start(bf16[128,384]{1,0:T(8,128)(2,1)S(1)} %get-tuple-element.39), channel_id=1, source_target_pairs={{0,28},{4,8},{8,4},{12,16},{16,12},{20,24},{24,20},{28,0},{1,29},{... | collective-permute-start | bytes 294920 | tf_op jit(solution)/shard_map/ppermute | solution.py:255
  17.2 1.5 %collective-permute-done.1 = s32[8,128,2]{1,2,0:T(2,128)S(1)} collective-permute-done((s32[8,128,2]{1,2,0:T(2,128)S(1)}, s32[8,128,2]{1,2,0:T(2,128)S(1)}, u32[]{:S(2)}, u32[]{:S(2)}) %collective-permute-start.1) | collective-permute-done | bytes 8224 | tf_op jit(solution)/shard_map/ppermute | solution.py:259
  18.7 1.3 %partner_tile.1 = (bf16[128,384]{1,0:T(8,128)(2,1)S(1)}, bf16[128,384]{1,0:T(8,128)(2,1)S(1)}, bf16[128,384]{1,0:T(8,128)(2,1)S(1)}, bf16[384,512]{1,0:T(8,128)(...) custom-call(bf16[3,1024,128]{2,1,0:T(8,128)(2,1)S(1)} %bitcast.6, s32[8,2,128]{2,1,0:T(2,128)S(1)} %bitcast.7, ...), custom_call_target="tpu_custom_call" | custom-call | flops 603979776 | bytes 4235264 | tf_op jit(solution)/shard_map/partner_tile/pallas_call | solution.py:29
  20.0 5.8 %collective-permute-start.12 = (bf16[128,384]{1,0:T(8,128)(2,1)S(1)}, bf16[128,384]{1,0:T(8,128)(2,1)S(1)}, u32[]{:S(2)}, u32[]{:S(2)}) collective-permute-start(bf16[128,384]{1,0:T(8,128)(2,1)S(1)} %get-tuple-element.52), channel_id=1, source_target_pairs={{0,29},{1,28},{2,31},{3,30},{4,10},{5,11},{6,8},{7,9},{8,5},{9,4},... | collective-permute-start | bytes 294920 | tf_op jit(solution)/shard_map/ppermute | solution.py:259
  25.8 0.8 %late_tiles.1 = (f32[128,384]{1,0:T(8,128)S(1)}, bf16[128,384]{1,0:T(8,128)(2,1)S(1)}, bf16[128,384]{1,0:T(8,128)(2,1)S(1)}, bf16[128,768]{1,0:T(8,128)(2,1)S(1)...) custom-call(bf16[128,384]{1,0:T(8,128)(2,1)S(1)} %get-tuple-element.37.part, ...), custom_call_target="tpu_custom_call" | custom-call | flops 301989888 | bytes 3440640 | tf_op jit(solution)/shard_map/late_tiles/pallas_call | solution.py:29
  26.6 0.1 collective-permute-start.8
  26.7 1.3 %collective-permute-done.12.refs_5_ = bf16[128,384]{1,0:T(8,128)(2,1)S(1)} collective-permute-done((bf16[128,384]{1,0:T(8,128)(2,1)S(1)}, bf16[128,384]{1,0:T(8,128)(2,1)S(1)}, u32[]{:S(2)}, u32[]{:S(2)}) %collective-permute-start.12) | collective-permute-done | bytes 98336 | tf_op jit(solution)/shard_map/ppermute | solution.py:259
  28.0 3.0 %collective-permute-start.13 = (bf16[128,768]{1,0:T(8,128)(2,1)S(1)}, bf16[128,768]{1,0:T(8,128)(2,1)S(1)}, u32[]{:S(2)}, u32[]{:S(2)}) collective-permute-start(bf16[128,768]{1,0:T(8,128)(2,1)S(1)} %get-tuple-element.54), channel_id=1, source_target_pairs={{0,1},{1,0},{2,3},{3,2},{4,6},{5,7},{6,4},{7,5},{8,9},{9,8},{10,11... | collective-permute-start | bytes 589832 | tf_op jit(solution)/shard_map/ppermute | solution.py:259
  31.0 3.4 %collective-permute-start.10 = (bf16[128,384]{1,0:T(8,128)(2,1)S(1)}, bf16[128,384]{1,0:T(8,128)(2,1)S(1)}, u32[]{:S(2)}, u32[]{:S(2)}) collective-permute-start(bf16[128,384]{1,0:T(8,128)(2,1)S(1)} %get-tuple-element.49), channel_id=1, source_target_pairs={{0,29},{1,28},{2,31},{3,30},{4,10},{5,11},{6,8},{7,9},{8,5},{9,4},... | collective-permute-start | bytes 294920 | tf_op jit(solution)/shard_map/ppermute | solution.py:259
  34.4 0.8 %add_own.1.refs_9_ = f32[5,128,512]{2,1,0:T(8,128)} custom-call(bf16[128,384]{1,0:T(8,128)(2,1)S(1)} %collective-permute-done.7.refs_0_, bf16[128,384]{1,0:T(8,128)(2,1)S(1)} %collective-permute-done.6.refs_1_, f32[128,384]{1,0:T(8,128)S(1)} %get-tuple-element.58.refs_2_), custom_call_target="tpu_custom_call" | custom-call | flops 81920 | bytes 1703936 | tf_op jit(solution)/shard_map/add_own/pallas_call | solution.py:29
  35.2 3.3 %collective-permute-done.10.refs_3_ = bf16[128,384]{1,0:T(8,128)(2,1)S(1)} collective-permute-done((bf16[128,384]{1,0:T(8,128)(2,1)S(1)}, bf16[128,384]{1,0:T(8,128)(2,1)S(1)}, u32[]{:S(2)}, u32[]{:S(2)}) %collective-permute-start.10) | collective-permute-done | bytes 98336 | tf_op jit(solution)/shard_map/ppermute | solution.py:259
  38.5 1.7 %collective-permute-done.11.refs_4_ = bf16[128,384]{1,0:T(8,128)(2,1)S(1)} collective-permute-done((bf16[128,384]{1,0:T(8,128)(2,1)S(1)}, bf16[128,384]{1,0:T(8,128)(2,1)S(1)}, u32[]{:S(2)}, u32[]{:S(2)}) %collective-permute-start.11) | collective-permute-done | bytes 98336 | tf_op jit(solution)/shard_map/ppermute | solution.py:255
  40.3 1.0 %add_rest.1 = f32[5,128,512]{2,1,0:T(8,128)} custom-call(bf16[128,768]{1,0:T(8,128)(2,1)S(1)} %collective-permute-done.8.refs_0_.refs_2_, bf16[128,384]{1,0:T(8,128)(2,1)S(1)} %collective-permute-done.9.refs_1_, bf16[128,768]{1,0:T(8,128)(2,1)S(1)} %collective-permute-done.8.refs_0_.refs_2_, ...), custom_call_target="tpu_custom_call", output_to_operand_aliasing={{}: (9, {})} | custom-call | flops 245760 | bytes 3997696 | tf_op jit(solution)/shard_map/add_rest/pallas_call | solution.py:29
  (17 shorter events, 0.0 us)
Async XLA Ops:
  0.0 12.2 %copy-start.1 = (s32[8,3]{0,1:T(4,128)S(1)}, s32[8,3]{0,1:T(4,128)}, u32[]{:S(2)}) copy-start(s32[8,3]{0,1:T(4,128)} %param.5) | copy-start | bytes 292
  0.0 12.2 %copy-start = (bf16[8,3,128,128]{3,2,1,0:T(8,128)(2,1)S(1)}, bf16[8,3,128,128]{3,2,1,0:T(8,128)(2,1)}, u32[]{:S(2)}) copy-start(bf16[8,3,128,128]{3,2,1,0:T(8,128)(2,1)} %stiffness.1) | copy-start | bytes 2359300
  0.0 18.7 %collective-permute-start = (bf16[1024,3,128]{2,0,1:T(8,128)(2,1)}, bf16[1024,3,128]{2,0,1:T(8,128)(2,1)S(1)}, u32[]{:S(2)}, u32[]{:S(2)}) collective-permute-start(bf16[1024,3,128]{2,0,1:T(8,128)(2,1)} %param.6), channel_id=1, source_target_pairs={{0,1},{1,0},{2,3},{3,2},{4,6},{5,7},{6,4},{7,5},{8,9},{9,8},{10,11... | collective-permute-start | bytes 2359304 | tf_op jit(solution)/shard_map/ppermute | solution.py:259
  4.8 10.1 %copy-start.2 = (s32[8,128,2]{1,2,0:T(2,128)S(1)}, s32[8,128,2]{1,2,0:T(2,128)}, u32[]{:S(2)}) copy-start(s32[8,128,2]{1,2,0:T(2,128)} %param.7) | copy-start | bytes 24580
  4.8 7.4 %collective-permute-start.2 = (bf16[256,256]{1,0:T(8,128)(2,1)S(1)}, bf16[256,256]{1,0:T(8,128)(2,1)S(1)}, u32[]{:S(2)}, u32[]{:S(2)}) collective-permute-start(bf16[256,256]{1,0:T(8,128)(2,1)S(1)} %get-tuple-element.34), channel_id=1, source_target_pairs={{0,28},{4,8},{8,4},{12,16},{16,12},{20,24},{24,20},{28,0},{1,29},{... | collective-permute-start | bytes 393224 | tf_op jit(solution)/shard_map/ppermute | solution.py:255
  7.7 4.5 %collective-permute-start.3 = (bf16[256,256]{1,0:T(8,128)(2,1)S(1)}, bf16[256,256]{1,0:T(8,128)(2,1)S(1)}, u32[]{:S(2)}, u32[]{:S(2)}) collective-permute-start(bf16[256,256]{1,0:T(8,128)(2,1)S(1)} %get-tuple-element.35), channel_id=1, source_target_pairs={{0,4},{4,0},{8,12},{12,8},{16,20},{20,16},{24,28},{28,24},{1,5},{5... | collective-permute-start | bytes 393224 | tf_op jit(solution)/shard_map/ppermute | solution.py:252
  7.7 11.1 %collective-permute-start.4 = (bf16[512,384]{1,0:T(8,128)(2,1)S(1)}, bf16[512,384]{1,0:T(8,128)(2,1)S(1)}, u32[]{:S(2)}, u32[]{:S(2)}) collective-permute-start(bf16[512,384]{1,0:T(8,128)(2,1)S(1)} %get-tuple-element.32.inner), channel_id=1, source_target_pairs={{0,2},{1,3},{2,0},{3,1},{4,5},{5,4},{6,7},{7,6},{8,10},{9,11},{10,... | collective-permute-start | bytes 1179656 | tf_op jit(solution)/shard_map/ppermute | solution.py:259
  13.3 12.5 %collective-permute-start.5 = (bf16[512,384]{1,0:T(8,128)(2,1)S(1)}, bf16[512,384]{1,0:T(8,128)(2,1)S(1)}, u32[]{:S(2)}, u32[]{:S(2)}) collective-permute-start(bf16[512,384]{1,0:T(8,128)(2,1)S(1)} %outer_image.1.outer), channel_id=1, source_target_pairs={{0,2},{1,3},{2,0},{3,1},{4,5},{5,4},{6,7},{7,6},{8,10},{9,11},{10,... | collective-permute-start | bytes 1179656 | tf_op jit(solution)/shard_map/ppermute | solution.py:259
  14.9 3.8 %collective-permute-start.1 = (s32[8,128,2]{1,2,0:T(2,128)S(1)}, s32[8,128,2]{1,2,0:T(2,128)S(1)}, u32[]{:S(2)}, u32[]{:S(2)}) collective-permute-start(s32[8,128,2]{1,2,0:T(2,128)S(1)} %copy-done.2), channel_id=1, source_target_pairs={{0,1},{1,0},{2,3},{3,2},{4,6},{5,7},{6,4},{7,5},{8,9},{9,8},{10,11... | collective-permute-start | bytes 24584 | tf_op jit(solution)/shard_map/ppermute | solution.py:259
  16.1 9.7 %collective-permute-start.6 = (bf16[128,384]{1,0:T(8,128)(2,1)S(1)}, bf16[128,384]{1,0:T(8,128)(2,1)S(1)}, u32[]{:S(2)}, u32[]{:S(2)}) collective-permute-start(bf16[128,384]{1,0:T(8,128)(2,1)S(1)} %get-tuple-element.39), channel_id=1, source_target_pairs={{0,28},{4,8},{8,4},{12,16},{16,12},{20,24},{24,20},{28,0},{1,29},{... | collective-permute-start | bytes 294920 | tf_op jit(solution)/shard_map/ppermute | solution.py:255
  18.7 7.1 %collective-permute-start.7 = (bf16[128,384]{1,0:T(8,128)(2,1)S(1)}, bf16[128,384]{1,0:T(8,128)(2,1)S(1)}, u32[]{:S(2)}, u32[]{:S(2)}) collective-permute-start(bf16[128,384]{1,0:T(8,128)(2,1)S(1)} %get-tuple-element.40), channel_id=1, source_target_pairs={{0,4},{4,0},{8,12},{12,8},{16,20},{20,16},{24,28},{28,24},{1,5},{5... | collective-permute-start | bytes 294920 | tf_op jit(solution)/shard_map/ppermute | solution.py:252
  20.0 8.0 %collective-permute-start.12 = (bf16[128,384]{1,0:T(8,128)(2,1)S(1)}, bf16[128,384]{1,0:T(8,128)(2,1)S(1)}, u32[]{:S(2)}, u32[]{:S(2)}) collective-permute-start(bf16[128,384]{1,0:T(8,128)(2,1)S(1)} %get-tuple-element.52), channel_id=1, source_target_pairs={{0,29},{1,28},{2,31},{3,30},{4,10},{5,11},{6,8},{7,9},{8,5},{9,4},... | collective-permute-start | bytes 294920 | tf_op jit(solution)/shard_map/ppermute | solution.py:259
  26.6 13.6 %collective-permute-start.8 = (bf16[128,768]{1,0:T(8,128)(2,1)S(1)}, bf16[128,768]{1,0:T(8,128)(2,1)S(1)}, u32[]{:S(2)}, u32[]{:S(2)}) collective-permute-start(bf16[128,768]{1,0:T(8,128)(2,1)S(1)} %get-tuple-element.47), channel_id=1, source_target_pairs={{0,5},{1,4},{2,7},{3,6},{4,2},{5,3},{6,0},{7,1},{8,13},{9,12},{10,... | collective-permute-start | bytes 589832 | tf_op jit(solution)/shard_map/ppermute | solution.py:259
  28.0 12.2 %collective-permute-start.13 = (bf16[128,768]{1,0:T(8,128)(2,1)S(1)}, bf16[128,768]{1,0:T(8,128)(2,1)S(1)}, u32[]{:S(2)}, u32[]{:S(2)}) collective-permute-start(bf16[128,768]{1,0:T(8,128)(2,1)S(1)} %get-tuple-element.54), channel_id=1, source_target_pairs={{0,1},{1,0},{2,3},{3,2},{4,6},{5,7},{6,4},{7,5},{8,9},{9,8},{10,11... | collective-permute-start | bytes 589832 | tf_op jit(solution)/shard_map/ppermute | solution.py:259
  31.0 7.5 %collective-permute-start.10 = (bf16[128,384]{1,0:T(8,128)(2,1)S(1)}, bf16[128,384]{1,0:T(8,128)(2,1)S(1)}, u32[]{:S(2)}, u32[]{:S(2)}) collective-permute-start(bf16[128,384]{1,0:T(8,128)(2,1)S(1)} %get-tuple-element.49), channel_id=1, source_target_pairs={{0,29},{1,28},{2,31},{3,30},{4,10},{5,11},{6,8},{7,9},{8,5},{9,4},... | collective-permute-start | bytes 294920 | tf_op jit(solution)/shard_map/ppermute | solution.py:259
  34.4 5.8 %collective-permute-start.11 = (bf16[128,384]{1,0:T(8,128)(2,1)S(1)}, bf16[128,384]{1,0:T(8,128)(2,1)S(1)}, u32[]{:S(2)}, u32[]{:S(2)}) collective-permute-start(bf16[128,384]{1,0:T(8,128)(2,1)S(1)} %get-tuple-element.50), channel_id=1, source_target_pairs={{0,28},{4,8},{8,4},{12,16},{16,12},{20,24},{24,20},{28,0},{1,29},{... | collective-permute-start | bytes 294920 | tf_op jit(solution)/shard_map/ppermute | solution.py:255
  34.4 5.8 %collective-permute-start.9 = (bf16[128,384]{1,0:T(8,128)(2,1)S(1)}, bf16[128,384]{1,0:T(8,128)(2,1)S(1)}, u32[]{:S(2)}, u32[]{:S(2)}) collective-permute-start(bf16[128,384]{1,0:T(8,128)(2,1)S(1)} %get-tuple-element.48), channel_id=1, source_target_pairs={{0,4},{4,0},{8,12},{12,8},{16,20},{20,16},{24,28},{28,24},{1,5},{5... | collective-permute-start | bytes 294920 | tf_op jit(solution)/shard_map/ppermute | solution.py:252

commit v15 on v13

--- a/solution.py
+++ b/solution.py
@@ -216,7 +216,7 @@
     even = parity() == 0
     copies = []
     for n, ((even_step, odd_step), chunks) in enumerate(steps):
-        chip, link, own = (
+        link, own, chip = (
             terms[n + k * count][:, m * 3 * width : (m + 1) * 3 * width].astype(F32) for k, m in enumerate(chunks)
         )
         prev = jnp.where(even, link, chip)
@@ -367,10 +367,10 @@
             name=name,
         )
 
-    coarse = add((((0, 0), (0, 0, 0)),), (own_chip, own_link, own), "add_own")
+    coarse = add((((0, 0), (0, 0, 0)),), (own_link, own, own_chip), "add_own")
     coarse = add(
         (((3, 3), (1, 1, 1)), ((1, 2), (0, 0, 0)), ((2, 1), (0, 0, 0))),
-        (far_chip, near_chip, far_chip, far_link, near_link, far_link, far, far, near),
+        (far_link, near_link, far_link, far, far, near, far_chip, near_chip, far_chip),
         "add_rest",
         coarse,
     )

time: 35.4 us -> 37.3 us (1.054)
  waiting for transfers between devices: 11.7 us -> 13.7 us
    ppermute x3, waiting for transfers between devices: 10.2 us -> 12.2 us  [over_link(): return lax.ppermute(value, 'blk', cross)]
    ppermute x3, starting transfers between devices: 5.67 us -> 4.66 us  [over_link(): return lax.ppermute(value, 'blk', cross)]
    ppermute x7, starting transfers between devices: 10.3 us -> 11.2 us  [to(): return lax.ppermute(value, ('blk', 'col'), perm)]
  transfers between devices with their start and end apart: 13 -> 13, of which waited for: 4 -> 4; matrix products, arithmetic and copies ran while one was open for 0% -> 0% of each run, Pallas kernels for 16% -> 15%
where the time goes in v15:
time: 37.3 us; the launch traced here: 37.1 us
  starting transfers between devices  15.9 us (43%)
  waiting for transfers between devices  13.7 us (37%)
  Pallas kernels  7.47 us (20%)
    ppermute x3, waiting for transfers between devices, over_link(): return lax.ppermute(value, 'blk', cross)  12.2 us
    ppermute x7, starting transfers between devices, to(): return lax.ppermute(value, ('blk', 'col'), perm)  11.2 us
    pallas_call x7, Pallas kernels, call(): pl.pallas_call(kernel, out_shape=out_shape, in_specs=in_specs, out_specs=...  7.47 us
    ppermute x3, starting transfers between devices, over_link(): return lax.ppermute(value, 'blk', cross)  4.66 us
    ppermute x7, waiting for transfers between devices, to(): return lax.ppermute(value, ('blk', 'col'), perm)  1.51 us
  transfers between devices with their start and end apart: 13, of which 4 were waited for; matrix products, arithmetic and copies ran while one was open for 0% of the time, Pallas kernels for 15%

profile of v15, /device:TPU:0, one launch (start us, length us, event | category | flops | bytes accessed | tf_op | source)
XLA Modules:
  0.0 37.1 jit_solution(13888625591327441236)
XLA Ops:
  0.0 2.9 %collective-permute-start = (bf16[1024,3,128]{2,0,1:T(8,128)(2,1)}, bf16[1024,3,128]{2,0,1:T(8,128)(2,1)S(1)}, u32[]{:S(2)}, u32[]{:S(2)}) collective-permute-start(bf16[1024,3,128]{2,0,1:T(8,128)(2,1)} %param.6), channel_id=1, source_target_pairs={{0,1},{1,0},{2,3},{3,2},{4,6},{5,7},{6,4},{7,5},{8,9},{9,8},{10,11... | collective-permute-start | bytes 2359304 | tf_op jit(solution)/shard_map/ppermute | solution.py:261
  2.9 1.8 %mask_and_inner.1 = (bf16[1024,384]{1,0:T(8,128)(2,1)S(1)}, bf16[256,256]{1,0:T(8,128)(2,1)S(1)}, bf16[256,256]{1,0:T(8,128)(2,1)S(1)}, bf16[512,384]{1,0:T(8,128)(2,1)S(1)}) custom-call(s32[3,8]{1,0:T(4,128)} %bitcast.8, bf16[3,1024,128]{2,1,0:T(8,128)(2,1)} %bitcast.10, s32[8,2,128]{2,1,0:T(2,128)} %bitcast.11, bf16[8,3,128,128]{3,2,1,0:T(8,128)(2,1)} %stiffness.1), custom_call_target="tpu_custom_call" | custom-call | flops 150994944 | bytes 3022944 | tf_op jit(solution)/shard_map/mask_and_inner/pallas_call | solution.py:29
  4.8 0.0 copy-start.2
  4.8 2.9 %collective-permute-start.2 = (bf16[256,256]{1,0:T(8,128)(2,1)S(1)}, bf16[256,256]{1,0:T(8,128)(2,1)S(1)}, u32[]{:S(2)}, u32[]{:S(2)}) collective-permute-start(bf16[256,256]{1,0:T(8,128)(2,1)S(1)} %get-tuple-element.32), channel_id=1, source_target_pairs={{0,28},{4,8},{8,4},{12,16},{16,12},{20,24},{24,20},{28,0},{1,29},{... | collective-permute-start | bytes 393224 | tf_op jit(solution)/shard_map/ppermute | solution.py:257
  7.7 0.0 collective-permute-start.3
  7.7 0.5 %collective-permute-start.4 = (bf16[512,384]{1,0:T(8,128)(2,1)S(1)}, bf16[512,384]{1,0:T(8,128)(2,1)S(1)}, u32[]{:S(2)}, u32[]{:S(2)}) collective-permute-start(bf16[512,384]{1,0:T(8,128)(2,1)S(1)} %get-tuple-element.30.inner), channel_id=1, source_target_pairs={{0,2},{1,3},{2,0},{3,1},{4,5},{5,4},{6,7},{7,6},{8,10},{9,11},{10,... | collective-permute-start | bytes 1179656 | tf_op jit(solution)/shard_map/ppermute | solution.py:261
  8.2 4.0 %collective-permute-done.2.from_link = bf16[256,256]{1,0:T(8,128)(2,1)S(1)} collective-permute-done((bf16[256,256]{1,0:T(8,128)(2,1)S(1)}, bf16[256,256]{1,0:T(8,128)(2,1)S(1)}, u32[]{:S(2)}, u32[]{:S(2)}) %collective-permute-start.2) | collective-permute-done | bytes 131104 | tf_op jit(solution)/shard_map/ppermute | solution.py:257
  12.2 1.1 %outer_image.1.outer = bf16[512,384]{1,0:T(8,128)(2,1)S(1)} custom-call(s32[3,8]{1,0:T(4,128)S(1)} %bitcast.9, bf16[8,3,128,128]{3,2,1,0:T(8,128)(2,1)S(1)} %copy-done, bf16[1024,384]{1,0:T(8,128)(2,1)S(1)} %get-tuple-element.31.masked, bf16[256,256]{1,0:T(8,128)(2,1)S(1)} %collective-permute-done.2.from_link, ...), custom_call_target="tpu_custom_call" | custom-call | flops 150994944 | bytes 2228320 | tf_op jit(solution)/shard_map/outer_image/pallas_call | solution.py:29
  13.3 1.6 %collective-permute-start.5 = (bf16[512,384]{1,0:T(8,128)(2,1)S(1)}, bf16[512,384]{1,0:T(8,128)(2,1)S(1)}, u32[]{:S(2)}, u32[]{:S(2)}) collective-permute-start(bf16[512,384]{1,0:T(8,128)(2,1)S(1)} %outer_image.1.outer), channel_id=1, source_target_pairs={{0,2},{1,3},{2,0},{3,1},{4,5},{5,4},{6,7},{7,6},{8,10},{9,11},{10,... | collective-permute-start | bytes 1179656 | tf_op jit(solution)/shard_map/ppermute | solution.py:261
  14.9 0.5 %collective-permute-start.1 = (s32[8,128,2]{1,2,0:T(2,128)S(1)}, s32[8,128,2]{1,2,0:T(2,128)S(1)}, u32[]{:S(2)}, u32[]{:S(2)}) collective-permute-start(s32[8,128,2]{1,2,0:T(2,128)S(1)} %copy-done.2), channel_id=1, source_target_pairs={{0,1},{1,0},{2,3},{3,2},{4,6},{5,7},{6,4},{7,5},{8,9},{9,8},{10,11... | collective-permute-start | bytes 24584 | tf_op jit(solution)/shard_map/ppermute | solution.py:261
  15.4 0.6 %own_tile.1 = (f32[128,384]{1,0:T(8,128)S(1)}, bf16[128,384]{1,0:T(8,128)(2,1)S(1)}, bf16[128,384]{1,0:T(8,128)(2,1)S(1)}, bf16[384,512]{1,0:T(8,128)(2,1)S(1)}, bf16[384,512]{1,0:T(8,128)(2,1)S(1)}) custom-call(bf16[1024,384]{1,0:T(8,128)(2,1)S(1)} %get-tuple-element.31.masked, bf16[512,384]{1,0:T(8,128)(2,1)S(1)} %get-tuple-element.30.inner, ...), custom_call_target="tpu_custom_call" | custom-call | flops 301989888 | bytes 2752512 | tf_op jit(solution)/shard_map/own_tile/pallas_call | solution.py:29
  16.1 1.1 %collective-permute-start.6 = (bf16[128,384]{1,0:T(8,128)(2,1)S(1)}, bf16[128,384]{1,0:T(8,128)(2,1)S(1)}, u32[]{:S(2)}, u32[]{:S(2)}) collective-permute-start(bf16[128,384]{1,0:T(8,128)(2,1)S(1)} %get-tuple-element.38), channel_id=1, source_target_pairs={{0,28},{4,8},{8,4},{12,16},{16,12},{20,24},{24,20},{28,0},{1,29},{... | collective-permute-start | bytes 294920 | tf_op jit(solution)/shard_map/ppermute | solution.py:257
  17.2 1.5 %collective-permute-done.1 = s32[8,128,2]{1,2,0:T(2,128)S(1)} collective-permute-done((s32[8,128,2]{1,2,0:T(2,128)S(1)}, s32[8,128,2]{1,2,0:T(2,128)S(1)}, u32[]{:S(2)}, u32[]{:S(2)}) %collective-permute-start.1) | collective-permute-done | bytes 8224 | tf_op jit(solution)/shard_map/ppermute | solution.py:261
  18.7 0.0 collective-permute-start.7
  18.7 1.3 %partner_tile.1 = (bf16[128,384]{1,0:T(8,128)(2,1)S(1)}, bf16[128,384]{1,0:T(8,128)(2,1)S(1)}, bf16[128,384]{1,0:T(8,128)(2,1)S(1)}, bf16[384,512]{1,0:T(8,128)(...) custom-call(bf16[3,1024,128]{2,1,0:T(8,128)(2,1)S(1)} %bitcast.6, s32[8,2,128]{2,1,0:T(2,128)S(1)} %bitcast.7, ...), custom_call_target="tpu_custom_call" | custom-call | flops 603979776 | bytes 4235264 | tf_op jit(solution)/shard_map/partner_tile/pallas_call | solution.py:29
  20.0 2.0 %collective-permute-done.6.refs_0_ = bf16[128,384]{1,0:T(8,128)(2,1)S(1)} collective-permute-done((bf16[128,384]{1,0:T(8,128)(2,1)S(1)}, bf16[128,384]{1,0:T(8,128)(2,1)S(1)}, u32[]{:S(2)}, u32[]{:S(2)}) %collective-permute-start.6) | collective-permute-done | bytes 98336 | tf_op jit(solution)/shard_map/ppermute | solution.py:257
  22.0 0.8 %late_tiles.1 = (f32[128,384]{1,0:T(8,128)S(1)}, bf16[128,384]{1,0:T(8,128)(2,1)S(1)}, bf16[128,384]{1,0:T(8,128)(2,1)S(1)}, bf16[128,768]{1,0:T(8,128)(2,1)S(1)...) custom-call(bf16[128,384]{1,0:T(8,128)(2,1)S(1)} %get-tuple-element.35.part, ...), custom_call_target="tpu_custom_call" | custom-call | flops 301989888 | bytes 3637248 | tf_op jit(solution)/shard_map/late_tiles/pallas_call | solution.py:29
  22.8 1.6 %collective-permute-start.10 = (bf16[128,768]{1,0:T(8,128)(2,1)S(1)}, bf16[128,768]{1,0:T(8,128)(2,1)S(1)}, u32[]{:S(2)}, u32[]{:S(2)}) collective-permute-start(bf16[128,768]{1,0:T(8,128)(2,1)S(1)} %get-tuple-element.48), channel_id=1, source_target_pairs={{0,1},{1,0},{2,3},{3,2},{4,6},{5,7},{6,4},{7,5},{8,9},{9,8},{10,11... | collective-permute-start | bytes 589832 | tf_op jit(solution)/shard_map/ppermute | solution.py:261
  24.3 0.8 %collective-permute-start.11 = (bf16[128,768]{1,0:T(8,128)(2,1)S(1)}, bf16[128,768]{1,0:T(8,128)(2,1)S(1)}, u32[]{:S(2)}, u32[]{:S(2)}) collective-permute-start(bf16[128,768]{1,0:T(8,128)(2,1)S(1)} %get-tuple-element.50), channel_id=1, source_target_pairs={{0,5},{1,4},{2,7},{3,6},{4,2},{5,3},{6,0},{7,1},{8,13},{9,12},{10,... | collective-permute-start | bytes 589832 | tf_op jit(solution)/shard_map/ppermute | solution.py:261
  25.2 3.2 %collective-permute-start.8 = (bf16[128,768]{1,0:T(8,128)(2,1)S(1)}, bf16[128,768]{1,0:T(8,128)(2,1)S(1)}, u32[]{:S(2)}, u32[]{:S(2)}) collective-permute-start(bf16[128,768]{1,0:T(8,128)(2,1)S(1)} %get-tuple-element.46), channel_id=1, source_target_pairs={{0,29},{1,28},{2,31},{3,30},{4,10},{5,11},{6,8},{7,9},{8,5},{9,4},... | collective-permute-start | bytes 589832 | tf_op jit(solution)/shard_map/ppermute | solution.py:261
  28.4 0.7 %collective-permute-start.9 = (bf16[128,384]{1,0:T(8,128)(2,1)S(1)}, bf16[128,384]{1,0:T(8,128)(2,1)S(1)}, u32[]{:S(2)}, u32[]{:S(2)}) collective-permute-start(bf16[128,384]{1,0:T(8,128)(2,1)S(1)} %get-tuple-element.47), channel_id=1, source_target_pairs={{0,28},{4,8},{8,4},{12,16},{16,12},{20,24},{24,20},{28,0},{1,29},{... | collective-permute-start | bytes 294920 | tf_op jit(solution)/shard_map/ppermute | solution.py:257
  29.1 0.8 %add_own.1.refs_9_ = f32[5,128,512]{2,1,0:T(8,128)} custom-call(bf16[128,384]{1,0:T(8,128)(2,1)S(1)} %collective-permute-done.6.refs_0_, f32[128,384]{1,0:T(8,128)S(1)} %get-tuple-element.53.refs_1_, bf16[128,384]{1,0:T(8,128)(2,1)S(1)} %collective-permute-done.7.refs_2_), custom_call_target="tpu_custom_call" | custom-call | flops 81920 | bytes 1703936 | tf_op jit(solution)/shard_map/add_own/pallas_call | solution.py:29
  29.9 6.2 %collective-permute-done.9.refs_1_ = bf16[128,384]{1,0:T(8,128)(2,1)S(1)} collective-permute-done((bf16[128,384]{1,0:T(8,128)(2,1)S(1)}, bf16[128,384]{1,0:T(8,128)(2,1)S(1)}, u32[]{:S(2)}, u32[]{:S(2)}) %collective-permute-start.9) | collective-permute-done | bytes 98336 | tf_op jit(solution)/shard_map/ppermute | solution.py:257
  36.1 1.0 %add_rest.1 = f32[5,128,512]{2,1,0:T(8,128)} custom-call(bf16[128,768]{1,0:T(8,128)(2,1)S(1)} %collective-permute-done.8.refs_0_.refs_2_, bf16[128,384]{1,0:T(8,128)(2,1)S(1)} %collective-permute-done.9.refs_1_, bf16[128,768]{1,0:T(8,128)(2,1)S(1)} %collective-permute-done.8.refs_0_.refs_2_, ...), custom_call_target="tpu_custom_call", output_to_operand_aliasing={{}: (9, {})} | custom-call | flops 245760 | bytes 4194304 | tf_op jit(solution)/shard_map/add_rest/pallas_call | solution.py:29
  (15 shorter events, 0.0 us)
Async XLA Ops:
  0.0 12.2 %copy-start.1 = (s32[8,3]{0,1:T(4,128)S(1)}, s32[8,3]{0,1:T(4,128)}, u32[]{:S(2)}) copy-start(s32[8,3]{0,1:T(4,128)} %param.5) | copy-start | bytes 292
  0.0 12.2 %copy-start = (bf16[8,3,128,128]{3,2,1,0:T(8,128)(2,1)S(1)}, bf16[8,3,128,128]{3,2,1,0:T(8,128)(2,1)}, u32[]{:S(2)}) copy-start(bf16[8,3,128,128]{3,2,1,0:T(8,128)(2,1)} %stiffness.1) | copy-start | bytes 2359300
  0.0 18.7 %collective-permute-start = (bf16[1024,3,128]{2,0,1:T(8,128)(2,1)}, bf16[1024,3,128]{2,0,1:T(8,128)(2,1)S(1)}, u32[]{:S(2)}, u32[]{:S(2)}) collective-permute-start(bf16[1024,3,128]{2,0,1:T(8,128)(2,1)} %param.6), channel_id=1, source_target_pairs={{0,1},{1,0},{2,3},{3,2},{4,6},{5,7},{6,4},{7,5},{8,9},{9,8},{10,11... | collective-permute-start | bytes 2359304 | tf_op jit(solution)/shard_map/ppermute | solution.py:261
  4.8 10.1 %copy-start.2 = (s32[8,128,2]{1,2,0:T(2,128)S(1)}, s32[8,128,2]{1,2,0:T(2,128)}, u32[]{:S(2)}) copy-start(s32[8,128,2]{1,2,0:T(2,128)} %param.7) | copy-start | bytes 24580
  4.8 7.4 %collective-permute-start.2 = (bf16[256,256]{1,0:T(8,128)(2,1)S(1)}, bf16[256,256]{1,0:T(8,128)(2,1)S(1)}, u32[]{:S(2)}, u32[]{:S(2)}) collective-permute-start(bf16[256,256]{1,0:T(8,128)(2,1)S(1)} %get-tuple-element.32), channel_id=1, source_target_pairs={{0,28},{4,8},{8,4},{12,16},{16,12},{20,24},{24,20},{28,0},{1,29},{... | collective-permute-start | bytes 393224 | tf_op jit(solution)/shard_map/ppermute | solution.py:257
  7.7 4.5 %collective-permute-start.3 = (bf16[256,256]{1,0:T(8,128)(2,1)S(1)}, bf16[256,256]{1,0:T(8,128)(2,1)S(1)}, u32[]{:S(2)}, u32[]{:S(2)}) collective-permute-start(bf16[256,256]{1,0:T(8,128)(2,1)S(1)} %get-tuple-element.33), channel_id=1, source_target_pairs={{0,4},{4,0},{8,12},{12,8},{16,20},{20,16},{24,28},{28,24},{1,5},{5... | collective-permute-start | bytes 393224 | tf_op jit(solution)/shard_map/ppermute | solution.py:254
  7.7 11.1 %collective-permute-start.4 = (bf16[512,384]{1,0:T(8,128)(2,1)S(1)}, bf16[512,384]{1,0:T(8,128)(2,1)S(1)}, u32[]{:S(2)}, u32[]{:S(2)}) collective-permute-start(bf16[512,384]{1,0:T(8,128)(2,1)S(1)} %get-tuple-element.30.inner), channel_id=1, source_target_pairs={{0,2},{1,3},{2,0},{3,1},{4,5},{5,4},{6,7},{7,6},{8,10},{9,11},{10,... | collective-permute-start | bytes 1179656 | tf_op jit(solution)/shard_map/ppermute | solution.py:261
  13.3 8.7 %collective-permute-start.5 = (bf16[512,384]{1,0:T(8,128)(2,1)S(1)}, bf16[512,384]{1,0:T(8,128)(2,1)S(1)}, u32[]{:S(2)}, u32[]{:S(2)}) collective-permute-start(bf16[512,384]{1,0:T(8,128)(2,1)S(1)} %outer_image.1.outer), channel_id=1, source_target_pairs={{0,2},{1,3},{2,0},{3,1},{4,5},{5,4},{6,7},{7,6},{8,10},{9,11},{10,... | collective-permute-start | bytes 1179656 | tf_op jit(solution)/shard_map/ppermute | solution.py:261
  14.9 3.8 %collective-permute-start.1 = (s32[8,128,2]{1,2,0:T(2,128)S(1)}, s32[8,128,2]{1,2,0:T(2,128)S(1)}, u32[]{:S(2)}, u32[]{:S(2)}) collective-permute-start(s32[8,128,2]{1,2,0:T(2,128)S(1)} %copy-done.2), channel_id=1, source_target_pairs={{0,1},{1,0},{2,3},{3,2},{4,6},{5,7},{6,4},{7,5},{8,9},{9,8},{10,11... | collective-permute-start | bytes 24584 | tf_op jit(solution)/shard_map/ppermute | solution.py:261
  16.1 5.9 %collective-permute-start.6 = (bf16[128,384]{1,0:T(8,128)(2,1)S(1)}, bf16[128,384]{1,0:T(8,128)(2,1)S(1)}, u32[]{:S(2)}, u32[]{:S(2)}) collective-permute-start(bf16[128,384]{1,0:T(8,128)(2,1)S(1)} %get-tuple-element.38), channel_id=1, source_target_pairs={{0,28},{4,8},{8,4},{12,16},{16,12},{20,24},{24,20},{28,0},{1,29},{... | collective-permute-start | bytes 294920 | tf_op jit(solution)/shard_map/ppermute | solution.py:257
  18.7 3.3 %collective-permute-start.7 = (bf16[128,384]{1,0:T(8,128)(2,1)S(1)}, bf16[128,384]{1,0:T(8,128)(2,1)S(1)}, u32[]{:S(2)}, u32[]{:S(2)}) collective-permute-start(bf16[128,384]{1,0:T(8,128)(2,1)S(1)} %get-tuple-element.39), channel_id=1, source_target_pairs={{0,4},{4,0},{8,12},{12,8},{16,20},{20,16},{24,28},{28,24},{1,5},{5... | collective-permute-start | bytes 294920 | tf_op jit(solution)/shard_map/ppermute | solution.py:254
  22.8 13.3 %collective-permute-start.10 = (bf16[128,768]{1,0:T(8,128)(2,1)S(1)}, bf16[128,768]{1,0:T(8,128)(2,1)S(1)}, u32[]{:S(2)}, u32[]{:S(2)}) collective-permute-start(bf16[128,768]{1,0:T(8,128)(2,1)S(1)} %get-tuple-element.48), channel_id=1, source_target_pairs={{0,1},{1,0},{2,3},{3,2},{4,6},{5,7},{6,4},{7,5},{8,9},{9,8},{10,11... | collective-permute-start | bytes 589832 | tf_op jit(solution)/shard_map/ppermute | solution.py:261
  24.3 11.8 %collective-permute-start.11 = (bf16[128,768]{1,0:T(8,128)(2,1)S(1)}, bf16[128,768]{1,0:T(8,128)(2,1)S(1)}, u32[]{:S(2)}, u32[]{:S(2)}) collective-permute-start(bf16[128,768]{1,0:T(8,128)(2,1)S(1)} %get-tuple-element.50), channel_id=1, source_target_pairs={{0,5},{1,4},{2,7},{3,6},{4,2},{5,3},{6,0},{7,1},{8,13},{9,12},{10,... | collective-permute-start | bytes 589832 | tf_op jit(solution)/shard_map/ppermute | solution.py:261
  25.2 10.9 %collective-permute-start.8 = (bf16[128,768]{1,0:T(8,128)(2,1)S(1)}, bf16[128,768]{1,0:T(8,128)(2,1)S(1)}, u32[]{:S(2)}, u32[]{:S(2)}) collective-permute-start(bf16[128,768]{1,0:T(8,128)(2,1)S(1)} %get-tuple-element.46), channel_id=1, source_target_pairs={{0,29},{1,28},{2,31},{3,30},{4,10},{5,11},{6,8},{7,9},{8,5},{9,4},... | collective-permute-start | bytes 589832 | tf_op jit(solution)/shard_map/ppermute | solution.py:261
  28.4 1.5 %collective-permute-start.12 = (bf16[128,384]{1,0:T(8,128)(2,1)S(1)}, bf16[128,384]{1,0:T(8,128)(2,1)S(1)}, u32[]{:S(2)}, u32[]{:S(2)}) collective-permute-start(bf16[128,384]{1,0:T(8,128)(2,1)S(1)} %get-tuple-element.51), channel_id=1, source_target_pairs={{0,4},{4,0},{8,12},{12,8},{16,20},{20,16},{24,28},{28,24},{1,5},{5... | collective-permute-start | bytes 294920 | tf_op jit(solution)/shard_map/ppermute | solution.py:254
  28.4 7.7 %collective-permute-start.9 = (bf16[128,384]{1,0:T(8,128)(2,1)S(1)}, bf16[128,384]{1,0:T(8,128)(2,1)S(1)}, u32[]{:S(2)}, u32[]{:S(2)}) collective-permute-start(bf16[128,384]{1,0:T(8,128)(2,1)S(1)} %get-tuple-element.47), channel_id=1, source_target_pairs={{0,28},{4,8},{8,4},{12,16},{16,12},{20,24},{24,20},{28,0},{1,29},{... | collective-permute-start | bytes 294920 | tf_op jit(solution)/shard_map/ppermute | solution.py:257

commit v16 on v15

--- a/solution.py
+++ b/solution.py
@@ -208,22 +208,21 @@
 
 
 def add_tiles(steps, *refs):
-    count = len(steps)
-    terms = refs[: 3 * count]
     coarse, total, sem = refs[-3:]
     width = total.shape[2]
     me = lax.axis_index("col")
     even = parity() == 0
     copies = []
-    for n, ((even_step, odd_step), chunks) in enumerate(steps):
-        link, own, chip = (
-            terms[n + k * count][:, m * 3 * width : (m + 1) * 3 * width].astype(F32) for k, m in enumerate(chunks)
-        )
-        prev = jnp.where(even, link, chip)
-        nxt = jnp.where(even, chip, link)
+    for n, ((even_step, odd_step), terms, chunks) in enumerate(steps):
+        own, *others = (refs[k][:, m * 3 * width : (m + 1) * 3 * width].astype(F32) for k, m in zip(terms, chunks))
+        if others:
+            chip, link = others
+            placed = ((0, jnp.where(even, link, chip)), (1, own), (2, jnp.where(even, chip, link)))
+        else:
+            placed = ((1, own),)
         for d in range(5):
-            value = None
-            for offset, term in ((0, prev), (1, own), (2, nxt)):
+            value = None if others else refs[terms[1]][:, d * width : (d + 1) * width]
+            for offset, term in placed:
                 if 0 <= d - offset <= 2:
                     part = term[:, (d - offset) * width : (d - offset + 1) * width]
                     value = part if value is None else value + part
@@ -235,6 +234,16 @@
         copies.append(copy)
     for copy in copies:
         copy.wait()
+
+
+def join_terms(link, chip, joined):
+    even = parity() == 0
+    width = chip.shape[0]
+    prev = jnp.where(even, link[...], chip[...]).astype(F32)
+    nxt = jnp.where(even, chip[...], link[...]).astype(F32)
+    joined[:, : 2 * width] = prev[:, : 2 * width]
+    joined[:, 2 * width : 3 * width] = prev[:, 2 * width :] + nxt[:, :width]
+    joined[:, 3 * width :] = nxt[:, width:]
 
 
 def tile_shapes(width, wide, own):
@@ -367,10 +376,19 @@
             name=name,
         )
 
-    coarse = add((((0, 0), (0, 0, 0)),), (own_link, own, own_chip), "add_own")
+    joined = call(
+        join_terms,
+        shape((width, 5 * width), F32),
+        [VMEM] * 2,
+        VMEM,
+        (near_link, near_chip),
+        flops=int(3e9),
+        name="join_terms",
+    )
+    coarse = add((((0, 0), (2, 0, 1), (0, 0, 0)),), (own_chip, own_link, own), "add_own")
     coarse = add(
-        (((3, 3), (1, 1, 1)), ((1, 2), (0, 0, 0)), ((2, 1), (0, 0, 0))),
-        (far_link, near_link, far_link, far, far, near, far_chip, near_chip, far_chip),
+        (((3, 3), (0, 1, 2), (1, 1, 1)), ((1, 2), (0, 4), (0,)), ((2, 1), (3, 1, 2), (0, 0, 0))),
+        (far, far_chip, far_link, near, joined),
         "add_rest",
         coarse,
     )

time: 37.3 us -> 37.5 us (level)
  the two profiles are of different devices: /device:TPU:0 before, /device:TPU:1 now
where the time goes in v16:
time: 37.5 us; the launch traced here: 37.4 us
  starting transfers between devices  22.2 us (59%)
  waiting for transfers between devices  7.56 us (20%)
  Pallas kernels  7.51 us (20%)
    ppermute x3, starting transfers between devices, over_chip(): return lax.ppermute(value, 'blk', pairs)  8.8 us
    ppermute x7, starting transfers between devices, to(): return lax.ppermute(value, ('blk', 'col'), perm)  7.99 us
    pallas_call x8, Pallas kernels, call(): pl.pallas_call(kernel, out_shape=out_shape, in_specs=in_specs, out_specs=...  7.51 us
    ppermute x7, waiting for transfers between devices, to(): return lax.ppermute(value, ('blk', 'col'), perm)  7.42 us
    ppermute x3, starting transfers between devices, over_link(): return lax.ppermute(value, 'blk', cross)  5.38 us
  transfers between devices with their start and end apart: 13, of which 4 were waited for; matrix products, arithmetic and copies ran while one was open for 0% of the time, Pallas kernels for 15%

profile of v16, /device:TPU:1, one launch (start us, length us, event | category | flops | bytes accessed | tf_op | source)
XLA Modules:
  0.0 37.4 jit_solution(13615006684978996524)
XLA Ops:
  0.0 2.1 %collective-permute-start = (bf16[1024,3,128]{2,0,1:T(8,128)(2,1)}, bf16[1024,3,128]{2,0,1:T(8,128)(2,1)S(1)}, u32[]{:S(2)}, u32[]{:S(2)}) collective-permute-start(bf16[1024,3,128]{2,0,1:T(8,128)(2,1)} %param.6), channel_id=1, source_target_pairs={{0,1},{1,0},{2,3},{3,2},{4,6},{5,7},{6,4},{7,5},{8,9},{9,8},{10,11... | collective-permute-start | bytes 2359304 | tf_op jit(solution)/shard_map/ppermute | solution.py:270
  2.1 1.8 %mask_and_inner.1 = (bf16[1024,384]{1,0:T(8,128)(2,1)S(1)}, bf16[256,256]{1,0:T(8,128)(2,1)S(1)}, bf16[256,256]{1,0:T(8,128)(2,1)S(1)}, bf16[512,384]{1,0:T(8,128)(2,1)S(1)}) custom-call(s32[3,8]{1,0:T(4,128)} %bitcast.8, bf16[3,1024,128]{2,1,0:T(8,128)(2,1)} %bitcast.10, s32[8,2,128]{2,1,0:T(2,128)} %bitcast.11, bf16[8,3,128,128]{3,2,1,0:T(8,128)(2,1)} %stiffness.1), custom_call_target="tpu_custom_call" | custom-call | flops 150994944 | bytes 3022944 | tf_op jit(solution)/shard_map/mask_and_inner/pallas_call | solution.py:29
  3.9 0.0 copy-start.2
  3.9 2.2 %collective-permute-start.2 = (bf16[256,256]{1,0:T(8,128)(2,1)S(1)}, bf16[256,256]{1,0:T(8,128)(2,1)S(1)}, u32[]{:S(2)}, u32[]{:S(2)}) collective-permute-start(bf16[256,256]{1,0:T(8,128)(2,1)S(1)} %get-tuple-element.32), channel_id=1, source_target_pairs={{0,28},{4,8},{8,4},{12,16},{16,12},{20,24},{24,20},{28,0},{1,29},{... | collective-permute-start | bytes 393224 | tf_op jit(solution)/shard_map/ppermute | solution.py:266
  6.1 1.6 %collective-permute-start.3 = (bf16[256,256]{1,0:T(8,128)(2,1)S(1)}, bf16[256,256]{1,0:T(8,128)(2,1)S(1)}, u32[]{:S(2)}, u32[]{:S(2)}) collective-permute-start(bf16[256,256]{1,0:T(8,128)(2,1)S(1)} %get-tuple-element.33), channel_id=1, source_target_pairs={{0,4},{4,0},{8,12},{12,8},{16,20},{20,16},{24,28},{28,24},{1,5},{5... | collective-permute-start | bytes 393224 | tf_op jit(solution)/shard_map/ppermute | solution.py:263
  7.7 1.2 %collective-permute-start.4 = (bf16[512,384]{1,0:T(8,128)(2,1)S(1)}, bf16[512,384]{1,0:T(8,128)(2,1)S(1)}, u32[]{:S(2)}, u32[]{:S(2)}) collective-permute-start(bf16[512,384]{1,0:T(8,128)(2,1)S(1)} %get-tuple-element.30.inner), channel_id=1, source_target_pairs={{0,2},{1,3},{2,0},{3,1},{4,5},{5,4},{6,7},{7,6},{8,10},{9,11},{10,... | collective-permute-start | bytes 1179656 | tf_op jit(solution)/shard_map/ppermute | solution.py:270
  8.9 0.1 collective-permute-done.2.from_link
  9.1 1.1 %outer_image.1.outer = bf16[512,384]{1,0:T(8,128)(2,1)S(1)} custom-call(s32[3,8]{1,0:T(4,128)S(1)} %bitcast.9, bf16[8,3,128,128]{3,2,1,0:T(8,128)(2,1)S(1)} %copy-done, bf16[1024,384]{1,0:T(8,128)(2,1)S(1)} %get-tuple-element.31.masked, bf16[256,256]{1,0:T(8,128)(2,1)S(1)} %collective-permute-done.2.from_link, ...), custom_call_target="tpu_custom_call" | custom-call | flops 150994944 | bytes 2228320 | tf_op jit(solution)/shard_map/outer_image/pallas_call | solution.py:29
  10.2 1.1 %collective-permute-start.5 = (bf16[512,384]{1,0:T(8,128)(2,1)S(1)}, bf16[512,384]{1,0:T(8,128)(2,1)S(1)}, u32[]{:S(2)}, u32[]{:S(2)}) collective-permute-start(bf16[512,384]{1,0:T(8,128)(2,1)S(1)} %outer_image.1.outer), channel_id=1, source_target_pairs={{0,2},{1,3},{2,0},{3,1},{4,5},{5,4},{6,7},{7,6},{8,10},{9,11},{10,... | collective-permute-start | bytes 1179656 | tf_op jit(solution)/shard_map/ppermute | solution.py:270
  11.2 0.5 %collective-permute-start.1 = (s32[8,128,2]{1,2,0:T(2,128)S(1)}, s32[8,128,2]{1,2,0:T(2,128)S(1)}, u32[]{:S(2)}, u32[]{:S(2)}) collective-permute-start(s32[8,128,2]{1,2,0:T(2,128)S(1)} %copy-done.2), channel_id=1, source_target_pairs={{0,1},{1,0},{2,3},{3,2},{4,6},{5,7},{6,4},{7,5},{8,9},{9,8},{10,11... | collective-permute-start | bytes 24584 | tf_op jit(solution)/shard_map/ppermute | solution.py:270
  11.7 0.6 %own_tile.1 = (f32[128,384]{1,0:T(8,128)S(1)}, bf16[128,384]{1,0:T(8,128)(2,1)S(1)}, bf16[128,384]{1,0:T(8,128)(2,1)S(1)}, bf16[384,512]{1,0:T(8,128)(2,1)S(1)}, bf16[384,512]{1,0:T(8,128)(2,1)S(1)}) custom-call(bf16[1024,384]{1,0:T(8,128)(2,1)S(1)} %get-tuple-element.31.masked, bf16[512,384]{1,0:T(8,128)(2,1)S(1)} %get-tuple-element.30.inner, ...), custom_call_target="tpu_custom_call" | custom-call | flops 301989888 | bytes 2752512 | tf_op jit(solution)/shard_map/own_tile/pallas_call | solution.py:29
  12.4 2.2 %collective-permute-start.6 = (bf16[128,384]{1,0:T(8,128)(2,1)S(1)}, bf16[128,384]{1,0:T(8,128)(2,1)S(1)}, u32[]{:S(2)}, u32[]{:S(2)}) collective-permute-start(bf16[128,384]{1,0:T(8,128)(2,1)S(1)} %get-tuple-element.38), channel_id=1, source_target_pairs={{0,28},{4,8},{8,4},{12,16},{16,12},{20,24},{24,20},{28,0},{1,29},{... | collective-permute-start | bytes 294920 | tf_op jit(solution)/shard_map/ppermute | solution.py:266
  14.6 4.2 %collective-permute-start.7 = (bf16[128,384]{1,0:T(8,128)(2,1)S(1)}, bf16[128,384]{1,0:T(8,128)(2,1)S(1)}, u32[]{:S(2)}, u32[]{:S(2)}) collective-permute-start(bf16[128,384]{1,0:T(8,128)(2,1)S(1)} %get-tuple-element.39), channel_id=1, source_target_pairs={{0,4},{4,0},{8,12},{12,8},{16,20},{20,16},{24,28},{28,24},{1,5},{5... | collective-permute-start | bytes 294920 | tf_op jit(solution)/shard_map/ppermute | solution.py:263
  18.8 1.3 %partner_tile.1 = (bf16[128,384]{1,0:T(8,128)(2,1)S(1)}, bf16[128,384]{1,0:T(8,128)(2,1)S(1)}, bf16[128,384]{1,0:T(8,128)(2,1)S(1)}, bf16[384,512]{1,0:T(8,128)(...) custom-call(bf16[3,1024,128]{2,1,0:T(8,128)(2,1)S(1)} %bitcast.6, s32[8,2,128]{2,1,0:T(2,128)S(1)} %bitcast.7, ...), custom_call_target="tpu_custom_call" | custom-call | flops 603979776 | bytes 4235264 | tf_op jit(solution)/shard_map/partner_tile/pallas_call | solution.py:29
  20.1 1.2 %collective-permute-done.5.outer_r = bf16[512,384]{1,0:T(8,128)(2,1)S(1)} collective-permute-done((bf16[512,384]{1,0:T(8,128)(2,1)S(1)}, bf16[512,384]{1,0:T(8,128)(2,1)S(1)}, u32[]{:S(2)}, u32[]{:S(2)}) %collective-permute-start.5) | collective-permute-done | bytes 393248 | tf_op jit(solution)/shard_map/ppermute | solution.py:270
  21.3 0.8 %late_tiles.1 = (f32[128,384]{1,0:T(8,128)S(1)}, bf16[128,384]{1,0:T(8,128)(2,1)S(1)}, bf16[128,384]{1,0:T(8,128)(2,1)S(1)}, bf16[128,768]{1,0:T(8,128)(2,1)S(1)...) custom-call(bf16[128,384]{1,0:T(8,128)(2,1)S(1)} %get-tuple-element.35.part, ...), custom_call_target="tpu_custom_call" | custom-call | flops 301989888 | bytes 3637248 | tf_op jit(solution)/shard_map/late_tiles/pallas_call | solution.py:29
  22.1 1.0 %collective-permute-start.11 = (bf16[128,384]{1,0:T(8,128)(2,1)S(1)}, bf16[128,384]{1,0:T(8,128)(2,1)S(1)}, u32[]{:S(2)}, u32[]{:S(2)}) collective-permute-start(bf16[128,384]{1,0:T(8,128)(2,1)S(1)} %get-tuple-element.50), channel_id=1, source_target_pairs={{0,28},{4,8},{8,4},{12,16},{16,12},{20,24},{24,20},{28,0},{1,29},{... | collective-permute-start | bytes 294920 | tf_op jit(solution)/shard_map/ppermute | solution.py:266
  23.1 3.0 %collective-permute-start.12 = (bf16[128,384]{1,0:T(8,128)(2,1)S(1)}, bf16[128,384]{1,0:T(8,128)(2,1)S(1)}, u32[]{:S(2)}, u32[]{:S(2)}) collective-permute-start(bf16[128,384]{1,0:T(8,128)(2,1)S(1)} %get-tuple-element.51), channel_id=1, source_target_pairs={{0,4},{4,0},{8,12},{12,8},{16,20},{20,16},{24,28},{28,24},{1,5},{5... | collective-permute-start | bytes 294920 | tf_op jit(solution)/shard_map/ppermute | solution.py:263
  26.1 1.2 %collective-permute-start.8 = (bf16[128,768]{1,0:T(8,128)(2,1)S(1)}, bf16[128,768]{1,0:T(8,128)(2,1)S(1)}, u32[]{:S(2)}, u32[]{:S(2)}) collective-permute-start(bf16[128,768]{1,0:T(8,128)(2,1)S(1)} %get-tuple-element.46), channel_id=1, source_target_pairs={{0,1},{1,0},{2,3},{3,2},{4,6},{5,7},{6,4},{7,5},{8,9},{9,8},{10,11... | collective-permute-start | bytes 589832 | tf_op jit(solution)/shard_map/ppermute | solution.py:270
  27.4 1.9 %collective-permute-start.9 = (bf16[128,768]{1,0:T(8,128)(2,1)S(1)}, bf16[128,768]{1,0:T(8,128)(2,1)S(1)}, u32[]{:S(2)}, u32[]{:S(2)}) collective-permute-start(bf16[128,768]{1,0:T(8,128)(2,1)S(1)} %get-tuple-element.47), channel_id=1, source_target_pairs={{0,5},{1,4},{2,7},{3,6},{4,2},{5,3},{6,0},{7,1},{8,13},{9,12},{10,... | collective-permute-start | bytes 589832 | tf_op jit(solution)/shard_map/ppermute | solution.py:270
  29.3 0.8 %add_own.1.refs_5_ = f32[5,128,512]{2,1,0:T(8,128)} custom-call(bf16[128,384]{1,0:T(8,128)(2,1)S(1)} %collective-permute-done.7.refs_0_, bf16[128,384]{1,0:T(8,128)(2,1)S(1)} %collective-permute-done.6.refs_1_, f32[128,384]{1,0:T(8,128)S(1)} %get-tuple-element.54.refs_2_), custom_call_target="tpu_custom_call" | custom-call | flops 81920 | bytes 1703936 | tf_op jit(solution)/shard_map/add_own/pallas_call | solution.py:29
  30.1 2.3 %collective-permute-done.10.refs_2_ = bf16[128,768]{1,0:T(8,128)(2,1)S(1)} collective-permute-done((bf16[128,768]{1,0:T(8,128)(2,1)S(1)}, bf16[128,768]{1,0:T(8,128)(2,1)S(1)}, u32[]{:S(2)}, u32[]{:S(2)}) %collective-permute-start.10) | collective-permute-done | bytes 196640 | tf_op jit(solution)/shard_map/ppermute | solution.py:270
  32.4 3.9 %collective-permute-done.9.refs_1_ = bf16[128,768]{1,0:T(8,128)(2,1)S(1)} collective-permute-done((bf16[128,768]{1,0:T(8,128)(2,1)S(1)}, bf16[128,768]{1,0:T(8,128)(2,1)S(1)}, u32[]{:S(2)}, u32[]{:S(2)}) %collective-permute-start.9) | collective-permute-done | bytes 196640 | tf_op jit(solution)/shard_map/ppermute | solution.py:270
  36.3 1.0 %add_rest.1 = f32[5,128,512]{2,1,0:T(8,128)} custom-call(bf16[128,768]{1,0:T(8,128)(2,1)S(1)} %collective-permute-done.8.refs_0_, bf16[128,768]{1,0:T(8,128)(2,1)S(1)} %collective-permute-done.9.refs_1_, bf16[128,768]{1,0:T(8,128)(2,1)S(1)} %collective-permute-done.10.refs_2_, ...), custom_call_target="tpu_custom_call", output_to_operand_aliasing={{}: (5, {})} | custom-call | flops 245760 | bytes 3735552 | tf_op jit(solution)/shard_map/add_rest/pallas_call | solution.py:29
  (16 shorter events, 0.1 us)
Async XLA Ops:
  0.0 9.1 %copy-start.1 = (s32[8,3]{0,1:T(4,128)S(1)}, s32[8,3]{0,1:T(4,128)}, u32[]{:S(2)}) copy-start(s32[8,3]{0,1:T(4,128)} %param.5) | copy-start | bytes 292
  0.0 9.1 %copy-start = (bf16[8,3,128,128]{3,2,1,0:T(8,128)(2,1)S(1)}, bf16[8,3,128,128]{3,2,1,0:T(8,128)(2,1)}, u32[]{:S(2)}) copy-start(bf16[8,3,128,128]{3,2,1,0:T(8,128)(2,1)} %stiffness.1) | copy-start | bytes 2359300
  0.0 18.8 %collective-permute-start = (bf16[1024,3,128]{2,0,1:T(8,128)(2,1)}, bf16[1024,3,128]{2,0,1:T(8,128)(2,1)S(1)}, u32[]{:S(2)}, u32[]{:S(2)}) collective-permute-start(bf16[1024,3,128]{2,0,1:T(8,128)(2,1)} %param.6), channel_id=1, source_target_pairs={{0,1},{1,0},{2,3},{3,2},{4,6},{5,7},{6,4},{7,5},{8,9},{9,8},{10,11... | collective-permute-start | bytes 2359304 | tf_op jit(solution)/shard_map/ppermute | solution.py:270
  3.9 7.3 %copy-start.2 = (s32[8,128,2]{1,2,0:T(2,128)S(1)}, s32[8,128,2]{1,2,0:T(2,128)}, u32[]{:S(2)}) copy-start(s32[8,128,2]{1,2,0:T(2,128)} %param.7) | copy-start | bytes 24580
  3.9 5.1 %collective-permute-start.2 = (bf16[256,256]{1,0:T(8,128)(2,1)S(1)}, bf16[256,256]{1,0:T(8,128)(2,1)S(1)}, u32[]{:S(2)}, u32[]{:S(2)}) collective-permute-start(bf16[256,256]{1,0:T(8,128)(2,1)S(1)} %get-tuple-element.32), channel_id=1, source_target_pairs={{0,28},{4,8},{8,4},{12,16},{16,12},{20,24},{24,20},{28,0},{1,29},{... | collective-permute-start | bytes 393224 | tf_op jit(solution)/shard_map/ppermute | solution.py:266
  6.1 3.0 %collective-permute-start.3 = (bf16[256,256]{1,0:T(8,128)(2,1)S(1)}, bf16[256,256]{1,0:T(8,128)(2,1)S(1)}, u32[]{:S(2)}, u32[]{:S(2)}) collective-permute-start(bf16[256,256]{1,0:T(8,128)(2,1)S(1)} %get-tuple-element.33), channel_id=1, source_target_pairs={{0,4},{4,0},{8,12},{12,8},{16,20},{20,16},{24,28},{28,24},{1,5},{5... | collective-permute-start | bytes 393224 | tf_op jit(solution)/shard_map/ppermute | solution.py:263
  7.7 11.1 %collective-permute-start.4 = (bf16[512,384]{1,0:T(8,128)(2,1)S(1)}, bf16[512,384]{1,0:T(8,128)(2,1)S(1)}, u32[]{:S(2)}, u32[]{:S(2)}) collective-permute-start(bf16[512,384]{1,0:T(8,128)(2,1)S(1)} %get-tuple-element.30.inner), channel_id=1, source_target_pairs={{0,2},{1,3},{2,0},{3,1},{4,5},{5,4},{6,7},{7,6},{8,10},{9,11},{10,... | collective-permute-start | bytes 1179656 | tf_op jit(solution)/shard_map/ppermute | solution.py:270
  10.2 11.1 %collective-permute-start.5 = (bf16[512,384]{1,0:T(8,128)(2,1)S(1)}, bf16[512,384]{1,0:T(8,128)(2,1)S(1)}, u32[]{:S(2)}, u32[]{:S(2)}) collective-permute-start(bf16[512,384]{1,0:T(8,128)(2,1)S(1)} %outer_image.1.outer), channel_id=1, source_target_pairs={{0,2},{1,3},{2,0},{3,1},{4,5},{5,4},{6,7},{7,6},{8,10},{9,11},{10,... | collective-permute-start | bytes 1179656 | tf_op jit(solution)/shard_map/ppermute | solution.py:270
  11.2 3.3 %collective-permute-start.1 = (s32[8,128,2]{1,2,0:T(2,128)S(1)}, s32[8,128,2]{1,2,0:T(2,128)S(1)}, u32[]{:S(2)}, u32[]{:S(2)}) collective-permute-start(s32[8,128,2]{1,2,0:T(2,128)S(1)} %copy-done.2), channel_id=1, source_target_pairs={{0,1},{1,0},{2,3},{3,2},{4,6},{5,7},{6,4},{7,5},{8,9},{9,8},{10,11... | collective-permute-start | bytes 24584 | tf_op jit(solution)/shard_map/ppermute | solution.py:270
  12.4 7.7 %collective-permute-start.6 = (bf16[128,384]{1,0:T(8,128)(2,1)S(1)}, bf16[128,384]{1,0:T(8,128)(2,1)S(1)}, u32[]{:S(2)}, u32[]{:S(2)}) collective-permute-start(bf16[128,384]{1,0:T(8,128)(2,1)S(1)} %get-tuple-element.38), channel_id=1, source_target_pairs={{0,28},{4,8},{8,4},{12,16},{16,12},{20,24},{24,20},{28,0},{1,29},{... | collective-permute-start | bytes 294920 | tf_op jit(solution)/shard_map/ppermute | solution.py:266
  14.6 5.5 %collective-permute-start.7 = (bf16[128,384]{1,0:T(8,128)(2,1)S(1)}, bf16[128,384]{1,0:T(8,128)(2,1)S(1)}, u32[]{:S(2)}, u32[]{:S(2)}) collective-permute-start(bf16[128,384]{1,0:T(8,128)(2,1)S(1)} %get-tuple-element.39), channel_id=1, source_target_pairs={{0,4},{4,0},{8,12},{12,8},{16,20},{20,16},{24,28},{28,24},{1,5},{5... | collective-permute-start | bytes 294920 | tf_op jit(solution)/shard_map/ppermute | solution.py:263
  22.1 8.0 %collective-permute-start.11 = (bf16[128,384]{1,0:T(8,128)(2,1)S(1)}, bf16[128,384]{1,0:T(8,128)(2,1)S(1)}, u32[]{:S(2)}, u32[]{:S(2)}) collective-permute-start(bf16[128,384]{1,0:T(8,128)(2,1)S(1)} %get-tuple-element.50), channel_id=1, source_target_pairs={{0,28},{4,8},{8,4},{12,16},{16,12},{20,24},{24,20},{28,0},{1,29},{... | collective-permute-start | bytes 294920 | tf_op jit(solution)/shard_map/ppermute | solution.py:266
  23.1 6.9 %collective-permute-start.12 = (bf16[128,384]{1,0:T(8,128)(2,1)S(1)}, bf16[128,384]{1,0:T(8,128)(2,1)S(1)}, u32[]{:S(2)}, u32[]{:S(2)}) collective-permute-start(bf16[128,384]{1,0:T(8,128)(2,1)S(1)} %get-tuple-element.51), channel_id=1, source_target_pairs={{0,4},{4,0},{8,12},{12,8},{16,20},{20,16},{24,28},{28,24},{1,5},{5... | collective-permute-start | bytes 294920 | tf_op jit(solution)/shard_map/ppermute | solution.py:263
  26.1 6.3 %collective-permute-start.10 = (bf16[128,768]{1,0:T(8,128)(2,1)S(1)}, bf16[128,768]{1,0:T(8,128)(2,1)S(1)}, u32[]{:S(2)}, u32[]{:S(2)}) collective-permute-start(bf16[128,768]{1,0:T(8,128)(2,1)S(1)} %get-tuple-element.48), channel_id=1, source_target_pairs={{0,29},{1,28},{2,31},{3,30},{4,10},{5,11},{6,8},{7,9},{8,5},{9,4},... | collective-permute-start | bytes 589832 | tf_op jit(solution)/shard_map/ppermute | solution.py:270
  26.1 6.3 %collective-permute-start.8 = (bf16[128,768]{1,0:T(8,128)(2,1)S(1)}, bf16[128,768]{1,0:T(8,128)(2,1)S(1)}, u32[]{:S(2)}, u32[]{:S(2)}) collective-permute-start(bf16[128,768]{1,0:T(8,128)(2,1)S(1)} %get-tuple-element.46), channel_id=1, source_target_pairs={{0,1},{1,0},{2,3},{3,2},{4,6},{5,7},{6,4},{7,5},{8,9},{9,8},{10,11... | collective-permute-start | bytes 589832 | tf_op jit(solution)/shard_map/ppermute | solution.py:270
  27.4 9.0 %collective-permute-start.9 = (bf16[128,768]{1,0:T(8,128)(2,1)S(1)}, bf16[128,768]{1,0:T(8,128)(2,1)S(1)}, u32[]{:S(2)}, u32[]{:S(2)}) collective-permute-start(bf16[128,768]{1,0:T(8,128)(2,1)S(1)} %get-tuple-element.47), channel_id=1, source_target_pairs={{0,5},{1,4},{2,7},{3,6},{4,2},{5,3},{6,0},{7,1},{8,13},{9,12},{10,... | collective-permute-start | bytes 589832 | tf_op jit(solution)/shard_map/ppermute | solution.py:270

commit v17 on v15

--- a/solution.py
+++ b/solution.py
@@ -216,8 +216,8 @@
     even = parity() == 0
     copies = []
     for n, ((even_step, odd_step), chunks) in enumerate(steps):
-        link, own, chip = (
-            terms[n + k * count][:, m * 3 * width : (m + 1) * 3 * width].astype(F32) for k, m in enumerate(chunks)
+        own, link, chip = (
+            ref[:, m * 3 * width : (m + 1) * 3 * width].astype(F32) for ref, m in zip(terms[3 * n : 3 * n + 3], chunks)
         )
         prev = jnp.where(even, link, chip)
         nxt = jnp.where(even, chip, link)
@@ -367,10 +367,10 @@
             name=name,
         )
 
-    coarse = add((((0, 0), (0, 0, 0)),), (own_link, own, own_chip), "add_own")
+    coarse = add((((0, 0), (0, 0, 0)),), (own, own_link, own_chip), "add_own")
     coarse = add(
-        (((3, 3), (1, 1, 1)), ((1, 2), (0, 0, 0)), ((2, 1), (0, 0, 0))),
-        (far_link, near_link, far_link, far, far, near, far_chip, near_chip, far_chip),
+        (((2, 1), (0, 0, 0)), ((1, 2), (0, 0, 0)), ((3, 3), (1, 1, 1))),
+        (near, far_link, far_chip, far, near_link, near_chip, far, far_link, far_chip),
         "add_rest",
         coarse,
     )

time: 37.3 us -> 36.6 us (0.981)
  waiting for transfers between devices: 13.7 us -> 13.2 us
    ppermute x3, waiting for transfers between devices: 12.2 us -> 11.7 us  [over_link(): return lax.ppermute(value, 'blk', cross)]
where the time goes in v17:
time: 36.6 us; the launch traced here: 36.5 us
  starting transfers between devices  15.7 us (43%)
  waiting for transfers between devices  13.2 us (36%)
  Pallas kernels  7.47 us (20%)
    ppermute x3, waiting for transfers between devices, over_link(): return lax.ppermute(value, 'blk', cross)  11.7 us
    ppermute x7, starting transfers between devices, to(): return lax.ppermute(value, ('blk', 'col'), perm)  11.2 us
    pallas_call x7, Pallas kernels, call(): pl.pallas_call(kernel, out_shape=out_shape, in_specs=in_specs, out_specs=...  7.47 us
    ppermute x3, starting transfers between devices, over_link(): return lax.ppermute(value, 'blk', cross)  4.48 us
    ppermute x7, waiting for transfers between devices, to(): return lax.ppermute(value, ('blk', 'col'), perm)  1.51 us
  transfers between devices with their start and end apart: 13, of which 4 were waited for; matrix products, arithmetic and copies ran while one was open for 0% of the time, Pallas kernels for 15%

profile of v17, /device:TPU:0, one launch (start us, length us, event | category | flops | bytes accessed | tf_op | source)
XLA Modules:
  0.0 36.5 jit_solution(12252004029316175059)
XLA Ops:
  0.0 2.9 %collective-permute-start = (bf16[1024,3,128]{2,0,1:T(8,128)(2,1)}, bf16[1024,3,128]{2,0,1:T(8,128)(2,1)S(1)}, u32[]{:S(2)}, u32[]{:S(2)}) collective-permute-start(bf16[1024,3,128]{2,0,1:T(8,128)(2,1)} %param.6), channel_id=1, source_target_pairs={{0,1},{1,0},{2,3},{3,2},{4,6},{5,7},{6,4},{7,5},{8,9},{9,8},{10,11... | collective-permute-start | bytes 2359304 | tf_op jit(solution)/shard_map/ppermute | solution.py:261
  2.9 1.8 %mask_and_inner.1 = (bf16[1024,384]{1,0:T(8,128)(2,1)S(1)}, bf16[256,256]{1,0:T(8,128)(2,1)S(1)}, bf16[256,256]{1,0:T(8,128)(2,1)S(1)}, bf16[512,384]{1,0:T(8,128)(2,1)S(1)}) custom-call(s32[3,8]{1,0:T(4,128)} %bitcast.8, bf16[3,1024,128]{2,1,0:T(8,128)(2,1)} %bitcast.10, s32[8,2,128]{2,1,0:T(2,128)} %bitcast.11, bf16[8,3,128,128]{3,2,1,0:T(8,128)(2,1)} %stiffness.1), custom_call_target="tpu_custom_call" | custom-call | flops 150994944 | bytes 3022944 | tf_op jit(solution)/shard_map/mask_and_inner/pallas_call | solution.py:29
  4.8 0.0 copy-start.2
  4.8 2.9 %collective-permute-start.2 = (bf16[256,256]{1,0:T(8,128)(2,1)S(1)}, bf16[256,256]{1,0:T(8,128)(2,1)S(1)}, u32[]{:S(2)}, u32[]{:S(2)}) collective-permute-start(bf16[256,256]{1,0:T(8,128)(2,1)S(1)} %get-tuple-element.32), channel_id=1, source_target_pairs={{0,28},{4,8},{8,4},{12,16},{16,12},{20,24},{24,20},{28,0},{1,29},{... | collective-permute-start | bytes 393224 | tf_op jit(solution)/shard_map/ppermute | solution.py:257
  7.7 0.5 %collective-permute-start.4 = (bf16[512,384]{1,0:T(8,128)(2,1)S(1)}, bf16[512,384]{1,0:T(8,128)(2,1)S(1)}, u32[]{:S(2)}, u32[]{:S(2)}) collective-permute-start(bf16[512,384]{1,0:T(8,128)(2,1)S(1)} %get-tuple-element.30.inner), channel_id=1, source_target_pairs={{0,2},{1,3},{2,0},{3,1},{4,5},{5,4},{6,7},{7,6},{8,10},{9,11},{10,... | collective-permute-start | bytes 1179656 | tf_op jit(solution)/shard_map/ppermute | solution.py:261
  8.2 4.0 %collective-permute-done.2.from_link = bf16[256,256]{1,0:T(8,128)(2,1)S(1)} collective-permute-done((bf16[256,256]{1,0:T(8,128)(2,1)S(1)}, bf16[256,256]{1,0:T(8,128)(2,1)S(1)}, u32[]{:S(2)}, u32[]{:S(2)}) %collective-permute-start.2) | collective-permute-done | bytes 131104 | tf_op jit(solution)/shard_map/ppermute | solution.py:257
  12.2 0.0 collective-permute-done.3.from_chip
  12.2 1.1 %outer_image.1.outer = bf16[512,384]{1,0:T(8,128)(2,1)S(1)} custom-call(s32[3,8]{1,0:T(4,128)S(1)} %bitcast.9, bf16[8,3,128,128]{3,2,1,0:T(8,128)(2,1)S(1)} %copy-done, bf16[1024,384]{1,0:T(8,128)(2,1)S(1)} %get-tuple-element.31.masked, bf16[256,256]{1,0:T(8,128)(2,1)S(1)} %collective-permute-done.2.from_link, ...), custom_call_target="tpu_custom_call" | custom-call | flops 150994944 | bytes 2228320 | tf_op jit(solution)/shard_map/outer_image/pallas_call | solution.py:29
  13.3 1.6 %collective-permute-start.5 = (bf16[512,384]{1,0:T(8,128)(2,1)S(1)}, bf16[512,384]{1,0:T(8,128)(2,1)S(1)}, u32[]{:S(2)}, u32[]{:S(2)}) collective-permute-start(bf16[512,384]{1,0:T(8,128)(2,1)S(1)} %outer_image.1.outer), channel_id=1, source_target_pairs={{0,2},{1,3},{2,0},{3,1},{4,5},{5,4},{6,7},{7,6},{8,10},{9,11},{10,... | collective-permute-start | bytes 1179656 | tf_op jit(solution)/shard_map/ppermute | solution.py:261
  14.9 0.5 %collective-permute-start.1 = (s32[8,128,2]{1,2,0:T(2,128)S(1)}, s32[8,128,2]{1,2,0:T(2,128)S(1)}, u32[]{:S(2)}, u32[]{:S(2)}) collective-permute-start(s32[8,128,2]{1,2,0:T(2,128)S(1)} %copy-done.2), channel_id=1, source_target_pairs={{0,1},{1,0},{2,3},{3,2},{4,6},{5,7},{6,4},{7,5},{8,9},{9,8},{10,11... | collective-permute-start | bytes 24584 | tf_op jit(solution)/shard_map/ppermute | solution.py:261
  15.4 0.6 %own_tile.1 = (f32[128,384]{1,0:T(8,128)S(1)}, bf16[128,384]{1,0:T(8,128)(2,1)S(1)}, bf16[128,384]{1,0:T(8,128)(2,1)S(1)}, bf16[384,512]{1,0:T(8,128)(2,1)S(1)}, bf16[384,512]{1,0:T(8,128)(2,1)S(1)}) custom-call(bf16[1024,384]{1,0:T(8,128)(2,1)S(1)} %get-tuple-element.31.masked, bf16[512,384]{1,0:T(8,128)(2,1)S(1)} %get-tuple-element.30.inner, ...), custom_call_target="tpu_custom_call" | custom-call | flops 301989888 | bytes 2752512 | tf_op jit(solution)/shard_map/own_tile/pallas_call | solution.py:29
  16.1 1.1 %collective-permute-start.6 = (bf16[128,384]{1,0:T(8,128)(2,1)S(1)}, bf16[128,384]{1,0:T(8,128)(2,1)S(1)}, u32[]{:S(2)}, u32[]{:S(2)}) collective-permute-start(bf16[128,384]{1,0:T(8,128)(2,1)S(1)} %get-tuple-element.38), channel_id=1, source_target_pairs={{0,28},{4,8},{8,4},{12,16},{16,12},{20,24},{24,20},{28,0},{1,29},{... | collective-permute-start | bytes 294920 | tf_op jit(solution)/shard_map/ppermute | solution.py:257
  17.2 1.5 %collective-permute-done.1 = s32[8,128,2]{1,2,0:T(2,128)S(1)} collective-permute-done((s32[8,128,2]{1,2,0:T(2,128)S(1)}, s32[8,128,2]{1,2,0:T(2,128)S(1)}, u32[]{:S(2)}, u32[]{:S(2)}) %collective-permute-start.1) | collective-permute-done | bytes 8224 | tf_op jit(solution)/shard_map/ppermute | solution.py:261
  18.7 1.3 %partner_tile.1 = (bf16[128,384]{1,0:T(8,128)(2,1)S(1)}, bf16[128,384]{1,0:T(8,128)(2,1)S(1)}, bf16[128,384]{1,0:T(8,128)(2,1)S(1)}, bf16[384,512]{1,0:T(8,128)(...) custom-call(bf16[3,1024,128]{2,1,0:T(8,128)(2,1)S(1)} %bitcast.6, s32[8,2,128]{2,1,0:T(2,128)S(1)} %bitcast.7, ...), custom_call_target="tpu_custom_call" | custom-call | flops 603979776 | bytes 4235264 | tf_op jit(solution)/shard_map/partner_tile/pallas_call | solution.py:29
  20.0 2.0 %collective-permute-done.6.refs_1_ = bf16[128,384]{1,0:T(8,128)(2,1)S(1)} collective-permute-done((bf16[128,384]{1,0:T(8,128)(2,1)S(1)}, bf16[128,384]{1,0:T(8,128)(2,1)S(1)}, u32[]{:S(2)}, u32[]{:S(2)}) %collective-permute-start.6) | collective-permute-done | bytes 98336 | tf_op jit(solution)/shard_map/ppermute | solution.py:257
  22.0 0.8 %late_tiles.1 = (f32[128,384]{1,0:T(8,128)S(1)}, bf16[128,384]{1,0:T(8,128)(2,1)S(1)}, bf16[128,384]{1,0:T(8,128)(2,1)S(1)}, bf16[128,768]{1,0:T(8,128)(2,1)S(1)...) custom-call(bf16[128,384]{1,0:T(8,128)(2,1)S(1)} %get-tuple-element.35.part, ...), custom_call_target="tpu_custom_call" | custom-call | flops 301989888 | bytes 3637248 | tf_op jit(solution)/shard_map/late_tiles/pallas_call | solution.py:29
  22.8 1.6 %collective-permute-start.10 = (bf16[128,768]{1,0:T(8,128)(2,1)S(1)}, bf16[128,768]{1,0:T(8,128)(2,1)S(1)}, u32[]{:S(2)}, u32[]{:S(2)}) collective-permute-start(bf16[128,768]{1,0:T(8,128)(2,1)S(1)} %get-tuple-element.49), channel_id=1, source_target_pairs={{0,1},{1,0},{2,3},{3,2},{4,6},{5,7},{6,4},{7,5},{8,9},{9,8},{10,11... | collective-permute-start | bytes 589832 | tf_op jit(solution)/shard_map/ppermute | solution.py:261
  24.3 4.1 %collective-permute-start.8 = (bf16[128,768]{1,0:T(8,128)(2,1)S(1)}, bf16[128,768]{1,0:T(8,128)(2,1)S(1)}, u32[]{:S(2)}, u32[]{:S(2)}) collective-permute-start(bf16[128,768]{1,0:T(8,128)(2,1)S(1)} %get-tuple-element.47), channel_id=1, source_target_pairs={{0,29},{1,28},{2,31},{3,30},{4,10},{5,11},{6,8},{7,9},{8,5},{9,4},... | collective-permute-start | bytes 589832 | tf_op jit(solution)/shard_map/ppermute | solution.py:261
  28.4 0.5 %collective-permute-start.11 = (bf16[128,384]{1,0:T(8,128)(2,1)S(1)}, bf16[128,384]{1,0:T(8,128)(2,1)S(1)}, u32[]{:S(2)}, u32[]{:S(2)}) collective-permute-start(bf16[128,384]{1,0:T(8,128)(2,1)S(1)} %get-tuple-element.50), channel_id=1, source_target_pairs={{0,28},{4,8},{8,4},{12,16},{16,12},{20,24},{24,20},{28,0},{1,29},{... | collective-permute-start | bytes 294920 | tf_op jit(solution)/shard_map/ppermute | solution.py:257
  28.9 0.0 collective-permute-start.12
  28.9 0.8 %add_own.1.refs_9_ = f32[5,128,512]{2,1,0:T(8,128)} custom-call(f32[128,384]{1,0:T(8,128)S(1)} %get-tuple-element.52.refs_0_, bf16[128,384]{1,0:T(8,128)(2,1)S(1)} %collective-permute-done.6.refs_1_, bf16[128,384]{1,0:T(8,128)(2,1)S(1)} %collective-permute-done.7.refs_2_), custom_call_target="tpu_custom_call" | custom-call | flops 81920 | bytes 1703936 | tf_op jit(solution)/shard_map/add_own/pallas_call | solution.py:29
  29.7 5.7 %collective-permute-done.11.refs_4_ = bf16[128,384]{1,0:T(8,128)(2,1)S(1)} collective-permute-done((bf16[128,384]{1,0:T(8,128)(2,1)S(1)}, bf16[128,384]{1,0:T(8,128)(2,1)S(1)}, u32[]{:S(2)}, u32[]{:S(2)}) %collective-permute-start.11) | collective-permute-done | bytes 98336 | tf_op jit(solution)/shard_map/ppermute | solution.py:257
  35.4 0.0 collective-permute-done.12.refs_5_
  35.4 1.0 %add_rest.1 = f32[5,128,512]{2,1,0:T(8,128)} custom-call(f32[128,384]{1,0:T(8,128)S(1)} %get-tuple-element.46.refs_0_, bf16[128,768]{1,0:T(8,128)(2,1)S(1)} %collective-permute-done.8.refs_1_.refs_7_, bf16[128,768]{1,0:T(8,128)(2,1)S(1)} %collective-permute-done.9.refs_2_.refs_8_, ...), custom_call_target="tpu_custom_call", output_to_operand_aliasing={{}: (9, {})} | custom-call | flops 245760 | bytes 4194304 | tf_op jit(solution)/shard_map/add_rest/pallas_call | solution.py:29
  (15 shorter events, 0.0 us)
Async XLA Ops:
  0.0 12.2 %copy-start.1 = (s32[8,3]{0,1:T(4,128)S(1)}, s32[8,3]{0,1:T(4,128)}, u32[]{:S(2)}) copy-start(s32[8,3]{0,1:T(4,128)} %param.5) | copy-start | bytes 292
  0.0 12.2 %copy-start = (bf16[8,3,128,128]{3,2,1,0:T(8,128)(2,1)S(1)}, bf16[8,3,128,128]{3,2,1,0:T(8,128)(2,1)}, u32[]{:S(2)}) copy-start(bf16[8,3,128,128]{3,2,1,0:T(8,128)(2,1)} %stiffness.1) | copy-start | bytes 2359300
  0.0 18.7 %collective-permute-start = (bf16[1024,3,128]{2,0,1:T(8,128)(2,1)}, bf16[1024,3,128]{2,0,1:T(8,128)(2,1)S(1)}, u32[]{:S(2)}, u32[]{:S(2)}) collective-permute-start(bf16[1024,3,128]{2,0,1:T(8,128)(2,1)} %param.6), channel_id=1, source_target_pairs={{0,1},{1,0},{2,3},{3,2},{4,6},{5,7},{6,4},{7,5},{8,9},{9,8},{10,11... | collective-permute-start | bytes 2359304 | tf_op jit(solution)/shard_map/ppermute | solution.py:261
  4.8 10.1 %copy-start.2 = (s32[8,128,2]{1,2,0:T(2,128)S(1)}, s32[8,128,2]{1,2,0:T(2,128)}, u32[]{:S(2)}) copy-start(s32[8,128,2]{1,2,0:T(2,128)} %param.7) | copy-start | bytes 24580
  4.8 7.4 %collective-permute-start.2 = (bf16[256,256]{1,0:T(8,128)(2,1)S(1)}, bf16[256,256]{1,0:T(8,128)(2,1)S(1)}, u32[]{:S(2)}, u32[]{:S(2)}) collective-permute-start(bf16[256,256]{1,0:T(8,128)(2,1)S(1)} %get-tuple-element.32), channel_id=1, source_target_pairs={{0,28},{4,8},{8,4},{12,16},{16,12},{20,24},{24,20},{28,0},{1,29},{... | collective-permute-start | bytes 393224 | tf_op jit(solution)/shard_map/ppermute | solution.py:257
  7.7 4.5 %collective-permute-start.3 = (bf16[256,256]{1,0:T(8,128)(2,1)S(1)}, bf16[256,256]{1,0:T(8,128)(2,1)S(1)}, u32[]{:S(2)}, u32[]{:S(2)}) collective-permute-start(bf16[256,256]{1,0:T(8,128)(2,1)S(1)} %get-tuple-element.33), channel_id=1, source_target_pairs={{0,4},{4,0},{8,12},{12,8},{16,20},{20,16},{24,28},{28,24},{1,5},{5... | collective-permute-start | bytes 393224 | tf_op jit(solution)/shard_map/ppermute | solution.py:254
  7.7 11.1 %collective-permute-start.4 = (bf16[512,384]{1,0:T(8,128)(2,1)S(1)}, bf16[512,384]{1,0:T(8,128)(2,1)S(1)}, u32[]{:S(2)}, u32[]{:S(2)}) collective-permute-start(bf16[512,384]{1,0:T(8,128)(2,1)S(1)} %get-tuple-element.30.inner), channel_id=1, source_target_pairs={{0,2},{1,3},{2,0},{3,1},{4,5},{5,4},{6,7},{7,6},{8,10},{9,11},{10,... | collective-permute-start | bytes 1179656 | tf_op jit(solution)/shard_map/ppermute | solution.py:261
  13.3 8.7 %collective-permute-start.5 = (bf16[512,384]{1,0:T(8,128)(2,1)S(1)}, bf16[512,384]{1,0:T(8,128)(2,1)S(1)}, u32[]{:S(2)}, u32[]{:S(2)}) collective-permute-start(bf16[512,384]{1,0:T(8,128)(2,1)S(1)} %outer_image.1.outer), channel_id=1, source_target_pairs={{0,2},{1,3},{2,0},{3,1},{4,5},{5,4},{6,7},{7,6},{8,10},{9,11},{10,... | collective-permute-start | bytes 1179656 | tf_op jit(solution)/shard_map/ppermute | solution.py:261
  14.9 3.8 %collective-permute-start.1 = (s32[8,128,2]{1,2,0:T(2,128)S(1)}, s32[8,128,2]{1,2,0:T(2,128)S(1)}, u32[]{:S(2)}, u32[]{:S(2)}) collective-permute-start(s32[8,128,2]{1,2,0:T(2,128)S(1)} %copy-done.2), channel_id=1, source_target_pairs={{0,1},{1,0},{2,3},{3,2},{4,6},{5,7},{6,4},{7,5},{8,9},{9,8},{10,11... | collective-permute-start | bytes 24584 | tf_op jit(solution)/shard_map/ppermute | solution.py:261
  16.1 5.9 %collective-permute-start.6 = (bf16[128,384]{1,0:T(8,128)(2,1)S(1)}, bf16[128,384]{1,0:T(8,128)(2,1)S(1)}, u32[]{:S(2)}, u32[]{:S(2)}) collective-permute-start(bf16[128,384]{1,0:T(8,128)(2,1)S(1)} %get-tuple-element.38), channel_id=1, source_target_pairs={{0,28},{4,8},{8,4},{12,16},{16,12},{20,24},{24,20},{28,0},{1,29},{... | collective-permute-start | bytes 294920 | tf_op jit(solution)/shard_map/ppermute | solution.py:257
  18.7 3.3 %collective-permute-start.7 = (bf16[128,384]{1,0:T(8,128)(2,1)S(1)}, bf16[128,384]{1,0:T(8,128)(2,1)S(1)}, u32[]{:S(2)}, u32[]{:S(2)}) collective-permute-start(bf16[128,384]{1,0:T(8,128)(2,1)S(1)} %get-tuple-element.39), channel_id=1, source_target_pairs={{0,4},{4,0},{8,12},{12,8},{16,20},{20,16},{24,28},{28,24},{1,5},{5... | collective-permute-start | bytes 294920 | tf_op jit(solution)/shard_map/ppermute | solution.py:254
  22.8 12.6 %collective-permute-start.10 = (bf16[128,768]{1,0:T(8,128)(2,1)S(1)}, bf16[128,768]{1,0:T(8,128)(2,1)S(1)}, u32[]{:S(2)}, u32[]{:S(2)}) collective-permute-start(bf16[128,768]{1,0:T(8,128)(2,1)S(1)} %get-tuple-element.49), channel_id=1, source_target_pairs={{0,1},{1,0},{2,3},{3,2},{4,6},{5,7},{6,4},{7,5},{8,9},{9,8},{10,11... | collective-permute-start | bytes 589832 | tf_op jit(solution)/shard_map/ppermute | solution.py:261
  24.3 11.1 %collective-permute-start.8 = (bf16[128,768]{1,0:T(8,128)(2,1)S(1)}, bf16[128,768]{1,0:T(8,128)(2,1)S(1)}, u32[]{:S(2)}, u32[]{:S(2)}) collective-permute-start(bf16[128,768]{1,0:T(8,128)(2,1)S(1)} %get-tuple-element.47), channel_id=1, source_target_pairs={{0,29},{1,28},{2,31},{3,30},{4,10},{5,11},{6,8},{7,9},{8,5},{9,4},... | collective-permute-start | bytes 589832 | tf_op jit(solution)/shard_map/ppermute | solution.py:261
  28.4 7.0 %collective-permute-start.9 = (bf16[128,768]{1,0:T(8,128)(2,1)S(1)}, bf16[128,768]{1,0:T(8,128)(2,1)S(1)}, u32[]{:S(2)}, u32[]{:S(2)}) collective-permute-start(bf16[128,768]{1,0:T(8,128)(2,1)S(1)} %get-tuple-element.48), channel_id=1, source_target_pairs={{0,5},{1,4},{2,7},{3,6},{4,2},{5,3},{6,0},{7,1},{8,13},{9,12},{10,... | collective-permute-start | bytes 589832 | tf_op jit(solution)/shard_map/ppermute | solution.py:261
  28.4 7.0 %collective-permute-start.11 = (bf16[128,384]{1,0:T(8,128)(2,1)S(1)}, bf16[128,384]{1,0:T(8,128)(2,1)S(1)}, u32[]{:S(2)}, u32[]{:S(2)}) collective-permute-start(bf16[128,384]{1,0:T(8,128)(2,1)S(1)} %get-tuple-element.50), channel_id=1, source_target_pairs={{0,28},{4,8},{8,4},{12,16},{16,12},{20,24},{24,20},{28,0},{1,29},{... | collective-permute-start | bytes 294920 | tf_op jit(solution)/shard_map/ppermute | solution.py:257
  28.9 6.5 %collective-permute-start.12 = (bf16[128,384]{1,0:T(8,128)(2,1)S(1)}, bf16[128,384]{1,0:T(8,128)(2,1)S(1)}, u32[]{:S(2)}, u32[]{:S(2)}) collective-permute-start(bf16[128,384]{1,0:T(8,128)(2,1)S(1)} %get-tuple-element.51), channel_id=1, source_target_pairs={{0,4},{4,0},{8,12},{12,8},{16,20},{20,16},{24,28},{28,24},{1,5},{5... | collective-permute-start | bytes 294920 | tf_op jit(solution)/shard_map/ppermute | solution.py:254

commit v18 on v13

--- a/solution.py
+++ b/solution.py
@@ -182,29 +182,17 @@
     near[...] = dot(near_left[...], inner_r[...])
 
 
-def late_tiles(
-    part,
-    part_link,
-    part_chip,
-    far_base,
-    near_base,
-    far_outer,
-    near_outer,
-    outer_r,
-    near,
-    near_link,
-    near_chip,
-    far,
-    far_link,
-    far_chip,
-):
+def far_tile(part, part_link, part_chip, base, left_outer, outer_r, far, far_link, far_chip):
     wide = outer_r.shape[1]
     far[:, :wide] = part[...]
     far_link[:, :wide] = part_link[...]
     far_chip[:, :wide] = part_chip[...]
-    tile = far_base[...] + dot(far_outer[...], outer_r[...])
+    tile = base[...] + dot(left_outer[...], outer_r[...])
     store_tile(tile, far.at[:, wide:], far_link.at[:, wide:], far_chip.at[:, wide:])
-    store_tile(near_base[...] + dot(near_outer[...], outer_r[...]), near, near_link, near_chip)
+
+
+def near_tile(base, left_outer, outer_r, near, near_link, near_chip):
+    store_tile(base[...] + dot(left_outer[...], outer_r[...]), near, near_link, near_chip)
 
 
 def add_tiles(steps, *refs):
@@ -338,14 +326,23 @@
         name="partner_tile",
     )
     outer_r, own_link, own_chip, far_base = lax.optimization_barrier((outer_r, own_link, own_chip, far_base))
-    near, near_link, near_chip, far, far_link, far_chip = call(
-        late_tiles,
-        (*tile_shapes(width, wide, F32), *(shape((width, 2 * wide), BF16),) * 3),
-        [VMEM] * 8,
+    far, far_link, far_chip = call(
+        far_tile,
+        (shape((width, 2 * wide), BF16),) * 3,
         [VMEM] * 6,
-        (part, part_link, part_chip, far_base, near_base, far_outer, left_outer, outer_r),
-        flops=tile_flops,
-        name="late_tiles",
+        [VMEM] * 3,
+        (part, part_link, part_chip, far_base, far_outer, outer_r),
+        flops=tile_flops // 2,
+        name="far_tile",
+    )
+    near, near_link, near_chip = call(
+        near_tile,
+        tile_shapes(width, wide, F32),
+        [VMEM] * 3,
+        [VMEM] * 3,
+        (near_base, left_outer, outer_r),
+        flops=tile_flops // 2,
+        name="near_tile",
     )
     far_link = to_partner_link(far_link)
     near_link = over_link(near_link)

time: 35.4 us -> 35.1 us (level)
  waiting for transfers between devices: 11.7 us -> 11.2 us
    ppermute x3, waiting for transfers between devices: 10.2 us -> 9.73 us  [over_link(): return lax.ppermute(value, 'blk', cross)]
    pallas_call x7 -> x8, Pallas kernels: 7.47 us -> 7.47 us  [call(): pl.pallas_call(kernel, out_shape=out_shape, in_specs=in_specs, out_specs=...]
  transfers between devices with their start and end apart: 13 -> 13, of which waited for: 4 -> 4; matrix products, arithmetic and copies ran while one was open for 0% -> 0% of each run, Pallas kernels for 16% -> 17%
where the time goes in v18:
time: 35.1 us; the launch traced here: 34.9 us
  starting transfers between devices  16.1 us (46%)
  waiting for transfers between devices  11.2 us (32%)
  Pallas kernels  7.47 us (21%)
    ppermute x7, starting transfers between devices, to(): return lax.ppermute(value, ('blk', 'col'), perm)  10.3 us
    ppermute x3, waiting for transfers between devices, over_link(): return lax.ppermute(value, 'blk', cross)  9.73 us
    pallas_call x8, Pallas kernels, call(): pl.pallas_call(kernel, out_shape=out_shape, in_specs=in_specs, out_specs=...  7.47 us
    ppermute x3, starting transfers between devices, over_link(): return lax.ppermute(value, 'blk', cross)  5.73 us
    ppermute x7, waiting for transfers between devices, to(): return lax.ppermute(value, ('blk', 'col'), perm)  1.51 us
  transfers between devices with their start and end apart: 13, of which 4 were waited for; matrix products, arithmetic and copies ran while one was open for 0% of the time, Pallas kernels for 17%

profile of v18, /device:TPU:0, one launch (start us, length us, event | category | flops | bytes accessed | tf_op | source)
XLA Modules:
  0.0 34.9 jit_solution(2269739873805600091)
XLA Ops:
  0.0 2.9 %collective-permute-start = (bf16[1024,3,128]{2,0,1:T(8,128)(2,1)}, bf16[1024,3,128]{2,0,1:T(8,128)(2,1)S(1)}, u32[]{:S(2)}, u32[]{:S(2)}) collective-permute-start(bf16[1024,3,128]{2,0,1:T(8,128)(2,1)} %param.6), channel_id=1, source_target_pairs={{0,1},{1,0},{2,3},{3,2},{4,6},{5,7},{6,4},{7,5},{8,9},{9,8},{10,11... | collective-permute-start | bytes 2359304 | tf_op jit(solution)/shard_map/ppermute | solution.py:249
  2.9 1.8 %mask_and_inner.1 = (bf16[1024,384]{1,0:T(8,128)(2,1)S(1)}, bf16[256,256]{1,0:T(8,128)(2,1)S(1)}, bf16[256,256]{1,0:T(8,128)(2,1)S(1)}, bf16[512,384]{1,0:T(8,128)(2,1)S(1)}) custom-call(s32[3,8]{1,0:T(4,128)} %bitcast.8, bf16[3,1024,128]{2,1,0:T(8,128)(2,1)} %bitcast.10, s32[8,2,128]{2,1,0:T(2,128)} %bitcast.11, bf16[8,3,128,128]{3,2,1,0:T(8,128)(2,1)} %stiffness.1), custom_call_target="tpu_custom_call" | custom-call | flops 150994944 | bytes 3022944 | tf_op jit(solution)/shard_map/mask_and_inner/pallas_call | solution.py:29
  4.8 0.0 copy-start.2
  4.8 2.9 %collective-permute-start.2 = (bf16[256,256]{1,0:T(8,128)(2,1)S(1)}, bf16[256,256]{1,0:T(8,128)(2,1)S(1)}, u32[]{:S(2)}, u32[]{:S(2)}) collective-permute-start(bf16[256,256]{1,0:T(8,128)(2,1)S(1)} %get-tuple-element.32), channel_id=1, source_target_pairs={{0,28},{4,8},{8,4},{12,16},{16,12},{20,24},{24,20},{28,0},{1,29},{... | collective-permute-start | bytes 393224 | tf_op jit(solution)/shard_map/ppermute | solution.py:245
  7.7 0.0 collective-permute-start.3
  7.7 0.5 %collective-permute-start.4 = (bf16[512,384]{1,0:T(8,128)(2,1)S(1)}, bf16[512,384]{1,0:T(8,128)(2,1)S(1)}, u32[]{:S(2)}, u32[]{:S(2)}) collective-permute-start(bf16[512,384]{1,0:T(8,128)(2,1)S(1)} %get-tuple-element.30.inner), channel_id=1, source_target_pairs={{0,2},{1,3},{2,0},{3,1},{4,5},{5,4},{6,7},{7,6},{8,10},{9,11},{10,... | collective-permute-start | bytes 1179656 | tf_op jit(solution)/shard_map/ppermute | solution.py:249
  8.2 4.0 %collective-permute-done.2.from_link = bf16[256,256]{1,0:T(8,128)(2,1)S(1)} collective-permute-done((bf16[256,256]{1,0:T(8,128)(2,1)S(1)}, bf16[256,256]{1,0:T(8,128)(2,1)S(1)}, u32[]{:S(2)}, u32[]{:S(2)}) %collective-permute-start.2) | collective-permute-done | bytes 131104 | tf_op jit(solution)/shard_map/ppermute | solution.py:245
  12.2 1.1 %outer_image.1.outer = bf16[512,384]{1,0:T(8,128)(2,1)S(1)} custom-call(s32[3,8]{1,0:T(4,128)S(1)} %bitcast.9, bf16[8,3,128,128]{3,2,1,0:T(8,128)(2,1)S(1)} %copy-done, bf16[1024,384]{1,0:T(8,128)(2,1)S(1)} %get-tuple-element.31.masked, bf16[256,256]{1,0:T(8,128)(2,1)S(1)} %collective-permute-done.2.from_link, ...), custom_call_target="tpu_custom_call" | custom-call | flops 150994944 | bytes 2228320 | tf_op jit(solution)/shard_map/outer_image/pallas_call | solution.py:29
  13.3 1.6 %collective-permute-start.5 = (bf16[512,384]{1,0:T(8,128)(2,1)S(1)}, bf16[512,384]{1,0:T(8,128)(2,1)S(1)}, u32[]{:S(2)}, u32[]{:S(2)}) collective-permute-start(bf16[512,384]{1,0:T(8,128)(2,1)S(1)} %outer_image.1.outer), channel_id=1, source_target_pairs={{0,2},{1,3},{2,0},{3,1},{4,5},{5,4},{6,7},{7,6},{8,10},{9,11},{10,... | collective-permute-start | bytes 1179656 | tf_op jit(solution)/shard_map/ppermute | solution.py:249
  14.9 0.5 %collective-permute-start.1 = (s32[8,128,2]{1,2,0:T(2,128)S(1)}, s32[8,128,2]{1,2,0:T(2,128)S(1)}, u32[]{:S(2)}, u32[]{:S(2)}) collective-permute-start(s32[8,128,2]{1,2,0:T(2,128)S(1)} %copy-done.2), channel_id=1, source_target_pairs={{0,1},{1,0},{2,3},{3,2},{4,6},{5,7},{6,4},{7,5},{8,9},{9,8},{10,11... | collective-permute-start | bytes 24584 | tf_op jit(solution)/shard_map/ppermute | solution.py:249
  15.4 0.6 %own_tile.1 = (f32[128,384]{1,0:T(8,128)S(1)}, bf16[128,384]{1,0:T(8,128)(2,1)S(1)}, bf16[128,384]{1,0:T(8,128)(2,1)S(1)}, bf16[384,512]{1,0:T(8,128)(2,1)S(1)}, bf16[384,512]{1,0:T(8,128)(2,1)S(1)}) custom-call(bf16[1024,384]{1,0:T(8,128)(2,1)S(1)} %get-tuple-element.31.masked, bf16[512,384]{1,0:T(8,128)(2,1)S(1)} %get-tuple-element.30.inner, ...), custom_call_target="tpu_custom_call" | custom-call | flops 301989888 | bytes 2752512 | tf_op jit(solution)/shard_map/own_tile/pallas_call | solution.py:29
  16.1 1.1 %collective-permute-start.6 = (bf16[128,384]{1,0:T(8,128)(2,1)S(1)}, bf16[128,384]{1,0:T(8,128)(2,1)S(1)}, u32[]{:S(2)}, u32[]{:S(2)}) collective-permute-start(bf16[128,384]{1,0:T(8,128)(2,1)S(1)} %get-tuple-element.38), channel_id=1, source_target_pairs={{0,28},{4,8},{8,4},{12,16},{16,12},{20,24},{24,20},{28,0},{1,29},{... | collective-permute-start | bytes 294920 | tf_op jit(solution)/shard_map/ppermute | solution.py:245
  17.2 1.5 %collective-permute-done.1 = s32[8,128,2]{1,2,0:T(2,128)S(1)} collective-permute-done((s32[8,128,2]{1,2,0:T(2,128)S(1)}, s32[8,128,2]{1,2,0:T(2,128)S(1)}, u32[]{:S(2)}, u32[]{:S(2)}) %collective-permute-start.1) | collective-permute-done | bytes 8224 | tf_op jit(solution)/shard_map/ppermute | solution.py:249
  18.7 1.3 %partner_tile.1 = (bf16[128,384]{1,0:T(8,128)(2,1)S(1)}, bf16[128,384]{1,0:T(8,128)(2,1)S(1)}, bf16[128,384]{1,0:T(8,128)(2,1)S(1)}, bf16[384,512]{1,0:T(8,128)(...) custom-call(bf16[3,1024,128]{2,1,0:T(8,128)(2,1)S(1)} %bitcast.6, s32[8,2,128]{2,1,0:T(2,128)S(1)} %bitcast.7, ...), custom_call_target="tpu_custom_call" | custom-call | flops 603979776 | bytes 4235264 | tf_op jit(solution)/shard_map/partner_tile/pallas_call | solution.py:29
  20.0 2.0 %collective-permute-done.6.refs_1_ = bf16[128,384]{1,0:T(8,128)(2,1)S(1)} collective-permute-done((bf16[128,384]{1,0:T(8,128)(2,1)S(1)}, bf16[128,384]{1,0:T(8,128)(2,1)S(1)}, u32[]{:S(2)}, u32[]{:S(2)}) %collective-permute-start.6) | collective-permute-done | bytes 98336 | tf_op jit(solution)/shard_map/ppermute | solution.py:245
  22.0 0.4 %far_tile.1 = (bf16[128,768]{1,0:T(8,128)(2,1)S(1)}, bf16[128,768]{1,0:T(8,128)(2,1)S(1)}, bf16[128,768]{1,0:T(8,128)(2,1)S(1)}) custom-call(bf16[128,384]{1,0:T(8,128)(2,1)S(1)} %get-tuple-element.35.part, bf16[128,384]{1,0:T(8,128)(2,1)S(1)} %get-tuple-element.36.part_link, bf16[128,384]{1,0:T(8,128)(2,1)S(1)} %get-tuple-element.37.part_chip, ...), custom_call_target="tpu_custom_call" | custom-call | flops 150994944 | bytes 2260992 | tf_op jit(solution)/shard_map/far_tile/pallas_call | solution.py:29
  22.4 4.2 %collective-permute-start.10 = (bf16[128,768]{1,0:T(8,128)(2,1)S(1)}, bf16[128,768]{1,0:T(8,128)(2,1)S(1)}, u32[]{:S(2)}, u32[]{:S(2)}) collective-permute-start(bf16[128,768]{1,0:T(8,128)(2,1)S(1)} %get-tuple-element.48), channel_id=1, source_target_pairs={{0,29},{1,28},{2,31},{3,30},{4,10},{5,11},{6,8},{7,9},{8,5},{9,4},... | collective-permute-start | bytes 589832 | tf_op jit(solution)/shard_map/ppermute | solution.py:249
  26.6 0.5 %collective-permute-start.12 = (bf16[128,768]{1,0:T(8,128)(2,1)S(1)}, bf16[128,768]{1,0:T(8,128)(2,1)S(1)}, u32[]{:S(2)}, u32[]{:S(2)}) collective-permute-start(bf16[128,768]{1,0:T(8,128)(2,1)S(1)} %get-tuple-element.50), channel_id=1, source_target_pairs={{0,1},{1,0},{2,3},{3,2},{4,6},{5,7},{6,4},{7,5},{8,9},{9,8},{10,11... | collective-permute-start | bytes 589832 | tf_op jit(solution)/shard_map/ppermute | solution.py:249
  27.1 0.4 %near_tile.1 = (f32[128,384]{1,0:T(8,128)S(1)}, bf16[128,384]{1,0:T(8,128)(2,1)S(1)}, bf16[128,384]{1,0:T(8,128)(2,1)S(1)}) custom-call(f32[384,384]{1,0:T(8,128)S(1)} %get-tuple-element.45.base, bf16[384,512]{1,0:T(8,128)(2,1)S(1)} %get-tuple-element.46.left_outer, bf16[512,384]{1,0:T(8,128)(2,1)S(1)} %collective-permute-done.5.outer_r), custom_call_target="tpu_custom_call" | custom-call | flops 150994944 | bytes 1769472 | tf_op jit(solution)/shard_map/near_tile/pallas_call | solution.py:29
  27.5 1.8 %collective-permute-start.11 = (bf16[128,384]{1,0:T(8,128)(2,1)S(1)}, bf16[128,384]{1,0:T(8,128)(2,1)S(1)}, u32[]{:S(2)}, u32[]{:S(2)}) collective-permute-start(bf16[128,384]{1,0:T(8,128)(2,1)S(1)} %get-tuple-element.49), channel_id=1, source_target_pairs={{0,28},{4,8},{8,4},{12,16},{16,12},{20,24},{24,20},{28,0},{1,29},{... | collective-permute-start | bytes 294920 | tf_op jit(solution)/shard_map/ppermute | solution.py:245
  29.3 0.0 collective-permute-start.9
  29.3 0.8 %add_own.1.refs_9_ = f32[5,128,512]{2,1,0:T(8,128)} custom-call(bf16[128,384]{1,0:T(8,128)(2,1)S(1)} %collective-permute-done.7.refs_0_, bf16[128,384]{1,0:T(8,128)(2,1)S(1)} %collective-permute-done.6.refs_1_, f32[128,384]{1,0:T(8,128)S(1)} %get-tuple-element.54.refs_2_), custom_call_target="tpu_custom_call" | custom-call | flops 81920 | bytes 1703936 | tf_op jit(solution)/shard_map/add_own/pallas_call | solution.py:29
  30.1 3.7 %collective-permute-done.11.refs_4_ = bf16[128,384]{1,0:T(8,128)(2,1)S(1)} collective-permute-done((bf16[128,384]{1,0:T(8,128)(2,1)S(1)}, bf16[128,384]{1,0:T(8,128)(2,1)S(1)}, u32[]{:S(2)}, u32[]{:S(2)}) %collective-permute-start.11) | collective-permute-done | bytes 98336 | tf_op jit(solution)/shard_map/ppermute | solution.py:245
  33.9 1.0 %add_rest.1 = f32[5,128,512]{2,1,0:T(8,128)} custom-call(bf16[128,768]{1,0:T(8,128)(2,1)S(1)} %collective-permute-done.8.refs_0_.refs_2_, bf16[128,384]{1,0:T(8,128)(2,1)S(1)} %collective-permute-done.9.refs_1_, bf16[128,768]{1,0:T(8,128)(2,1)S(1)} %collective-permute-done.8.refs_0_.refs_2_, ...), custom_call_target="tpu_custom_call", output_to_operand_aliasing={{}: (9, {})} | custom-call | flops 245760 | bytes 4194304 | tf_op jit(solution)/shard_map/add_rest/pallas_call | solution.py:29
  (16 shorter events, 0.0 us)
Async XLA Ops:
  0.0 12.2 %copy-start.1 = (s32[8,3]{0,1:T(4,128)S(1)}, s32[8,3]{0,1:T(4,128)}, u32[]{:S(2)}) copy-start(s32[8,3]{0,1:T(4,128)} %param.5) | copy-start | bytes 292
  0.0 12.2 %copy-start = (bf16[8,3,128,128]{3,2,1,0:T(8,128)(2,1)S(1)}, bf16[8,3,128,128]{3,2,1,0:T(8,128)(2,1)}, u32[]{:S(2)}) copy-start(bf16[8,3,128,128]{3,2,1,0:T(8,128)(2,1)} %stiffness.1) | copy-start | bytes 2359300
  0.0 18.7 %collective-permute-start = (bf16[1024,3,128]{2,0,1:T(8,128)(2,1)}, bf16[1024,3,128]{2,0,1:T(8,128)(2,1)S(1)}, u32[]{:S(2)}, u32[]{:S(2)}) collective-permute-start(bf16[1024,3,128]{2,0,1:T(8,128)(2,1)} %param.6), channel_id=1, source_target_pairs={{0,1},{1,0},{2,3},{3,2},{4,6},{5,7},{6,4},{7,5},{8,9},{9,8},{10,11... | collective-permute-start | bytes 2359304 | tf_op jit(solution)/shard_map/ppermute | solution.py:249
  4.8 10.1 %copy-start.2 = (s32[8,128,2]{1,2,0:T(2,128)S(1)}, s32[8,128,2]{1,2,0:T(2,128)}, u32[]{:S(2)}) copy-start(s32[8,128,2]{1,2,0:T(2,128)} %param.7) | copy-start | bytes 24580
  4.8 7.4 %collective-permute-start.2 = (bf16[256,256]{1,0:T(8,128)(2,1)S(1)}, bf16[256,256]{1,0:T(8,128)(2,1)S(1)}, u32[]{:S(2)}, u32[]{:S(2)}) collective-permute-start(bf16[256,256]{1,0:T(8,128)(2,1)S(1)} %get-tuple-element.32), channel_id=1, source_target_pairs={{0,28},{4,8},{8,4},{12,16},{16,12},{20,24},{24,20},{28,0},{1,29},{... | collective-permute-start | bytes 393224 | tf_op jit(solution)/shard_map/ppermute | solution.py:245
  7.7 4.5 %collective-permute-start.3 = (bf16[256,256]{1,0:T(8,128)(2,1)S(1)}, bf16[256,256]{1,0:T(8,128)(2,1)S(1)}, u32[]{:S(2)}, u32[]{:S(2)}) collective-permute-start(bf16[256,256]{1,0:T(8,128)(2,1)S(1)} %get-tuple-element.33), channel_id=1, source_target_pairs={{0,4},{4,0},{8,12},{12,8},{16,20},{20,16},{24,28},{28,24},{1,5},{5... | collective-permute-start | bytes 393224 | tf_op jit(solution)/shard_map/ppermute | solution.py:242
  7.7 11.1 %collective-permute-start.4 = (bf16[512,384]{1,0:T(8,128)(2,1)S(1)}, bf16[512,384]{1,0:T(8,128)(2,1)S(1)}, u32[]{:S(2)}, u32[]{:S(2)}) collective-permute-start(bf16[512,384]{1,0:T(8,128)(2,1)S(1)} %get-tuple-element.30.inner), channel_id=1, source_target_pairs={{0,2},{1,3},{2,0},{3,1},{4,5},{5,4},{6,7},{7,6},{8,10},{9,11},{10,... | collective-permute-start | bytes 1179656 | tf_op jit(solution)/shard_map/ppermute | solution.py:249
  13.3 8.7 %collective-permute-start.5 = (bf16[512,384]{1,0:T(8,128)(2,1)S(1)}, bf16[512,384]{1,0:T(8,128)(2,1)S(1)}, u32[]{:S(2)}, u32[]{:S(2)}) collective-permute-start(bf16[512,384]{1,0:T(8,128)(2,1)S(1)} %outer_image.1.outer), channel_id=1, source_target_pairs={{0,2},{1,3},{2,0},{3,1},{4,5},{5,4},{6,7},{7,6},{8,10},{9,11},{10,... | collective-permute-start | bytes 1179656 | tf_op jit(solution)/shard_map/ppermute | solution.py:249
  14.9 3.8 %collective-permute-start.1 = (s32[8,128,2]{1,2,0:T(2,128)S(1)}, s32[8,128,2]{1,2,0:T(2,128)S(1)}, u32[]{:S(2)}, u32[]{:S(2)}) collective-permute-start(s32[8,128,2]{1,2,0:T(2,128)S(1)} %copy-done.2), channel_id=1, source_target_pairs={{0,1},{1,0},{2,3},{3,2},{4,6},{5,7},{6,4},{7,5},{8,9},{9,8},{10,11... | collective-permute-start | bytes 24584 | tf_op jit(solution)/shard_map/ppermute | solution.py:249
  16.1 5.9 %collective-permute-start.6 = (bf16[128,384]{1,0:T(8,128)(2,1)S(1)}, bf16[128,384]{1,0:T(8,128)(2,1)S(1)}, u32[]{:S(2)}, u32[]{:S(2)}) collective-permute-start(bf16[128,384]{1,0:T(8,128)(2,1)S(1)} %get-tuple-element.38), channel_id=1, source_target_pairs={{0,28},{4,8},{8,4},{12,16},{16,12},{20,24},{24,20},{28,0},{1,29},{... | collective-permute-start | bytes 294920 | tf_op jit(solution)/shard_map/ppermute | solution.py:245
  18.7 3.3 %collective-permute-start.7 = (bf16[128,384]{1,0:T(8,128)(2,1)S(1)}, bf16[128,384]{1,0:T(8,128)(2,1)S(1)}, u32[]{:S(2)}, u32[]{:S(2)}) collective-permute-start(bf16[128,384]{1,0:T(8,128)(2,1)S(1)} %get-tuple-element.39), channel_id=1, source_target_pairs={{0,4},{4,0},{8,12},{12,8},{16,20},{20,16},{24,28},{28,24},{1,5},{5... | collective-permute-start | bytes 294920 | tf_op jit(solution)/shard_map/ppermute | solution.py:242
  22.4 11.4 %collective-permute-start.10 = (bf16[128,768]{1,0:T(8,128)(2,1)S(1)}, bf16[128,768]{1,0:T(8,128)(2,1)S(1)}, u32[]{:S(2)}, u32[]{:S(2)}) collective-permute-start(bf16[128,768]{1,0:T(8,128)(2,1)S(1)} %get-tuple-element.48), channel_id=1, source_target_pairs={{0,29},{1,28},{2,31},{3,30},{4,10},{5,11},{6,8},{7,9},{8,5},{9,4},... | collective-permute-start | bytes 589832 | tf_op jit(solution)/shard_map/ppermute | solution.py:249
  26.6 7.3 %collective-permute-start.12 = (bf16[128,768]{1,0:T(8,128)(2,1)S(1)}, bf16[128,768]{1,0:T(8,128)(2,1)S(1)}, u32[]{:S(2)}, u32[]{:S(2)}) collective-permute-start(bf16[128,768]{1,0:T(8,128)(2,1)S(1)} %get-tuple-element.50), channel_id=1, source_target_pairs={{0,1},{1,0},{2,3},{3,2},{4,6},{5,7},{6,4},{7,5},{8,9},{9,8},{10,11... | collective-permute-start | bytes 589832 | tf_op jit(solution)/shard_map/ppermute | solution.py:249
  27.1 6.7 %collective-permute-start.8 = (bf16[128,768]{1,0:T(8,128)(2,1)S(1)}, bf16[128,768]{1,0:T(8,128)(2,1)S(1)}, u32[]{:S(2)}, u32[]{:S(2)}) collective-permute-start(bf16[128,768]{1,0:T(8,128)(2,1)S(1)} %get-tuple-element.44), channel_id=1, source_target_pairs={{0,5},{1,4},{2,7},{3,6},{4,2},{5,3},{6,0},{7,1},{8,13},{9,12},{10,... | collective-permute-start | bytes 589832 | tf_op jit(solution)/shard_map/ppermute | solution.py:249
  27.5 6.3 %collective-permute-start.11 = (bf16[128,384]{1,0:T(8,128)(2,1)S(1)}, bf16[128,384]{1,0:T(8,128)(2,1)S(1)}, u32[]{:S(2)}, u32[]{:S(2)}) collective-permute-start(bf16[128,384]{1,0:T(8,128)(2,1)S(1)} %get-tuple-element.49), channel_id=1, source_target_pairs={{0,28},{4,8},{8,4},{12,16},{16,12},{20,24},{24,20},{28,0},{1,29},{... | collective-permute-start | bytes 294920 | tf_op jit(solution)/shard_map/ppermute | solution.py:245
  29.3 4.6 %collective-permute-start.9 = (bf16[128,384]{1,0:T(8,128)(2,1)S(1)}, bf16[128,384]{1,0:T(8,128)(2,1)S(1)}, u32[]{:S(2)}, u32[]{:S(2)}) collective-permute-start(bf16[128,384]{1,0:T(8,128)(2,1)S(1)} %get-tuple-element.47), channel_id=1, source_target_pairs={{0,4},{4,0},{8,12},{12,8},{16,20},{20,16},{24,28},{28,24},{1,5},{5... | collective-permute-start | bytes 294920 | tf_op jit(solution)/shard_map/ppermute | solution.py:242

commit v19 on v18

--- a/solution.py
+++ b/solution.py
@@ -191,8 +191,10 @@
     store_tile(tile, far.at[:, wide:], far_link.at[:, wide:], far_chip.at[:, wide:])
 
 
-def near_tile(base, left_outer, outer_r, near, near_link, near_chip):
-    store_tile(base[...] + dot(left_outer[...], outer_r[...]), near, near_link, near_chip)
+def near_tile(own_chip, base, left_outer, outer_r, near, near_link, near_chip):
+    wide = outer_r.shape[1]
+    near_chip[:, :wide] = own_chip[...]
+    store_tile(base[...] + dot(left_outer[...], outer_r[...]), near, near_link, near_chip.at[:, wide:])
 
 
 def add_tiles(steps, *refs):
@@ -204,7 +206,7 @@
     even = parity() == 0
     copies = []
     for n, ((even_step, odd_step), chunks) in enumerate(steps):
-        chip, link, own = (
+        own, chip, link = (
             terms[n + k * count][:, m * 3 * width : (m + 1) * 3 * width].astype(F32) for k, m in enumerate(chunks)
         )
         prev = jnp.where(even, link, chip)
@@ -314,7 +316,7 @@
         flops=tile_flops,
         name="own_tile",
     )
-    own_link, own_chip = over_link(own_link), over_chip(own_chip)
+    own_link = over_link(own_link)
     part, part_link, part_chip, far_outer, far_base, near_base = call(
         functools.partial(partner_tile, size),
         (*tile_shapes(width, wide, BF16), left_shapes[1], base_shape, base_shape),
@@ -325,7 +327,7 @@
         flops=2 * tile_flops,
         name="partner_tile",
     )
-    outer_r, own_link, own_chip, far_base = lax.optimization_barrier((outer_r, own_link, own_chip, far_base))
+    outer_r, own_link, far_base = lax.optimization_barrier((outer_r, own_link, far_base))
     far, far_link, far_chip = call(
         far_tile,
         (shape((width, 2 * wide), BF16),) * 3,
@@ -337,10 +339,10 @@
     )
     near, near_link, near_chip = call(
         near_tile,
-        tile_shapes(width, wide, F32),
+        (shape((width, wide), F32), shape((width, wide), BF16), shape((width, 2 * wide), BF16)),
+        [VMEM] * 4,
         [VMEM] * 3,
-        [VMEM] * 3,
-        (near_base, left_outer, outer_r),
+        (own_chip, near_base, left_outer, outer_r),
         flops=tile_flops // 2,
         name="near_tile",
     )
@@ -364,10 +366,10 @@
             name=name,
         )
 
-    coarse = add((((0, 0), (0, 0, 0)),), (own_chip, own_link, own), "add_own")
+    coarse = add((((0, 0), (0, 0, 0)),), (own, near_chip, own_link), "add_own")
     coarse = add(
-        (((3, 3), (1, 1, 1)), ((1, 2), (0, 0, 0)), ((2, 1), (0, 0, 0))),
-        (far_chip, near_chip, far_chip, far_link, near_link, far_link, far, far, near),
+        (((3, 3), (1, 1, 1)), ((1, 2), (0, 1, 0)), ((2, 1), (0, 0, 0))),
+        (far, far, near, far_chip, near_chip, far_chip, far_link, near_link, far_link),
         "add_rest",
         coarse,
     )

time: 35.1 us -> 35.9 us (1.023)
  waiting for transfers between devices: 11.2 us -> 11.8 us
    ppermute x7, waiting for transfers between devices: 1.51 us -> 3.28 us  [to(): return lax.ppermute(value, ('blk', 'col'), perm)]
    ppermute x3, waiting for transfers between devices: 9.73 us -> 8.54 us  [over_link(): return lax.ppermute(value, 'blk', cross)]
  transfers between devices with their start and end apart: 13 -> 12, of which waited for: 4 -> 3; matrix products, arithmetic and copies ran while one was open for 0% -> 0% of each run, Pallas kernels for 17% -> 17%
where the time goes in v19:
time: 35.9 us; the launch traced here: 35.7 us
  starting transfers between devices  16.3 us (45%)
  waiting for transfers between devices  11.8 us (33%)
  Pallas kernels  7.49 us (21%)
    ppermute x7, starting transfers between devices, to(): return lax.ppermute(value, ('blk', 'col'), perm)  10.2 us
    ppermute x3, waiting for transfers between devices, over_link(): return lax.ppermute(value, 'blk', cross)  8.54 us
    pallas_call x8, Pallas kernels, call(): pl.pallas_call(kernel, out_shape=out_shape, in_specs=in_specs, out_specs=...  7.49 us
    ppermute x3, starting transfers between devices, over_link(): return lax.ppermute(value, 'blk', cross)  5.99 us
    ppermute x7, waiting for transfers between devices, to(): return lax.ppermute(value, ('blk', 'col'), perm)  3.28 us
  transfers between devices with their start and end apart: 12, of which 3 were waited for; matrix products, arithmetic and copies ran while one was open for 0% of the time, Pallas kernels for 17%

profile of v19, /device:TPU:0, one launch (start us, length us, event | category | flops | bytes accessed | tf_op | source)
XLA Modules:
  0.0 35.7 jit_solution(12851228408588455997)
XLA Ops:
  0.0 2.9 %collective-permute-start = (bf16[1024,3,128]{2,0,1:T(8,128)(2,1)}, bf16[1024,3,128]{2,0,1:T(8,128)(2,1)S(1)}, u32[]{:S(2)}, u32[]{:S(2)}) collective-permute-start(bf16[1024,3,128]{2,0,1:T(8,128)(2,1)} %param.6), channel_id=1, source_target_pairs={{0,1},{1,0},{2,3},{3,2},{4,6},{5,7},{6,4},{7,5},{8,9},{9,8},{10,11... | collective-permute-start | bytes 2359304 | tf_op jit(solution)/shard_map/ppermute | solution.py:251
  2.9 1.8 %mask_and_inner.1 = (bf16[1024,384]{1,0:T(8,128)(2,1)S(1)}, bf16[256,256]{1,0:T(8,128)(2,1)S(1)}, bf16[256,256]{1,0:T(8,128)(2,1)S(1)}, bf16[512,384]{1,0:T(8,128)(2,1)S(1)}) custom-call(s32[3,8]{1,0:T(4,128)} %bitcast.8, bf16[3,1024,128]{2,1,0:T(8,128)(2,1)} %bitcast.10, s32[8,2,128]{2,1,0:T(2,128)} %bitcast.11, bf16[8,3,128,128]{3,2,1,0:T(8,128)(2,1)} %stiffness.1), custom_call_target="tpu_custom_call" | custom-call | flops 150994944 | bytes 3022944 | tf_op jit(solution)/shard_map/mask_and_inner/pallas_call | solution.py:29
  4.8 2.9 %collective-permute-start.2 = (bf16[256,256]{1,0:T(8,128)(2,1)S(1)}, bf16[256,256]{1,0:T(8,128)(2,1)S(1)}, u32[]{:S(2)}, u32[]{:S(2)}) collective-permute-start(bf16[256,256]{1,0:T(8,128)(2,1)S(1)} %get-tuple-element.31), channel_id=1, source_target_pairs={{0,28},{4,8},{8,4},{12,16},{16,12},{20,24},{24,20},{28,0},{1,29},{... | collective-permute-start | bytes 393224 | tf_op jit(solution)/shard_map/ppermute | solution.py:247
  7.6 0.5 %collective-permute-start.4 = (bf16[512,384]{1,0:T(8,128)(2,1)S(1)}, bf16[512,384]{1,0:T(8,128)(2,1)S(1)}, u32[]{:S(2)}, u32[]{:S(2)}) collective-permute-start(bf16[512,384]{1,0:T(8,128)(2,1)S(1)} %get-tuple-element.29.inner), channel_id=1, source_target_pairs={{0,2},{1,3},{2,0},{3,1},{4,5},{5,4},{6,7},{7,6},{8,10},{9,11},{10,... | collective-permute-start | bytes 1179656 | tf_op jit(solution)/shard_map/ppermute | solution.py:251
  8.2 4.0 %collective-permute-done.2.from_link = bf16[256,256]{1,0:T(8,128)(2,1)S(1)} collective-permute-done((bf16[256,256]{1,0:T(8,128)(2,1)S(1)}, bf16[256,256]{1,0:T(8,128)(2,1)S(1)}, u32[]{:S(2)}, u32[]{:S(2)}) %collective-permute-start.2) | collective-permute-done | bytes 131104 | tf_op jit(solution)/shard_map/ppermute | solution.py:247
  12.2 0.0 collective-permute-done.3.from_chip
  12.2 1.1 %outer_image.1.outer = bf16[512,384]{1,0:T(8,128)(2,1)S(1)} custom-call(s32[3,8]{1,0:T(4,128)S(1)} %bitcast.9, bf16[8,3,128,128]{3,2,1,0:T(8,128)(2,1)S(1)} %copy-done, bf16[1024,384]{1,0:T(8,128)(2,1)S(1)} %get-tuple-element.30.masked, bf16[256,256]{1,0:T(8,128)(2,1)S(1)} %collective-permute-done.2.from_link, ...), custom_call_target="tpu_custom_call" | custom-call | flops 150994944 | bytes 2228320 | tf_op jit(solution)/shard_map/outer_image/pallas_call | solution.py:29
  13.3 0.0 copy-start.2
  13.3 1.6 %collective-permute-start.5 = (bf16[512,384]{1,0:T(8,128)(2,1)S(1)}, bf16[512,384]{1,0:T(8,128)(2,1)S(1)}, u32[]{:S(2)}, u32[]{:S(2)}) collective-permute-start(bf16[512,384]{1,0:T(8,128)(2,1)S(1)} %outer_image.1.outer), channel_id=1, source_target_pairs={{0,2},{1,3},{2,0},{3,1},{4,5},{5,4},{6,7},{7,6},{8,10},{9,11},{10,... | collective-permute-start | bytes 1179656 | tf_op jit(solution)/shard_map/ppermute | solution.py:251
  14.9 0.6 %own_tile.1 = (f32[128,384]{1,0:T(8,128)S(1)}, bf16[128,384]{1,0:T(8,128)(2,1)S(1)}, bf16[128,384]{1,0:T(8,128)(2,1)S(1)}, bf16[384,512]{1,0:T(8,128)(2,1)S(1)}, bf16[384,512]{1,0:T(8,128)(2,1)S(1)}) custom-call(bf16[1024,384]{1,0:T(8,128)(2,1)S(1)} %get-tuple-element.30.masked, bf16[512,384]{1,0:T(8,128)(2,1)S(1)} %get-tuple-element.29.inner, ...), custom_call_target="tpu_custom_call" | custom-call | flops 301989888 | bytes 2752512 | tf_op jit(solution)/shard_map/own_tile/pallas_call | solution.py:29
  15.5 1.4 %collective-permute-start.6 = (bf16[128,384]{1,0:T(8,128)(2,1)S(1)}, bf16[128,384]{1,0:T(8,128)(2,1)S(1)}, u32[]{:S(2)}, u32[]{:S(2)}) collective-permute-start(bf16[128,384]{1,0:T(8,128)(2,1)S(1)} %get-tuple-element.37), channel_id=1, source_target_pairs={{0,28},{4,8},{8,4},{12,16},{16,12},{20,24},{24,20},{28,0},{1,29},{... | collective-permute-start | bytes 294920 | tf_op jit(solution)/shard_map/ppermute | solution.py:247
  16.9 0.5 %collective-permute-start.1 = (s32[8,128,2]{1,2,0:T(2,128)S(1)}, s32[8,128,2]{1,2,0:T(2,128)S(1)}, u32[]{:S(2)}, u32[]{:S(2)}) collective-permute-start(s32[8,128,2]{1,2,0:T(2,128)S(1)} %copy-done.2), channel_id=1, source_target_pairs={{0,1},{1,0},{2,3},{3,2},{4,6},{5,7},{6,4},{7,5},{8,9},{9,8},{10,11... | collective-permute-start | bytes 24584 | tf_op jit(solution)/shard_map/ppermute | solution.py:251
  17.5 3.3 %collective-permute-done.1 = s32[8,128,2]{1,2,0:T(2,128)S(1)} collective-permute-done((s32[8,128,2]{1,2,0:T(2,128)S(1)}, s32[8,128,2]{1,2,0:T(2,128)S(1)}, u32[]{:S(2)}, u32[]{:S(2)}) %collective-permute-start.1) | collective-permute-done | bytes 8224 | tf_op jit(solution)/shard_map/ppermute | solution.py:251
  20.8 1.3 %partner_tile.1 = (bf16[128,384]{1,0:T(8,128)(2,1)S(1)}, bf16[128,384]{1,0:T(8,128)(2,1)S(1)}, bf16[128,384]{1,0:T(8,128)(2,1)S(1)}, bf16[384,512]{1,0:T(8,128)(...) custom-call(bf16[3,1024,128]{2,1,0:T(8,128)(2,1)S(1)} %bitcast.6, s32[8,2,128]{2,1,0:T(2,128)S(1)} %bitcast.7, ...), custom_call_target="tpu_custom_call" | custom-call | flops 603979776 | bytes 4235264 | tf_op jit(solution)/shard_map/partner_tile/pallas_call | solution.py:29
  22.0 0.0 collective-permute-done.6.refs_2_
  22.1 0.4 %near_tile.1 = (f32[128,384]{1,0:T(8,128)S(1)}, bf16[128,384]{1,0:T(8,128)(2,1)S(1)}, bf16[128,768]{1,0:T(8,128)(2,1)S(1)}) custom-call(bf16[128,384]{1,0:T(8,128)(2,1)S(1)} %get-tuple-element.43.own_chip, f32[384,384]{1,0:T(8,128)S(1)} %get-tuple-element.44.base, bf16[384,512]{1,0:T(8,128)(2,1)S(1)} %get-tuple-element.45.left_outer, ...), custom_call_target="tpu_custom_call" | custom-call | flops 150994944 | bytes 1966080 | tf_op jit(solution)/shard_map/near_tile/pallas_call | solution.py:29
  22.5 0.1 collective-permute-start.9
  22.5 0.4 %far_tile.1 = (bf16[128,768]{1,0:T(8,128)(2,1)S(1)}, bf16[128,768]{1,0:T(8,128)(2,1)S(1)}, bf16[128,768]{1,0:T(8,128)(2,1)S(1)}) custom-call(bf16[128,384]{1,0:T(8,128)(2,1)S(1)} %get-tuple-element.34.part, bf16[128,384]{1,0:T(8,128)(2,1)S(1)} %get-tuple-element.35.part_link, bf16[128,384]{1,0:T(8,128)(2,1)S(1)} %get-tuple-element.36.part_chip, ...), custom_call_target="tpu_custom_call" | custom-call | flops 150994944 | bytes 2260992 | tf_op jit(solution)/shard_map/far_tile/pallas_call | solution.py:29
  23.0 4.1 %collective-permute-start.10 = (bf16[128,768]{1,0:T(8,128)(2,1)S(1)}, bf16[128,768]{1,0:T(8,128)(2,1)S(1)}, u32[]{:S(2)}, u32[]{:S(2)}) collective-permute-start(bf16[128,768]{1,0:T(8,128)(2,1)S(1)} %get-tuple-element.49), channel_id=1, source_target_pairs={{0,29},{1,28},{2,31},{3,30},{4,10},{5,11},{6,8},{7,9},{8,5},{9,4},... | collective-permute-start | bytes 589832 | tf_op jit(solution)/shard_map/ppermute | solution.py:251
  27.1 0.5 %collective-permute-start.7 = (bf16[128,768]{1,0:T(8,128)(2,1)S(1)}, bf16[128,768]{1,0:T(8,128)(2,1)S(1)}, u32[]{:S(2)}, u32[]{:S(2)}) collective-permute-start(bf16[128,768]{1,0:T(8,128)(2,1)S(1)} %get-tuple-element.42), channel_id=1, source_target_pairs={{0,1},{1,0},{2,3},{3,2},{4,6},{5,7},{6,4},{7,5},{8,9},{9,8},{10,11... | collective-permute-start | bytes 589832 | tf_op jit(solution)/shard_map/ppermute | solution.py:251
  27.6 1.7 %collective-permute-start.11 = (bf16[128,384]{1,0:T(8,128)(2,1)S(1)}, bf16[128,384]{1,0:T(8,128)(2,1)S(1)}, u32[]{:S(2)}, u32[]{:S(2)}) collective-permute-start(bf16[128,384]{1,0:T(8,128)(2,1)S(1)} %get-tuple-element.50), channel_id=1, source_target_pairs={{0,28},{4,8},{8,4},{12,16},{16,12},{20,24},{24,20},{28,0},{1,29},{... | collective-permute-start | bytes 294920 | tf_op jit(solution)/shard_map/ppermute | solution.py:247
  29.3 0.8 %add_own.1.refs_9_ = f32[5,128,512]{2,1,0:T(8,128)} custom-call(f32[128,384]{1,0:T(8,128)S(1)} %get-tuple-element.51.refs_0_, bf16[128,768]{1,0:T(8,128)(2,1)S(1)} %collective-permute-done.9.refs_1_.refs_4_, bf16[128,384]{1,0:T(8,128)(2,1)S(1)} %collective-permute-done.6.refs_2_), custom_call_target="tpu_custom_call" | custom-call | flops 81920 | bytes 1802240 | tf_op jit(solution)/shard_map/add_own/pallas_call | solution.py:29
  30.1 4.5 %collective-permute-done.11.refs_7_ = bf16[128,384]{1,0:T(8,128)(2,1)S(1)} collective-permute-done((bf16[128,384]{1,0:T(8,128)(2,1)S(1)}, bf16[128,384]{1,0:T(8,128)(2,1)S(1)}, u32[]{:S(2)}, u32[]{:S(2)}) %collective-permute-start.11) | collective-permute-done | bytes 98336 | tf_op jit(solution)/shard_map/ppermute | solution.py:247
  34.7 1.0 %add_rest.1 = f32[5,128,512]{2,1,0:T(8,128)} custom-call(bf16[128,768]{1,0:T(8,128)(2,1)S(1)} %collective-permute-done.7.refs_0_.refs_1_, bf16[128,768]{1,0:T(8,128)(2,1)S(1)} %collective-permute-done.7.refs_0_.refs_1_, f32[128,384]{1,0:T(8,128)S(1)} %get-tuple-element.46.refs_2_, ...), custom_call_target="tpu_custom_call", output_to_operand_aliasing={{}: (9, {})} | custom-call | flops 245760 | bytes 4292608 | tf_op jit(solution)/shard_map/add_rest/pallas_call | solution.py:29
  (14 shorter events, 0.0 us)
Async XLA Ops:
  0.0 12.2 %copy-start.1 = (s32[8,3]{0,1:T(4,128)S(1)}, s32[8,3]{0,1:T(4,128)}, u32[]{:S(2)}) copy-start(s32[8,3]{0,1:T(4,128)} %param.5) | copy-start | bytes 292
  0.0 12.2 %copy-start = (bf16[8,3,128,128]{3,2,1,0:T(8,128)(2,1)S(1)}, bf16[8,3,128,128]{3,2,1,0:T(8,128)(2,1)}, u32[]{:S(2)}) copy-start(bf16[8,3,128,128]{3,2,1,0:T(8,128)(2,1)} %stiffness.1) | copy-start | bytes 2359300
  0.0 20.8 %collective-permute-start = (bf16[1024,3,128]{2,0,1:T(8,128)(2,1)}, bf16[1024,3,128]{2,0,1:T(8,128)(2,1)S(1)}, u32[]{:S(2)}, u32[]{:S(2)}) collective-permute-start(bf16[1024,3,128]{2,0,1:T(8,128)(2,1)} %param.6), channel_id=1, source_target_pairs={{0,1},{1,0},{2,3},{3,2},{4,6},{5,7},{6,4},{7,5},{8,9},{9,8},{10,11... | collective-permute-start | bytes 2359304 | tf_op jit(solution)/shard_map/ppermute | solution.py:251
  4.8 7.4 %collective-permute-start.2 = (bf16[256,256]{1,0:T(8,128)(2,1)S(1)}, bf16[256,256]{1,0:T(8,128)(2,1)S(1)}, u32[]{:S(2)}, u32[]{:S(2)}) collective-permute-start(bf16[256,256]{1,0:T(8,128)(2,1)S(1)} %get-tuple-element.31), channel_id=1, source_target_pairs={{0,28},{4,8},{8,4},{12,16},{16,12},{20,24},{24,20},{28,0},{1,29},{... | collective-permute-start | bytes 393224 | tf_op jit(solution)/shard_map/ppermute | solution.py:247
  7.6 4.5 %collective-permute-start.3 = (bf16[256,256]{1,0:T(8,128)(2,1)S(1)}, bf16[256,256]{1,0:T(8,128)(2,1)S(1)}, u32[]{:S(2)}, u32[]{:S(2)}) collective-permute-start(bf16[256,256]{1,0:T(8,128)(2,1)S(1)} %get-tuple-element.32), channel_id=1, source_target_pairs={{0,4},{4,0},{8,12},{12,8},{16,20},{20,16},{24,28},{28,24},{1,5},{5... | collective-permute-start | bytes 393224 | tf_op jit(solution)/shard_map/ppermute | solution.py:244
  7.6 13.1 %collective-permute-start.4 = (bf16[512,384]{1,0:T(8,128)(2,1)S(1)}, bf16[512,384]{1,0:T(8,128)(2,1)S(1)}, u32[]{:S(2)}, u32[]{:S(2)}) collective-permute-start(bf16[512,384]{1,0:T(8,128)(2,1)S(1)} %get-tuple-element.29.inner), channel_id=1, source_target_pairs={{0,2},{1,3},{2,0},{3,1},{4,5},{5,4},{6,7},{7,6},{8,10},{9,11},{10,... | collective-permute-start | bytes 1179656 | tf_op jit(solution)/shard_map/ppermute | solution.py:251
  13.3 3.6 %copy-start.2 = (s32[8,128,2]{1,2,0:T(2,128)S(1)}, s32[8,128,2]{1,2,0:T(2,128)}, u32[]{:S(2)}) copy-start(s32[8,128,2]{1,2,0:T(2,128)} %param.7) | copy-start | bytes 24580
  13.3 8.7 %collective-permute-start.5 = (bf16[512,384]{1,0:T(8,128)(2,1)S(1)}, bf16[512,384]{1,0:T(8,128)(2,1)S(1)}, u32[]{:S(2)}, u32[]{:S(2)}) collective-permute-start(bf16[512,384]{1,0:T(8,128)(2,1)S(1)} %outer_image.1.outer), channel_id=1, source_target_pairs={{0,2},{1,3},{2,0},{3,1},{4,5},{5,4},{6,7},{7,6},{8,10},{9,11},{10,... | collective-permute-start | bytes 1179656 | tf_op jit(solution)/shard_map/ppermute | solution.py:251
  15.5 6.5 %collective-permute-start.6 = (bf16[128,384]{1,0:T(8,128)(2,1)S(1)}, bf16[128,384]{1,0:T(8,128)(2,1)S(1)}, u32[]{:S(2)}, u32[]{:S(2)}) collective-permute-start(bf16[128,384]{1,0:T(8,128)(2,1)S(1)} %get-tuple-element.37), channel_id=1, source_target_pairs={{0,28},{4,8},{8,4},{12,16},{16,12},{20,24},{24,20},{28,0},{1,29},{... | collective-permute-start | bytes 294920 | tf_op jit(solution)/shard_map/ppermute | solution.py:247
  16.9 3.8 %collective-permute-start.1 = (s32[8,128,2]{1,2,0:T(2,128)S(1)}, s32[8,128,2]{1,2,0:T(2,128)S(1)}, u32[]{:S(2)}, u32[]{:S(2)}) collective-permute-start(s32[8,128,2]{1,2,0:T(2,128)S(1)} %copy-done.2), channel_id=1, source_target_pairs={{0,1},{1,0},{2,3},{3,2},{4,6},{5,7},{6,4},{7,5},{8,9},{9,8},{10,11... | collective-permute-start | bytes 24584 | tf_op jit(solution)/shard_map/ppermute | solution.py:251
  22.5 6.9 %collective-permute-start.9 = (bf16[128,768]{1,0:T(8,128)(2,1)S(1)}, bf16[128,768]{1,0:T(8,128)(2,1)S(1)}, u32[]{:S(2)}, u32[]{:S(2)}) collective-permute-start(bf16[128,768]{1,0:T(8,128)(2,1)S(1)} %get-tuple-element.48), channel_id=1, source_target_pairs={{0,4},{4,0},{8,12},{12,8},{16,20},{20,16},{24,28},{28,24},{1,5},{5... | collective-permute-start | bytes 589832 | tf_op jit(solution)/shard_map/ppermute | solution.py:244
  23.0 11.7 %collective-permute-start.10 = (bf16[128,768]{1,0:T(8,128)(2,1)S(1)}, bf16[128,768]{1,0:T(8,128)(2,1)S(1)}, u32[]{:S(2)}, u32[]{:S(2)}) collective-permute-start(bf16[128,768]{1,0:T(8,128)(2,1)S(1)} %get-tuple-element.49), channel_id=1, source_target_pairs={{0,29},{1,28},{2,31},{3,30},{4,10},{5,11},{6,8},{7,9},{8,5},{9,4},... | collective-permute-start | bytes 589832 | tf_op jit(solution)/shard_map/ppermute | solution.py:251
  27.1 7.6 %collective-permute-start.7 = (bf16[128,768]{1,0:T(8,128)(2,1)S(1)}, bf16[128,768]{1,0:T(8,128)(2,1)S(1)}, u32[]{:S(2)}, u32[]{:S(2)}) collective-permute-start(bf16[128,768]{1,0:T(8,128)(2,1)S(1)} %get-tuple-element.42), channel_id=1, source_target_pairs={{0,1},{1,0},{2,3},{3,2},{4,6},{5,7},{6,4},{7,5},{8,9},{9,8},{10,11... | collective-permute-start | bytes 589832 | tf_op jit(solution)/shard_map/ppermute | solution.py:251
  27.6 7.1 %collective-permute-start.8 = (bf16[128,768]{1,0:T(8,128)(2,1)S(1)}, bf16[128,768]{1,0:T(8,128)(2,1)S(1)}, u32[]{:S(2)}, u32[]{:S(2)}) collective-permute-start(bf16[128,768]{1,0:T(8,128)(2,1)S(1)} %get-tuple-element.47), channel_id=1, source_target_pairs={{0,5},{1,4},{2,7},{3,6},{4,2},{5,3},{6,0},{7,1},{8,13},{9,12},{10,... | collective-permute-start | bytes 589832 | tf_op jit(solution)/shard_map/ppermute | solution.py:251
  27.6 7.1 %collective-permute-start.11 = (bf16[128,384]{1,0:T(8,128)(2,1)S(1)}, bf16[128,384]{1,0:T(8,128)(2,1)S(1)}, u32[]{:S(2)}, u32[]{:S(2)}) collective-permute-start(bf16[128,384]{1,0:T(8,128)(2,1)S(1)} %get-tuple-element.50), channel_id=1, source_target_pairs={{0,28},{4,8},{8,4},{12,16},{16,12},{20,24},{24,20},{28,0},{1,29},{... | collective-permute-start | bytes 294920 | tf_op jit(solution)/shard_map/ppermute | solution.py:247

commit v20 on v18

--- a/solution.py
+++ b/solution.py
@@ -315,6 +315,7 @@
         name="own_tile",
     )
     own_link, own_chip = over_link(own_link), over_chip(own_chip)
+    inner_r, own_chip = lax.optimization_barrier((inner_r, own_chip))
     part, part_link, part_chip, far_outer, far_base, near_base = call(
         functools.partial(partner_tile, size),
         (*tile_shapes(width, wide, BF16), left_shapes[1], base_shape, base_shape),

time: 35.1 us -> 35.3 us (level)
  waiting for transfers between devices: 11.2 us -> 11.8 us
  starting transfers between devices: 16.1 us -> 15.7 us
    ppermute x7, waiting for transfers between devices: 1.51 us -> 3.8 us  [to(): return lax.ppermute(value, ('blk', 'col'), perm)]
    ppermute x3, waiting for transfers between devices: 9.73 us -> 7.97 us  [over_link(): return lax.ppermute(value, 'blk', cross)]
    ppermute x7, starting transfers between devices: 10.3 us -> 8.87 us  [to(): return lax.ppermute(value, ('blk', 'col'), perm)]
    ppermute x3, starting transfers between devices: 5.73 us -> 6.78 us  [over_link(): return lax.ppermute(value, 'blk', cross)]
  transfers between devices with their start and end apart: 13 -> 13, of which waited for: 4 -> 3; matrix products, arithmetic and copies ran while one was open for 0% -> 0% of each run, Pallas kernels for 17% -> 17%
where the time goes in v20:
time: 35.3 us; the launch traced here: 35.1 us
  starting transfers between devices  15.7 us (44%)
  waiting for transfers between devices  11.8 us (33%)
  Pallas kernels  7.47 us (21%)
    ppermute x7, starting transfers between devices, to(): return lax.ppermute(value, ('blk', 'col'), perm)  8.87 us
    ppermute x3, waiting for transfers between devices, over_link(): return lax.ppermute(value, 'blk', cross)  7.97 us
    pallas_call x8, Pallas kernels, call(): pl.pallas_call(kernel, out_shape=out_shape, in_specs=in_specs, out_specs=...  7.47 us
    ppermute x3, starting transfers between devices, over_link(): return lax.ppermute(value, 'blk', cross)  6.78 us
    ppermute x7, waiting for transfers between devices, to(): return lax.ppermute(value, ('blk', 'col'), perm)  3.8 us
  transfers between devices with their start and end apart: 13, of which 3 were waited for; matrix products, arithmetic and copies ran while one was open for 0% of the time, Pallas kernels for 17%

profile of v20, /device:TPU:0, one launch (start us, length us, event | category | flops | bytes accessed | tf_op | source)
XLA Modules:
  0.0 35.1 jit_solution(5627639547425584192)
XLA Ops:
  0.0 2.9 %collective-permute-start = (bf16[1024,3,128]{2,0,1:T(8,128)(2,1)}, bf16[1024,3,128]{2,0,1:T(8,128)(2,1)S(1)}, u32[]{:S(2)}, u32[]{:S(2)}) collective-permute-start(bf16[1024,3,128]{2,0,1:T(8,128)(2,1)} %param.6), channel_id=1, source_target_pairs={{0,1},{1,0},{2,3},{3,2},{4,6},{5,7},{6,4},{7,5},{8,9},{9,8},{10,11... | collective-permute-start | bytes 2359304 | tf_op jit(solution)/shard_map/ppermute | solution.py:249
  2.9 1.8 %mask_and_inner.1 = (bf16[1024,384]{1,0:T(8,128)(2,1)S(1)}, bf16[256,256]{1,0:T(8,128)(2,1)S(1)}, bf16[256,256]{1,0:T(8,128)(2,1)S(1)}, bf16[512,384]{1,0:T(8,128)(2,1)S(1)}) custom-call(s32[3,8]{1,0:T(4,128)} %bitcast.8, bf16[3,1024,128]{2,1,0:T(8,128)(2,1)} %bitcast.10, s32[8,2,128]{2,1,0:T(2,128)} %bitcast.11, bf16[8,3,128,128]{3,2,1,0:T(8,128)(2,1)} %stiffness.1), custom_call_target="tpu_custom_call" | custom-call | flops 150994944 | bytes 3022944 | tf_op jit(solution)/shard_map/mask_and_inner/pallas_call | solution.py:29
  4.8 2.9 %collective-permute-start.2 = (bf16[256,256]{1,0:T(8,128)(2,1)S(1)}, bf16[256,256]{1,0:T(8,128)(2,1)S(1)}, u32[]{:S(2)}, u32[]{:S(2)}) collective-permute-start(bf16[256,256]{1,0:T(8,128)(2,1)S(1)} %get-tuple-element.34), channel_id=1, source_target_pairs={{0,28},{4,8},{8,4},{12,16},{16,12},{20,24},{24,20},{28,0},{1,29},{... | collective-permute-start | bytes 393224 | tf_op jit(solution)/shard_map/ppermute | solution.py:245
  7.6 0.0 collective-permute-start.3
  7.6 0.5 %collective-permute-start.4 = (bf16[512,384]{1,0:T(8,128)(2,1)S(1)}, bf16[512,384]{1,0:T(8,128)(2,1)S(1)}, u32[]{:S(2)}, u32[]{:S(2)}) collective-permute-start(bf16[512,384]{1,0:T(8,128)(2,1)S(1)} %get-tuple-element.32.inner), channel_id=1, source_target_pairs={{0,2},{1,3},{2,0},{3,1},{4,5},{5,4},{6,7},{7,6},{8,10},{9,11},{10,... | collective-permute-start | bytes 1179656 | tf_op jit(solution)/shard_map/ppermute | solution.py:249
  8.2 4.0 %collective-permute-done.2.from_link = bf16[256,256]{1,0:T(8,128)(2,1)S(1)} collective-permute-done((bf16[256,256]{1,0:T(8,128)(2,1)S(1)}, bf16[256,256]{1,0:T(8,128)(2,1)S(1)}, u32[]{:S(2)}, u32[]{:S(2)}) %collective-permute-start.2) | collective-permute-done | bytes 131104 | tf_op jit(solution)/shard_map/ppermute | solution.py:245
  12.2 0.0 collective-permute-done.3.from_chip
  12.2 1.1 %outer_image.1.outer = bf16[512,384]{1,0:T(8,128)(2,1)S(1)} custom-call(s32[3,8]{1,0:T(4,128)S(1)} %bitcast.9, bf16[8,3,128,128]{3,2,1,0:T(8,128)(2,1)S(1)} %copy-done, bf16[1024,384]{1,0:T(8,128)(2,1)S(1)} %get-tuple-element.33.masked, bf16[256,256]{1,0:T(8,128)(2,1)S(1)} %collective-permute-done.2.from_link, ...), custom_call_target="tpu_custom_call" | custom-call | flops 150994944 | bytes 2228320 | tf_op jit(solution)/shard_map/outer_image/pallas_call | solution.py:29
  13.3 0.0 copy-start.2
  13.3 1.6 %collective-permute-start.6 = (bf16[512,384]{1,0:T(8,128)(2,1)S(1)}, bf16[512,384]{1,0:T(8,128)(2,1)S(1)}, u32[]{:S(2)}, u32[]{:S(2)}) collective-permute-start(bf16[512,384]{1,0:T(8,128)(2,1)S(1)} %outer_image.1.outer), channel_id=1, source_target_pairs={{0,2},{1,3},{2,0},{3,1},{4,5},{5,4},{6,7},{7,6},{8,10},{9,11},{10,... | collective-permute-start | bytes 1179656 | tf_op jit(solution)/shard_map/ppermute | solution.py:249
  14.9 0.6 %own_tile.1 = (f32[128,384]{1,0:T(8,128)S(1)}, bf16[128,384]{1,0:T(8,128)(2,1)S(1)}, bf16[128,384]{1,0:T(8,128)(2,1)S(1)}, bf16[384,512]{1,0:T(8,128)(2,1)S(1)}, bf16[384,512]{1,0:T(8,128)(2,1)S(1)}) custom-call(bf16[1024,384]{1,0:T(8,128)(2,1)S(1)} %get-tuple-element.33.masked, bf16[512,384]{1,0:T(8,128)(2,1)S(1)} %get-tuple-element.32.inner, ...), custom_call_target="tpu_custom_call" | custom-call | flops 301989888 | bytes 2752512 | tf_op jit(solution)/shard_map/own_tile/pallas_call | solution.py:29
  15.5 0.1 collective-permute-start.5
  15.6 2.2 %collective-permute-start.7 = (bf16[128,384]{1,0:T(8,128)(2,1)S(1)}, bf16[128,384]{1,0:T(8,128)(2,1)S(1)}, u32[]{:S(2)}, u32[]{:S(2)}) collective-permute-start(bf16[128,384]{1,0:T(8,128)(2,1)S(1)} %get-tuple-element.42), channel_id=1, source_target_pairs={{0,28},{4,8},{8,4},{12,16},{16,12},{20,24},{24,20},{28,0},{1,29},{... | collective-permute-start | bytes 294920 | tf_op jit(solution)/shard_map/ppermute | solution.py:245
  17.8 3.8 %collective-permute-done.1 = s32[8,128,2]{1,2,0:T(2,128)S(1)} collective-permute-done((s32[8,128,2]{1,2,0:T(2,128)S(1)}, s32[8,128,2]{1,2,0:T(2,128)S(1)}, u32[]{:S(2)}, u32[]{:S(2)}) %collective-permute-start.1) | collective-permute-done | bytes 8224 | tf_op jit(solution)/shard_map/ppermute | solution.py:249
  21.6 1.3 %partner_tile.1 = (bf16[128,384]{1,0:T(8,128)(2,1)S(1)}, bf16[128,384]{1,0:T(8,128)(2,1)S(1)}, bf16[128,384]{1,0:T(8,128)(2,1)S(1)}, bf16[384,512]{1,0:T(8,128)(...) custom-call(bf16[3,1024,128]{2,1,0:T(8,128)(2,1)S(1)} %bitcast.6, s32[8,2,128]{2,1,0:T(2,128)S(1)} %bitcast.7, ...), custom_call_target="tpu_custom_call" | custom-call | flops 603979776 | bytes 4235264 | tf_op jit(solution)/shard_map/partner_tile/pallas_call | solution.py:29
  22.9 0.4 %far_tile.1 = (bf16[128,768]{1,0:T(8,128)(2,1)S(1)}, bf16[128,768]{1,0:T(8,128)(2,1)S(1)}, bf16[128,768]{1,0:T(8,128)(2,1)S(1)}) custom-call(bf16[128,384]{1,0:T(8,128)(2,1)S(1)} %get-tuple-element.39.part, bf16[128,384]{1,0:T(8,128)(2,1)S(1)} %get-tuple-element.40.part_link, bf16[128,384]{1,0:T(8,128)(2,1)S(1)} %get-tuple-element.41.part_chip, ...), custom_call_target="tpu_custom_call" | custom-call | flops 150994944 | bytes 2260992 | tf_op jit(solution)/shard_map/far_tile/pallas_call | solution.py:29
  23.3 3.3 %collective-permute-start.10 = (bf16[128,768]{1,0:T(8,128)(2,1)S(1)}, bf16[128,768]{1,0:T(8,128)(2,1)S(1)}, u32[]{:S(2)}, u32[]{:S(2)}) collective-permute-start(bf16[128,768]{1,0:T(8,128)(2,1)S(1)} %get-tuple-element.52), channel_id=1, source_target_pairs={{0,29},{1,28},{2,31},{3,30},{4,10},{5,11},{6,8},{7,9},{8,5},{9,4},... | collective-permute-start | bytes 589832 | tf_op jit(solution)/shard_map/ppermute | solution.py:249
  26.6 0.5 %collective-permute-start.12 = (bf16[128,768]{1,0:T(8,128)(2,1)S(1)}, bf16[128,768]{1,0:T(8,128)(2,1)S(1)}, u32[]{:S(2)}, u32[]{:S(2)}) collective-permute-start(bf16[128,768]{1,0:T(8,128)(2,1)S(1)} %get-tuple-element.54), channel_id=1, source_target_pairs={{0,1},{1,0},{2,3},{3,2},{4,6},{5,7},{6,4},{7,5},{8,9},{9,8},{10,11... | collective-permute-start | bytes 589832 | tf_op jit(solution)/shard_map/ppermute | solution.py:249
  27.1 0.4 %near_tile.1 = (f32[128,384]{1,0:T(8,128)S(1)}, bf16[128,384]{1,0:T(8,128)(2,1)S(1)}, bf16[128,384]{1,0:T(8,128)(2,1)S(1)}) custom-call(f32[384,384]{1,0:T(8,128)S(1)} %get-tuple-element.49.base, bf16[384,512]{1,0:T(8,128)(2,1)S(1)} %get-tuple-element.50.left_outer, bf16[512,384]{1,0:T(8,128)(2,1)S(1)} %collective-permute-done.6.outer_r), custom_call_target="tpu_custom_call" | custom-call | flops 150994944 | bytes 1769472 | tf_op jit(solution)/shard_map/near_tile/pallas_call | solution.py:29
  27.5 1.8 %collective-permute-start.11 = (bf16[128,384]{1,0:T(8,128)(2,1)S(1)}, bf16[128,384]{1,0:T(8,128)(2,1)S(1)}, u32[]{:S(2)}, u32[]{:S(2)}) collective-permute-start(bf16[128,384]{1,0:T(8,128)(2,1)S(1)} %get-tuple-element.53), channel_id=1, source_target_pairs={{0,28},{4,8},{8,4},{12,16},{16,12},{20,24},{24,20},{28,0},{1,29},{... | collective-permute-start | bytes 294920 | tf_op jit(solution)/shard_map/ppermute | solution.py:245
  29.3 0.0 collective-permute-start.9
  29.3 0.8 %add_own.1.refs_9_ = f32[5,128,512]{2,1,0:T(8,128)} custom-call(bf16[128,384]{1,0:T(8,128)(2,1)S(1)} %collective-permute-done.5.refs_0_, bf16[128,384]{1,0:T(8,128)(2,1)S(1)} %collective-permute-done.7.refs_1_, f32[128,384]{1,0:T(8,128)S(1)} %get-tuple-element.58.refs_2_), custom_call_target="tpu_custom_call" | custom-call | flops 81920 | bytes 1703936 | tf_op jit(solution)/shard_map/add_own/pallas_call | solution.py:29
  30.1 4.0 %collective-permute-done.11.refs_4_ = bf16[128,384]{1,0:T(8,128)(2,1)S(1)} collective-permute-done((bf16[128,384]{1,0:T(8,128)(2,1)S(1)}, bf16[128,384]{1,0:T(8,128)(2,1)S(1)}, u32[]{:S(2)}, u32[]{:S(2)}) %collective-permute-start.11) | collective-permute-done | bytes 98336 | tf_op jit(solution)/shard_map/ppermute | solution.py:245
  34.1 1.0 %add_rest.1 = f32[5,128,512]{2,1,0:T(8,128)} custom-call(bf16[128,768]{1,0:T(8,128)(2,1)S(1)} %collective-permute-done.8.refs_0_.refs_2_, bf16[128,384]{1,0:T(8,128)(2,1)S(1)} %collective-permute-done.9.refs_1_, bf16[128,768]{1,0:T(8,128)(2,1)S(1)} %collective-permute-done.8.refs_0_.refs_2_, ...), custom_call_target="tpu_custom_call", output_to_operand_aliasing={{}: (9, {})} | custom-call | flops 245760 | bytes 4194304 | tf_op jit(solution)/shard_map/add_rest/pallas_call | solution.py:29
  (16 shorter events, 0.0 us)
Async XLA Ops:
  0.0 12.2 %copy-start.1 = (s32[8,3]{0,1:T(4,128)S(1)}, s32[8,3]{0,1:T(4,128)}, u32[]{:S(2)}) copy-start(s32[8,3]{0,1:T(4,128)} %param.5) | copy-start | bytes 292
  0.0 12.2 %copy-start = (bf16[8,3,128,128]{3,2,1,0:T(8,128)(2,1)S(1)}, bf16[8,3,128,128]{3,2,1,0:T(8,128)(2,1)}, u32[]{:S(2)}) copy-start(bf16[8,3,128,128]{3,2,1,0:T(8,128)(2,1)} %stiffness.1) | copy-start | bytes 2359300
  0.0 21.6 %collective-permute-start = (bf16[1024,3,128]{2,0,1:T(8,128)(2,1)}, bf16[1024,3,128]{2,0,1:T(8,128)(2,1)S(1)}, u32[]{:S(2)}, u32[]{:S(2)}) collective-permute-start(bf16[1024,3,128]{2,0,1:T(8,128)(2,1)} %param.6), channel_id=1, source_target_pairs={{0,1},{1,0},{2,3},{3,2},{4,6},{5,7},{6,4},{7,5},{8,9},{9,8},{10,11... | collective-permute-start | bytes 2359304 | tf_op jit(solution)/shard_map/ppermute | solution.py:249
  4.8 7.4 %collective-permute-start.2 = (bf16[256,256]{1,0:T(8,128)(2,1)S(1)}, bf16[256,256]{1,0:T(8,128)(2,1)S(1)}, u32[]{:S(2)}, u32[]{:S(2)}) collective-permute-start(bf16[256,256]{1,0:T(8,128)(2,1)S(1)} %get-tuple-element.34), channel_id=1, source_target_pairs={{0,28},{4,8},{8,4},{12,16},{16,12},{20,24},{24,20},{28,0},{1,29},{... | collective-permute-start | bytes 393224 | tf_op jit(solution)/shard_map/ppermute | solution.py:245
  7.6 4.5 %collective-permute-start.3 = (bf16[256,256]{1,0:T(8,128)(2,1)S(1)}, bf16[256,256]{1,0:T(8,128)(2,1)S(1)}, u32[]{:S(2)}, u32[]{:S(2)}) collective-permute-start(bf16[256,256]{1,0:T(8,128)(2,1)S(1)} %get-tuple-element.35), channel_id=1, source_target_pairs={{0,4},{4,0},{8,12},{12,8},{16,20},{20,16},{24,28},{28,24},{1,5},{5... | collective-permute-start | bytes 393224 | tf_op jit(solution)/shard_map/ppermute | solution.py:242
  7.6 10.2 %collective-permute-start.4 = (bf16[512,384]{1,0:T(8,128)(2,1)S(1)}, bf16[512,384]{1,0:T(8,128)(2,1)S(1)}, u32[]{:S(2)}, u32[]{:S(2)}) collective-permute-start(bf16[512,384]{1,0:T(8,128)(2,1)S(1)} %get-tuple-element.32.inner), channel_id=1, source_target_pairs={{0,2},{1,3},{2,0},{3,1},{4,5},{5,4},{6,7},{7,6},{8,10},{9,11},{10,... | collective-permute-start | bytes 1179656 | tf_op jit(solution)/shard_map/ppermute | solution.py:249
  13.3 4.5 %copy-start.2 = (s32[8,128,2]{1,2,0:T(2,128)S(1)}, s32[8,128,2]{1,2,0:T(2,128)}, u32[]{:S(2)}) copy-start(s32[8,128,2]{1,2,0:T(2,128)} %param.7) | copy-start | bytes 24580
  13.3 9.6 %collective-permute-start.6 = (bf16[512,384]{1,0:T(8,128)(2,1)S(1)}, bf16[512,384]{1,0:T(8,128)(2,1)S(1)}, u32[]{:S(2)}, u32[]{:S(2)}) collective-permute-start(bf16[512,384]{1,0:T(8,128)(2,1)S(1)} %outer_image.1.outer), channel_id=1, source_target_pairs={{0,2},{1,3},{2,0},{3,1},{4,5},{5,4},{6,7},{7,6},{8,10},{9,11},{10,... | collective-permute-start | bytes 1179656 | tf_op jit(solution)/shard_map/ppermute | solution.py:249
  15.5 2.3 %collective-permute-start.5 = (bf16[128,384]{1,0:T(8,128)(2,1)S(1)}, bf16[128,384]{1,0:T(8,128)(2,1)S(1)}, u32[]{:S(2)}, u32[]{:S(2)}) collective-permute-start(bf16[128,384]{1,0:T(8,128)(2,1)S(1)} %get-tuple-element.37), channel_id=1, source_target_pairs={{0,4},{4,0},{8,12},{12,8},{16,20},{20,16},{24,28},{28,24},{1,5},{5... | collective-permute-start | bytes 294920 | tf_op jit(solution)/shard_map/ppermute | solution.py:242
  15.6 7.3 %collective-permute-start.7 = (bf16[128,384]{1,0:T(8,128)(2,1)S(1)}, bf16[128,384]{1,0:T(8,128)(2,1)S(1)}, u32[]{:S(2)}, u32[]{:S(2)}) collective-permute-start(bf16[128,384]{1,0:T(8,128)(2,1)S(1)} %get-tuple-element.42), channel_id=1, source_target_pairs={{0,28},{4,8},{8,4},{12,16},{16,12},{20,24},{24,20},{28,0},{1,29},{... | collective-permute-start | bytes 294920 | tf_op jit(solution)/shard_map/ppermute | solution.py:245
  17.8 3.8 %collective-permute-start.1 = (s32[8,128,2]{1,2,0:T(2,128)S(1)}, s32[8,128,2]{1,2,0:T(2,128)S(1)}, u32[]{:S(2)}, u32[]{:S(2)}) collective-permute-start(s32[8,128,2]{1,2,0:T(2,128)S(1)} %copy-done.2), channel_id=1, source_target_pairs={{0,1},{1,0},{2,3},{3,2},{4,6},{5,7},{6,4},{7,5},{8,9},{9,8},{10,11... | collective-permute-start | bytes 24584 | tf_op jit(solution)/shard_map/ppermute | solution.py:249
  23.3 10.8 %collective-permute-start.10 = (bf16[128,768]{1,0:T(8,128)(2,1)S(1)}, bf16[128,768]{1,0:T(8,128)(2,1)S(1)}, u32[]{:S(2)}, u32[]{:S(2)}) collective-permute-start(bf16[128,768]{1,0:T(8,128)(2,1)S(1)} %get-tuple-element.52), channel_id=1, source_target_pairs={{0,29},{1,28},{2,31},{3,30},{4,10},{5,11},{6,8},{7,9},{8,5},{9,4},... | collective-permute-start | bytes 589832 | tf_op jit(solution)/shard_map/ppermute | solution.py:249
  26.6 7.5 %collective-permute-start.12 = (bf16[128,768]{1,0:T(8,128)(2,1)S(1)}, bf16[128,768]{1,0:T(8,128)(2,1)S(1)}, u32[]{:S(2)}, u32[]{:S(2)}) collective-permute-start(bf16[128,768]{1,0:T(8,128)(2,1)S(1)} %get-tuple-element.54), channel_id=1, source_target_pairs={{0,1},{1,0},{2,3},{3,2},{4,6},{5,7},{6,4},{7,5},{8,9},{9,8},{10,11... | collective-permute-start | bytes 589832 | tf_op jit(solution)/shard_map/ppermute | solution.py:249
  27.1 7.0 %collective-permute-start.8 = (bf16[128,768]{1,0:T(8,128)(2,1)S(1)}, bf16[128,768]{1,0:T(8,128)(2,1)S(1)}, u32[]{:S(2)}, u32[]{:S(2)}) collective-permute-start(bf16[128,768]{1,0:T(8,128)(2,1)S(1)} %get-tuple-element.48), channel_id=1, source_target_pairs={{0,5},{1,4},{2,7},{3,6},{4,2},{5,3},{6,0},{7,1},{8,13},{9,12},{10,... | collective-permute-start | bytes 589832 | tf_op jit(solution)/shard_map/ppermute | solution.py:249
  27.5 6.5 %collective-permute-start.11 = (bf16[128,384]{1,0:T(8,128)(2,1)S(1)}, bf16[128,384]{1,0:T(8,128)(2,1)S(1)}, u32[]{:S(2)}, u32[]{:S(2)}) collective-permute-start(bf16[128,384]{1,0:T(8,128)(2,1)S(1)} %get-tuple-element.53), channel_id=1, source_target_pairs={{0,28},{4,8},{8,4},{12,16},{16,12},{20,24},{24,20},{28,0},{1,29},{... | collective-permute-start | bytes 294920 | tf_op jit(solution)/shard_map/ppermute | solution.py:245
  29.3 4.8 %collective-permute-start.9 = (bf16[128,384]{1,0:T(8,128)(2,1)S(1)}, bf16[128,384]{1,0:T(8,128)(2,1)S(1)}, u32[]{:S(2)}, u32[]{:S(2)}) collective-permute-start(bf16[128,384]{1,0:T(8,128)(2,1)S(1)} %get-tuple-element.51), channel_id=1, source_target_pairs={{0,4},{4,0},{8,12},{12,8},{16,20},{20,16},{24,28},{28,24},{1,5},{5... | collective-permute-start | bytes 294920 | tf_op jit(solution)/shard_map/ppermute | solution.py:242

commit v21 on v18

--- a/solution.py
+++ b/solution.py
@@ -204,7 +204,7 @@
     even = parity() == 0
     copies = []
     for n, ((even_step, odd_step), chunks) in enumerate(steps):
-        chip, link, own = (
+        own, chip, link = (
             terms[n + k * count][:, m * 3 * width : (m + 1) * 3 * width].astype(F32) for k, m in enumerate(chunks)
         )
         prev = jnp.where(even, link, chip)
@@ -364,10 +364,10 @@
             name=name,
         )
 
-    coarse = add((((0, 0), (0, 0, 0)),), (own_chip, own_link, own), "add_own")
+    coarse = add((((0, 0), (0, 0, 0)),), (own, own_chip, own_link), "add_own")
     coarse = add(
         (((3, 3), (1, 1, 1)), ((1, 2), (0, 0, 0)), ((2, 1), (0, 0, 0))),
-        (far_chip, near_chip, far_chip, far_link, near_link, far_link, far, far, near),
+        (far, far, near, far_chip, near_chip, far_chip, far_link, near_link, far_link),
         "add_rest",
         coarse,
     )

time: 35.1 us -> 36.3 us (1.034)
  waiting for transfers between devices: 11.2 us -> 12.4 us
    ppermute x3, starting transfers between devices: 0.03 us -> 1.7 us  [over_chip(): return lax.ppermute(value, 'blk', pairs)]
    ppermute x3, starting transfers between devices: 5.73 us -> 4.12 us  [over_link(): return lax.ppermute(value, 'blk', cross)]
    ppermute x3, waiting for transfers between devices: 9.73 us -> 10.9 us  [over_link(): return lax.ppermute(value, 'blk', cross)]
where the time goes in v21:
time: 36.3 us; the launch traced here: 36.1 us
  starting transfers between devices  16.1 us (44%)
  waiting for transfers between devices  12.4 us (34%)
  Pallas kernels  7.47 us (21%)
    ppermute x3, waiting for transfers between devices, over_link(): return lax.ppermute(value, 'blk', cross)  10.9 us
    ppermute x7, starting transfers between devices, to(): return lax.ppermute(value, ('blk', 'col'), perm)  10.3 us
    pallas_call x8, Pallas kernels, call(): pl.pallas_call(kernel, out_shape=out_shape, in_specs=in_specs, out_specs=...  7.47 us
    ppermute x3, starting transfers between devices, over_link(): return lax.ppermute(value, 'blk', cross)  4.12 us
    ppermute x3, starting transfers between devices, over_chip(): return lax.ppermute(value, 'blk', pairs)  1.7 us
    ppermute x7, waiting for transfers between devices, to(): return lax.ppermute(value, ('blk', 'col'), perm)  1.51 us
  transfers between devices with their start and end apart: 13, of which 4 were waited for; matrix products, arithmetic and copies ran while one was open for 0% of the time, Pallas kernels for 17%

profile of v21, /device:TPU:0, one launch (start us, length us, event | category | flops | bytes accessed | tf_op | source)
XLA Modules:
  0.0 36.1 jit_solution(6827463035440615215)
XLA Ops:
  0.0 2.9 %collective-permute-start = (bf16[1024,3,128]{2,0,1:T(8,128)(2,1)}, bf16[1024,3,128]{2,0,1:T(8,128)(2,1)S(1)}, u32[]{:S(2)}, u32[]{:S(2)}) collective-permute-start(bf16[1024,3,128]{2,0,1:T(8,128)(2,1)} %param.6), channel_id=1, source_target_pairs={{0,1},{1,0},{2,3},{3,2},{4,6},{5,7},{6,4},{7,5},{8,9},{9,8},{10,11... | collective-permute-start | bytes 2359304 | tf_op jit(solution)/shard_map/ppermute | solution.py:249
  2.9 1.8 %mask_and_inner.1 = (bf16[1024,384]{1,0:T(8,128)(2,1)S(1)}, bf16[256,256]{1,0:T(8,128)(2,1)S(1)}, bf16[256,256]{1,0:T(8,128)(2,1)S(1)}, bf16[512,384]{1,0:T(8,128)(2,1)S(1)}) custom-call(s32[3,8]{1,0:T(4,128)} %bitcast.8, bf16[3,1024,128]{2,1,0:T(8,128)(2,1)} %bitcast.10, s32[8,2,128]{2,1,0:T(2,128)} %bitcast.11, bf16[8,3,128,128]{3,2,1,0:T(8,128)(2,1)} %stiffness.1), custom_call_target="tpu_custom_call" | custom-call | flops 150994944 | bytes 3022944 | tf_op jit(solution)/shard_map/mask_and_inner/pallas_call | solution.py:29
  4.8 0.0 copy-start.2
  4.8 2.9 %collective-permute-start.2 = (bf16[256,256]{1,0:T(8,128)(2,1)S(1)}, bf16[256,256]{1,0:T(8,128)(2,1)S(1)}, u32[]{:S(2)}, u32[]{:S(2)}) collective-permute-start(bf16[256,256]{1,0:T(8,128)(2,1)S(1)} %get-tuple-element.32), channel_id=1, source_target_pairs={{0,28},{4,8},{8,4},{12,16},{16,12},{20,24},{24,20},{28,0},{1,29},{... | collective-permute-start | bytes 393224 | tf_op jit(solution)/shard_map/ppermute | solution.py:245
  7.7 0.5 %collective-permute-start.4 = (bf16[512,384]{1,0:T(8,128)(2,1)S(1)}, bf16[512,384]{1,0:T(8,128)(2,1)S(1)}, u32[]{:S(2)}, u32[]{:S(2)}) collective-permute-start(bf16[512,384]{1,0:T(8,128)(2,1)S(1)} %get-tuple-element.30.inner), channel_id=1, source_target_pairs={{0,2},{1,3},{2,0},{3,1},{4,5},{5,4},{6,7},{7,6},{8,10},{9,11},{10,... | collective-permute-start | bytes 1179656 | tf_op jit(solution)/shard_map/ppermute | solution.py:249
  8.2 4.0 %collective-permute-done.2.from_link = bf16[256,256]{1,0:T(8,128)(2,1)S(1)} collective-permute-done((bf16[256,256]{1,0:T(8,128)(2,1)S(1)}, bf16[256,256]{1,0:T(8,128)(2,1)S(1)}, u32[]{:S(2)}, u32[]{:S(2)}) %collective-permute-start.2) | collective-permute-done | bytes 131104 | tf_op jit(solution)/shard_map/ppermute | solution.py:245
  12.2 1.1 %outer_image.1.outer = bf16[512,384]{1,0:T(8,128)(2,1)S(1)} custom-call(s32[3,8]{1,0:T(4,128)S(1)} %bitcast.9, bf16[8,3,128,128]{3,2,1,0:T(8,128)(2,1)S(1)} %copy-done, bf16[1024,384]{1,0:T(8,128)(2,1)S(1)} %get-tuple-element.31.masked, bf16[256,256]{1,0:T(8,128)(2,1)S(1)} %collective-permute-done.2.from_link, ...), custom_call_target="tpu_custom_call" | custom-call | flops 150994944 | bytes 2228320 | tf_op jit(solution)/shard_map/outer_image/pallas_call | solution.py:29
  13.3 1.6 %collective-permute-start.5 = (bf16[512,384]{1,0:T(8,128)(2,1)S(1)}, bf16[512,384]{1,0:T(8,128)(2,1)S(1)}, u32[]{:S(2)}, u32[]{:S(2)}) collective-permute-start(bf16[512,384]{1,0:T(8,128)(2,1)S(1)} %outer_image.1.outer), channel_id=1, source_target_pairs={{0,2},{1,3},{2,0},{3,1},{4,5},{5,4},{6,7},{7,6},{8,10},{9,11},{10,... | collective-permute-start | bytes 1179656 | tf_op jit(solution)/shard_map/ppermute | solution.py:249
  14.9 0.5 %collective-permute-start.1 = (s32[8,128,2]{1,2,0:T(2,128)S(1)}, s32[8,128,2]{1,2,0:T(2,128)S(1)}, u32[]{:S(2)}, u32[]{:S(2)}) collective-permute-start(s32[8,128,2]{1,2,0:T(2,128)S(1)} %copy-done.2), channel_id=1, source_target_pairs={{0,1},{1,0},{2,3},{3,2},{4,6},{5,7},{6,4},{7,5},{8,9},{9,8},{10,11... | collective-permute-start | bytes 24584 | tf_op jit(solution)/shard_map/ppermute | solution.py:249
  15.4 0.6 %own_tile.1 = (f32[128,384]{1,0:T(8,128)S(1)}, bf16[128,384]{1,0:T(8,128)(2,1)S(1)}, bf16[128,384]{1,0:T(8,128)(2,1)S(1)}, bf16[384,512]{1,0:T(8,128)(2,1)S(1)}, bf16[384,512]{1,0:T(8,128)(2,1)S(1)}) custom-call(bf16[1024,384]{1,0:T(8,128)(2,1)S(1)} %get-tuple-element.31.masked, bf16[512,384]{1,0:T(8,128)(2,1)S(1)} %get-tuple-element.30.inner, ...), custom_call_target="tpu_custom_call" | custom-call | flops 301989888 | bytes 2752512 | tf_op jit(solution)/shard_map/own_tile/pallas_call | solution.py:29
  16.1 1.1 %collective-permute-start.6 = (bf16[128,384]{1,0:T(8,128)(2,1)S(1)}, bf16[128,384]{1,0:T(8,128)(2,1)S(1)}, u32[]{:S(2)}, u32[]{:S(2)}) collective-permute-start(bf16[128,384]{1,0:T(8,128)(2,1)S(1)} %get-tuple-element.38), channel_id=1, source_target_pairs={{0,28},{4,8},{8,4},{12,16},{16,12},{20,24},{24,20},{28,0},{1,29},{... | collective-permute-start | bytes 294920 | tf_op jit(solution)/shard_map/ppermute | solution.py:245
  17.2 1.5 %collective-permute-done.1 = s32[8,128,2]{1,2,0:T(2,128)S(1)} collective-permute-done((s32[8,128,2]{1,2,0:T(2,128)S(1)}, s32[8,128,2]{1,2,0:T(2,128)S(1)}, u32[]{:S(2)}, u32[]{:S(2)}) %collective-permute-start.1) | collective-permute-done | bytes 8224 | tf_op jit(solution)/shard_map/ppermute | solution.py:249
  18.7 1.3 %partner_tile.1 = (bf16[128,384]{1,0:T(8,128)(2,1)S(1)}, bf16[128,384]{1,0:T(8,128)(2,1)S(1)}, bf16[128,384]{1,0:T(8,128)(2,1)S(1)}, bf16[384,512]{1,0:T(8,128)(...) custom-call(bf16[3,1024,128]{2,1,0:T(8,128)(2,1)S(1)} %bitcast.6, s32[8,2,128]{2,1,0:T(2,128)S(1)} %bitcast.7, ...), custom_call_target="tpu_custom_call" | custom-call | flops 603979776 | bytes 4235264 | tf_op jit(solution)/shard_map/partner_tile/pallas_call | solution.py:29
  20.0 2.0 %collective-permute-done.6.refs_2_ = bf16[128,384]{1,0:T(8,128)(2,1)S(1)} collective-permute-done((bf16[128,384]{1,0:T(8,128)(2,1)S(1)}, bf16[128,384]{1,0:T(8,128)(2,1)S(1)}, u32[]{:S(2)}, u32[]{:S(2)}) %collective-permute-start.6) | collective-permute-done | bytes 98336 | tf_op jit(solution)/shard_map/ppermute | solution.py:245
  22.0 0.4 %far_tile.1 = (bf16[128,768]{1,0:T(8,128)(2,1)S(1)}, bf16[128,768]{1,0:T(8,128)(2,1)S(1)}, bf16[128,768]{1,0:T(8,128)(2,1)S(1)}) custom-call(bf16[128,384]{1,0:T(8,128)(2,1)S(1)} %get-tuple-element.35.part, bf16[128,384]{1,0:T(8,128)(2,1)S(1)} %get-tuple-element.36.part_link, bf16[128,384]{1,0:T(8,128)(2,1)S(1)} %get-tuple-element.37.part_chip, ...), custom_call_target="tpu_custom_call" | custom-call | flops 150994944 | bytes 2260992 | tf_op jit(solution)/shard_map/far_tile/pallas_call | solution.py:29
  22.4 4.2 %collective-permute-start.11 = (bf16[128,768]{1,0:T(8,128)(2,1)S(1)}, bf16[128,768]{1,0:T(8,128)(2,1)S(1)}, u32[]{:S(2)}, u32[]{:S(2)}) collective-permute-start(bf16[128,768]{1,0:T(8,128)(2,1)S(1)} %get-tuple-element.50), channel_id=1, source_target_pairs={{0,29},{1,28},{2,31},{3,30},{4,10},{5,11},{6,8},{7,9},{8,5},{9,4},... | collective-permute-start | bytes 589832 | tf_op jit(solution)/shard_map/ppermute | solution.py:249
  26.6 0.5 %collective-permute-start.8 = (bf16[128,768]{1,0:T(8,128)(2,1)S(1)}, bf16[128,768]{1,0:T(8,128)(2,1)S(1)}, u32[]{:S(2)}, u32[]{:S(2)}) collective-permute-start(bf16[128,768]{1,0:T(8,128)(2,1)S(1)} %get-tuple-element.44), channel_id=1, source_target_pairs={{0,1},{1,0},{2,3},{3,2},{4,6},{5,7},{6,4},{7,5},{8,9},{9,8},{10,11... | collective-permute-start | bytes 589832 | tf_op jit(solution)/shard_map/ppermute | solution.py:249
  27.1 0.4 %near_tile.1 = (f32[128,384]{1,0:T(8,128)S(1)}, bf16[128,384]{1,0:T(8,128)(2,1)S(1)}, bf16[128,384]{1,0:T(8,128)(2,1)S(1)}) custom-call(f32[384,384]{1,0:T(8,128)S(1)} %get-tuple-element.45.base, bf16[384,512]{1,0:T(8,128)(2,1)S(1)} %get-tuple-element.46.left_outer, bf16[512,384]{1,0:T(8,128)(2,1)S(1)} %collective-permute-done.5.outer_r), custom_call_target="tpu_custom_call" | custom-call | flops 150994944 | bytes 1769472 | tf_op jit(solution)/shard_map/near_tile/pallas_call | solution.py:29
  27.5 1.7 %collective-permute-start.10 = (bf16[128,384]{1,0:T(8,128)(2,1)S(1)}, bf16[128,384]{1,0:T(8,128)(2,1)S(1)}, u32[]{:S(2)}, u32[]{:S(2)}) collective-permute-start(bf16[128,384]{1,0:T(8,128)(2,1)S(1)} %get-tuple-element.49), channel_id=1, source_target_pairs={{0,4},{4,0},{8,12},{12,8},{16,20},{20,16},{24,28},{28,24},{1,5},{5... | collective-permute-start | bytes 294920 | tf_op jit(solution)/shard_map/ppermute | solution.py:242
  29.2 0.1 collective-permute-start.12
  29.4 0.8 %add_own.1.refs_9_ = f32[5,128,512]{2,1,0:T(8,128)} custom-call(f32[128,384]{1,0:T(8,128)S(1)} %get-tuple-element.52.refs_0_, bf16[128,384]{1,0:T(8,128)(2,1)S(1)} %collective-permute-done.7.refs_1_, bf16[128,384]{1,0:T(8,128)(2,1)S(1)} %collective-permute-done.6.refs_2_), custom_call_target="tpu_custom_call" | custom-call | flops 81920 | bytes 1703936 | tf_op jit(solution)/shard_map/add_own/pallas_call | solution.py:29
  30.2 0.0 collective-permute-done.10.refs_4_
  30.2 4.9 %collective-permute-done.12.refs_7_ = bf16[128,384]{1,0:T(8,128)(2,1)S(1)} collective-permute-done((bf16[128,384]{1,0:T(8,128)(2,1)S(1)}, bf16[128,384]{1,0:T(8,128)(2,1)S(1)}, u32[]{:S(2)}, u32[]{:S(2)}) %collective-permute-start.12) | collective-permute-done | bytes 98336 | tf_op jit(solution)/shard_map/ppermute | solution.py:245
  35.1 1.0 %add_rest.1 = f32[5,128,512]{2,1,0:T(8,128)} custom-call(bf16[128,768]{1,0:T(8,128)(2,1)S(1)} %collective-permute-done.8.refs_0_.refs_1_, bf16[128,768]{1,0:T(8,128)(2,1)S(1)} %collective-permute-done.8.refs_0_.refs_1_, f32[128,384]{1,0:T(8,128)S(1)} %get-tuple-element.47.refs_2_, ...), custom_call_target="tpu_custom_call", output_to_operand_aliasing={{}: (9, {})} | custom-call | flops 245760 | bytes 4194304 | tf_op jit(solution)/shard_map/add_rest/pallas_call | solution.py:29
  (16 shorter events, 0.0 us)
Async XLA Ops:
  0.0 12.2 %copy-start.1 = (s32[8,3]{0,1:T(4,128)S(1)}, s32[8,3]{0,1:T(4,128)}, u32[]{:S(2)}) copy-start(s32[8,3]{0,1:T(4,128)} %param.5) | copy-start | bytes 292
  0.0 12.2 %copy-start = (bf16[8,3,128,128]{3,2,1,0:T(8,128)(2,1)S(1)}, bf16[8,3,128,128]{3,2,1,0:T(8,128)(2,1)}, u32[]{:S(2)}) copy-start(bf16[8,3,128,128]{3,2,1,0:T(8,128)(2,1)} %stiffness.1) | copy-start | bytes 2359300
  0.0 18.7 %collective-permute-start = (bf16[1024,3,128]{2,0,1:T(8,128)(2,1)}, bf16[1024,3,128]{2,0,1:T(8,128)(2,1)S(1)}, u32[]{:S(2)}, u32[]{:S(2)}) collective-permute-start(bf16[1024,3,128]{2,0,1:T(8,128)(2,1)} %param.6), channel_id=1, source_target_pairs={{0,1},{1,0},{2,3},{3,2},{4,6},{5,7},{6,4},{7,5},{8,9},{9,8},{10,11... | collective-permute-start | bytes 2359304 | tf_op jit(solution)/shard_map/ppermute | solution.py:249
  4.8 10.1 %copy-start.2 = (s32[8,128,2]{1,2,0:T(2,128)S(1)}, s32[8,128,2]{1,2,0:T(2,128)}, u32[]{:S(2)}) copy-start(s32[8,128,2]{1,2,0:T(2,128)} %param.7) | copy-start | bytes 24580
  4.8 7.4 %collective-permute-start.2 = (bf16[256,256]{1,0:T(8,128)(2,1)S(1)}, bf16[256,256]{1,0:T(8,128)(2,1)S(1)}, u32[]{:S(2)}, u32[]{:S(2)}) collective-permute-start(bf16[256,256]{1,0:T(8,128)(2,1)S(1)} %get-tuple-element.32), channel_id=1, source_target_pairs={{0,28},{4,8},{8,4},{12,16},{16,12},{20,24},{24,20},{28,0},{1,29},{... | collective-permute-start | bytes 393224 | tf_op jit(solution)/shard_map/ppermute | solution.py:245
  7.7 4.5 %collective-permute-start.3 = (bf16[256,256]{1,0:T(8,128)(2,1)S(1)}, bf16[256,256]{1,0:T(8,128)(2,1)S(1)}, u32[]{:S(2)}, u32[]{:S(2)}) collective-permute-start(bf16[256,256]{1,0:T(8,128)(2,1)S(1)} %get-tuple-element.33), channel_id=1, source_target_pairs={{0,4},{4,0},{8,12},{12,8},{16,20},{20,16},{24,28},{28,24},{1,5},{5... | collective-permute-start | bytes 393224 | tf_op jit(solution)/shard_map/ppermute | solution.py:242
  7.7 11.1 %collective-permute-start.4 = (bf16[512,384]{1,0:T(8,128)(2,1)S(1)}, bf16[512,384]{1,0:T(8,128)(2,1)S(1)}, u32[]{:S(2)}, u32[]{:S(2)}) collective-permute-start(bf16[512,384]{1,0:T(8,128)(2,1)S(1)} %get-tuple-element.30.inner), channel_id=1, source_target_pairs={{0,2},{1,3},{2,0},{3,1},{4,5},{5,4},{6,7},{7,6},{8,10},{9,11},{10,... | collective-permute-start | bytes 1179656 | tf_op jit(solution)/shard_map/ppermute | solution.py:249
  13.3 8.7 %collective-permute-start.5 = (bf16[512,384]{1,0:T(8,128)(2,1)S(1)}, bf16[512,384]{1,0:T(8,128)(2,1)S(1)}, u32[]{:S(2)}, u32[]{:S(2)}) collective-permute-start(bf16[512,384]{1,0:T(8,128)(2,1)S(1)} %outer_image.1.outer), channel_id=1, source_target_pairs={{0,2},{1,3},{2,0},{3,1},{4,5},{5,4},{6,7},{7,6},{8,10},{9,11},{10,... | collective-permute-start | bytes 1179656 | tf_op jit(solution)/shard_map/ppermute | solution.py:249
  14.9 3.8 %collective-permute-start.1 = (s32[8,128,2]{1,2,0:T(2,128)S(1)}, s32[8,128,2]{1,2,0:T(2,128)S(1)}, u32[]{:S(2)}, u32[]{:S(2)}) collective-permute-start(s32[8,128,2]{1,2,0:T(2,128)S(1)} %copy-done.2), channel_id=1, source_target_pairs={{0,1},{1,0},{2,3},{3,2},{4,6},{5,7},{6,4},{7,5},{8,9},{9,8},{10,11... | collective-permute-start | bytes 24584 | tf_op jit(solution)/shard_map/ppermute | solution.py:249
  16.1 5.9 %collective-permute-start.6 = (bf16[128,384]{1,0:T(8,128)(2,1)S(1)}, bf16[128,384]{1,0:T(8,128)(2,1)S(1)}, u32[]{:S(2)}, u32[]{:S(2)}) collective-permute-start(bf16[128,384]{1,0:T(8,128)(2,1)S(1)} %get-tuple-element.38), channel_id=1, source_target_pairs={{0,28},{4,8},{8,4},{12,16},{16,12},{20,24},{24,20},{28,0},{1,29},{... | collective-permute-start | bytes 294920 | tf_op jit(solution)/shard_map/ppermute | solution.py:245
  18.7 3.3 %collective-permute-start.7 = (bf16[128,384]{1,0:T(8,128)(2,1)S(1)}, bf16[128,384]{1,0:T(8,128)(2,1)S(1)}, u32[]{:S(2)}, u32[]{:S(2)}) collective-permute-start(bf16[128,384]{1,0:T(8,128)(2,1)S(1)} %get-tuple-element.39), channel_id=1, source_target_pairs={{0,4},{4,0},{8,12},{12,8},{16,20},{20,16},{24,28},{28,24},{1,5},{5... | collective-permute-start | bytes 294920 | tf_op jit(solution)/shard_map/ppermute | solution.py:242
  22.4 12.7 %collective-permute-start.11 = (bf16[128,768]{1,0:T(8,128)(2,1)S(1)}, bf16[128,768]{1,0:T(8,128)(2,1)S(1)}, u32[]{:S(2)}, u32[]{:S(2)}) collective-permute-start(bf16[128,768]{1,0:T(8,128)(2,1)S(1)} %get-tuple-element.50), channel_id=1, source_target_pairs={{0,29},{1,28},{2,31},{3,30},{4,10},{5,11},{6,8},{7,9},{8,5},{9,4},... | collective-permute-start | bytes 589832 | tf_op jit(solution)/shard_map/ppermute | solution.py:249
  26.6 8.5 %collective-permute-start.8 = (bf16[128,768]{1,0:T(8,128)(2,1)S(1)}, bf16[128,768]{1,0:T(8,128)(2,1)S(1)}, u32[]{:S(2)}, u32[]{:S(2)}) collective-permute-start(bf16[128,768]{1,0:T(8,128)(2,1)S(1)} %get-tuple-element.44), channel_id=1, source_target_pairs={{0,1},{1,0},{2,3},{3,2},{4,6},{5,7},{6,4},{7,5},{8,9},{9,8},{10,11... | collective-permute-start | bytes 589832 | tf_op jit(solution)/shard_map/ppermute | solution.py:249
  27.1 7.9 %collective-permute-start.9 = (bf16[128,768]{1,0:T(8,128)(2,1)S(1)}, bf16[128,768]{1,0:T(8,128)(2,1)S(1)}, u32[]{:S(2)}, u32[]{:S(2)}) collective-permute-start(bf16[128,768]{1,0:T(8,128)(2,1)S(1)} %get-tuple-element.48), channel_id=1, source_target_pairs={{0,5},{1,4},{2,7},{3,6},{4,2},{5,3},{6,0},{7,1},{8,13},{9,12},{10,... | collective-permute-start | bytes 589832 | tf_op jit(solution)/shard_map/ppermute | solution.py:249
  27.5 2.6 %collective-permute-start.10 = (bf16[128,384]{1,0:T(8,128)(2,1)S(1)}, bf16[128,384]{1,0:T(8,128)(2,1)S(1)}, u32[]{:S(2)}, u32[]{:S(2)}) collective-permute-start(bf16[128,384]{1,0:T(8,128)(2,1)S(1)} %get-tuple-element.49), channel_id=1, source_target_pairs={{0,4},{4,0},{8,12},{12,8},{16,20},{20,16},{24,28},{28,24},{1,5},{5... | collective-permute-start | bytes 294920 | tf_op jit(solution)/shard_map/ppermute | solution.py:242
  29.2 5.8 %collective-permute-start.12 = (bf16[128,384]{1,0:T(8,128)(2,1)S(1)}, bf16[128,384]{1,0:T(8,128)(2,1)S(1)}, u32[]{:S(2)}, u32[]{:S(2)}) collective-permute-start(bf16[128,384]{1,0:T(8,128)(2,1)S(1)} %get-tuple-element.51), channel_id=1, source_target_pairs={{0,28},{4,8},{8,4},{12,16},{16,12},{20,24},{24,20},{28,0},{1,29},{... | collective-permute-start | bytes 294920 | tf_op jit(solution)/shard_map/ppermute | solution.py:245

commit v22 on v18

--- a/solution.py
+++ b/solution.py
@@ -315,6 +315,7 @@
         name="own_tile",
     )
     own_link, own_chip = over_link(own_link), over_chip(own_chip)
+    inner_r, own_link = lax.optimization_barrier((inner_r, own_link))
     part, part_link, part_chip, far_outer, far_base, near_base = call(
         functools.partial(partner_tile, size),
         (*tile_shapes(width, wide, BF16), left_shapes[1], base_shape, base_shape),

time: 35.1 us -> 36.9 us (1.051)
  waiting for transfers between devices: 11.2 us -> 14.5 us
  starting transfers between devices: 16.1 us -> 14.7 us
    ppermute x7, starting transfers between devices: 10.3 us -> 7.31 us  [to(): return lax.ppermute(value, ('blk', 'col'), perm)]
    ppermute x7, waiting for transfers between devices: 1.51 us -> 3.22 us  [to(): return lax.ppermute(value, ('blk', 'col'), perm)]
    ppermute x3, starting transfers between devices: 5.73 us -> 7.39 us  [over_link(): return lax.ppermute(value, 'blk', cross)]
    ppermute x3, waiting for transfers between devices: 9.73 us -> 11.2 us  [over_link(): return lax.ppermute(value, 'blk', cross)]
  transfers between devices with their start and end apart: 13 -> 13, of which waited for: 4 -> 5; matrix products, arithmetic and copies ran while one was open for 0% -> 0% of each run, Pallas kernels for 17% -> 16%
where the time goes in v22:
time: 36.9 us; the launch traced here: 36.8 us
  starting transfers between devices  14.7 us (40%)
  waiting for transfers between devices  14.5 us (39%)
  Pallas kernels  7.47 us (20%)
    ppermute x3, waiting for transfers between devices, over_link(): return lax.ppermute(value, 'blk', cross)  11.2 us
    pallas_call x8, Pallas kernels, call(): pl.pallas_call(kernel, out_shape=out_shape, in_specs=in_specs, out_specs=...  7.47 us
    ppermute x3, starting transfers between devices, over_link(): return lax.ppermute(value, 'blk', cross)  7.39 us
    ppermute x7, starting transfers between devices, to(): return lax.ppermute(value, ('blk', 'col'), perm)  7.31 us
    ppermute x7, waiting for transfers between devices, to(): return lax.ppermute(value, ('blk', 'col'), perm)  3.22 us
  transfers between devices with their start and end apart: 13, of which 5 were waited for; matrix products, arithmetic and copies ran while one was open for 0% of the time, Pallas kernels for 16%

profile of v22, /device:TPU:0, one launch (start us, length us, event | category | flops | bytes accessed | tf_op | source)
XLA Modules:
  0.0 36.8 jit_solution(5103988056230348920)
XLA Ops:
  0.0 2.9 %collective-permute-start = (bf16[1024,3,128]{2,0,1:T(8,128)(2,1)}, bf16[1024,3,128]{2,0,1:T(8,128)(2,1)S(1)}, u32[]{:S(2)}, u32[]{:S(2)}) collective-permute-start(bf16[1024,3,128]{2,0,1:T(8,128)(2,1)} %param.6), channel_id=1, source_target_pairs={{0,1},{1,0},{2,3},{3,2},{4,6},{5,7},{6,4},{7,5},{8,9},{9,8},{10,11... | collective-permute-start | bytes 2359304 | tf_op jit(solution)/shard_map/ppermute | solution.py:249
  2.9 1.8 %mask_and_inner.1 = (bf16[1024,384]{1,0:T(8,128)(2,1)S(1)}, bf16[256,256]{1,0:T(8,128)(2,1)S(1)}, bf16[256,256]{1,0:T(8,128)(2,1)S(1)}, bf16[512,384]{1,0:T(8,128)(2,1)S(1)}) custom-call(s32[3,8]{1,0:T(4,128)} %bitcast.8, bf16[3,1024,128]{2,1,0:T(8,128)(2,1)} %bitcast.10, s32[8,2,128]{2,1,0:T(2,128)} %bitcast.11, bf16[8,3,128,128]{3,2,1,0:T(8,128)(2,1)} %stiffness.1), custom_call_target="tpu_custom_call" | custom-call | flops 150994944 | bytes 3022944 | tf_op jit(solution)/shard_map/mask_and_inner/pallas_call | solution.py:29
  4.8 2.9 %collective-permute-start.2 = (bf16[256,256]{1,0:T(8,128)(2,1)S(1)}, bf16[256,256]{1,0:T(8,128)(2,1)S(1)}, u32[]{:S(2)}, u32[]{:S(2)}) collective-permute-start(bf16[256,256]{1,0:T(8,128)(2,1)S(1)} %get-tuple-element.34), channel_id=1, source_target_pairs={{0,28},{4,8},{8,4},{12,16},{16,12},{20,24},{24,20},{28,0},{1,29},{... | collective-permute-start | bytes 393224 | tf_op jit(solution)/shard_map/ppermute | solution.py:245
  7.6 0.5 %collective-permute-start.4 = (bf16[512,384]{1,0:T(8,128)(2,1)S(1)}, bf16[512,384]{1,0:T(8,128)(2,1)S(1)}, u32[]{:S(2)}, u32[]{:S(2)}) collective-permute-start(bf16[512,384]{1,0:T(8,128)(2,1)S(1)} %get-tuple-element.32.inner), channel_id=1, source_target_pairs={{0,2},{1,3},{2,0},{3,1},{4,5},{5,4},{6,7},{7,6},{8,10},{9,11},{10,... | collective-permute-start | bytes 1179656 | tf_op jit(solution)/shard_map/ppermute | solution.py:249
  8.2 4.0 %collective-permute-done.2.from_link = bf16[256,256]{1,0:T(8,128)(2,1)S(1)} collective-permute-done((bf16[256,256]{1,0:T(8,128)(2,1)S(1)}, bf16[256,256]{1,0:T(8,128)(2,1)S(1)}, u32[]{:S(2)}, u32[]{:S(2)}) %collective-permute-start.2) | collective-permute-done | bytes 131104 | tf_op jit(solution)/shard_map/ppermute | solution.py:245
  12.2 0.0 collective-permute-done.3.from_chip
  12.2 1.1 %outer_image.1.outer = bf16[512,384]{1,0:T(8,128)(2,1)S(1)} custom-call(s32[3,8]{1,0:T(4,128)S(1)} %bitcast.9, bf16[8,3,128,128]{3,2,1,0:T(8,128)(2,1)S(1)} %copy-done, bf16[1024,384]{1,0:T(8,128)(2,1)S(1)} %get-tuple-element.33.masked, bf16[256,256]{1,0:T(8,128)(2,1)S(1)} %collective-permute-done.2.from_link, ...), custom_call_target="tpu_custom_call" | custom-call | flops 150994944 | bytes 2228320 | tf_op jit(solution)/shard_map/outer_image/pallas_call | solution.py:29
  13.3 0.0 copy-start.2
  13.3 1.6 %collective-permute-start.6 = (bf16[512,384]{1,0:T(8,128)(2,1)S(1)}, bf16[512,384]{1,0:T(8,128)(2,1)S(1)}, u32[]{:S(2)}, u32[]{:S(2)}) collective-permute-start(bf16[512,384]{1,0:T(8,128)(2,1)S(1)} %outer_image.1.outer), channel_id=1, source_target_pairs={{0,2},{1,3},{2,0},{3,1},{4,5},{5,4},{6,7},{7,6},{8,10},{9,11},{10,... | collective-permute-start | bytes 1179656 | tf_op jit(solution)/shard_map/ppermute | solution.py:249
  14.9 0.6 %own_tile.1 = (f32[128,384]{1,0:T(8,128)S(1)}, bf16[128,384]{1,0:T(8,128)(2,1)S(1)}, bf16[128,384]{1,0:T(8,128)(2,1)S(1)}, bf16[384,512]{1,0:T(8,128)(2,1)S(1)}, bf16[384,512]{1,0:T(8,128)(2,1)S(1)}) custom-call(bf16[1024,384]{1,0:T(8,128)(2,1)S(1)} %get-tuple-element.33.masked, bf16[512,384]{1,0:T(8,128)(2,1)S(1)} %get-tuple-element.32.inner, ...), custom_call_target="tpu_custom_call" | custom-call | flops 301989888 | bytes 2752512 | tf_op jit(solution)/shard_map/own_tile/pallas_call | solution.py:29
  15.5 1.4 %collective-permute-start.5 = (bf16[128,384]{1,0:T(8,128)(2,1)S(1)}, bf16[128,384]{1,0:T(8,128)(2,1)S(1)}, u32[]{:S(2)}, u32[]{:S(2)}) collective-permute-start(bf16[128,384]{1,0:T(8,128)(2,1)S(1)} %get-tuple-element.37), channel_id=1, source_target_pairs={{0,28},{4,8},{8,4},{12,16},{16,12},{20,24},{24,20},{28,0},{1,29},{... | collective-permute-start | bytes 294920 | tf_op jit(solution)/shard_map/ppermute | solution.py:245
  16.9 4.5 %collective-permute-done.5.refs_1_ = bf16[128,384]{1,0:T(8,128)(2,1)S(1)} collective-permute-done((bf16[128,384]{1,0:T(8,128)(2,1)S(1)}, bf16[128,384]{1,0:T(8,128)(2,1)S(1)}, u32[]{:S(2)}, u32[]{:S(2)}) %collective-permute-start.5) | collective-permute-done | bytes 98336 | tf_op jit(solution)/shard_map/ppermute | solution.py:245
  21.4 0.5 %collective-permute-start.1 = (s32[8,128,2]{1,2,0:T(2,128)S(1)}, s32[8,128,2]{1,2,0:T(2,128)S(1)}, u32[]{:S(2)}, u32[]{:S(2)}) collective-permute-start(s32[8,128,2]{1,2,0:T(2,128)S(1)} %copy-done.2), channel_id=1, source_target_pairs={{0,1},{1,0},{2,3},{3,2},{4,6},{5,7},{6,4},{7,5},{8,9},{9,8},{10,11... | collective-permute-start | bytes 24584 | tf_op jit(solution)/shard_map/ppermute | solution.py:249
  22.0 3.1 %collective-permute-done.1 = s32[8,128,2]{1,2,0:T(2,128)S(1)} collective-permute-done((s32[8,128,2]{1,2,0:T(2,128)S(1)}, s32[8,128,2]{1,2,0:T(2,128)S(1)}, u32[]{:S(2)}, u32[]{:S(2)}) %collective-permute-start.1) | collective-permute-done | bytes 8224 | tf_op jit(solution)/shard_map/ppermute | solution.py:249
  25.1 1.3 %partner_tile.1 = (bf16[128,384]{1,0:T(8,128)(2,1)S(1)}, bf16[128,384]{1,0:T(8,128)(2,1)S(1)}, bf16[128,384]{1,0:T(8,128)(2,1)S(1)}, bf16[384,512]{1,0:T(8,128)(...) custom-call(bf16[3,1024,128]{2,1,0:T(8,128)(2,1)S(1)} %bitcast.6, s32[8,2,128]{2,1,0:T(2,128)S(1)} %bitcast.7, ...), custom_call_target="tpu_custom_call" | custom-call | flops 603979776 | bytes 4235264 | tf_op jit(solution)/shard_map/partner_tile/pallas_call | solution.py:29
  26.4 0.4 %far_tile.1 = (bf16[128,768]{1,0:T(8,128)(2,1)S(1)}, bf16[128,768]{1,0:T(8,128)(2,1)S(1)}, bf16[128,768]{1,0:T(8,128)(2,1)S(1)}) custom-call(bf16[128,384]{1,0:T(8,128)(2,1)S(1)} %get-tuple-element.39.part, bf16[128,384]{1,0:T(8,128)(2,1)S(1)} %get-tuple-element.40.part_link, bf16[128,384]{1,0:T(8,128)(2,1)S(1)} %get-tuple-element.41.part_chip, ...), custom_call_target="tpu_custom_call" | custom-call | flops 150994944 | bytes 2260992 | tf_op jit(solution)/shard_map/far_tile/pallas_call | solution.py:29
  26.8 0.2 collective-permute-start.10
  27.0 1.5 %collective-permute-start.12 = (bf16[128,768]{1,0:T(8,128)(2,1)S(1)}, bf16[128,768]{1,0:T(8,128)(2,1)S(1)}, u32[]{:S(2)}, u32[]{:S(2)}) collective-permute-start(bf16[128,768]{1,0:T(8,128)(2,1)S(1)} %get-tuple-element.54), channel_id=1, source_target_pairs={{0,1},{1,0},{2,3},{3,2},{4,6},{5,7},{6,4},{7,5},{8,9},{9,8},{10,11... | collective-permute-start | bytes 589832 | tf_op jit(solution)/shard_map/ppermute | solution.py:249
  28.5 0.4 %near_tile.1 = (f32[128,384]{1,0:T(8,128)S(1)}, bf16[128,384]{1,0:T(8,128)(2,1)S(1)}, bf16[128,384]{1,0:T(8,128)(2,1)S(1)}) custom-call(f32[384,384]{1,0:T(8,128)S(1)} %get-tuple-element.49.base, bf16[384,512]{1,0:T(8,128)(2,1)S(1)} %get-tuple-element.50.left_outer, bf16[512,384]{1,0:T(8,128)(2,1)S(1)} %collective-permute-done.6.outer_r), custom_call_target="tpu_custom_call" | custom-call | flops 150994944 | bytes 1769472 | tf_op jit(solution)/shard_map/near_tile/pallas_call | solution.py:29
  28.9 3.1 %collective-permute-start.11 = (bf16[128,384]{1,0:T(8,128)(2,1)S(1)}, bf16[128,384]{1,0:T(8,128)(2,1)S(1)}, u32[]{:S(2)}, u32[]{:S(2)}) collective-permute-start(bf16[128,384]{1,0:T(8,128)(2,1)S(1)} %get-tuple-element.53), channel_id=1, source_target_pairs={{0,28},{4,8},{8,4},{12,16},{16,12},{20,24},{24,20},{28,0},{1,29},{... | collective-permute-start | bytes 294920 | tf_op jit(solution)/shard_map/ppermute | solution.py:245
  32.1 0.8 %add_own.1.refs_9_ = f32[5,128,512]{2,1,0:T(8,128)} custom-call(bf16[128,384]{1,0:T(8,128)(2,1)S(1)} %collective-permute-done.7.refs_0_, bf16[128,384]{1,0:T(8,128)(2,1)S(1)} %collective-permute-done.5.refs_1_, f32[128,384]{1,0:T(8,128)S(1)} %get-tuple-element.58.refs_2_), custom_call_target="tpu_custom_call" | custom-call | flops 81920 | bytes 1703936 | tf_op jit(solution)/shard_map/add_own/pallas_call | solution.py:29
  32.9 2.8 %collective-permute-done.11.refs_4_ = bf16[128,384]{1,0:T(8,128)(2,1)S(1)} collective-permute-done((bf16[128,384]{1,0:T(8,128)(2,1)S(1)}, bf16[128,384]{1,0:T(8,128)(2,1)S(1)}, u32[]{:S(2)}, u32[]{:S(2)}) %collective-permute-start.11) | collective-permute-done | bytes 98336 | tf_op jit(solution)/shard_map/ppermute | solution.py:245
  35.6 0.1 collective-permute-done.8.refs_0_.refs_2_
  35.7 1.0 %add_rest.1 = f32[5,128,512]{2,1,0:T(8,128)} custom-call(bf16[128,768]{1,0:T(8,128)(2,1)S(1)} %collective-permute-done.8.refs_0_.refs_2_, bf16[128,384]{1,0:T(8,128)(2,1)S(1)} %collective-permute-done.9.refs_1_, bf16[128,768]{1,0:T(8,128)(2,1)S(1)} %collective-permute-done.8.refs_0_.refs_2_, ...), custom_call_target="tpu_custom_call", output_to_operand_aliasing={{}: (9, {})} | custom-call | flops 245760 | bytes 4194304 | tf_op jit(solution)/shard_map/add_rest/pallas_call | solution.py:29
  (16 shorter events, 0.0 us)
Async XLA Ops:
  0.0 12.2 %copy-start.1 = (s32[8,3]{0,1:T(4,128)S(1)}, s32[8,3]{0,1:T(4,128)}, u32[]{:S(2)}) copy-start(s32[8,3]{0,1:T(4,128)} %param.5) | copy-start | bytes 292
  0.0 12.2 %copy-start = (bf16[8,3,128,128]{3,2,1,0:T(8,128)(2,1)S(1)}, bf16[8,3,128,128]{3,2,1,0:T(8,128)(2,1)}, u32[]{:S(2)}) copy-start(bf16[8,3,128,128]{3,2,1,0:T(8,128)(2,1)} %stiffness.1) | copy-start | bytes 2359300
  0.0 25.1 %collective-permute-start = (bf16[1024,3,128]{2,0,1:T(8,128)(2,1)}, bf16[1024,3,128]{2,0,1:T(8,128)(2,1)S(1)}, u32[]{:S(2)}, u32[]{:S(2)}) collective-permute-start(bf16[1024,3,128]{2,0,1:T(8,128)(2,1)} %param.6), channel_id=1, source_target_pairs={{0,1},{1,0},{2,3},{3,2},{4,6},{5,7},{6,4},{7,5},{8,9},{9,8},{10,11... | collective-permute-start | bytes 2359304 | tf_op jit(solution)/shard_map/ppermute | solution.py:249
  4.8 7.4 %collective-permute-start.2 = (bf16[256,256]{1,0:T(8,128)(2,1)S(1)}, bf16[256,256]{1,0:T(8,128)(2,1)S(1)}, u32[]{:S(2)}, u32[]{:S(2)}) collective-permute-start(bf16[256,256]{1,0:T(8,128)(2,1)S(1)} %get-tuple-element.34), channel_id=1, source_target_pairs={{0,28},{4,8},{8,4},{12,16},{16,12},{20,24},{24,20},{28,0},{1,29},{... | collective-permute-start | bytes 393224 | tf_op jit(solution)/shard_map/ppermute | solution.py:245
  7.6 4.5 %collective-permute-start.3 = (bf16[256,256]{1,0:T(8,128)(2,1)S(1)}, bf16[256,256]{1,0:T(8,128)(2,1)S(1)}, u32[]{:S(2)}, u32[]{:S(2)}) collective-permute-start(bf16[256,256]{1,0:T(8,128)(2,1)S(1)} %get-tuple-element.35), channel_id=1, source_target_pairs={{0,4},{4,0},{8,12},{12,8},{16,20},{20,16},{24,28},{28,24},{1,5},{5... | collective-permute-start | bytes 393224 | tf_op jit(solution)/shard_map/ppermute | solution.py:242
  7.6 14.3 %collective-permute-start.4 = (bf16[512,384]{1,0:T(8,128)(2,1)S(1)}, bf16[512,384]{1,0:T(8,128)(2,1)S(1)}, u32[]{:S(2)}, u32[]{:S(2)}) collective-permute-start(bf16[512,384]{1,0:T(8,128)(2,1)S(1)} %get-tuple-element.32.inner), channel_id=1, source_target_pairs={{0,2},{1,3},{2,0},{3,1},{4,5},{5,4},{6,7},{7,6},{8,10},{9,11},{10,... | collective-permute-start | bytes 1179656 | tf_op jit(solution)/shard_map/ppermute | solution.py:249
  13.3 8.1 %copy-start.2 = (s32[8,128,2]{1,2,0:T(2,128)S(1)}, s32[8,128,2]{1,2,0:T(2,128)}, u32[]{:S(2)}) copy-start(s32[8,128,2]{1,2,0:T(2,128)} %param.7) | copy-start | bytes 24580
  13.3 13.1 %collective-permute-start.6 = (bf16[512,384]{1,0:T(8,128)(2,1)S(1)}, bf16[512,384]{1,0:T(8,128)(2,1)S(1)}, u32[]{:S(2)}, u32[]{:S(2)}) collective-permute-start(bf16[512,384]{1,0:T(8,128)(2,1)S(1)} %outer_image.1.outer), channel_id=1, source_target_pairs={{0,2},{1,3},{2,0},{3,1},{4,5},{5,4},{6,7},{7,6},{8,10},{9,11},{10,... | collective-permute-start | bytes 1179656 | tf_op jit(solution)/shard_map/ppermute | solution.py:249
  15.5 5.9 %collective-permute-start.5 = (bf16[128,384]{1,0:T(8,128)(2,1)S(1)}, bf16[128,384]{1,0:T(8,128)(2,1)S(1)}, u32[]{:S(2)}, u32[]{:S(2)}) collective-permute-start(bf16[128,384]{1,0:T(8,128)(2,1)S(1)} %get-tuple-element.37), channel_id=1, source_target_pairs={{0,28},{4,8},{8,4},{12,16},{16,12},{20,24},{24,20},{28,0},{1,29},{... | collective-permute-start | bytes 294920 | tf_op jit(solution)/shard_map/ppermute | solution.py:245
  16.9 9.4 %collective-permute-start.7 = (bf16[128,384]{1,0:T(8,128)(2,1)S(1)}, bf16[128,384]{1,0:T(8,128)(2,1)S(1)}, u32[]{:S(2)}, u32[]{:S(2)}) collective-permute-start(bf16[128,384]{1,0:T(8,128)(2,1)S(1)} %get-tuple-element.43), channel_id=1, source_target_pairs={{0,4},{4,0},{8,12},{12,8},{16,20},{20,16},{24,28},{28,24},{1,5},{5... | collective-permute-start | bytes 294920 | tf_op jit(solution)/shard_map/ppermute | solution.py:242
  21.4 3.7 %collective-permute-start.1 = (s32[8,128,2]{1,2,0:T(2,128)S(1)}, s32[8,128,2]{1,2,0:T(2,128)S(1)}, u32[]{:S(2)}, u32[]{:S(2)}) collective-permute-start(s32[8,128,2]{1,2,0:T(2,128)S(1)} %copy-done.2), channel_id=1, source_target_pairs={{0,1},{1,0},{2,3},{3,2},{4,6},{5,7},{6,4},{7,5},{8,9},{9,8},{10,11... | collective-permute-start | bytes 24584 | tf_op jit(solution)/shard_map/ppermute | solution.py:249
  26.8 8.8 %collective-permute-start.10 = (bf16[128,768]{1,0:T(8,128)(2,1)S(1)}, bf16[128,768]{1,0:T(8,128)(2,1)S(1)}, u32[]{:S(2)}, u32[]{:S(2)}) collective-permute-start(bf16[128,768]{1,0:T(8,128)(2,1)S(1)} %get-tuple-element.52), channel_id=1, source_target_pairs={{0,29},{1,28},{2,31},{3,30},{4,10},{5,11},{6,8},{7,9},{8,5},{9,4},... | collective-permute-start | bytes 589832 | tf_op jit(solution)/shard_map/ppermute | solution.py:249
  27.0 8.6 %collective-permute-start.12 = (bf16[128,768]{1,0:T(8,128)(2,1)S(1)}, bf16[128,768]{1,0:T(8,128)(2,1)S(1)}, u32[]{:S(2)}, u32[]{:S(2)}) collective-permute-start(bf16[128,768]{1,0:T(8,128)(2,1)S(1)} %get-tuple-element.54), channel_id=1, source_target_pairs={{0,1},{1,0},{2,3},{3,2},{4,6},{5,7},{6,4},{7,5},{8,9},{9,8},{10,11... | collective-permute-start | bytes 589832 | tf_op jit(solution)/shard_map/ppermute | solution.py:249
  28.5 7.2 %collective-permute-start.8 = (bf16[128,768]{1,0:T(8,128)(2,1)S(1)}, bf16[128,768]{1,0:T(8,128)(2,1)S(1)}, u32[]{:S(2)}, u32[]{:S(2)}) collective-permute-start(bf16[128,768]{1,0:T(8,128)(2,1)S(1)} %get-tuple-element.48), channel_id=1, source_target_pairs={{0,5},{1,4},{2,7},{3,6},{4,2},{5,3},{6,0},{7,1},{8,13},{9,12},{10,... | collective-permute-start | bytes 589832 | tf_op jit(solution)/shard_map/ppermute | solution.py:249
  28.9 6.7 %collective-permute-start.11 = (bf16[128,384]{1,0:T(8,128)(2,1)S(1)}, bf16[128,384]{1,0:T(8,128)(2,1)S(1)}, u32[]{:S(2)}, u32[]{:S(2)}) collective-permute-start(bf16[128,384]{1,0:T(8,128)(2,1)S(1)} %get-tuple-element.53), channel_id=1, source_target_pairs={{0,28},{4,8},{8,4},{12,16},{16,12},{20,24},{24,20},{28,0},{1,29},{... | collective-permute-start | bytes 294920 | tf_op jit(solution)/shard_map/ppermute | solution.py:245
  32.1 3.6 %collective-permute-start.9 = (bf16[128,384]{1,0:T(8,128)(2,1)S(1)}, bf16[128,384]{1,0:T(8,128)(2,1)S(1)}, u32[]{:S(2)}, u32[]{:S(2)}) collective-permute-start(bf16[128,384]{1,0:T(8,128)(2,1)S(1)} %get-tuple-element.51), channel_id=1, source_target_pairs={{0,4},{4,0},{8,12},{12,8},{16,20},{20,16},{24,28},{28,24},{1,5},{5... | collective-permute-start | bytes 294920 | tf_op jit(solution)/shard_map/ppermute | solution.py:242
